TPU v7x, 32 devices: a whole 2x2x4 slice. The times are simulated.
32 devices in a mesh: section: 2 (over core), ctx: 4 (over z), fsdp: 4 (over y, x).
Axes of the slice: x: 2, y: 2, z: 4, core: 2. Of those that a mesh axis runs over, the one named last changes fastest.
Arguments:
- inputs: bfloat16 [8, 1024, 1024], P('fsdp', 'ctx'), may hold values from -6 to 6
- cotangent: bfloat16 [8, 1024, 1024], P('fsdp', 'ctx'), may hold values from -6 to 6
- lengths: int32 [8], replicated, may hold values from 512 to 1024, as said below
- norm_gains: float32 [4, 1024], replicated, may hold values from 0.5 to 1.5
- conv_in: bfloat16 [1024, 3072], P('fsdp'), may hold values from -0.1875 to 0.1875
- conv_kernel: float32 [3, 1024], replicated, may hold values from -3.5 to 3.5
- conv_out: bfloat16 [1024, 1024], P('fsdp'), may hold values from -0.1875 to 0.1875
- attn_q: bfloat16 [1024, 1024], P('fsdp'), may hold values from -0.1875 to 0.1875
- attn_k: bfloat16 [1024, 512], P('fsdp'), may hold values from -0.1875 to 0.1875
- attn_v: bfloat16 [1024, 512], P('fsdp'), may hold values from -0.1875 to 0.1875
- attn_out: bfloat16 [1024, 1024], P('fsdp'), may hold values from -6 to 6
- head_gains: float32 [2, 64], replicated, may hold values from 0.5 to 1.5
- ffn_gate: bfloat16 [2, 1024, 4608], P('section', 'fsdp'), may hold values from -0.1875 to 0.1875
- ffn_up: bfloat16 [2, 1024, 4608], P('section', 'fsdp'), may hold values from -0.1875 to 0.1875
- ffn_down: bfloat16 [2, 4608, 1024], P('section', 'fsdp'), may hold values from -0.09375 to 0.09375
Outputs:
- ends: bfloat16 [2, 8, 1024, 1024], P('section', 'fsdp', 'ctx')
- grad_norm_gains: float32 [3, 1024], P(None, 'fsdp')
- grad_ffn_norm: float32 [1024], P('fsdp')
- grad_conv_in: float32 [1024, 3072], P('fsdp')
- grad_conv_kernel: float32 [3, 1024], P(None, 'fsdp')
- grad_conv_out: float32 [1024, 1024], P('fsdp')
- grad_attn_q: float32 [1024, 1024], P('fsdp')
- grad_attn_k: float32 [1024, 512], P('fsdp')
- grad_attn_v: float32 [1024, 512], P('fsdp')
- grad_attn_out: float32 [1024, 1024], P('fsdp')
- grad_head_gains: float32 [2, 64], P(None, 'fsdp')
- grad_ffn_gate: float32 [2, 1024, 4608], P('section', 'fsdp')
- grad_ffn_up: float32 [2, 1024, 4608], P('section', 'fsdp')
- grad_ffn_down: float32 [2, 4608, 1024], P('section', 'fsdp')
- rms: float32 [8], P('fsdp')
Inputs may be any that keep to these rules, and one draw needn't show every extreme that they name: `lengths`: in each group of 2 consecutive sequences (those of one index of fsdp) one sequence has length 1024.
All inputs are finite; a program needn't handle non-finite values.
Results may differ from a plain program's by a relative error of at most 0.025.
Values may be sent and summed in bfloat16 or wider, within the bound.
A program may use at most 576 MiB of HBM per device.

v0:
```python
import jax
import jax.numpy as jnp
from jax import lax
from jax.sharding import PartitionSpec as P

EPSILON = 1e-05
NEGATIVE = -1e30


def passed_along(block, axis, distance):
    devices = range(lax.axis_size(axis))
    route = [(i - distance, i) for i in devices if i - distance in devices]
    return lax.ppermute(block, axis, route)


def rounded(values):
    return lax.optimization_barrier(values.astype(jnp.bfloat16)).astype(jnp.float32)


def matmul(left_op, right_op):
    return jnp.dot(left_op, right_op, preferred_element_type=jnp.float32)


def matmul_left(left_op, right_op):
    return lax.dot_general(
        left_op, right_op, (((0,), (0,)), ((), ())), preferred_element_type=jnp.float32
    )


def matmul_right(left_op, right_op):
    return lax.dot_general(
        left_op, right_op, (((1,), (1,)), ((), ())), preferred_element_type=jnp.float32
    )


def norm_rows(values):
    inv_rms = lax.rsqrt(jnp.mean(values * values, axis=-1, keepdims=True) + EPSILON)
    return (values * inv_rms, inv_rms)


def norm_back(dnormed, normed, inv_rms):
    return inv_rms * dnormed - normed * inv_rms * jnp.mean(dnormed * normed, axis=-1, keepdims=True)


def masked_square(row_mask, values):
    return jnp.sum(row_mask * values * values)


def fold_heads(values, kv_heads):
    key_rows, q_heads, head_size = values.shape
    return jnp.sum(
        values.reshape(key_rows, kv_heads, q_heads // kv_heads, head_size), axis=2
    ).reshape(key_rows, -1)


def ffn_forward(residual, norm_gain, w_gate, w_up, w_down):
    normed, inv_rms = norm_rows(residual)
    normed_low = (normed * norm_gain).astype(jnp.bfloat16)
    gate_pre = matmul(normed_low, w_gate)
    up_pre = matmul(normed_low, w_up)
    hidden = (jax.nn.silu(gate_pre) * up_pre).astype(jnp.bfloat16)
    return (matmul(hidden, w_down), (normed, inv_rms, normed_low, gate_pre, up_pre, hidden))


def ffn_backward(d_out, kept_values, norm_gain, w_gate, w_up, w_down):
    normed, inv_rms, normed_low, gate_pre, up_pre, hidden = kept_values
    d_low = d_out.astype(jnp.bfloat16)
    grad_down = matmul_left(hidden, d_low)
    d_hidden = matmul_right(d_low, w_down)
    sigmoid_gate = jax.nn.sigmoid(gate_pre)
    d_up = (d_hidden * gate_pre * sigmoid_gate).astype(jnp.bfloat16)
    d_gate = (d_hidden * up_pre * sigmoid_gate * (1.0 + gate_pre * (1.0 - sigmoid_gate))).astype(
        jnp.bfloat16
    )
    grad_gate = matmul_left(normed_low, d_gate)
    grad_up = matmul_left(normed_low, d_up)
    d_act = matmul_right(d_gate, w_gate) + matmul_right(d_up, w_up)
    grad_gain = jnp.sum(d_act * normed, axis=0)
    return (
        norm_back(d_act * norm_gain, normed, inv_rms),
        grad_gain,
        (grad_gate, grad_up, grad_down),
    )


def conv_head(x_rows, norm_gain, w_in):
    normed, inv_rms = norm_rows(x_rows)
    normed_low = (normed * norm_gain).astype(jnp.bfloat16)
    projected = matmul(normed_low, w_in)
    model_width = x_rows.shape[1]
    b_gate = projected[:, :model_width]
    c_gate = projected[:, model_width : 2 * model_width]
    x_value = projected[:, 2 * model_width :]
    b_product = (b_gate * x_value).astype(jnp.bfloat16)
    return (normed, inv_rms, normed_low, b_gate, c_gate, x_value, b_product)


def conv_tail(head, rim_rows, kernel, w_out):
    c_gate = head[4]
    b_product = head[6]
    extended = jnp.concatenate([rim_rows, b_product], axis=0).astype(jnp.float32)
    convolved = kernel[0] * extended[:-2] + kernel[1] * extended[1:-1] + kernel[2] * extended[2:]
    z_low = (c_gate * convolved).astype(jnp.bfloat16)
    return (matmul(z_low, w_out), extended, convolved, z_low)


def key_blocks(all_kv, span_rows, head_size):
    kv_width = all_kv.shape[1] // 2
    kv_heads = kv_width // head_size
    count_blocks = all_kv.shape[0] // span_rows
    key_stack = all_kv[:, :kv_width].reshape(count_blocks, span_rows, kv_heads, head_size)
    value_stack = all_kv[:, kv_width:].reshape(count_blocks, span_rows, kv_heads, head_size)
    starts = jnp.arange(count_blocks, dtype=jnp.int32) * span_rows
    return (key_stack, value_stack, starts)


def block_scores(query_low, key_block, start_at, positions, length):
    group_size = query_low.shape[1] // key_block.shape[1]
    key_rep = jnp.repeat(key_block, group_size, axis=1)
    head_scale = query_low.shape[2] ** (-0.5)
    scores = (
        jnp.einsum("qhd,khd->hqk", query_low, key_rep, preferred_element_type=jnp.float32)
        * head_scale
    )
    key_pos = start_at + jnp.arange(key_block.shape[0])
    allowed = (key_pos[None, :] <= positions[:, None]) & (key_pos[None, :] < length)
    return (scores, allowed[None], key_rep)


def attend(query_low, all_kv, positions, length):
    span_rows, q_heads, head_size = query_low.shape
    key_stack, value_stack, starts = key_blocks(all_kv, span_rows, head_size)
    group_size = q_heads // key_stack.shape[2]
    needed = (starts <= positions[-1]) & (starts < length)

    def max_step(carried, block_in):
        key_block, start_at, use_it = block_in

        def max_compute(running):
            running_max, running_sum = running
            scores, allowed, _ = block_scores(query_low, key_block, start_at, positions, length)
            new_max = jnp.maximum(
                running_max, jnp.max(jnp.where(allowed, scores, NEGATIVE), axis=-1)
            )
            weights = jnp.where(allowed, jnp.exp(scores - new_max[..., None]), 0.0)
            return (
                new_max,
                running_sum * jnp.exp(running_max - new_max) + jnp.sum(weights, axis=-1),
            )

        return (lax.cond(use_it, max_compute, lambda running: running, carried), None)

    start_state = (
        jnp.full((q_heads, span_rows), NEGATIVE, jnp.float32),
        jnp.zeros((q_heads, span_rows), jnp.float32),
    )
    (run_max, run_sum), _ = lax.scan(max_step, start_state, (key_stack, starts, needed))
    log_total = run_max + jnp.log(run_sum)

    def value_step(carried, block_in):
        key_block, value_block, start_at, use_it = block_in

        def value_compute(summed):
            scores, allowed, _ = block_scores(query_low, key_block, start_at, positions, length)
            weights = jnp.where(allowed, jnp.exp(scores - log_total[..., None]), 0.0).astype(
                jnp.bfloat16
            )
            value_rep = jnp.repeat(value_block, group_size, axis=1)
            return summed + jnp.einsum(
                "hqk,khd->qhd", weights, value_rep, preferred_element_type=jnp.float32
            )

        return (lax.cond(use_it, value_compute, lambda summed: summed, carried), None)

    attended, _ = lax.scan(
        value_step,
        jnp.zeros((span_rows, q_heads, head_size), jnp.float32),
        (key_stack, value_stack, starts, needed),
    )
    return (attended, log_total)


def attend_back(query_low, all_kv, positions, length, log_total, d_low, row_delta):
    span_rows, q_heads, head_size = query_low.shape
    key_stack, value_stack, starts = key_blocks(all_kv, span_rows, head_size)
    kv_heads = key_stack.shape[2]
    group_size = q_heads // kv_heads
    head_scale = head_size ** (-0.5)
    needed = (starts <= positions[-1]) & (starts < length)
    term_width = 2 * kv_heads * head_size

    def back_step(d_query, block_in):
        key_block, value_block, start_at, use_it = block_in

        def back_compute(d_before):
            scores, allowed, key_rep = block_scores(
                query_low, key_block, start_at, positions, length
            )
            probability = jnp.where(allowed, jnp.exp(scores - log_total[..., None]), 0.0)
            value_rep = jnp.repeat(value_block, group_size, axis=1)
            d_prob = jnp.einsum(
                "qhd,khd->hqk", d_low, value_rep, preferred_element_type=jnp.float32
            )
            d_scores = (probability * (d_prob - row_delta[..., None])).astype(jnp.bfloat16)
            d_after = (
                d_before
                + jnp.einsum("hqk,khd->qhd", d_scores, key_rep, preferred_element_type=jnp.float32)
                * head_scale
            )
            d_key = (
                jnp.einsum("hqk,qhd->khd", d_scores, query_low, preferred_element_type=jnp.float32)
                * head_scale
            )
            d_value = jnp.einsum(
                "hqk,qhd->khd",
                probability.astype(jnp.bfloat16),
                d_low,
                preferred_element_type=jnp.float32,
            )
            return (
                d_after,
                jnp.concatenate(
                    [fold_heads(d_key, kv_heads), fold_heads(d_value, kv_heads)], axis=1
                ),
            )

        def skipped(d_before):
            return (d_before, jnp.zeros((span_rows, term_width), jnp.float32))

        return lax.cond(use_it, back_compute, skipped, d_query)

    d_query, kv_terms = lax.scan(
        back_step,
        jnp.zeros((span_rows, q_heads, head_size), jnp.float32),
        (key_stack, value_stack, starts, needed),
    )
    return (d_query, kv_terms.reshape(-1, term_width))


def shards(
    inputs,
    cotangent,
    lengths,
    norm_gains,
    conv_in,
    conv_kernel,
    conv_out,
    attn_q,
    attn_k,
    attn_v,
    attn_out,
    head_gains,
    ffn_gate,
    ffn_up,
    ffn_down,
):
    micro_count, span_rows, model_width = inputs.shape
    gate_full, up_full, down_full = (
        lax.all_gather(ffn_gate, "fsdp", axis=1, tiled=True),
        lax.all_gather(ffn_up, "fsdp", axis=1, tiled=True),
        lax.all_gather(ffn_down, "fsdp", axis=1, tiled=True),
    )
    gate_full, up_full, down_full = (gate_full[0], up_full[0], down_full[0])
    in_full, out_full, query_full, key_full, value_full, proj_full = (
        lax.all_gather(conv_in, "fsdp", axis=0, tiled=True),
        lax.all_gather(conv_out, "fsdp", axis=0, tiled=True),
        lax.all_gather(attn_q, "fsdp", axis=0, tiled=True),
        lax.all_gather(attn_k, "fsdp", axis=0, tiled=True),
        lax.all_gather(attn_v, "fsdp", axis=0, tiled=True),
        lax.all_gather(attn_out, "fsdp", axis=0, tiled=True),
    )
    head_size = head_gains.shape[1]
    q_heads = query_full.shape[1] // head_size
    kv_heads = key_full.shape[1] // head_size
    kv_width = kv_heads * head_size
    q_width = q_heads * head_size
    ctx_count = lax.axis_size("ctx")
    is_first = lax.axis_index("section") == 0
    positions = lax.axis_index("ctx") * span_rows + jnp.arange(span_rows)
    group_lengths = lax.dynamic_slice_in_dim(
        lengths, lax.axis_index("fsdp") * micro_count, micro_count
    )
    empty_four = jnp.zeros((4,), jnp.float32)

    def attn_head(x_rows):
        normed, inv_rms = norm_rows(x_rows)
        normed_low = (normed * norm_gains[2]).astype(jnp.bfloat16)
        query_pre = matmul(normed_low, query_full).reshape(span_rows, q_heads, head_size)
        key_pre = matmul(normed_low, key_full).reshape(span_rows, kv_heads, head_size)
        value_low = matmul(normed_low, value_full).astype(jnp.bfloat16)
        q_normed, q_inv = norm_rows(query_pre)
        k_normed, k_inv = norm_rows(key_pre)
        query_low = (q_normed * head_gains[0]).astype(jnp.bfloat16)
        key_low = (k_normed * head_gains[1]).astype(jnp.bfloat16)
        local_kv = jnp.concatenate([key_low.reshape(span_rows, kv_width), value_low], axis=1)
        return (
            normed,
            inv_rms,
            normed_low,
            q_normed,
            q_inv,
            k_normed,
            k_inv,
            query_low,
            key_low,
            value_low,
            local_kv,
        )

    def attn_tail(x_rows, length, head, all_kv):
        row_mask = (positions < length).astype(jnp.float32)[:, None]
        query_low = head[7]
        attended, log_total = attend(query_low, all_kv, positions, length)
        attended_low = attended.reshape(span_rows, -1).astype(jnp.bfloat16)
        attn_rows = matmul(attended_low, proj_full)
        residual = x_rows + attn_rows
        ffn_out, ffn_kept = ffn_forward(residual, norm_gains[3], gate_full, up_full, down_full)
        result = (residual + ffn_out) * row_mask
        squares = jnp.stack(
            [
                masked_square(row_mask, attn_rows),
                masked_square(row_mask, residual),
                masked_square(row_mask, ffn_out),
                masked_square(row_mask, result),
            ]
        )
        return (
            result.astype(jnp.bfloat16),
            jnp.concatenate([empty_four, squares]),
            (row_mask, attended, log_total, attended_low, ffn_kept),
        )

    def front_messages(x_rows, length):

        def conv_side(rows, size):
            head = conv_head(rows, norm_gains[0], in_full)
            return (head[6][-2:], jnp.zeros((span_rows, 2 * kv_width), jnp.bfloat16))

        def attn_side(rows, size):
            head = attn_head(rows)
            return (jnp.zeros((2, model_width), jnp.bfloat16), head[10])

        return lax.cond(is_first, conv_side, attn_side, x_rows, length)

    def skip_messages(x_rows, length):
        return (
            jnp.zeros((2, model_width), jnp.bfloat16),
            jnp.zeros((span_rows, 2 * kv_width), jnp.bfloat16),
        )

    def exchange_front(x_rows, length, is_valid):
        rim_send, kv_send = lax.cond(is_valid, front_messages, skip_messages, x_rows, length)
        rim_rows = passed_along(rim_send, "ctx", 1)
        all_kv = lax.all_gather(kv_send, "ctx", axis=0, tiled=True)
        return (rim_rows, all_kv)

    def conv_forward(rows, size, rim_rows, all_kv):
        row_mask = (positions < size).astype(jnp.float32)[:, None]
        head = conv_head(rows, norm_gains[0], in_full)
        mixer_out, _, _, _ = conv_tail(head, rim_rows, conv_kernel, out_full)
        residual = rows + mixer_out
        ffn_out, _ = ffn_forward(residual, norm_gains[1], gate_full, up_full, down_full)
        passed = (residual + ffn_out).astype(jnp.bfloat16)
        squares = jnp.stack(
            [
                masked_square(row_mask, rows),
                masked_square(row_mask, mixer_out),
                masked_square(row_mask, ffn_out),
                masked_square(row_mask, passed.astype(jnp.float32)),
            ]
        )
        return (passed, jnp.concatenate([squares, empty_four]))

    def attn_forward(rows, size, rim_rows, all_kv):
        head = attn_head(rows)
        result, squares, _ = attn_tail(rows, size, head, all_kv)
        return (result, squares)

    def run_forward(rows, size, rim_rows, all_kv):
        return lax.cond(is_first, conv_forward, attn_forward, rows, size, rim_rows, all_kv)

    def skip_forward(rows, size, rim_rows, all_kv):
        return (jnp.zeros((span_rows, model_width), jnp.bfloat16), jnp.zeros((8,), jnp.float32))

    received = jnp.zeros((span_rows, model_width), jnp.bfloat16)
    squares_total = jnp.zeros((8,), jnp.float32)
    section_inputs = []
    produced = []
    for tick_no in range(micro_count + 1):
        first_mb = min(tick_no, micro_count - 1)
        second_mb = max(tick_no - 1, 0)
        is_valid = jnp.where(is_first, tick_no < micro_count, tick_no >= 1)
        x_rows = jnp.where(is_first, inputs[first_mb], received).astype(jnp.float32)
        length = jnp.where(is_first, group_lengths[first_mb], group_lengths[second_mb])
        section_inputs.append(received)
        rim_rows, all_kv = exchange_front(x_rows, length, is_valid)
        output_rows, squares = lax.cond(
            is_valid, run_forward, skip_forward, x_rows, length, rim_rows, all_kv
        )
        squares_total = squares_total + squares
        produced.append(output_rows)
        if tick_no < micro_count:
            received = passed_along(output_rows, "section", 1)
    totals = (
        jnp.zeros(in_full.shape, jnp.float32),
        jnp.zeros(conv_kernel.shape, jnp.float32),
        jnp.zeros(out_full.shape, jnp.float32),
        jnp.zeros(query_full.shape, jnp.float32),
        jnp.zeros(key_full.shape, jnp.float32),
        jnp.zeros(value_full.shape, jnp.float32),
        jnp.zeros(proj_full.shape, jnp.float32),
        jnp.zeros(head_gains.shape, jnp.float32),
        jnp.zeros(norm_gains.shape, jnp.float32),
        jnp.zeros(gate_full.shape, jnp.float32),
        jnp.zeros(up_full.shape, jnp.float32),
        jnp.zeros(down_full.shape, jnp.float32),
    )

    def zero_sends():
        rim_zero = jnp.zeros((2, model_width), jnp.float32)
        return (rim_zero, jnp.zeros((span_rows * ctx_count, 2 * kv_width), jnp.float32))

    def zero_carry():
        wide = jnp.zeros((span_rows, model_width), jnp.float32)
        return (
            wide,
            wide,
            wide,
            wide,
            wide,
            wide,
            jnp.zeros((span_rows, kv_width), jnp.float32),
            jnp.zeros((span_rows, 1), jnp.float32),
            jnp.zeros((span_rows, q_heads), jnp.float32),
            jnp.zeros((span_rows, kv_heads), jnp.float32),
        )

    def conv_mid(rows, upstream, size, rim_rows, all_kv, running):
        head = conv_head(rows, norm_gains[0], in_full)
        normed, inv_rms, normed_low, b_gate, c_gate, x_value, b_product = head
        mixer_out, extended, convolved, z_low = conv_tail(head, rim_rows, conv_kernel, out_full)
        residual = rows + mixer_out
        _, ffn_kept = ffn_forward(residual, norm_gains[1], gate_full, up_full, down_full)
        d_ffn_res, gain_one, ffn_grads = ffn_backward(
            upstream, ffn_kept, norm_gains[1], gate_full, up_full, down_full
        )
        d_residual = upstream + d_ffn_res
        d_mixer = d_residual.astype(jnp.bfloat16)
        grad_out = matmul_left(z_low, d_mixer)
        d_z = matmul_right(d_mixer, out_full)
        d_cgate = d_z * convolved
        d_conv = d_z * c_gate
        grad_kernel = jnp.stack(
            [
                jnp.sum(d_conv * extended[:-2], axis=0),
                jnp.sum(d_conv * extended[1:-1], axis=0),
                jnp.sum(d_conv * extended[2:], axis=0),
            ]
        )
        d_extended = (
            jnp.pad(d_conv * conv_kernel[0], ((0, 2), (0, 0)))
            + jnp.pad(d_conv * conv_kernel[1], ((1, 1), (0, 0)))
            + jnp.pad(d_conv * conv_kernel[2], ((2, 0), (0, 0)))
        )
        sends = (d_extended[:2],) + zero_sends()[1:]
        blank = zero_carry()
        carry = (
            d_extended[2:],
            x_value,
            b_gate,
            d_cgate,
            normed,
            d_residual,
            blank[6],
            inv_rms,
            blank[8],
            blank[9],
        )
        (
            g_in,
            g_kernel,
            g_out,
            g_query,
            g_key,
            g_value,
            g_proj,
            g_heads,
            g_norms,
            g_gate,
            g_up,
            g_down,
        ) = running
        updated = (
            g_in,
            g_kernel + grad_kernel,
            g_out + grad_out,
            g_query,
            g_key,
            g_value,
            g_proj,
            g_heads,
            g_norms.at[1].add(gain_one),
            g_gate + ffn_grads[0],
            g_up + ffn_grads[1],
            g_down + ffn_grads[2],
        )
        return (sends, carry, updated)

    def attn_mid(rows, upstream, size, rim_rows, all_kv, running):
        head = attn_head(rows)
        (
            normed,
            inv_rms,
            normed_low,
            q_normed,
            q_inv,
            k_normed,
            k_inv,
            query_low,
            key_low,
            value_low,
            local_kv,
        ) = head
        _, _, tail_kept = attn_tail(rows, size, head, all_kv)
        row_mask, attended, log_total, attended_low, ffn_kept = tail_kept
        d_sum = upstream * row_mask
        d_ffn_res, gain_three, ffn_grads = ffn_backward(
            d_sum, ffn_kept, norm_gains[3], gate_full, up_full, down_full
        )
        d_residual = d_sum + d_ffn_res
        d_attn = d_residual.astype(jnp.bfloat16)
        grad_proj = matmul_left(attended_low, d_attn)
        d_att_low = matmul_right(d_attn, proj_full).astype(jnp.bfloat16)
        d_att_rows = d_att_low.reshape(span_rows, q_heads, head_size)
        row_delta = jnp.sum(d_att_rows.astype(jnp.float32) * attended, axis=-1)
        rim_zero = jnp.zeros((2, model_width), jnp.float32)
        d_query, kv_terms = attend_back(
            query_low, all_kv, positions, size, log_total, d_att_rows, row_delta.T
        )
        sends = (rim_zero, kv_terms)
        blank = zero_carry()
        carry = (
            d_query.reshape(span_rows, -1),
            q_normed.reshape(span_rows, -1),
            blank[2],
            blank[3],
            normed,
            d_residual,
            k_normed.reshape(span_rows, -1),
            inv_rms,
            q_inv[..., 0],
            k_inv[..., 0],
        )
        (
            g_in,
            g_kernel,
            g_out,
            g_query,
            g_key,
            g_value,
            g_proj,
            g_heads,
            g_norms,
            g_gate,
            g_up,
            g_down,
        ) = running
        updated = (
            g_in,
            g_kernel,
            g_out,
            g_query,
            g_key,
            g_value,
            g_proj + grad_proj,
            g_heads,
            g_norms.at[3].add(gain_three),
            g_gate + ffn_grads[0],
            g_up + ffn_grads[1],
            g_down + ffn_grads[2],
        )
        return (sends, carry, updated)

    def run_mid(rows, upstream, size, rim_rows, all_kv, running):
        return lax.cond(
            is_first, conv_mid, attn_mid, rows, upstream, size, rim_rows, all_kv, running
        )

    def skip_mid(rows, upstream, size, rim_rows, all_kv, running):
        return (zero_sends(), zero_carry(), running)

    def conv_post(carry, from_next, d_kv, running):
        d_tail, x_value, b_gate, d_cgate, normed, d_residual, _, inv_rms, _, _ = carry
        normed_low = (normed * norm_gains[0]).astype(jnp.bfloat16)
        d_bproduct = rounded(d_tail + jnp.pad(from_next, ((span_rows - 2, 0), (0, 0))))
        d_projected = jnp.concatenate(
            [d_bproduct * x_value, d_cgate, d_bproduct * b_gate], axis=1
        ).astype(jnp.bfloat16)
        grad_in = matmul_left(normed_low, d_projected)
        d_act = matmul_right(d_projected, in_full)
        gain_zero = jnp.sum(d_act * normed, axis=0)
        d_input = d_residual + norm_back(d_act * norm_gains[0], normed, inv_rms)
        (
            g_in,
            g_kernel,
            g_out,
            g_query,
            g_key,
            g_value,
            g_proj,
            g_heads,
            g_norms,
            g_gate,
            g_up,
            g_down,
        ) = running
        updated = (
            g_in + grad_in,
            g_kernel,
            g_out,
            g_query,
            g_key,
            g_value,
            g_proj,
            g_heads,
            g_norms.at[0].add(gain_zero),
            g_gate,
            g_up,
            g_down,
        )
        return (d_input.astype(jnp.bfloat16), updated)

    def attn_post(carry, from_next, d_kv, running):
        d_qflat, q_nflat, _, _, normed, d_residual, k_nflat, inv_rms, q_invs, k_invs = carry
        normed_low = (normed * norm_gains[2]).astype(jnp.bfloat16)
        q_normed = q_nflat.reshape(span_rows, q_heads, head_size)
        k_normed = k_nflat.reshape(span_rows, kv_heads, head_size)
        q_inv = q_invs[..., None]
        k_inv = k_invs[..., None]
        d_qnormed = rounded(d_qflat.reshape(span_rows, q_heads, head_size))
        grad_qgain = jnp.sum(d_qnormed * q_normed, axis=(0, 1))
        d_qpre = (
            norm_back(d_qnormed * head_gains[0], q_normed, q_inv)
            .reshape(span_rows, -1)
            .astype(jnp.bfloat16)
        )
        d_knormed = rounded(d_kv[:, :kv_width]).reshape(span_rows, kv_heads, head_size)
        grad_kgain = jnp.sum(d_knormed * k_normed, axis=(0, 1))
        d_kpre = (
            norm_back(d_knormed * head_gains[1], k_normed, k_inv)
            .reshape(span_rows, -1)
            .astype(jnp.bfloat16)
        )
        d_vpre = d_kv[:, kv_width:].astype(jnp.bfloat16)
        grad_query = matmul_left(normed_low, d_qpre)
        grad_key = matmul_left(normed_low, d_kpre)
        grad_value = matmul_left(normed_low, d_vpre)
        d_act = (
            matmul_right(d_qpre, query_full)
            + matmul_right(d_kpre, key_full)
            + matmul_right(d_vpre, value_full)
        )
        gain_two = jnp.sum(d_act * normed, axis=0)
        d_input = d_residual + norm_back(d_act * norm_gains[2], normed, inv_rms)
        (
            g_in,
            g_kernel,
            g_out,
            g_query,
            g_key,
            g_value,
            g_proj,
            g_heads,
            g_norms,
            g_gate,
            g_up,
            g_down,
        ) = running
        updated = (
            g_in,
            g_kernel,
            g_out,
            g_query + grad_query,
            g_key + grad_key,
            g_value + grad_value,
            g_proj,
            g_heads + jnp.stack([grad_qgain, grad_kgain]),
            g_norms.at[2].add(gain_two),
            g_gate,
            g_up,
            g_down,
        )
        return (d_input.astype(jnp.bfloat16), updated)

    def run_post(carry, from_next, d_kv, running):
        return lax.cond(is_first, conv_post, attn_post, carry, from_next, d_kv, running)

    def skip_post(carry, from_next, d_kv, running):
        return (jnp.zeros((span_rows, model_width), jnp.bfloat16), running)

    back_received = jnp.zeros((span_rows, model_width), jnp.bfloat16)
    input_grads = [back_received] * micro_count
    for tick_no in range(micro_count + 1):
        second_mb = max(micro_count - 1 - tick_no, 0)
        first_mb = min(max(micro_count - tick_no, 0), micro_count - 1)
        is_valid = jnp.where(is_first, tick_no >= 1, tick_no < micro_count)
        x_rows = jnp.where(is_first, inputs[first_mb], section_inputs[second_mb + 1]).astype(
            jnp.float32
        )
        upstream = jnp.where(is_first, back_received, cotangent[second_mb]).astype(jnp.float32)
        length = jnp.where(is_first, group_lengths[first_mb], group_lengths[second_mb])
        rim_rows, all_kv = exchange_front(x_rows, length, is_valid)
        sends, carry, totals = lax.cond(
            is_valid, run_mid, skip_mid, x_rows, upstream, length, rim_rows, all_kv, totals
        )
        from_next = passed_along(sends[0], "ctx", -1)
        d_kv = lax.psum_scatter(
            sends[1].astype(jnp.bfloat16), "ctx", scatter_dimension=0, tiled=True
        ).astype(jnp.float32)
        d_rows, totals = lax.cond(is_valid, run_post, skip_post, carry, from_next, d_kv, totals)
        if tick_no >= 1:
            input_grads[first_mb] = d_rows
        if tick_no < micro_count:
            back_received = passed_along(d_rows, "section", -1)
    ends = jnp.where(is_first, jnp.stack(input_grads), jnp.stack(produced[1:]))[None]
    (
        g_in,
        g_kernel,
        g_out,
        g_query,
        g_key,
        g_value,
        g_proj,
        g_heads,
        g_norms,
        g_gate,
        g_up,
        g_down,
    ) = totals
    conv_pack = jnp.concatenate([g_in, g_out], axis=1)
    attn_pack = jnp.concatenate([g_query, g_key, g_value, g_proj], axis=1)
    attn_padded = jnp.pad(attn_pack, ((0, 0), (0, conv_pack.shape[1] - attn_pack.shape[1])))
    packed = jnp.stack([conv_pack, attn_padded])
    shares = (
        lax.psum_scatter(
            g_gate[None].astype(jnp.bfloat16), "fsdp", scatter_dimension=1, tiled=True
        ).astype(jnp.float32),
        lax.psum_scatter(
            g_up[None].astype(jnp.bfloat16), "fsdp", scatter_dimension=1, tiled=True
        ).astype(jnp.float32),
        lax.psum_scatter(
            g_down[None].astype(jnp.bfloat16), "fsdp", scatter_dimension=1, tiled=True
        ).astype(jnp.float32),
        lax.psum_scatter(
            packed.astype(jnp.bfloat16), "fsdp", scatter_dimension=1, tiled=True
        ).astype(jnp.float32),
        lax.psum_scatter(
            g_kernel.astype(jnp.bfloat16), "fsdp", scatter_dimension=1, tiled=True
        ).astype(jnp.float32),
        lax.psum_scatter(
            g_norms.astype(jnp.bfloat16), "fsdp", scatter_dimension=1, tiled=True
        ).astype(jnp.float32),
        lax.psum_scatter(
            g_heads.astype(jnp.bfloat16), "fsdp", scatter_dimension=1, tiled=True
        ).astype(jnp.float32),
        lax.psum_scatter(
            squares_total.astype(jnp.bfloat16), "fsdp", scatter_dimension=0, tiled=True
        ).astype(jnp.float32),
    )
    ffn_sums = (
        lax.psum(shares[0].astype(jnp.bfloat16), "ctx").astype(jnp.float32),
        lax.psum(shares[1].astype(jnp.bfloat16), "ctx").astype(jnp.float32),
        lax.psum(shares[2].astype(jnp.bfloat16), "ctx").astype(jnp.float32),
    )
    mixed = (
        lax.psum(shares[3].astype(jnp.bfloat16), ("section", "ctx")).astype(jnp.float32),
        lax.psum(shares[4].astype(jnp.bfloat16), ("section", "ctx")).astype(jnp.float32),
        lax.psum(shares[5].astype(jnp.bfloat16), ("section", "ctx")).astype(jnp.float32),
        lax.psum(shares[6].astype(jnp.bfloat16), ("section", "ctx")).astype(jnp.float32),
        lax.psum(shares[7].astype(jnp.bfloat16), ("section", "ctx")).astype(jnp.float32),
    )
    both_packs, kernel_sum, norms_sum, heads_sum, squares_sum = mixed
    grad_in_out = both_packs[0]
    grad_attn = both_packs[1]
    token_total = jnp.sum(lengths).astype(jnp.float32) * model_width
    rms = jnp.sqrt(squares_sum / token_total)
    return (
        ends,
        norms_sum[:3],
        norms_sum[3],
        grad_in_out[:, : 3 * model_width],
        kernel_sum,
        grad_in_out[:, 3 * model_width : 4 * model_width],
        grad_attn[:, :q_width],
        grad_attn[:, q_width : q_width + kv_width],
        grad_attn[:, q_width + kv_width : q_width + 2 * kv_width],
        grad_attn[:, q_width + 2 * kv_width : q_width + 2 * kv_width + model_width],
        heads_sum,
        ffn_sums[0],
        ffn_sums[1],
        ffn_sums[2],
        rms,
    )


def solution(mesh):
    return jax.shard_map(
        shards,
        mesh=mesh,
        in_specs=(
            P("fsdp", "ctx", None),
            P("fsdp", "ctx", None),
            P(),
            P(),
            P("fsdp", None),
            P(),
            P("fsdp", None),
            P("fsdp", None),
            P("fsdp", None),
            P("fsdp", None),
            P("fsdp", None),
            P(),
            P("section", "fsdp", None),
            P("section", "fsdp", None),
            P("section", "fsdp", None),
        ),
        out_specs=(
            P("section", "fsdp", "ctx", None),
            P(None, "fsdp"),
            P("fsdp"),
            P("fsdp", None),
            P(None, "fsdp"),
            P("fsdp", None),
            P("fsdp", None),
            P("fsdp", None),
            P("fsdp", None),
            P("fsdp", None),
            P(None, "fsdp"),
            P("section", "fsdp", None),
            P("section", "fsdp", None),
            P("section", "fsdp", None),
            P("fsdp"),
        ),
        check_vma=False,
    )
```

profile of v0, /device:TPU:0, one launch (start us, length us, event | category | flops | bytes accessed | tf_op | source)
XLA Modules:
  0.0 2680.8 jit_solution(7604134647311510749)
XLA Ops:
  67.7 72.0 %all-gather.19.cloned.1.call-done = bf16[1024,3072]{1,0:T(8,128)(2,1)} async-done(((bf16[256,3072]{1,0:T(8,128)(2,1)}), bf16[1024,3072]{1,0:T(8,128)(2,1)}) %all-gather.19.cloned.1.call-update) | async-done | bytes 6291472 | tf_op jit(solution)/shard_map/all_gather | solution.py:265
  213.9 37.0 %all-gather.33.cloned.1.call-done = bf16[1024,1024]{1,0:T(8,128)(2,1)} async-done(((bf16[256,1024]{1,0:T(8,128)(2,1)}), bf16[1024,1024]{1,0:T(8,128)(2,1)}) %all-gather.33.cloned.1.call-update) | async-done | bytes 2097168 | tf_op jit(solution)/shard_map/all_gather | solution.py:266
  250.9 48.4 %all-gather.21.cloned.1.call-done = bf16[1024,1024]{0,1:T(8,128)(2,1)} async-done(((bf16[256,1024]{0,1:T(8,128)(2,1)}), bf16[1024,1024]{0,1:T(8,128)(2,1)}) %all-gather.21.cloned.1.call-update) | async-done | bytes 2097168 | tf_op jit(solution)/shard_map/all_gather | solution.py:354
  299.3 96.4 %all-gather.27.cloned.1.call-done = bf16[1,1024,4608]{2,1,0:T(8,128)(2,1)} async-done(((bf16[1,256,4608]{2,1,0:T(8,128)(2,1)}), bf16[1,1024,4608]{2,1,0:T(8,128)(2,1)}) %all-gather.27.cloned.1.call-update) | async-done | bytes 9437200 | tf_op jit(solution)/shard_map/all_gather | solution.py:259
  395.7 98.2 %all-gather.29.cloned.1.call-done = bf16[1,1024,4608]{2,1,0:T(8,128)(2,1)} async-done(((bf16[1,256,4608]{2,1,0:T(8,128)(2,1)}), bf16[1,1024,4608]{2,1,0:T(8,128)(2,1)}) %all-gather.29.cloned.1.call-update) | async-done | bytes 9437200 | tf_op jit(solution)/shard_map/all_gather | solution.py:260
  494.0 98.1 %all-gather.31.cloned.1.call-done = bf16[1,4608,1024]{2,1,0:T(8,128)(2,1)} async-done(((bf16[1,1152,1024]{2,1,0:T(8,128)(2,1)}), bf16[1,4608,1024]{2,1,0:T(8,128)(2,1)}) %all-gather.31.cloned.1.call-update) | async-done | bytes 9437200 | tf_op jit(solution)/shard_map/all_gather | solution.py:261
  592.0 39.7 %conditional.75 = ((bf16[256,1024]{1,0:T(8,128)(2,1)}, f32[8]{0:T(128)})) conditional(s32[]{:T(128)} %convert_element_type.961, () %tuple.517, (pred[]{:T(512)}, bf16[1024,1024]{0,1:T(8,128)(2,1)}, s32[256]{0:T(256)S(1)}, s32[]{:T(128)}, f32[256,1024]{1,0:T(8,128)S(1)}, /*index=5*/f32[4,1024]{1,0:T(4,128)S(1)}, bf16[1024,1024]{1,0:T(8,128)(2,1)}, ...), branch_computations={%region_7.8_spmd, %region_8.34_spmd} | conditional | flops 9413338112 | bytes 118457296 | solution.py:397
  592.0 39.3 %conditional.7 = (bf16[256,1024]{1,0:T(8,128)(2,1)}, f32[8]{0:T(128)}) conditional(s32[]{:T(128)} %convert_element_type.717, (bf16[1024,1024]{0,1:T(8,128)(2,1)}, s32[256]{0:T(256)S(1)}, s32[]{:T(128)}, f32[256,1024]{1,0:T(8,128)S(1)}, f32[4,1024]{1,0:T(4,128)S(1)}, /*index=5*/bf16[1024,1024]{1,0:T(8,128)(2,1)}, f32[2,64]{1,0:T(2,128)S(1)}, ...), branch_computations={%region_9.26_spmd, %region_27.33_spmd} | conditional | flops 9413338112 | bytes 118457104 | solution.py:380
  650.2 48.7 %all-gather.35.cloned.1.call-done = bf16[1024,1024]{0,1:T(8,128)(2,1)} async-done(((bf16[256,1024]{0,1:T(8,128)(2,1)}), bf16[1024,1024]{0,1:T(8,128)(2,1)}) %all-gather.35.cloned.1.call-update) | async-done | bytes 2097168 | tf_op jit(solution)/shard_map/all_gather | solution.py:354
  698.9 41.4 %conditional.77 = (bf16[256,1024]{1,0:T(8,128)(2,1)}, f32[8]{0:T(128)S(1)}, bf16[1,1,256,1024]{3,2,1,0:T(8,128)(2,1)S(1)}) conditional(s32[]{:T(128)} %convert_element_type.961, (bf16[1024,1024]{0,1:T(8,128)(2,1)}, s32[256]{0:T(256)S(1)}, s32[]{:T(128)}, f32[256,1024]{1,0:T(8,128)S(1)}, f32[4,1024]{1,0:T(4,128)S(1)}, ...), branch_computations={%region_39.57_spmd, %region_57.0_spmd} | conditional | flops 9413338112 | bytes 112813336 | solution.py:380
  800.5 80.1 %all-gather.37.cloned.1.call-done = bf16[1024,1024]{0,1:T(8,128)(2,1)} async-done(((bf16[256,1024]{0,1:T(8,128)(2,1)}), bf16[1024,1024]{0,1:T(8,128)(2,1)}) %all-gather.37.cloned.1.call-update) | async-done | bytes 2097168 | tf_op jit(solution)/shard_map/all_gather | solution.py:354
  880.7 51.5 %conditional.79 = ((f32[2,1024]{1,0:T(2,128)}, f32[1024,1024]{1,0:T(8,128)}, f32[256,1024]{0,1:T(8,128)}, f32[256,1024]{1,0:T(8,128)}, f32[256,1024]{1,0:T(8,128...) conditional(s32[]{:T(128)} %convert_element_type.964, ...), branch_computations={%region_71.72_spmd, %region_72.105_spmd} | conditional | flops 22876143616 | bytes 408279936 | solution.py:713
  942.6 237.2 %reduce-scatter.15.cloned.1.call-done = bf16[256,1024]{0,1:T(8,128)(2,1)} async-done(((bf16[1024,1024]{0,1:T(8,128)(2,1)}), bf16[256,1024]{0,1:T(8,128)(2,1)}) %reduce-scatter.15.cloned.1.call-update) | async-done | bytes 524304 | tf_op jit(solution)/shard_map/reduce_scatter | solution.py:717
  1233.9 116.3 %conditional.81 = (f32[2,1024]{1,0:T(2,128)S(1)}, bf16[1024,1024]{1,0:T(8,128)(2,1)}, f32[256,1024]{0,1:T(8,128)S(1)}, f32[256,1024]{1,0:T(8,128)}, f32[256,1024...) conditional(s32[]{:T(128)} %convert_element_type.961, ...), branch_computations={%region_119.143_spmd, %region_143.0_spmd} | conditional | flops 22891610112 | bytes 445930368 | solution.py:585
  1370.6 168.7 %reduce-scatter.17.cloned.1.call-done = bf16[256,1024]{0,1:T(8,128)(2,1)} async-done(((bf16[1024,1024]{0,1:T(8,128)(2,1)}), bf16[256,1024]{0,1:T(8,128)(2,1)}) %reduce-scatter.17.cloned.1.call-update) | async-done | bytes 524304 | tf_op jit(solution)/shard_map/reduce_scatter | solution.py:717
  1586.2 128.0 %conditional.84 = ((f32[2,1024]{1,0:T(2,128)}, bf16[1024,1024]{1,0:T(8,128)(2,1)}, f32[256,1024]{0,1:T(8,128)}, f32[256,1024]{1,0:T(8,128)}, f32[256,1024]{1,0:T...) conditional(s32[]{:T(128)} %convert_element_type.961, ...), branch_computations={%region_170.171_spmd, %region_171.204_spmd} | conditional | flops 22891610112 | bytes 452308032 | solution.py:713
  1586.2 122.1 %conditional.33 = (f32[2,1024]{1,0:T(2,128)}, bf16[1024,1024]{1,0:T(8,128)(2,1)}, f32[256,1024]{0,1:T(8,128)}, f32[256,1024]{1,0:T(8,128)}, f32[256,1024]{1,0:T(...) conditional(s32[]{:T(128)} %convert_element_type.881, ...), branch_computations={%region_172.195_spmd, %region_196.203_spmd} | conditional | flops 22891610112 | bytes 452307744 | solution.py:585
  1858.2 98.3 %reduce-scatter.25.cloned.1.call-done = bf16[1,256,4608]{2,1,0:T(8,128)(2,1)} async-done(((bf16[1,1024,4608]{2,1,0:T(8,128)(2,1)}), bf16[1,256,4608]{2,1,0:T(8,128)(2,1)}) %reduce-scatter.25.cloned.1.call-update) | async-done | bytes 2359312 | tf_op jit(solution)/shard_map/reduce_scatter | solution.py:748
  1956.5 98.5 %reduce-scatter.27.cloned.1.call-done = bf16[1,1152,1024]{2,1,0:T(8,128)(2,1)} async-done(((bf16[1,4608,1024]{2,1,0:T(8,128)(2,1)}), bf16[1,1152,1024]{2,1,0:T(8,128)(2,1)}) %reduce-scatter.27.cloned.1.call-update) | async-done | bytes 2359312 | tf_op jit(solution)/shard_map/reduce_scatter | solution.py:751
  2055.0 157.0 %reduce-scatter.21.cloned.1.call-done = bf16[2,256,4096]{2,1,0:T(8,128)(2,1)} async-done(((bf16[2,1024,4096]{2,1,0:T(8,128)(2,1)}), bf16[2,256,4096]{2,1,0:T(8,128)(2,1)}) %reduce-scatter.21.cloned.1.call-update) | async-done | bytes 4194320 | tf_op jit(solution)/shard_map/reduce_scatter | solution.py:754
  2218.6 41.9 %all-gather.41.cloned.1.call-done = bf16[1024,1024]{0,1:T(8,128)(2,1)} async-done(((bf16[256,1024]{0,1:T(8,128)(2,1)}), bf16[1024,1024]{0,1:T(8,128)(2,1)}) %all-gather.41.cloned.1.call-update) | async-done | bytes 2097168 | tf_op jit(solution)/shard_map/all_gather | solution.py:354
  2314.2 100.5 %all-reduce.17 = (bf16[4,256]{1,0:T(4,128)(2,1)S(1)}, bf16[3,256]{1,0:T(4,128)(2,1)S(1)}, bf16[2,16]{1,0:T(2,128)(2,1)S(1)}, bf16[2]{0:T(256)(128)(2,1)S(1)}) all-reduce(bf16[4,256]{1,0:T(4,128)(2,1)S(1)} %copy.418, bf16[3,256]{1,0:T(4,128)(2,1)S(1)} %copy.420, ...), channel_id=1, replica_groups=mesh['section'=2,'ctx'=4,'fsdp'=4] {'section','ctx'}, use_global_device_ids=true, to_apply=%region_253.254 | all-reduce | flops 1826 | bytes 7304 | tf_op jit(solution)/shard_map/psum | solution.py:778
  2417.5 148.6 %all-reduce.25.cloned.1.call-done = (bf16[1,256,4608]{2,1,0:T(8,128)(2,1)}, bf16[1,256,4608]{2,1,0:T(8,128)(2,1)}, bf16[1,1152,1024]{2,1,0:T(8,128)(2,1)}) async-done(((bf16[1,256,4608]{2,1,0:T(8,128)(2,1)}, bf16[1,256,4608]{2,1,0:T(8,128)(2,1)}, bf16[1,1152,1024]{2,1,0:T(8,128)(2,1)}), (bf16[1,256,4608]{2,1,0:T(8,128)(2,1)}, bf16[1,256,4608]{2,1,0:T(8,128)(2,1)}, ...) | async-done | bytes 7077904 | tf_op jit(solution)/shard_map/psum | solution.py:771
  2576.1 87.9 %all-reduce.23.cloned.1.call-done = bf16[2,256,4096]{2,1,0:T(8,128)(2,1)} async-done(((bf16[2,256,4096]{2,1,0:T(8,128)(2,1)}), bf16[2,256,4096]{2,1,0:T(8,128)(2,1)}) %all-reduce.23.cloned.1.call-update) | async-done | bytes 4194320 | tf_op jit(solution)/shard_map/psum | solution.py:776
  (530 shorter events, 1037.9 us)
Async XLA Ops:
  8.7 131.1 %all-gather.19.cloned.1.call-start = ((), (), s32[]{:S(2)}) async-start(), calls=%async_computation.11 | async-start | bytes 7864320 | tf_op jit(solution)/shard_map/all_gather | solution.py:265
  9.4 167.4 %all-gather.23.cloned.1.call-start = ((), (), s32[]{:S(2)}) async-start(), calls=%async_computation.13 | async-start | bytes 2621440 | tf_op jit(solution)/shard_map/all_gather | solution.py:267
  10.0 203.9 %all-gather.25.cloned.1.call-start = ((), (), s32[]{:S(2)}) async-start(), calls=%async_computation.14 | async-start | bytes 2621440 | tf_op jit(solution)/shard_map/all_gather | solution.py:270
  10.6 240.3 %all-gather.33.cloned.1.call-start = ((), (), s32[]{:S(2)}) async-start(), calls=%async_computation.18 | async-start | bytes 2621440 | tf_op jit(solution)/shard_map/all_gather | solution.py:266
  11.2 288.1 %all-gather.21.cloned.1.call-start = ((), (), s32[]{:S(2)}) async-start(), calls=%async_computation.12 | async-start | bytes 2621440 | tf_op jit(solution)/shard_map/all_gather | solution.py:354
  148.3 247.5 %all-gather.27.cloned.1.call-start = ((), (), s32[]{:S(2)}) async-start(), calls=%async_computation.15 | async-start | bytes 11796480 | tf_op jit(solution)/shard_map/all_gather | solution.py:259
  149.0 344.9 %all-gather.29.cloned.1.call-start = ((), (), s32[]{:S(2)}) async-start(), calls=%async_computation.16 | async-start | bytes 11796480 | tf_op jit(solution)/shard_map/all_gather | solution.py:260
  149.8 442.2 %all-gather.31.cloned.1.call-start = ((), (), s32[]{:S(2)}) async-start(), calls=%async_computation.17 | async-start | bytes 11796480 | tf_op jit(solution)/shard_map/all_gather | solution.py:261
  150.4 548.5 %all-gather.35.cloned.1.call-start = ((), (), s32[]{:S(2)}) async-start(), calls=%async_computation.19 | async-start | bytes 2621440 | tf_op jit(solution)/shard_map/all_gather | solution.py:354
  151.1 99.8 %collective-permute-start = (bf16[2,1024]{1,0:T(2,128)(2,1)}, bf16[2,1024]{1,0:T(2,128)(2,1)S(1)}, u32[]{:S(2)}, u32[]{:S(2)}) collective-permute-start(bf16[2,1024]{1,0:T(2,128)(2,1)} %get-tuple-element.3834), channel_id=1, source_target_pairs={{0,4},{4,8},{8,12},{1,5},{5,9},{9,13},{2,6},{6,10},{10,14},{3,7},{... | collective-permute-start | bytes 12296 | tf_op jit(solution)/shard_map/ppermute | solution.py:13
  645.5 235.2 %all-gather.37.cloned.1.call-start = ((), (), s32[]{:S(2)}) async-start(), calls=%async_computation.20 | async-start | bytes 2621440 | tf_op jit(solution)/shard_map/all_gather | solution.py:354
  781.6 398.2 %reduce-scatter.15.cloned.1.call-start = ((), (), s32[]{:S(2)}) async-start(), calls=%async_computation.21 | async-start | bytes 2621440 | tf_op jit(solution)/shard_map/reduce_scatter | solution.py:717
  936.8 602.5 %reduce-scatter.17.cloned.1.call-start = ((), (), s32[]{:S(2)}) async-start(), calls=%async_computation.22 | async-start | bytes 2621440 | tf_op jit(solution)/shard_map/reduce_scatter | solution.py:717
  1354.6 231.6 %all-gather.39.cloned.1.call-start = ((), (), s32[]{:S(2)}) async-start(), calls=%async_computation.23 | async-start | bytes 2621440 | tf_op jit(solution)/shard_map/all_gather | solution.py:354
  1365.0 396.7 %reduce-scatter.19.cloned.1.call-start = ((), (), s32[]{:S(2)}) async-start(), calls=%async_computation.24 | async-start | bytes 2621440 | tf_op jit(solution)/shard_map/reduce_scatter | solution.py:717
  1718.2 140.0 %reduce-scatter.23.cloned.1.call-start = ((), (), s32[]{:S(2)}) async-start(), calls=%async_computation.28 | async-start | bytes 11796480 | tf_op jit(solution)/shard_map/reduce_scatter | solution.py:745
  1729.5 226.9 %reduce-scatter.25.cloned.1.call-start = ((), (), s32[]{:S(2)}) async-start(), calls=%async_computation.29 | async-start | bytes 11796480 | tf_op jit(solution)/shard_map/reduce_scatter | solution.py:748
  1740.9 314.0 %reduce-scatter.27.cloned.1.call-start = ((), (), s32[]{:S(2)}) async-start(), calls=%async_computation.30 | async-start | bytes 11796480 | tf_op jit(solution)/shard_map/reduce_scatter | solution.py:751
  1752.5 459.5 %reduce-scatter.21.cloned.1.call-start = ((), (), s32[]{:S(2)}) async-start(), calls=%async_computation.26 | async-start | bytes 20971520 | tf_op jit(solution)/shard_map/reduce_scatter | solution.py:754
  1820.0 440.5 %all-gather.41.cloned.1.call-start = ((), (), s32[]{:S(2)}) async-start(), calls=%async_computation.25 | async-start | bytes 2621440 | tf_op jit(solution)/shard_map/all_gather | solution.py:354
  1824.7 461.0 %reduce-scatter.31.cloned.1.call-start = ((), (), s32[]{:S(2)}) async-start(), calls=%async_computation.32 | async-start | bytes 327680
  1826.4 486.8 %reduce-scatter.29.cloned.1.call-start = ((), (), s32[]{:S(2)}) async-start(), calls=%async_computation.31 | async-start | bytes 327680
  1828.1 738.0 %all-reduce.25.cloned.1.call-start = ((), (), s32[]{:S(2)}) async-start(), calls=%async_computation.33 | async-start | bytes 14155776 | tf_op jit(solution)/shard_map/psum | solution.py:771
  2055.0 609.1 %all-reduce.23.cloned.1.call-start = ((), (), s32[]{:S(2)}) async-start(), calls=%async_computation.27 | async-start | bytes 8388608 | tf_op jit(solution)/shard_map/psum | solution.py:776
  (115 other events, 4332.7 us)
Sparse Core Ops, SparseCore 0:
  9.9 29.3 all-gather.14
  41.1 26.6 all-gather.16
  69.6 70.1 all-gather.18
  141.5 35.3 all-gather.22
  178.5 35.2 all-gather.24
  215.6 35.2 all-gather.32
  253.0 46.2 all-gather.20
  301.1 94.5 all-gather.26
  397.6 96.3 all-gather.28
  495.6 96.3 all-gather.30
  645.6 53.2 all-gather.34
  781.8 98.8 all-gather.36
  936.9 242.8 reduce-scatter.14
  1354.8 184.4 reduce-scatter.16
  1540.7 45.5 all-gather.38
  1718.3 42.1 reduce-scatter.18
  1763.8 94.3 reduce-scatter.22
  1861.4 95.0 reduce-scatter.24
  1959.9 95.0 reduce-scatter.26
  2058.1 153.7 reduce-scatter.20
  2214.2 46.2 all-gather.40
  2289.1 24.0 reduce-scatter.28
  2315.8 250.2 all-reduce.24
  2568.6 95.4 all-reduce.22
  (1 shorter events, 22.2 us)
where the time goes:
time: 2690 us; the launch traced here: 2680 us
  waiting for transfers between devices  1860 us (69%)
  matrix products  284 us (11%)
  other arithmetic  148 us (6%)
  local copies, waits for them, and re-layouts  138 us (5%)
  blocking collectives  109 us (4%)
  starting transfers between devices  72.3 us (3%)
  loops' own time  51.8 us (2%)
    reduce_scatter x3, waiting for transfers between devices, shards(): lax.psum_scatter(sends[1].astype(jnp.bfloat16), 'ctx', scatter_dimension=...  406 us
    all_gather x5, waiting for transfers between devices, exchange_front(): all_kv = lax.all_gather(kv_send, 'ctx', axis=0, tiled=True)  229 us
    reduce_scatter x1, waiting for transfers between devices, shards(): lax.psum_scatter(packed.astype(jnp.bfloat16), 'fsdp', scatter_dimension=1...  157 us
    psum x1, waiting for transfers between devices, shards(): lax.psum(shares[0].astype(jnp.bfloat16), 'ctx').astype(jnp.float32)  149 us
    dot_general x10, matrix products, matmul_left(): lax.dot_general(left_op, right_op, (((0,), (0,)), ((), ())), preferred_el...  128 us
    psum x1, blocking collectives, shards(): lax.psum(shares[5].astype(jnp.bfloat16), ('section', 'ctx'))  101 us
    reduce_scatter x1, waiting for transfers between devices, shards(): lax.psum_scatter(g_down[None].astype(jnp.bfloat16), 'fsdp', scatter_dimen...  98.5 us
    reduce_scatter x1, waiting for transfers between devices, shards(): lax.psum_scatter(g_up[None].astype(jnp.bfloat16), 'fsdp', scatter_dimensi...  98.3 us
  transfers between devices with their start and end apart: 37, of which 32 were waited for; matrix products, arithmetic and copies ran while one was open for 7% of the time, Pallas kernels for 0%

commit v1 on v0

v1 whole, which is shorter than its diff:
```python
import functools

import jax
import jax.numpy as jnp
from jax import lax
from jax.experimental import pallas as pl
from jax.experimental.pallas import tpu as pltpu
from jax.sharding import PartitionSpec as P

EPSILON = 1e-05
NEGATIVE = -1e30
MESH = pl.DeviceIdType.MESH
F32 = jnp.float32
BF16 = jnp.bfloat16


def passed_along(block, axis, distance):
    devices = range(lax.axis_size(axis))
    route = [(i - distance, i) for i in devices if i - distance in devices]
    return lax.ppermute(block, axis, route)


def swapped(block, axis):
    return lax.ppermute(block, axis, [(0, 1), (1, 0)])


def rounded(values):
    return lax.optimization_barrier(values.astype(BF16)).astype(F32)


def matmul(left_op, right_op):
    return jnp.dot(left_op, right_op, preferred_element_type=F32)


def matmul_left(left_op, right_op):
    return lax.dot_general(left_op, right_op, (((0,), (0,)), ((), ())), preferred_element_type=F32)


def matmul_right(left_op, right_op):
    return lax.dot_general(left_op, right_op, (((1,), (1,)), ((), ())), preferred_element_type=F32)


def norm_rows(values):
    inv_rms = lax.rsqrt(jnp.mean(values * values, axis=-1, keepdims=True) + EPSILON)
    return (values * inv_rms, inv_rms)


def norm_back(dnormed, normed, inv_rms):
    return inv_rms * dnormed - normed * inv_rms * jnp.mean(dnormed * normed, axis=-1, keepdims=True)


def greet(axis, count):
    me = lax.axis_index(axis)
    barrier = pltpu.get_barrier_semaphore()
    for step in range(1, count):
        pl.semaphore_signal(
            barrier,
            inc=1,
            device_id={axis: lax.rem(me + step, count)},
            device_id_type=MESH,
        )
    pl.semaphore_wait(barrier, count - 1)


def gather_kernel(axis, count, rows, block, whole, send_sem, recv_sem, own_sem):
    me = lax.axis_index(axis)
    greet(axis, count)
    own_rows = pl.ds(pl.multiple_of(me * rows, rows), rows)
    copies = []
    for step in range(1, count):
        copy = pltpu.make_async_remote_copy(
            src_ref=block,
            dst_ref=whole.at[own_rows],
            send_sem=send_sem.at[step],
            recv_sem=recv_sem.at[step],
            device_id={axis: lax.rem(me + step, count)},
            device_id_type=MESH,
        )
        copy.start()
        copies.append(copy)
    own = pltpu.make_async_copy(block, whole.at[own_rows], own_sem)
    own.start()
    own.wait()
    for copy in copies:
        copy.wait()


def swap_kernel(axis, count, rows, blocks, whole, send_sem, recv_sem, own_sem):
    me = lax.axis_index(axis)
    greet(axis, count)
    own_rows = pl.ds(pl.multiple_of(me * rows, rows), rows)
    copies = []
    for step in range(1, count):
        target = lax.rem(me + step, count)
        copy = pltpu.make_async_remote_copy(
            src_ref=blocks.at[pl.ds(pl.multiple_of(target * rows, rows), rows)],
            dst_ref=whole.at[own_rows],
            send_sem=send_sem.at[step],
            recv_sem=recv_sem.at[step],
            device_id={axis: target},
            device_id_type=MESH,
        )
        copy.start()
        copies.append(copy)
    own = pltpu.make_async_copy(blocks.at[own_rows], whole.at[own_rows], own_sem)
    own.start()
    own.wait()
    for copy in copies:
        copy.wait()


def exchange(kernel, axis, array, rows, collective_id):
    count = lax.axis_size(axis)
    return pl.pallas_call(
        functools.partial(kernel, axis, count, rows),
        out_shape=jax.ShapeDtypeStruct((count * rows,) + array.shape[1:], array.dtype),
        in_specs=[pl.BlockSpec(memory_space=pl.ANY)],
        out_specs=pl.BlockSpec(memory_space=pl.ANY),
        scratch_shapes=[
            pltpu.SemaphoreType.DMA((count,)),
            pltpu.SemaphoreType.DMA((count,)),
            pltpu.SemaphoreType.DMA,
        ],
        compiler_params=pltpu.CompilerParams(
            collective_id=collective_id, has_side_effects=True, vmem_limit_bytes=8 << 20
        ),
    )(array)


def gathered(array, axis, collective_id):
    return exchange(gather_kernel, axis, array, array.shape[0], collective_id)


def swapped_blocks(array, axis, collective_id):
    return exchange(swap_kernel, axis, array, array.shape[0] // lax.axis_size(axis), collective_id)


def reduced(partial, axis, collective_id):
    count = lax.axis_size(axis)
    terms = swapped_blocks(partial.astype(BF16), axis, collective_id)
    return jnp.sum(terms.reshape(count, -1, partial.shape[1]).astype(F32), axis=0)


def attend(query, key_all, value_all, allowed):
    kv_heads = key_all.shape[1]
    rows, q_heads, head = query.shape
    grouped = query.reshape(rows, kv_heads, q_heads // kv_heads, head)
    scores = jnp.einsum("qghd,kgd->ghqk", grouped, key_all, preferred_element_type=F32) * head ** (-0.5)
    scores = jnp.where(allowed, scores, NEGATIVE)
    peak = jnp.max(scores, axis=-1, keepdims=True)
    weights = jnp.where(allowed, jnp.exp(scores - peak), 0.0)
    total = jnp.sum(weights, axis=-1, keepdims=True)
    log_total = peak + jnp.log(total)
    prob = (weights / total).astype(BF16)
    out = jnp.einsum("ghqk,kgd->qghd", prob, value_all, preferred_element_type=F32)
    return out.reshape(rows, q_heads * head), log_total


def attend_back(query, key_all, value_all, allowed, log_total, attended, d_out):
    kv_heads = key_all.shape[1]
    rows, q_heads, head = query.shape
    scale = head ** (-0.5)
    grouped = query.reshape(rows, kv_heads, q_heads // kv_heads, head)
    d_group = d_out.reshape(rows, kv_heads, q_heads // kv_heads, head)
    delta = jnp.sum(d_group.astype(F32) * attended.reshape(d_group.shape), axis=-1)
    scores = jnp.einsum("qghd,kgd->ghqk", grouped, key_all, preferred_element_type=F32) * scale
    prob = jnp.where(allowed, jnp.exp(scores - log_total), 0.0)
    d_prob = jnp.einsum("qghd,kgd->ghqk", d_group, value_all, preferred_element_type=F32)
    d_scores = (prob * (d_prob - delta.transpose(1, 2, 0)[..., None])).astype(BF16)
    d_query = jnp.einsum("ghqk,kgd->qghd", d_scores, key_all, preferred_element_type=F32) * scale
    d_key = jnp.einsum("ghqk,qghd->kgd", d_scores, grouped, preferred_element_type=F32) * scale
    d_value = jnp.einsum("ghqk,qghd->kgd", prob.astype(BF16), d_group, preferred_element_type=F32)
    return d_query.reshape(rows, q_heads, head), d_key, d_value


def ffn_forward(residual, gain, w_gate, w_up, w_down):
    normed, inv_rms = norm_rows(residual)
    act = gathered((normed * gain).astype(BF16), "fsdp", 0)
    gate_pre = matmul(act, w_gate)
    up_pre = matmul(act, w_up)
    hidden = (jax.nn.silu(gate_pre) * up_pre).astype(BF16)
    out = reduced(matmul(hidden, w_down), "fsdp", 1)
    return out, (normed, inv_rms, act, gate_pre, up_pre, hidden)


def ffn_backward(d_low, kept, gain, w_gate, w_up, w_down):
    normed, inv_rms, act, gate_pre, up_pre, hidden = kept
    d_all = gathered(d_low, "fsdp", 0)
    d_hidden = matmul_right(d_all, w_down)
    sigmoid = jax.nn.sigmoid(gate_pre)
    d_up = (d_hidden * gate_pre * sigmoid).astype(BF16)
    d_gate = (d_hidden * up_pre * sigmoid * (1.0 + gate_pre * (1.0 - sigmoid))).astype(BF16)
    d_act = reduced(matmul_right(d_gate, w_gate) + matmul_right(d_up, w_up), "fsdp", 1)
    grad_gate = matmul_left(act, d_gate).astype(BF16)
    grad_up = matmul_left(act, d_up).astype(BF16)
    grad_down = matmul_left(hidden, d_all).astype(BF16)
    grad_gain = jnp.sum(d_act * normed, axis=0)
    return norm_back(d_act * gain, normed, inv_rms), grad_gain, (grad_gate, grad_up, grad_down)


def shards(
    inputs,
    cotangent,
    lengths,
    norm_gains,
    conv_in,
    conv_kernel,
    conv_out,
    attn_q,
    attn_k,
    attn_v,
    attn_out,
    head_gains,
    ffn_gate,
    ffn_up,
    ffn_down,
):
    micro, rows, width = inputs.shape
    section = lax.axis_index("section")
    group = lax.axis_index("fsdp")
    fsdp = lax.axis_size("fsdp")
    assert micro == lax.axis_size("section")
    head = head_gains.shape[1]
    q_width, kv_width = attn_q.shape[1], attn_k.shape[1]
    q_heads, kv_heads = q_width // head, kv_width // head
    positions = lax.axis_index("ctx") * rows + jnp.arange(rows)
    length = lax.dynamic_index_in_dim(lengths, group * micro + section, keepdims=False)
    mask = (positions < length).astype(F32)[:, None]

    def whole_rows(weight):
        half = weight.shape[0] // micro
        mine = lax.dynamic_slice_in_dim(weight, section * half, half, 0)
        return lax.all_gather(mine, ("fsdp", "section"), axis=0, tiled=True)

    def to_columns(weight):
        deep, wide = weight.shape
        blocks = weight.reshape(deep, fsdp, wide // fsdp).transpose(1, 0, 2)
        return swapped_blocks(blocks.reshape(fsdp * deep, wide // fsdp), "fsdp", 2)

    def both(weight):
        other = swapped(weight, "section")
        first = section == 0
        return jnp.where(first, weight, other), jnp.where(first, other, weight)

    in_full = whole_rows(conv_in)
    out_full = whole_rows(conv_out)
    gate_up = to_columns(jnp.concatenate([ffn_gate[0], ffn_up[0]], axis=0))
    part = ffn_gate.shape[1]
    gate_up = gate_up.reshape(fsdp, 2, part, -1)
    gates = both(gate_up[:, 0].reshape(fsdp * part, -1))
    ups = both(gate_up[:, 1].reshape(fsdp * part, -1))
    downs = both(ffn_down[0])
    query_full, key_full, value_full, proj_full = (
        whole_rows(attn_q),
        whole_rows(attn_k),
        whole_rows(attn_v),
        whole_rows(attn_out),
    )

    x = lax.dynamic_index_in_dim(inputs, section, keepdims=False).astype(F32)
    normed0, inv0 = norm_rows(x)
    act1 = (normed0 * norm_gains[0]).astype(BF16)
    projected = matmul(act1, in_full)
    b_gate, c_gate, x_value = (
        projected[:, :width],
        projected[:, width : 2 * width],
        projected[:, 2 * width :],
    )
    b_product = (b_gate * x_value).astype(BF16)
    rim = passed_along(b_product[-2:], "ctx", 1)
    extended = jnp.concatenate([rim, b_product], axis=0).astype(F32)
    convolved = (
        conv_kernel[0] * extended[:-2]
        + conv_kernel[1] * extended[1:-1]
        + conv_kernel[2] * extended[2:]
    )
    z_low = (c_gate * convolved).astype(BF16)
    mixed = matmul(z_low, out_full)
    res1 = x + mixed
    ffn1, kept1 = ffn_forward(res1, norm_gains[1], gates[0], ups[0], downs[0])
    h_low = (res1 + ffn1).astype(BF16)

    h = h_low.astype(F32)
    normed2, inv2 = norm_rows(h)
    act2 = (normed2 * norm_gains[2]).astype(BF16)
    q_normed, q_inv = norm_rows(matmul(act2, query_full).reshape(rows, q_heads, head))
    k_normed, k_inv = norm_rows(matmul(act2, key_full).reshape(rows, kv_heads, head))
    query = (q_normed * head_gains[0]).astype(BF16)
    key = (k_normed * head_gains[1]).astype(BF16)
    value = matmul(act2, value_full).astype(BF16)
    kv_all = gathered(jnp.concatenate([key.reshape(rows, kv_width), value], axis=1), "ctx", 3)
    key_all = kv_all[:, :kv_width].reshape(-1, kv_heads, head)
    value_all = kv_all[:, kv_width:].reshape(-1, kv_heads, head)
    key_pos = jnp.arange(kv_all.shape[0])
    allowed = (key_pos[None, :] <= positions[:, None]) & (key_pos[None, :] < length)
    attended, log_total = attend(query, key_all, value_all, allowed)
    attended_low = attended.astype(BF16)
    attn_rows = matmul(attended_low, proj_full)
    res2 = h + attn_rows
    ffn2, kept2 = ffn_forward(res2, norm_gains[3], gates[1], ups[1], downs[1])
    result = (res2 + ffn2) * mask

    def square(values):
        return jnp.sum(mask * values * values)

    squares = jnp.stack(
        [square(v) for v in (x, mixed, ffn1, h, attn_rows, res2, ffn2, result)]
    )

    d_sum_low = (lax.dynamic_index_in_dim(cotangent, section, keepdims=False).astype(F32) * mask).astype(BF16)
    d_sum = d_sum_low.astype(F32)
    d_ffn, gain3, grads2 = ffn_backward(d_sum_low, kept2, norm_gains[3], gates[1], ups[1], downs[1])
    d_res2 = d_sum + d_ffn
    d_attn = d_res2.astype(BF16)
    grad_proj = matmul_left(attended_low, d_attn)
    d_att = matmul_right(d_attn, proj_full).astype(BF16)
    d_query, d_key_all, d_value_all = attend_back(
        query, key_all, value_all, allowed, log_total, attended, d_att
    )
    d_kv = reduced(
        jnp.concatenate(
            [d_key_all.reshape(-1, kv_width), d_value_all.reshape(-1, kv_width)], axis=1
        ),
        "ctx",
        4,
    )
    d_qn = rounded(d_query)
    grad_qgain = jnp.sum(d_qn * q_normed, axis=(0, 1))
    d_qpre = norm_back(d_qn * head_gains[0], q_normed, q_inv).reshape(rows, -1).astype(BF16)
    d_kn = rounded(d_kv[:, :kv_width]).reshape(rows, kv_heads, head)
    grad_kgain = jnp.sum(d_kn * k_normed, axis=(0, 1))
    d_kpre = norm_back(d_kn * head_gains[1], k_normed, k_inv).reshape(rows, -1).astype(BF16)
    d_vpre = d_kv[:, kv_width:].astype(BF16)
    grad_query = matmul_left(act2, d_qpre)
    grad_key = matmul_left(act2, d_kpre)
    grad_value = matmul_left(act2, d_vpre)
    d_act2 = (
        matmul_right(d_qpre, query_full)
        + matmul_right(d_kpre, key_full)
        + matmul_right(d_vpre, value_full)
    )
    gain2 = jnp.sum(d_act2 * normed2, axis=0)
    d_h_low = (d_res2 + norm_back(d_act2 * norm_gains[2], normed2, inv2)).astype(BF16)

    d_ffn1, gain1, grads1 = ffn_backward(d_h_low, kept1, norm_gains[1], gates[0], ups[0], downs[0])
    d_res1 = d_h_low.astype(F32) + d_ffn1
    d_mixed = d_res1.astype(BF16)
    grad_out = matmul_left(z_low, d_mixed)
    d_z = matmul_right(d_mixed, out_full)
    d_cgate = d_z * convolved
    d_conv = d_z * c_gate
    grad_kernel = jnp.stack(
        [
            jnp.sum(d_conv * extended[:-2], axis=0),
            jnp.sum(d_conv * extended[1:-1], axis=0),
            jnp.sum(d_conv * extended[2:], axis=0),
        ]
    )
    d_extended = (
        jnp.pad(d_conv * conv_kernel[0], ((0, 2), (0, 0)))
        + jnp.pad(d_conv * conv_kernel[1], ((1, 1), (0, 0)))
        + jnp.pad(d_conv * conv_kernel[2], ((2, 0), (0, 0)))
    )
    from_next = passed_along(d_extended[:2], "ctx", -1)
    d_bproduct = rounded(d_extended[2:] + jnp.pad(from_next, ((rows - 2, 0), (0, 0))))
    d_projected = jnp.concatenate(
        [d_bproduct * x_value, d_cgate, d_bproduct * b_gate], axis=1
    ).astype(BF16)
    grad_in = matmul_left(act1, d_projected)
    d_act1 = matmul_right(d_projected, in_full)
    gain0 = jnp.sum(d_act1 * normed0, axis=0)
    d_x = (d_res1 + norm_back(d_act1 * norm_gains[0], normed0, inv0)).astype(BF16)

    y_low = result.astype(BF16)
    is_first = section == 0
    other_end = swapped(jnp.where(is_first, y_low, d_x), "section")
    ends = jnp.where(is_first, jnp.stack([d_x, other_end]), jnp.stack([other_end, y_low]))[None]

    def own_rows(grad):
        share = lax.psum_scatter(
            grad.astype(BF16), ("fsdp", "section"), scatter_dimension=0, tiled=True
        )
        total = lax.psum(share, "ctx")
        return lax.all_gather(total, "section", axis=0, tiled=True).astype(F32)

    conv_grads = own_rows(jnp.concatenate([grad_in, grad_out], axis=1))
    attn_grads = own_rows(jnp.concatenate([grad_query, grad_key, grad_value, grad_proj], axis=1))

    def own_section(first, second):
        mine = jnp.where(is_first, first, second)
        other = swapped(jnp.where(is_first, second, first), "section")
        return (mine.astype(F32) + other.astype(F32)).astype(BF16)

    ffn_grads = lax.psum(tuple(own_section(a, b) for a, b in zip(grads1, grads2)), "ctx")

    def to_rows(grad):
        return swapped_blocks(grad, "fsdp", 5).reshape(fsdp, part, -1).transpose(1, 0, 2).reshape(part, -1)

    small = jnp.concatenate(
        [
            jnp.stack([gain0, gain1, gain2, gain3]).reshape(-1),
            grad_kernel.reshape(-1),
            grad_qgain,
            grad_kgain,
            squares,
            jnp.zeros((width - 2 * head - squares.shape[0],), F32),
        ]
    ).reshape(-1, width)
    small = lax.psum(small, ("section", "ctx", "fsdp"))
    cut = width // fsdp
    mine = lax.dynamic_slice_in_dim(small, group * cut, cut, 1)
    head_cut = head // fsdp
    heads = lax.dynamic_slice_in_dim(small[7, : 2 * head].reshape(2, head), group * head_cut, head_cut, 1)
    token_total = jnp.sum(lengths).astype(F32) * width
    rms_all = jnp.sqrt(small[7, 2 * head : 2 * head + 8] / token_total)
    rms = lax.dynamic_slice_in_dim(rms_all, group * (8 // fsdp), 8 // fsdp)
    return (
        ends,
        mine[:3],
        mine[3],
        conv_grads[:, : 3 * width],
        mine[4:7],
        conv_grads[:, 3 * width :],
        attn_grads[:, :q_width],
        attn_grads[:, q_width : q_width + kv_width],
        attn_grads[:, q_width + kv_width : q_width + 2 * kv_width],
        attn_grads[:, q_width + 2 * kv_width :],
        heads,
        to_rows(ffn_grads[0])[None].astype(F32),
        to_rows(ffn_grads[1])[None].astype(F32),
        ffn_grads[2][None].astype(F32),
        rms,
    )


def solution(mesh):
    return jax.shard_map(
        shards,
        mesh=mesh,
        in_specs=(
            P("fsdp", "ctx", None),
            P("fsdp", "ctx", None),
            P(),
            P(),
            P("fsdp", None),
            P(),
            P("fsdp", None),
            P("fsdp", None),
            P("fsdp", None),
            P("fsdp", None),
            P("fsdp", None),
            P(),
            P("section", "fsdp", None),
            P("section", "fsdp", None),
            P("section", "fsdp", None),
        ),
        out_specs=(
            P("section", "fsdp", "ctx", None),
            P(None, "fsdp"),
            P("fsdp"),
            P("fsdp", None),
            P(None, "fsdp"),
            P("fsdp", None),
            P("fsdp", None),
            P("fsdp", None),
            P("fsdp", None),
            P("fsdp", None),
            P(None, "fsdp"),
            P("section", "fsdp", None),
            P("section", "fsdp", None),
            P("section", "fsdp", None),
            P("fsdp"),
        ),
        check_vma=False,
    )
```

time: 2690 us -> 1210 us (0.45)
  waiting for transfers between devices: 1860 us -> 377 us
  Pallas kernels: 0 us -> 437 us
  matrix products: 284 us -> 166 us
  other arithmetic: 148 us -> 62.4 us
  blocking collectives: 109 us -> 39.4 us
  starting transfers between devices: 72.3 us -> 6.94 us
  loops' own time: 51.8 us -> 0 us
  local copies, waits for them, and re-layouts: 138 us -> 98.1 us
    reduce_scatter x7 -> x1, waiting for transfers between devices: 790 us -> 44 us  [own_rows(): lax.psum_scatter(grad.astype(BF16), ('fsdp', 'section'), scatter_dimensio...]
    all_gather x14 -> x8, waiting for transfers between devices: 745 us -> 1.74 us  [the longest x6 1.74 us: whole_rows(): return lax.all_gather(mine, ('fsdp', 'section'), axis=0, tiled=True)]
    pallas_call x0 -> x13, Pallas kernels: none -> 437 us  [exchange(): pl.pallas_call(functools.partial(kernel, axis, count, rows), out_shape=ja...]
    dot_general x10 -> x12, matrix products: 128 us -> 32.9 us  [matmul_left(): lax.dot_general(left_op, right_op, (((0,), (0,)), ((), ())), preferred_el...]
    psum x2 -> x1, waiting for transfers between devices: 237 us -> 313 us  [own_rows(): total = lax.psum(share, 'ctx')]
    ppermute x12 -> x2, starting transfers between devices: 71.3 us -> 5.26 us  [passed_along(): return lax.ppermute(block, axis, route)]
    psum x1, blocking collectives: 101 us -> 39.4 us  [shards(): small = lax.psum(small, ('section', 'ctx', 'fsdp'))]
    another operation x44 -> x1, local copies, waits for them, and re-layouts: 60.3 us -> 0.08 us  [shards(): small[7, :2 * head].reshape(2, head)]
  transfers between devices with their start and end apart: 37 -> 20, of which waited for: 32 -> 4; matrix products, arithmetic and copies ran while one was open for 7% -> 17% of each run, Pallas kernels for 0% -> 26%
where the time goes in v1:
time: 1210 us; the launch traced here: 1200 us
  Pallas kernels  437 us (36%)
  waiting for transfers between devices  377 us (31%)
  matrix products  166 us (14%)
  local copies, waits for them, and re-layouts  98.1 us (8%)
  other arithmetic  62.4 us (5%)
  blocking collectives  39.4 us (3%)
  between operations  16.7 us (1%)
    pallas_call x13, Pallas kernels, exchange(): pl.pallas_call(functools.partial(kernel, axis, count, rows), out_shape=ja...  437 us
    psum x1, waiting for transfers between devices, own_rows(): total = lax.psum(share, 'ctx')  313 us
    dot_general x12, matrix products, matmul(): return jnp.dot(left_op, right_op, preferred_element_type=F32)  53.8 us
    dot_general x12, matrix products, matmul_right(): lax.dot_general(left_op, right_op, (((1,), (1,)), ((), ())), preferred_el...  48.3 us
    reduce_scatter x1, waiting for transfers between devices, own_rows(): lax.psum_scatter(grad.astype(BF16), ('fsdp', 'section'), scatter_dimensio...  44 us
    psum x1, blocking collectives, shards(): small = lax.psum(small, ('section', 'ctx', 'fsdp'))  39.4 us
    unnamed x217, local copies, waits for them, and re-layouts  34.3 us
    dot_general x12, matrix products, matmul_left(): lax.dot_general(left_op, right_op, (((0,), (0,)), ((), ())), preferred_el...  32.9 us
  transfers between devices with their start and end apart: 20, of which 4 were waited for; matrix products, arithmetic and copies ran while one was open for 17% of the time, Pallas kernels for 26%

profile of v1, /device:TPU:0, one launch (start us, length us, event | category | flops | bytes accessed | tf_op | source)
XLA Modules:
  0.0 1204.1 jit_solution(11352886178423390755)
XLA Ops:
  22.1 74.5 %shard_map.263 = bf16[2048,1152]{1,0:T(8,128)(2,1)S(1)} custom-call(bf16[2048,1152]{1,0:T(8,128)(2,1)S(1)} %bitcast.244), custom_call_target="tpu_custom_call" | custom-call | tf_op jit(solution)/shard_map/pallas_call | solution.py:114
  102.2 29.7 %shard_map.266 = bf16[1024,1024]{1,0:T(8,128)(2,1)S(1)} custom-call(bf16[256,1024]{1,0:T(8,128)(2,1)S(1)} %fusion.58.block), custom_call_target="tpu_custom_call" | custom-call | tf_op jit(solution)/shard_map/pallas_call | solution.py:114
  142.0 7.0 fusion.67
  155.1 29.5 %shard_map.262 = bf16[1024,1024]{1,0:T(8,128)(2,1)S(1)} custom-call(bf16[256,1024]{1,0:T(8,128)(2,1)S(1)} %multiply_convert_fusion.9.block), custom_call_target="tpu_custom_call" | custom-call | tf_op jit(solution)/shard_map/pallas_call | solution.py:114
  190.1 8.1 multiply_convert_fusion.5
  203.9 27.3 %shard_map.264 = bf16[1024,1024]{1,0:T(8,128)(2,1)S(1)} custom-call(bf16[1024,1024]{1,0:T(8,128)(2,1)S(1)} %convolution_convert_fusion.8.blocks), custom_call_target="tpu_custom_call" | custom-call | tf_op jit(solution)/shard_map/pallas_call | solution.py:114
  243.9 38.6 %shard_map.265 = bf16[1024,1024]{1,0:T(8,128)(2,1)S(1)} custom-call(bf16[256,1024]{1,0:T(8,128)(2,1)S(1)} %pad_maximum_fusion.7.block), custom_call_target="tpu_custom_call" | custom-call | tf_op jit(solution)/shard_map/pallas_call | solution.py:114
  304.8 26.1 %shard_map.267 = bf16[1024,1024]{1,0:T(8,128)(2,1)S(1)} custom-call(bf16[256,1024]{1,0:T(8,128)(2,1)S(1)} %multiply_convert_fusion.7.block), custom_call_target="tpu_custom_call" | custom-call | tf_op jit(solution)/shard_map/pallas_call | solution.py:114
  353.6 25.2 %shard_map.268 = bf16[1024,1024]{1,0:T(8,128)(2,1)S(1)} custom-call(bf16[1024,1024]{1,0:T(8,128)(2,1)S(1)} %add_convert_fusion.4.blocks), custom_call_target="tpu_custom_call" | custom-call | tf_op jit(solution)/shard_map/pallas_call | solution.py:114
  384.5 24.6 %shard_map.272 = bf16[1024,1024]{1,0:T(8,128)(2,1)S(1)} custom-call(bf16[1024,1024]{1,0:T(8,128)(2,1)S(1)} %convolution_convert_fusion.7.blocks), custom_call_target="tpu_custom_call" | custom-call | tf_op jit(solution)/shard_map/pallas_call | solution.py:114
  417.3 8.6 bitcast_convert_fusion
  425.9 9.1 fusion.1
  442.4 46.9 %shard_map.269 = bf16[1024,1024]{1,0:T(8,128)(2,1)S(1)} custom-call(bf16[1024,1024]{1,0:T(8,128)(2,1)S(1)} %pad_maximum_fusion.3.blocks), custom_call_target="tpu_custom_call" | custom-call | tf_op jit(solution)/shard_map/pallas_call | solution.py:114
  503.4 15.3 %pad_maximum_fusion.1 = bf16[1024,3072]{0,1:T(8,128)(2,1)} fusion(bf16[1024,1024]{0,1:T(8,128)(2,1)S(1)} %copy-done.28, bf16[1024,512]{0,1:T(8,128)(2,1)S(1)} %copy-done.52, bf16[1024,512]{0,1:T(8,128)(2,1)S(1)} %convolution_convert_fusion.13, bf16[1024,1024]{0,1:T(8,128)(2,1)S(1)} %convolution_convert_fusion.9), kind=kLoop, calls=%fused_computation.16 | loop fusion | flops 25165824 | bytes 12582912 | tf_op jit(solution)/shard_map/concatenate | solution.py:387
  518.7 8.7 copy.149
  533.8 24.7 %shard_map.270 = bf16[1024,1024]{1,0:T(8,128)(2,1)S(1)} custom-call(bf16[256,1024]{1,0:T(8,128)(2,1)S(1)} %fusion.50.block), custom_call_target="tpu_custom_call" | custom-call | tf_op jit(solution)/shard_map/pallas_call | solution.py:114
  558.5 8.2 multiply_convert_fusion.2
  577.2 31.0 %shard_map.271 = bf16[1024,1024]{1,0:T(8,128)(2,1)S(1)} custom-call(bf16[1024,1024]{1,0:T(8,128)(2,1)S(1)} %add_convert_fusion.3.blocks), custom_call_target="tpu_custom_call" | custom-call | tf_op jit(solution)/shard_map/pallas_call | solution.py:114
  617.1 18.9 %collective-permute-done.4 = f32[2,1024]{1,0:T(2,128)S(1)} collective-permute-done((f32[2,1024]{1,0:T(2,128)S(1)}, f32[2,1024]{1,0:T(2,128)S(1)}, u32[]{:S(2)}, u32[]{:S(2)}) %collective-permute-start.4) | collective-permute-done | bytes 8224 | tf_op jit(solution)/shard_map/ppermute | solution.py:20
  681.8 44.0 %reduce-scatter.5.cloned.1.call-done = bf16[128,4096]{1,0:T(8,128)(2,1)} async-done(((bf16[1024,4096]{1,0:T(8,128)(2,1)}), bf16[128,4096]{1,0:T(8,128)(2,1)}) %reduce-scatter.5.cloned.1.call-update) | async-done | bytes 1048592 | tf_op jit(solution)/shard_map/reduce_scatter | solution.py:380
  727.9 312.7 %all-reduce.7.cloned.1.call-done = (bf16[128,4096]{1,0:T(8,128)(2,1)}, bf16[128,3072]{0,1:T(8,128)(2,1)}, bf16[1024,1152]{1,0:T(8,128)(2,1)}, bf16[1024,1152]{1,0:T(8,128)(2,1)}, bf16[1,1152,1024]{2,1,0:T(8,128)(2,1)}) async-done(((bf16[128,4096]{1,0:T(8,128)(2,1)}, bf16[128,3072]{0,1:T(8,128)(2,1)}, bf16[1024,1152]{1,0:T(8,128)(2,1)}, bf16[1024,1152]{1,0:T(8,128)(2,1)}, bf16[1,1152,1024]{2,1,0:T(8,128)(2,1)}), ...) | async-done | bytes 8912912 | tf_op jit(solution)/shard_map/psum | solution.py:383
  1052.5 39.4 %psum.42 = f32[8,1024]{1,0:T(8,128)S(1)} all-reduce(f32[8,1024]{1,0:T(8,128)S(1)} %reshape.335), channel_id=1, replica_groups=mesh['section'=2,'ctx'=4,'fsdp'=4] {'section','ctx','fsdp'}, use_global_device_ids=true, to_apply=%region_38.39 | all-reduce | flops 8192 | bytes 65536 | tf_op jit(solution)/shard_map/psum | solution.py:409
  1099.6 30.2 %shard_map.273 = bf16[1024,1152]{1,0:T(8,128)(2,1)S(1)} custom-call(bf16[1024,1152]{1,0:T(8,128)(2,1)S(1)} %copy-done.3), custom_call_target="tpu_custom_call" | custom-call | tf_op jit(solution)/shard_map/pallas_call | solution.py:114
  1141.5 28.5 %shard_map.274 = bf16[1024,1152]{1,0:T(8,128)(2,1)S(1)} custom-call(bf16[1024,1152]{1,0:T(8,128)(2,1)S(1)} %copy-done.2), custom_call_target="tpu_custom_call" | custom-call | tf_op jit(solution)/shard_map/pallas_call | solution.py:114
  (419 shorter events, 270.5 us)
Async XLA Ops:
  7.2 126.0 %all-gather.9.cloned.1.call-start = ((), (), s32[]{:S(2)}) async-start(), calls=%async_computation.2 | async-start | bytes 7077888 | tf_op jit(solution)/shard_map/all_gather | solution.py:233
  9.6 141.9 %all-gather.11.cloned.1.call-start = ((), (), s32[]{:S(2)}) async-start(), calls=%async_computation.3 | async-start | bytes 2359296 | tf_op jit(solution)/shard_map/all_gather | solution.py:233
  10.4 222.3 %all-gather.17.cloned.1.call-start = ((), (), s32[]{:S(2)}) async-start(), calls=%async_computation.6 | async-start | bytes 2359296 | tf_op jit(solution)/shard_map/all_gather | solution.py:233
  11.2 224.3 %all-gather.13.cloned.1.call-start = ((), (), s32[]{:S(2)}) async-start(), calls=%async_computation.4 | async-start | bytes 1179648 | tf_op jit(solution)/shard_map/all_gather | solution.py:233
  11.9 230.1 %all-gather.15.cloned.1.call-start = ((), (), s32[]{:S(2)}) async-start(), calls=%async_computation.5 | async-start | bytes 1179648 | tf_op jit(solution)/shard_map/all_gather | solution.py:233
  12.7 289.3 %all-gather.19.cloned.1.call-start = ((), (), s32[]{:S(2)}) async-start(), calls=%async_computation.7 | async-start | bytes 2359296 | tf_op jit(solution)/shard_map/all_gather | solution.py:233
  99.3 85.4 %collective-permute-start.1 = (bf16[1024,1152]{1,0:T(8,128)(2,1)}, bf16[1024,1152]{1,0:T(8,128)(2,1)}, u32[]{:S(2)}, u32[]{:S(2)}) collective-permute-start(bf16[1024,1152]{1,0:T(8,128)(2,1)} %bitcast.12), channel_id=1, source_target_pairs={{0,16},{16,0},{1,17},{17,1},{2,18},{18,2},{3,19},{19,3},{4,20},{20... | collective-permute-start | bytes 7077896 | tf_op jit(solution)/shard_map/ppermute | solution.py:24
  99.3 90.8 %collective-permute-start.2 = (bf16[1024,1152]{1,0:T(8,128)(2,1)}, bf16[1024,1152]{1,0:T(8,128)(2,1)}, u32[]{:S(2)}, u32[]{:S(2)}) collective-permute-start(bf16[1024,1152]{1,0:T(8,128)(2,1)} %bitcast.13), channel_id=1, source_target_pairs={{0,16},{16,0},{1,17},{17,1},{2,18},{18,2},{3,19},{19,3},{4,20},{20... | collective-permute-start | bytes 7077896 | tf_op jit(solution)/shard_map/ppermute | solution.py:24
  99.8 42.2 %collective-permute-start.3 = (bf16[1152,1024]{1,0:T(8,128)(2,1)}, bf16[1152,1024]{1,0:T(8,128)(2,1)}, u32[]{:S(2)}, u32[]{:S(2)}) collective-permute-start(bf16[1152,1024]{1,0:T(8,128)(2,1)} %bitcast.14), channel_id=1, source_target_pairs={{0,16},{16,0},{1,17},{17,1},{2,18},{18,2},{3,19},{19,3},{4,20},{20... | collective-permute-start | bytes 7077896 | tf_op jit(solution)/shard_map/ppermute | solution.py:24
  100.6 578.7 %reduce-scatter.7.cloned.1.call-start = ((), (), s32[]{:S(2)}) async-start(), calls=%async_computation.11 | async-start | bytes 7077888
  138.1 10.8 collective-permute-start
  154.9 76.7 %copy-start.14 = (f32[256,1024]{1,0:T(8,128)}, f32[256,1024]{1,0:T(8,128)S(1)}, u32[]{:S(2)}) copy-start(f32[256,1024]{1,0:T(8,128)S(1)} %get-tuple-element.112) | copy-start | bytes 3145732
  232.6 69.4 %copy-start.18 = (bf16[256,1024]{1,0:T(8,128)(2,1)}, bf16[256,1024]{1,0:T(8,128)(2,1)S(1)}, u32[]{:S(2)}) copy-start(bf16[256,1024]{1,0:T(8,128)(2,1)S(1)} %get-tuple-element.110) | copy-start | bytes 1572868
  527.4 198.3 %reduce-scatter.5.cloned.1.call-start = ((), (), s32[]{:S(2)}) async-start(), calls=%async_computation.8 | async-start | bytes 9437184 | tf_op jit(solution)/shard_map/reduce_scatter | solution.py:380
  614.4 21.6 %collective-permute-start.4 = (f32[2,1024]{1,0:T(2,128)S(1)}, f32[2,1024]{1,0:T(2,128)S(1)}, u32[]{:S(2)}, u32[]{:S(2)}) collective-permute-start(f32[2,1024]{1,0:T(2,128)S(1)} %pad_add_fusion.1), channel_id=1, source_target_pairs={{4,0},{8,4},{12,8},{5,1},{9,5},{13,9},{6,2},{10,6},{14,10},{7,3},{... | collective-permute-start | bytes 24584 | tf_op jit(solution)/shard_map/ppermute | solution.py:20
  649.0 391.5 %all-reduce.7.cloned.1.call-start = ((), (), s32[]{:S(2)}) async-start(), calls=%async_computation.12 | async-start | bytes 17825792 | tf_op jit(solution)/shard_map/psum | solution.py:383
  657.6 13.8 %collective-permute-start.8 = (bf16[1152,1024]{1,0:T(8,128)(2,1)S(1)}, bf16[1152,1024]{1,0:T(8,128)(2,1)S(1)}, u32[]{:S(2)}, u32[]{:S(2)}) collective-permute-start(bf16[1152,1024]{1,0:T(8,128)(2,1)S(1)} %get-tuple-element.169), channel_id=1, source_target_pairs={{0,16},{16,0},{1,17},{17,1},{2,18},{18,2},{3,19},{19,3},{4,20},{20... | collective-permute-start | bytes 7077896 | tf_op jit(solution)/shard_map/ppermute | solution.py:24
  664.2 10.3 collective-permute-start.7
  671.3 5.6 collective-permute-start.6
  725.8 314.8 %copy-start.45 = (bf16[2,256,1024]{2,1,0:T(8,128)(2,1)S(1)}, bf16[2,256,1024]{2,1,0:T(8,128)(2,1)}, u32[]{:S(2)}) copy-start(bf16[2,256,1024]{2,1,0:T(8,128)(2,1)} %param.15) | copy-start | bytes 3145732
  725.8 314.8 %copy-start.59 = (bf16[256,1024]{1,0:T(8,128)(2,1)S(1)}, bf16[256,1024]{1,0:T(8,128)(2,1)}, u32[]{:S(2)}) copy-start(bf16[256,1024]{1,0:T(8,128)(2,1)} %copy-done.58) | copy-start | bytes 1572868
  725.8 458.5 %all-gather.23.cloned.1.call-start = ((), (), s32[]{:S(2)}) async-start(), calls=%async_computation.10 | async-start | bytes 2359296 | tf_op jit(solution)/shard_map/all_gather | solution.py:384
  1040.5 152.2 %all-gather.21.cloned.1.call-start = ((), (), s32[]{:S(2)}) async-start(), calls=%async_computation.9 | async-start | bytes 3145728 | tf_op jit(solution)/shard_map/all_gather | solution.py:384
  1094.7 2.6 collective-permute-start.5
  (101 other events, 784.2 us)
Sparse Core Ops, SparseCore 0:
  10.5 94.2 all-gather.8
  107.3 30.7 all-gather.10
  140.5 40.1 all-gather.16
  183.0 22.4 all-gather.12
  207.8 34.1 all-gather.14
  243.8 27.8 all-gather.18
  527.5 84.3 reduce-scatter.6
  649.1 76.6 reduce-scatter.4
  730.0 310.4 all-reduce.6
  1041.9 8.5 all-gather.22
  1097.4 10.4 all-gather.20

commit v2 on v1

--- a/solution.py
+++ b/solution.py
@@ -139,6 +139,592 @@
     count = lax.axis_size(axis)
     terms = swapped_blocks(partial.astype(BF16), axis, collective_id)
     return jnp.sum(terms.reshape(count, -1, partial.shape[1]).astype(F32), axis=0)
+
+
+def tail_kernel(
+    counts,
+    gate_in,
+    up_in,
+    down_in,
+    attn_in,
+    conv_b_in,
+    conv_c_in,
+    conv_x_in,
+    conv_o_in,
+    small_in,
+    second_gu_in,
+    second_down_in,
+    gu_out,
+    down_out,
+    rest_out,
+    a_own,
+    a_other,
+    a_sum,
+    a_done,
+    b_own,
+    b_other,
+    b_sum,
+    b_done,
+    c_own,
+    c_other,
+    c_got,
+    own_sem,
+    pair_send,
+    pair_recv,
+    c_own_sem,
+    c_pair_send,
+    c_pair_recv,
+    c_send,
+    c_recv,
+    a_up_send,
+    a_up_recv,
+    a_back_send,
+    a_back_recv,
+    a_out_send,
+    b_up_send,
+    b_up_recv,
+    b_back_send,
+    b_back_recv,
+    b_out_send,
+    b_keep_sem,
+    gu_recv,
+    down_recv,
+    rest_recv,
+    second_send,
+):
+    n_ctx, n_fsdp = counts
+    section = lax.axis_index("section")
+    place = lax.axis_index("ctx")
+    group = lax.axis_index("fsdp")
+    other = 1 - section
+    a_chunks, a_rows, a_width = a_own.shape
+    b_chunks, b_rows, b_width = b_own.shape
+    half = gate_in.shape[0] // n_fsdp // 2
+    subs = half // a_rows
+    per_kind = n_fsdp * subs
+    down_half = down_in.shape[0] // 2
+    down_chunks = down_half // b_rows
+    attn_rows = attn_in.shape[0]
+    attn_chunks = attn_rows // b_rows
+    conv_start = down_chunks + attn_chunks
+    c_rows = c_own.shape[1]
+    conv_chunks = c_rows // b_rows
+    ticks = a_chunks // 2
+    tail = 2 * (n_ctx - 1)
+
+    barrier = pltpu.get_barrier_semaphore()
+    for step in range(1, 2 * n_fsdp):
+        flat = lax.rem(section * n_fsdp + group + step, 2 * n_fsdp)
+        pl.semaphore_signal(
+            barrier,
+            inc=1,
+            device_id={"section": flat // n_fsdp, "fsdp": lax.rem(flat, n_fsdp)},
+            device_id_type=MESH,
+        )
+
+    @pl.when(place > 0)
+    def _():
+        pl.semaphore_signal(barrier, inc=1, device_id={"ctx": place - 1}, device_id_type=MESH)
+
+    @pl.when(place < n_ctx - 1)
+    def _():
+        pl.semaphore_signal(barrier, inc=1, device_id={"ctx": place + 1}, device_id_type=MESH)
+
+    at_edge = (place == 0) | (place == n_ctx - 1)
+
+    @pl.when(at_edge)
+    def _():
+        pl.semaphore_wait(barrier, 2 * n_fsdp)
+
+    @pl.when(jnp.logical_not(at_edge))
+    def _():
+        pl.semaphore_wait(barrier, 2 * n_fsdp + 1)
+
+    def half_rows(owner, which):
+        return pl.ds(pl.multiple_of(owner * (2 * half) + which * half, half), half)
+
+    local, pair = [], []
+    for kind, source in enumerate((gate_in, up_in)):
+        for owner in range(n_fsdp):
+            index = kind * n_fsdp + owner
+            slot = pl.ds(index * subs, subs)
+            for sub in range(subs):
+                src_own = source.at[pl.ds(pl.multiple_of(owner * (2 * half) + section * half + sub * a_rows, a_rows), a_rows)]
+                src_other = source.at[pl.ds(pl.multiple_of(owner * (2 * half) + other * half + sub * a_rows, a_rows), a_rows)]
+                spot = index * subs + sub
+                local.append(pltpu.make_async_copy(src_own, a_own.at[spot], own_sem.at[spot]))
+                pair.append(
+                    pltpu.make_async_remote_copy(
+                        src_ref=src_other,
+                        dst_ref=a_other.at[spot],
+                        send_sem=pair_send.at[spot],
+                        recv_sem=pair_recv.at[spot],
+                        device_id={"section": other},
+                        device_id_type=MESH,
+                    )
+                )
+    for chunk in range(down_chunks):
+        spot = a_chunks + chunk
+        src_own = down_in.at[pl.ds(pl.multiple_of(section * down_half + chunk * b_rows, b_rows), b_rows)]
+        src_other = down_in.at[pl.ds(pl.multiple_of(other * down_half + chunk * b_rows, b_rows), b_rows)]
+        local.append(pltpu.make_async_copy(src_own, b_own.at[chunk], own_sem.at[spot]))
+        pair.append(
+            pltpu.make_async_remote_copy(
+                src_ref=src_other,
+                dst_ref=b_other.at[chunk],
+                send_sem=pair_send.at[spot],
+                recv_sem=pair_recv.at[spot],
+                device_id={"section": other},
+                device_id_type=MESH,
+            )
+        )
+    for chunk in range(attn_chunks):
+        local.append(
+            pltpu.make_async_copy(
+                attn_in.at[pl.ds(chunk * b_rows, b_rows)],
+                b_own.at[down_chunks + chunk],
+                own_sem.at[a_chunks + down_chunks + chunk],
+            )
+        )
+    for copy in pair:
+        copy.start()
+    for copy in local:
+        copy.start()
+    c_local, c_pair = [], []
+    for owner in range(n_fsdp):
+        for kind, source in enumerate((conv_b_in, conv_c_in, conv_x_in, conv_o_in)):
+            index = owner * 5 + kind
+            place_at = pl.ds(kind * half, half)
+            c_local.append(
+                pltpu.make_async_copy(
+                    source.at[half_rows(owner, section)], c_own.at[owner, place_at], c_own_sem.at[index]
+                )
+            )
+            c_pair.append(
+                pltpu.make_async_remote_copy(
+                    src_ref=source.at[half_rows(owner, other)],
+                    dst_ref=c_other.at[owner, place_at],
+                    send_sem=c_pair_send.at[index],
+                    recv_sem=c_pair_recv.at[index],
+                    device_id={"section": other},
+                    device_id_type=MESH,
+                )
+            )
+        small_at = pl.ds(4 * half, c_rows - 4 * half)
+        index = owner * 5 + 4
+        c_local.append(
+            pltpu.make_async_copy(small_in.at[owner, section], c_own.at[owner, small_at], c_own_sem.at[index])
+        )
+        c_pair.append(
+            pltpu.make_async_remote_copy(
+                src_ref=small_in.at[owner, other],
+                dst_ref=c_other.at[owner, small_at],
+                send_sem=c_pair_send.at[index],
+                recv_sem=c_pair_recv.at[index],
+                device_id={"section": other},
+                device_id_type=MESH,
+            )
+        )
+    for copy in c_pair:
+        copy.start()
+    for copy in c_local:
+        copy.start()
+    b_own[b_chunks - 1] = jnp.zeros((b_rows, b_width), BF16)
+    for copy in local:
+        copy.wait()
+    for copy in pair:
+        copy.wait_recv()
+
+    def conv_copy(step):
+        target = lax.rem(group + step, n_fsdp)
+        return pltpu.make_async_remote_copy(
+            src_ref=c_own.at[target],
+            dst_ref=c_got.at[step - 1],
+            send_sem=c_send.at[step],
+            recv_sem=c_recv.at[step],
+            device_id={"fsdp": target},
+            device_id_type=MESH,
+        )
+
+    def conv_out_step():
+        for copy in c_local:
+            copy.wait()
+        for copy in c_pair:
+            copy.wait_recv()
+
+        def add(index, carry):
+            owner = index // conv_chunks
+            at = pl.ds(pl.multiple_of(lax.rem(index, conv_chunks) * b_rows, b_rows), b_rows)
+            c_own[owner, at] = (c_own[owner, at].astype(F32) + c_other[owner, at].astype(F32)).astype(BF16)
+            return carry
+
+        lax.fori_loop(0, n_fsdp * conv_chunks, add, 0)
+        for step in range(1, n_fsdp):
+            conv_copy(step).start()
+
+    def conv_in_step():
+        for step in range(1, n_fsdp):
+            conv_copy(step).wait_recv()
+
+        def add(index, carry):
+            at = pl.ds(pl.multiple_of(index * b_rows, b_rows), b_rows)
+            total = c_own[group, at].astype(F32)
+            for step in range(1, n_fsdp):
+                total = total + c_got[step - 1, at].astype(F32)
+            b_own[conv_start + index] = total.astype(BF16)
+            return carry
+
+        lax.fori_loop(0, conv_chunks, add, 0)
+
+    def second_start():
+        for kind in range(2):
+            for owner in range(n_fsdp):
+                index = kind * n_fsdp + owner
+                src = second_gu_in.at[kind, owner]
+                dst = gu_out.at[
+                    kind,
+                    pl.ds(pl.multiple_of(section * half, half), half),
+                    pl.ds(pl.multiple_of(group * a_width, 128), a_width),
+                ]
+                is_mine = (section == 1) & (group == owner)
+
+                @pl.when(is_mine)
+                def _(src=src, dst=dst, index=index):
+                    pltpu.make_async_copy(src, dst, second_send.at[index]).start()
+
+                @pl.when(jnp.logical_not(is_mine))
+                def _(src=src, dst=dst, index=index, kind=kind, owner=owner):
+                    pltpu.make_async_remote_copy(
+                        src_ref=src,
+                        dst_ref=dst,
+                        send_sem=second_send.at[index],
+                        recv_sem=gu_recv.at[kind, section * n_fsdp + group],
+                        device_id={"section": 1, "fsdp": owner},
+                        device_id_type=MESH,
+                    ).start()
+
+        down_at = down_out.at[pl.ds(pl.multiple_of(section * down_half, b_rows), down_half)]
+
+        @pl.when(section == 1)
+        def _():
+            pltpu.make_async_copy(second_down_in, down_at, second_send.at[2 * n_fsdp]).start()
+
+        @pl.when(section == 0)
+        def _():
+            pltpu.make_async_remote_copy(
+                src_ref=second_down_in,
+                dst_ref=down_at,
+                send_sem=second_send.at[2 * n_fsdp],
+                recv_sem=down_recv,
+                device_id={"section": 1},
+                device_id_type=MESH,
+            ).start()
+
+    def a_target(k):
+        kind = k // per_kind
+        rest = lax.rem(k, per_kind)
+        owner = rest // subs
+        sub = lax.rem(rest, subs)
+        spot = gu_out.at[
+            kind,
+            pl.ds(pl.multiple_of(section * half + sub * a_rows, a_rows), a_rows),
+            pl.ds(pl.multiple_of(group * a_width, 128), a_width),
+        ]
+        return kind, owner, spot
+
+    def hand_out(k):
+        kind, owner, spot = a_target(k)
+        is_mine = (section == 0) & (group == owner)
+
+        @pl.when(is_mine)
+        def _():
+            pltpu.make_async_copy(a_done.at[k], spot, a_out_send.at[k]).start()
+
+        @pl.when(jnp.logical_not(is_mine))
+        def _():
+            pltpu.make_async_remote_copy(
+                src_ref=a_done.at[k],
+                dst_ref=spot,
+                send_sem=a_out_send.at[k],
+                recv_sem=gu_recv.at[kind, section * n_fsdp + group],
+                device_id={"section": 0, "fsdp": owner},
+                device_id_type=MESH,
+            ).start()
+
+        @pl.when(k < down_chunks)
+        def _():
+            at = down_out.at[pl.ds(pl.multiple_of(section * down_half + k * b_rows, b_rows), b_rows)]
+
+            @pl.when(section == 0)
+            def _():
+                pltpu.make_async_copy(b_done.at[k], at, b_out_send.at[k]).start()
+
+            @pl.when(section == 1)
+            def _():
+                pltpu.make_async_remote_copy(
+                    src_ref=b_done.at[k],
+                    dst_ref=at,
+                    send_sem=b_out_send.at[k],
+                    recv_sem=down_recv,
+                    device_id={"section": 0},
+                    device_id_type=MESH,
+                ).start()
+
+        @pl.when(k >= down_chunks)
+        def _():
+            at = rest_out.at[section, pl.ds(pl.multiple_of((k - down_chunks) * b_rows, b_rows), b_rows)]
+            pltpu.make_async_copy(b_done.at[k], at, b_keep_sem.at[k]).start()
+            pltpu.make_async_remote_copy(
+                src_ref=b_done.at[k],
+                dst_ref=at,
+                send_sem=b_out_send.at[k],
+                recv_sem=rest_recv,
+                device_id={"section": other},
+                device_id_type=MESH,
+            ).start()
+
+    def up_copies(k, target):
+        return (
+            pltpu.make_async_remote_copy(
+                src_ref=a_sum.at[k],
+                dst_ref=a_sum.at[k],
+                send_sem=a_up_send.at[k],
+                recv_sem=a_up_recv.at[k],
+                device_id={"ctx": target},
+                device_id_type=MESH,
+            ),
+            pltpu.make_async_remote_copy(
+                src_ref=b_sum.at[k],
+                dst_ref=b_sum.at[k],
+                send_sem=b_up_send.at[k],
+                recv_sem=b_up_recv.at[k],
+                device_id={"ctx": target},
+                device_id_type=MESH,
+            ),
+        )
+
+    def back_copies(k, target):
+        return (
+            pltpu.make_async_remote_copy(
+                src_ref=a_done.at[k],
+                dst_ref=a_done.at[k],
+                send_sem=a_back_send.at[k],
+                recv_sem=a_back_recv.at[k],
+                device_id={"ctx": target},
+                device_id_type=MESH,
+            ),
+            pltpu.make_async_remote_copy(
+                src_ref=b_done.at[k],
+                dst_ref=b_done.at[k],
+                send_sem=b_back_send.at[k],
+                recv_sem=b_back_recv.at[k],
+                device_id={"ctx": target},
+                device_id_type=MESH,
+            ),
+        )
+
+    def own_term(k):
+        @pl.when(k < down_chunks)
+        def _():
+            b_own[k] = (b_own[k].astype(F32) + b_other[k].astype(F32)).astype(BF16)
+
+        return a_own[k].astype(F32) + a_other[k].astype(F32)
+
+    lanes = []
+    for way in range(2):
+        rank = place if way == 0 else n_ctx - 1 - place
+        ahead = place + 1 if way == 0 else place - 1
+        behind = place - 1 if way == 0 else place + 1
+        lanes.append((way, rank, ahead, behind))
+
+    def tick_step(tick, carry):
+        @pl.when(tick == 1)
+        def _():
+            conv_out_step()
+
+        @pl.when(tick == ticks // 2)
+        def _():
+            second_start()
+
+        @pl.when(tick == conv_start // 2)
+        def _():
+            conv_in_step()
+
+        for way, rank, ahead, behind in lanes:
+            step = tick - rank
+            k = 2 * jnp.clip(step, 0, ticks - 1) + way
+
+            @pl.when((step >= 0) & (step < ticks))
+            def _(k=k, rank=rank, ahead=ahead, behind=behind):
+                term = own_term(k)
+
+                @pl.when(rank == 0)
+                def _():
+                    a_sum[k] = term.astype(BF16)
+                    b_sum[k] = b_own[k]
+
+                @pl.when(rank > 0)
+                def _():
+                    for copy in up_copies(k, behind):
+                        copy.wait_recv()
+
+                @pl.when((rank > 0) & (rank < n_ctx - 1))
+                def _():
+                    a_sum[k] = (term + a_sum[k].astype(F32)).astype(BF16)
+                    b_sum[k] = (b_own[k].astype(F32) + b_sum[k].astype(F32)).astype(BF16)
+
+                @pl.when(rank < n_ctx - 1)
+                def _():
+                    for copy in up_copies(k, ahead):
+                        copy.start()
+
+                @pl.when(rank == n_ctx - 1)
+                def _():
+                    a_done[k] = (term + a_sum[k].astype(F32)).astype(BF16)
+                    b_done[k] = (b_own[k].astype(F32) + b_sum[k].astype(F32)).astype(BF16)
+                    for copy in back_copies(k, behind):
+                        copy.start()
+                    hand_out(k)
+
+            late = tick - (tail - rank)
+            j = 2 * jnp.clip(late, 0, ticks - 1) + way
+
+            @pl.when((late >= 0) & (late < ticks) & (rank < n_ctx - 1))
+            def _(j=j, rank=rank, ahead=ahead, behind=behind):
+                for copy in back_copies(j, ahead):
+                    copy.wait_recv()
+
+                @pl.when(rank > 0)
+                def _():
+                    for copy in back_copies(j, behind):
+                        copy.start()
+
+                hand_out(j)
+
+        return carry
+
+    lax.fori_loop(0, ticks + tail, tick_step, 0)
+
+    for copy in pair:
+        copy.wait_send()
+    for copy in c_pair:
+        copy.wait_send()
+    for step in range(1, n_fsdp):
+        conv_copy(step).wait_send()
+
+    def settle(step, carry):
+        for way, rank, ahead, behind in lanes:
+            k = 2 * step + way
+
+            @pl.when(rank < n_ctx - 1)
+            def _(k=k, ahead=ahead):
+                for copy in up_copies(k, ahead):
+                    copy.wait_send()
+
+            @pl.when(rank > 0)
+            def _(k=k, behind=behind):
+                for copy in back_copies(k, behind):
+                    copy.wait_send()
+
+            _, _, spot = a_target(k)
+            pltpu.make_async_copy(a_done.at[k], spot, a_out_send.at[k]).wait()
+            pltpu.make_async_copy(b_done.at[k], b_own.at[k], b_out_send.at[k]).wait()
+
+            @pl.when(k >= down_chunks)
+            def _(k=k):
+                pltpu.make_async_copy(b_done.at[k], b_own.at[k], b_keep_sem.at[k]).wait()
+
+        return carry
+
+    lax.fori_loop(0, ticks, settle, 0)
+    for kind in range(2):
+        for owner in range(n_fsdp):
+            src = second_gu_in.at[kind, owner]
+            pltpu.make_async_copy(src, src, second_send.at[kind * n_fsdp + owner]).wait()
+    pltpu.make_async_copy(second_down_in, second_down_in, second_send.at[2 * n_fsdp]).wait()
+    for kind in range(2):
+        for source in range(2 * n_fsdp):
+
+            @pl.when(section * n_fsdp + group != source)
+            def _(kind=kind, source=source):
+                region = gu_out.at[
+                    kind,
+                    pl.ds((source // n_fsdp) * half, half),
+                    pl.ds((source % n_fsdp) * a_width, a_width),
+                ]
+                pltpu.make_async_copy(region, region, gu_recv.at[kind, source]).wait()
+
+    region = down_out.at[pl.ds(pl.multiple_of(other * down_half, b_rows), down_half)]
+    pltpu.make_async_copy(region, region, down_recv).wait()
+    region = rest_out.at[other]
+    pltpu.make_async_copy(region, region, rest_recv).wait()
+
+
+def summed_gradients(first, attn_half, conv_grads, small, second_gu, second_down):
+    n_ctx, n_fsdp = lax.axis_size("ctx"), lax.axis_size("fsdp")
+    gate, up, down = first
+    half = gate.shape[0] // n_fsdp // 2
+    a_rows, b_rows = half // 4, half * 3 // 8
+    a_chunks = 2 * n_fsdp * 4
+    a_width, b_width = gate.shape[1], down.shape[1]
+    c_rows = 4 * half + small.shape[2]
+    down_chunks = down.shape[0] // 2 // b_rows
+    attn_chunks = attn_half.shape[0] // b_rows
+    conv_chunks = c_rows // b_rows
+    b_chunks = down_chunks + attn_chunks + conv_chunks + 1
+    assert a_chunks == b_chunks and c_rows % b_rows == 0
+    rest = b_chunks - down_chunks
+    dma = pltpu.SemaphoreType.DMA
+    loads = a_chunks + down_chunks + attn_chunks
+    return pl.pallas_call(
+        functools.partial(tail_kernel, (n_ctx, n_fsdp)),
+        out_shape=(
+            jax.ShapeDtypeStruct((2, 2 * half, n_fsdp * a_width), BF16),
+            jax.ShapeDtypeStruct(down.shape, BF16),
+            jax.ShapeDtypeStruct((2, rest * b_rows, b_width), BF16),
+        ),
+        in_specs=[pl.BlockSpec(memory_space=pl.ANY)] * 11,
+        out_specs=[pl.BlockSpec(memory_space=pl.ANY)] * 3,
+        scratch_shapes=[
+            pltpu.VMEM((a_chunks, a_rows, a_width), BF16),
+            pltpu.VMEM((a_chunks, a_rows, a_width), BF16),
+            pltpu.VMEM((a_chunks, a_rows, a_width), BF16),
+            pltpu.VMEM((a_chunks, a_rows, a_width), BF16),
+            pltpu.VMEM((b_chunks, b_rows, b_width), BF16),
+            pltpu.VMEM((down_chunks, b_rows, b_width), BF16),
+            pltpu.VMEM((b_chunks, b_rows, b_width), BF16),
+            pltpu.VMEM((b_chunks, b_rows, b_width), BF16),
+            pltpu.VMEM((n_fsdp, c_rows, b_width), BF16),
+            pltpu.VMEM((n_fsdp, c_rows, b_width), BF16),
+            pltpu.VMEM((n_fsdp - 1, c_rows, b_width), BF16),
+            dma((loads,)),
+            dma((loads,)),
+            dma((loads,)),
+            dma((n_fsdp * 5,)),
+            dma((n_fsdp * 5,)),
+            dma((n_fsdp * 5,)),
+            dma((n_fsdp,)),
+            dma((n_fsdp,)),
+            dma((a_chunks,)),
+            dma((a_chunks,)),
+            dma((a_chunks,)),
+            dma((a_chunks,)),
+            dma((a_chunks,)),
+            dma((b_chunks,)),
+            dma((b_chunks,)),
+            dma((b_chunks,)),
+            dma((b_chunks,)),
+            dma((b_chunks,)),
+            dma((b_chunks,)),
+            dma((2, 2 * n_fsdp)),
+            dma,
+            dma,
+            dma((2 * n_fsdp + 1,)),
+        ],
+        compiler_params=pltpu.CompilerParams(
+            collective_id=6, has_side_effects=True, vmem_limit_bytes=56 << 20
+        ),
+    )(gate, up, down, attn_half, *conv_grads, small, second_gu, second_down)
 
 
 def attend(query, key_all, value_all, allowed):
@@ -366,7 +952,6 @@
     d_projected = jnp.concatenate(
         [d_bproduct * x_value, d_cgate, d_bproduct * b_gate], axis=1
     ).astype(BF16)
-    grad_in = matmul_left(act1, d_projected)
     d_act1 = matmul_right(d_projected, in_full)
     gain0 = jnp.sum(d_act1 * normed0, axis=0)
     d_x = (d_res1 + norm_back(d_act1 * norm_gains[0], normed0, inv0)).astype(BF16)
@@ -376,59 +961,91 @@
     other_end = swapped(jnp.where(is_first, y_low, d_x), "section")
     ends = jnp.where(is_first, jnp.stack([d_x, other_end]), jnp.stack([other_end, y_low]))[None]
 
-    def own_rows(grad):
-        share = lax.psum_scatter(
-            grad.astype(BF16), ("fsdp", "section"), scatter_dimension=0, tiled=True
-        )
-        total = lax.psum(share, "ctx")
-        return lax.all_gather(total, "section", axis=0, tiled=True).astype(F32)
-
-    conv_grads = own_rows(jnp.concatenate([grad_in, grad_out], axis=1))
-    attn_grads = own_rows(jnp.concatenate([grad_query, grad_key, grad_value, grad_proj], axis=1))
-
-    def own_section(first, second):
-        mine = jnp.where(is_first, first, second)
-        other = swapped(jnp.where(is_first, second, first), "section")
+    grad_parts = [
+        matmul_left(act1, d_projected[:, i * width : (i + 1) * width]).astype(BF16) for i in range(3)
+    ]
+    attn_half = lax.psum_scatter(
+        jnp.concatenate([grad_query, grad_key, grad_value, grad_proj], axis=1).astype(BF16),
+        ("fsdp", "section"),
+        scatter_dimension=0,
+        tiled=True,
+    )
+    attn_half = jnp.concatenate(
+        [attn_half[:, i * width : (i + 1) * width] for i in range(attn_half.shape[1] // width)], axis=0
+    )
+
+    half = part // 2
+
+    def shared_halves(grad, lead):
+        pieces = grad.reshape(lead, 2, -1, grad.shape[1])
+        mine = lax.dynamic_index_in_dim(pieces, section, 1, keepdims=False)
+        other = swapped(lax.dynamic_index_in_dim(pieces, 1 - section, 1, keepdims=False), "section")
         return (mine.astype(F32) + other.astype(F32)).astype(BF16)
 
-    ffn_grads = lax.psum(tuple(own_section(a, b) for a, b in zip(grads1, grads2)), "ctx")
-
-    def to_rows(grad):
-        return swapped_blocks(grad, "fsdp", 5).reshape(fsdp, part, -1).transpose(1, 0, 2).reshape(part, -1)
-
-    small = jnp.concatenate(
+    second = lax.psum(
+        (
+            shared_halves(grads2[0], fsdp),
+            shared_halves(grads2[1], fsdp),
+            shared_halves(grads2[2], 1)[0],
+        ),
+        "ctx",
+    )
+    cut = width // fsdp
+    head_cut = head // fsdp
+    square_cut = squares.shape[0] // fsdp
+    by_owner = jnp.concatenate(
         [
-            jnp.stack([gain0, gain1, gain2, gain3]).reshape(-1),
-            grad_kernel.reshape(-1),
-            grad_qgain,
-            grad_kgain,
-            squares,
-            jnp.zeros((width - 2 * head - squares.shape[0],), F32),
-        ]
-    ).reshape(-1, width)
-    small = lax.psum(small, ("section", "ctx", "fsdp"))
-    cut = width // fsdp
-    mine = lax.dynamic_slice_in_dim(small, group * cut, cut, 1)
-    head_cut = head // fsdp
-    heads = lax.dynamic_slice_in_dim(small[7, : 2 * head].reshape(2, head), group * head_cut, head_cut, 1)
+            jnp.concatenate([jnp.stack([gain0, gain1, gain2, gain3]), grad_kernel])
+            .reshape(7, fsdp, cut)
+            .transpose(1, 0, 2)
+            .reshape(fsdp, 7 * cut),
+            jnp.stack([grad_qgain, grad_kgain])
+            .reshape(2, fsdp, head_cut)
+            .transpose(1, 0, 2)
+            .reshape(fsdp, 2 * head_cut),
+            squares.reshape(fsdp, square_cut),
+            jnp.zeros((fsdp, cut - 2 * head_cut - square_cut), F32),
+        ],
+        axis=1,
+    ).reshape(fsdp, 1, -1, width)
+    small = jnp.pad(by_owner, ((0, 0), (0, 1), (0, 16 - by_owner.shape[2]), (0, 0))).astype(BF16)
+    gu_sum, down_sum, rest_sum = summed_gradients(
+        grads1,
+        attn_half,
+        grad_parts + [grad_out.astype(BF16)],
+        small,
+        jnp.stack([second[0], second[1]]),
+        second[2],
+    )
+    rest_sum = rest_sum.astype(F32)
+
+    def block(index):
+        rows_at = slice(index * half, (index + 1) * half)
+        return rest_sum[:, rows_at].reshape(2 * half, width)
+
+    attn_blocks = [block(i) for i in range(3)]
+    conv_blocks = [block(3 + i) for i in range(4)]
+    small_sum = rest_sum[0, 7 * half : 7 * half + 2].reshape(-1)
+    mine = small_sum[: 7 * cut].reshape(7, cut)
+    heads = small_sum[7 * cut : 7 * cut + 2 * head_cut].reshape(2, head_cut)
+    square_sum = small_sum[7 * cut + 2 * head_cut : 7 * cut + 2 * head_cut + square_cut]
     token_total = jnp.sum(lengths).astype(F32) * width
-    rms_all = jnp.sqrt(small[7, 2 * head : 2 * head + 8] / token_total)
-    rms = lax.dynamic_slice_in_dim(rms_all, group * (8 // fsdp), 8 // fsdp)
+    rms = jnp.sqrt(square_sum / token_total)
     return (
         ends,
         mine[:3],
         mine[3],
-        conv_grads[:, : 3 * width],
+        jnp.concatenate(conv_blocks[:3], axis=1),
         mine[4:7],
-        conv_grads[:, 3 * width :],
-        attn_grads[:, :q_width],
-        attn_grads[:, q_width : q_width + kv_width],
-        attn_grads[:, q_width + kv_width : q_width + 2 * kv_width],
-        attn_grads[:, q_width + 2 * kv_width :],
+        conv_blocks[3],
+        attn_blocks[0],
+        attn_blocks[1][:, :kv_width],
+        attn_blocks[1][:, kv_width:],
+        attn_blocks[2],
         heads,
-        to_rows(ffn_grads[0])[None].astype(F32),
-        to_rows(ffn_grads[1])[None].astype(F32),
-        ffn_grads[2][None].astype(F32),
+        gu_sum[0][None].astype(F32),
+        gu_sum[1][None].astype(F32),
+        down_sum[None].astype(F32),
         rms,
     )
 

time: 1210 us -> 921 us (0.76)
  waiting for transfers between devices: 377 us -> 70.6 us
  Pallas kernels: 437 us -> 524 us
  blocking collectives: 39.4 us -> 0 us
  local copies, waits for them, and re-layouts: 98.1 us -> 64.8 us
    psum x1, waiting for transfers between devices: 313 us -> 9.48 us  [shards(): lax.psum((shared_halves(grads2[0], fsdp), shared_halves(grads2[1], fsdp),...]
    pallas_call x0 -> x1, Pallas kernels: none -> 155 us  [summed_gradients(): pl.pallas_call(functools.partial(tail_kernel, (n_ctx, n_fsdp)), out_shape...]
    pallas_call x13 -> x11, Pallas kernels: 437 us -> 369 us  [exchange(): pl.pallas_call(functools.partial(kernel, axis, count, rows), out_shape=ja...]
    psum x1 -> x0, blocking collectives: 39.4 us -> none  [shards(): small = lax.psum(small, ('section', 'ctx', 'fsdp'))]
    convert_element_type x4 -> x0, local copies, waits for them, and re-layouts: 22.6 us -> none  [the longest x2 11.3 us: shards(): to_rows(ffn_grads[0])[None].astype(F32)]
    ppermute x2, waiting for transfers between devices: 18.9 us -> 0.01 us  [passed_along(): return lax.ppermute(block, axis, route)]
    unnamed x217 -> x206, local copies, waits for them, and re-layouts: 34.3 us -> 15.9 us
    reduce_scatter x1, waiting for transfers between devices: 44 us -> 61 us  [shards(): lax.psum_scatter(jnp.concatenate([grad_query, grad_key, grad_value, grad_...]
  transfers between devices with their start and end apart: 20 -> 17, of which waited for: 4 -> 2; matrix products, arithmetic and copies ran while one was open for 17% -> 20% of each run, Pallas kernels for 26% -> 32%
where the time goes in v2:
time: 921 us; the launch traced here: 912 us
  Pallas kernels  524 us (57%)
  matrix products  173 us (19%)
  waiting for transfers between devices  70.6 us (8%)
  local copies, waits for them, and re-layouts  64.8 us (7%)
  other arithmetic  57.2 us (6%)
  between operations  16.7 us (2%)
    pallas_call x11, Pallas kernels, exchange(): pl.pallas_call(functools.partial(kernel, axis, count, rows), out_shape=ja...  369 us
    pallas_call x1, Pallas kernels, summed_gradients(): pl.pallas_call(functools.partial(tail_kernel, (n_ctx, n_fsdp)), out_shape...  155 us
    reduce_scatter x1, waiting for transfers between devices, shards(): lax.psum_scatter(jnp.concatenate([grad_query, grad_key, grad_value, grad_...  61 us
    dot_general x12, matrix products, matmul(): return jnp.dot(left_op, right_op, preferred_element_type=F32)  54.3 us
    dot_general x12, matrix products, matmul_right(): lax.dot_general(left_op, right_op, (((1,), (1,)), ((), ())), preferred_el...  49.1 us
    dot_general x14, matrix products, matmul_left(): lax.dot_general(left_op, right_op, (((0,), (0,)), ((), ())), preferred_el...  36.9 us
  transfers between devices with their start and end apart: 17, of which 2 were waited for; matrix products, arithmetic and copies ran while one was open for 20% of the time, Pallas kernels for 32%

profile of v2, /device:TPU:0, one launch (start us, length us, event | category | flops | bytes accessed | tf_op | source)
XLA Modules:
  0.0 912.5 jit_solution(541751870753636898)
XLA Ops:
  22.1 74.6 %shard_map.263 = bf16[2048,1152]{1,0:T(8,128)(2,1)S(1)} custom-call(bf16[2048,1152]{1,0:T(8,128)(2,1)S(1)} %bitcast.267), custom_call_target="tpu_custom_call" | custom-call | tf_op jit(solution)/shard_map/pallas_call | solution.py:114
  103.5 29.8 %shard_map.266 = bf16[1024,1024]{1,0:T(8,128)(2,1)S(1)} custom-call(bf16[256,1024]{1,0:T(8,128)(2,1)S(1)} %fusion.69.block), custom_call_target="tpu_custom_call" | custom-call | tf_op jit(solution)/shard_map/pallas_call | solution.py:114
  143.1 6.9 fusion.78
  156.4 26.8 %shard_map.262 = bf16[1024,1024]{1,0:T(8,128)(2,1)S(1)} custom-call(bf16[256,1024]{1,0:T(8,128)(2,1)S(1)} %multiply_convert_fusion.9.block), custom_call_target="tpu_custom_call" | custom-call | tf_op jit(solution)/shard_map/pallas_call | solution.py:114
  188.7 8.1 multiply_convert_fusion.5
  202.5 27.1 %shard_map.264 = bf16[1024,1024]{1,0:T(8,128)(2,1)S(1)} custom-call(bf16[1024,1024]{1,0:T(8,128)(2,1)S(1)} %convolution_convert_fusion.7.blocks), custom_call_target="tpu_custom_call" | custom-call | tf_op jit(solution)/shard_map/pallas_call | solution.py:114
  245.1 38.0 %shard_map.265 = bf16[1024,1024]{1,0:T(8,128)(2,1)S(1)} custom-call(bf16[256,1024]{1,0:T(8,128)(2,1)S(1)} %pad_maximum_fusion.6.block), custom_call_target="tpu_custom_call" | custom-call | tf_op jit(solution)/shard_map/pallas_call | solution.py:114
  299.0 5.8 fusion.120
  307.6 24.4 %shard_map.267 = bf16[1024,1024]{1,0:T(8,128)(2,1)S(1)} custom-call(bf16[256,1024]{1,0:T(8,128)(2,1)S(1)} %multiply_convert_fusion.7.block), custom_call_target="tpu_custom_call" | custom-call | tf_op jit(solution)/shard_map/pallas_call | solution.py:114
  336.7 6.8 multiply_convert_fusion.4
  353.4 23.5 %shard_map.272 = bf16[1024,1024]{1,0:T(8,128)(2,1)S(1)} custom-call(bf16[1024,1024]{1,0:T(8,128)(2,1)S(1)} %convolution_convert_fusion.6.blocks), custom_call_target="tpu_custom_call" | custom-call | tf_op jit(solution)/shard_map/pallas_call | solution.py:114
  394.8 24.2 %shard_map.268 = bf16[1024,1024]{1,0:T(8,128)(2,1)S(1)} custom-call(bf16[1024,1024]{1,0:T(8,128)(2,1)S(1)} %add_convert_fusion.1.blocks), custom_call_target="tpu_custom_call" | custom-call | tf_op jit(solution)/shard_map/pallas_call | solution.py:114
  426.3 8.8 bitcast_convert_fusion.1
  435.1 8.9 fusion.1
  456.2 48.7 %shard_map.269 = bf16[1024,1024]{1,0:T(8,128)(2,1)S(1)} custom-call(bf16[1024,1024]{1,0:T(8,128)(2,1)S(1)} %pad_maximum_fusion.4.blocks), custom_call_target="tpu_custom_call" | custom-call | tf_op jit(solution)/shard_map/pallas_call | solution.py:114
  525.8 24.7 %shard_map.270 = bf16[1024,1024]{1,0:T(8,128)(2,1)S(1)} custom-call(bf16[256,1024]{1,0:T(8,128)(2,1)S(1)} %fusion.61.block), custom_call_target="tpu_custom_call" | custom-call | tf_op jit(solution)/shard_map/pallas_call | solution.py:114
  556.3 8.5 multiply_convert_fusion.2
  564.8 7.0 fusion.72
  572.1 6.6 add_convert_fusion.blocks
  578.7 26.8 %shard_map.271 = bf16[1024,1024]{1,0:T(8,128)(2,1)S(1)} custom-call(bf16[1024,1024]{1,0:T(8,128)(2,1)S(1)} %add_convert_fusion.blocks), custom_call_target="tpu_custom_call" | custom-call | tf_op jit(solution)/shard_map/pallas_call | solution.py:114
  635.0 6.7 fusion.56
  655.2 9.5 %all-reduce.8.cloned.1.call-done = (bf16[1,4,128,1152]{3,2,1,0:T(8,128)(2,1)}, bf16[1,4,128,1152]{3,2,1,0:T(8,128)(2,1)}, bf16[576,1024]{1,0:T(8,128)(2,1)}) async-done(((bf16[1,4,128,1152]{3,2,1,0:T(8,128)(2,1)}, bf16[1,4,128,1152]{3,2,1,0:T(8,128)(2,1)}, bf16[576,1024]{1,0:T(8,128)(2,1)}), (bf16[1,4,128,1152]{3,2,1,0:T(8,128)(2,1)}, bf16[1,4,128,1152]{3,2,1,0:T(8,128)(2,1)}, ...) | async-done | bytes 3538960 | tf_op jit(solution)/shard_map/psum | solution.py:985
  668.0 61.0 %reduce-scatter.2.cloned.1.call-done = bf16[128,3072]{1,0:T(8,128)(2,1)} async-done(((bf16[1024,3072]{1,0:T(8,128)(2,1)}), bf16[128,3072]{1,0:T(8,128)(2,1)}) %reduce-scatter.2.cloned.1.call-update) | async-done | bytes 786448 | tf_op jit(solution)/shard_map/reduce_scatter | solution.py:967
  731.0 155.3 %shard_map.273 = (bf16[2,256,4608]{2,1,0:T(8,128)(2,1)}, bf16[1152,1024]{1,0:T(8,128)(2,1)}, bf16[2,960,1024]{2,1,0:T(8,128)(2,1)}) custom-call(bf16[1024,1152]{1,0:T(8,128)(2,1)} %convolution_convert_fusion.5.gate_in, bf16[1024,1152]{1,0:T(8,128)(2,1)} %convolution_convert_fusion.4.up_in, bf16[1152,1024]{1,0:T(8,128)(2,1)} %convolution_convert_fusion.3.down_in, ...), custom_call_target="tpu_custom_call" | custom-call | tf_op jit(solution)/shard_map/pallas_call | solution.py:679
  (412 shorter events, 227.3 us)
Async XLA Ops:
  7.2 127.4 %all-gather.7.cloned.1.call-start = ((), (), s32[]{:S(2)}) async-start(), calls=%async_computation.1 | async-start | bytes 7077888 | tf_op jit(solution)/shard_map/all_gather | solution.py:819
  9.6 143.2 %all-gather.9.cloned.1.call-start = ((), (), s32[]{:S(2)}) async-start(), calls=%async_computation.2 | async-start | bytes 2359296 | tf_op jit(solution)/shard_map/all_gather | solution.py:819
  10.4 220.7 %all-gather.11.cloned.1.call-start = ((), (), s32[]{:S(2)}) async-start(), calls=%async_computation.3 | async-start | bytes 1179648 | tf_op jit(solution)/shard_map/all_gather | solution.py:819
  11.1 226.9 %all-gather.15.cloned.1.call-start = ((), (), s32[]{:S(2)}) async-start(), calls=%async_computation.5 | async-start | bytes 2359296 | tf_op jit(solution)/shard_map/all_gather | solution.py:819
  12.0 231.1 %all-gather.13.cloned.1.call-start = ((), (), s32[]{:S(2)}) async-start(), calls=%async_computation.4 | async-start | bytes 1179648 | tf_op jit(solution)/shard_map/all_gather | solution.py:819
  12.7 292.0 %all-gather.17.cloned.1.call-start = ((), (), s32[]{:S(2)}) async-start(), calls=%async_computation.6 | async-start | bytes 2359296 | tf_op jit(solution)/shard_map/all_gather | solution.py:819
  99.3 34.0 %copy-start.17 = (bf16[2,256,1024]{2,1,0:T(8,128)(2,1)S(1)}, bf16[2,256,1024]{2,1,0:T(8,128)(2,1)}, u32[]{:S(2)}) copy-start(bf16[2,256,1024]{2,1,0:T(8,128)(2,1)} %param.15) | copy-start | bytes 3145732
  99.3 89.4 %collective-permute-start.2 = (bf16[1024,1152]{1,0:T(8,128)(2,1)}, bf16[1024,1152]{1,0:T(8,128)(2,1)}, u32[]{:S(2)}, u32[]{:S(2)}) collective-permute-start(bf16[1024,1152]{1,0:T(8,128)(2,1)} %bitcast.13), channel_id=1, source_target_pairs={{0,16},{16,0},{1,17},{17,1},{2,18},{18,2},{3,19},{19,3},{4,20},{20... | collective-permute-start | bytes 7077896 | tf_op jit(solution)/shard_map/ppermute | solution.py:24
  99.3 83.9 %collective-permute-start.1 = (bf16[1024,1152]{1,0:T(8,128)(2,1)}, bf16[1024,1152]{1,0:T(8,128)(2,1)}, u32[]{:S(2)}, u32[]{:S(2)}) collective-permute-start(bf16[1024,1152]{1,0:T(8,128)(2,1)} %bitcast.12), channel_id=1, source_target_pairs={{0,16},{16,0},{1,17},{17,1},{2,18},{18,2},{3,19},{19,3},{4,20},{20... | collective-permute-start | bytes 7077896 | tf_op jit(solution)/shard_map/ppermute | solution.py:24
  99.8 43.3 %collective-permute-start.3 = (bf16[1152,1024]{1,0:T(8,128)(2,1)}, bf16[1152,1024]{1,0:T(8,128)(2,1)}, u32[]{:S(2)}, u32[]{:S(2)}) collective-permute-start(bf16[1152,1024]{1,0:T(8,128)(2,1)} %bitcast.14), channel_id=1, source_target_pairs={{0,16},{16,0},{1,17},{17,1},{2,18},{18,2},{3,19},{19,3},{4,20},{20... | collective-permute-start | bytes 7077896 | tf_op jit(solution)/shard_map/ppermute | solution.py:24
  100.6 33.7 %copy-start.83 = (f32[3,1024]{1,0:T(4,128)S(1)}, f32[3,1024]{1,0:T(4,128)}, u32[]{:S(2)}) copy-start(f32[3,1024]{1,0:T(4,128)} %param.20) | copy-start | bytes 36868
  100.6 33.7 %copy-start.78 = (f32[4,1024]{1,0:T(4,128)S(1)}, f32[4,1024]{1,0:T(4,128)}, u32[]{:S(2)}) copy-start(f32[4,1024]{1,0:T(4,128)} %param.18) | copy-start | bytes 49156
  100.6 564.1 %all-reduce.8.cloned.1.call-start = ((), (), s32[]{:S(2)}) async-start(), calls=%async_computation.8 | async-start | bytes 7077888 | tf_op jit(solution)/shard_map/psum | solution.py:985
  100.7 38.7 %copy-start.84 = (f32[64]{0:T(128)}, f32[64]{0:T(128)S(1)}, u32[]{:S(2)}) copy-start(f32[64]{0:T(128)S(1)} %get-tuple-element.106) | copy-start | bytes 772
  134.4 108.7 %copy-start.72 = (f32[1,1024]{1,0:T(1,128)}, f32[1,1024]{1,0:T(1,128)S(1)}, u32[]{:S(2)}) copy-start(f32[1,1024]{1,0:T(1,128)S(1)} %get-tuple-element.99) | copy-start | bytes 12292
  139.6 10.5 %collective-permute-start = (bf16[2,1024]{1,0:T(2,128)(2,1)S(1)}, bf16[2,1024]{1,0:T(2,128)(2,1)S(1)}, u32[]{:S(2)}, u32[]{:S(2)}) collective-permute-start(bf16[2,1024]{1,0:T(2,128)(2,1)S(1)} %slice.223), channel_id=1, source_target_pairs={{0,4},{4,8},{8,12},{1,5},{5,9},{9,13},{2,6},{6,10},{10,14},{3,7},{... | collective-permute-start | bytes 12296 | tf_op jit(solution)/shard_map/ppermute | solution.py:20
  156.2 73.9 %copy-start.8 = (f32[256,1024]{1,0:T(8,128)}, f32[256,1024]{1,0:T(8,128)S(1)}, u32[]{:S(2)}) copy-start(f32[256,1024]{1,0:T(8,128)S(1)} %get-tuple-element.56) | copy-start | bytes 3145732
  156.2 32.5 %copy-start.79 = (f32[256]{0:T(256)}, f32[256]{0:T(256)S(1)}, u32[]{:S(2)}) copy-start(f32[256]{0:T(256)S(1)} %add_rsqrt_fusion.4) | copy-start | bytes 3076
  450.1 61.5 %collective-permute-start.8 = (bf16[1,576,1024]{2,1,0:T(8,128)(2,1)}, bf16[1,576,1024]{2,1,0:T(8,128)(2,1)}, u32[]{:S(2)}, u32[]{:S(2)}) collective-permute-start(bf16[1,576,1024]{2,1,0:T(8,128)(2,1)} %dynamic-slice_bitcast_fusion), channel_id=1, source_target_pairs={{0,16},{16,0},{1,17},{17,1},{2,18},{18,2},{3,19},{19,3},{4,20},{20... | collective-permute-start | bytes 3538952 | tf_op jit(solution)/shard_map/ppermute | solution.py:24
  453.4 61.4 %collective-permute-start.6 = (bf16[4,128,1152]{2,1,0:T(8,128)(2,1)}, bf16[4,128,1152]{2,1,0:T(8,128)(2,1)}, u32[]{:S(2)}, u32[]{:S(2)}) collective-permute-start(bf16[4,128,1152]{2,1,0:T(8,128)(2,1)} %dynamic-slice_bitcast_fusion.2), channel_id=1, source_target_pairs={{0,16},{16,0},{1,17},{17,1},{2,18},{18,2},{3,19},{19,3},{4,20},{20... | collective-permute-start | bytes 3538952 | tf_op jit(solution)/shard_map/ppermute | solution.py:24
  453.4 64.1 %collective-permute-start.7 = (bf16[4,128,1152]{2,1,0:T(8,128)(2,1)}, bf16[4,128,1152]{2,1,0:T(8,128)(2,1)}, u32[]{:S(2)}, u32[]{:S(2)}) collective-permute-start(bf16[4,128,1152]{2,1,0:T(8,128)(2,1)} %dynamic-slice_bitcast_fusion.1), channel_id=1, source_target_pairs={{0,16},{16,0},{1,17},{17,1},{2,18},{18,2},{3,19},{19,3},{4,20},{20... | collective-permute-start | bytes 3538952 | tf_op jit(solution)/shard_map/ppermute | solution.py:24
  520.1 208.8 %reduce-scatter.2.cloned.1.call-start = ((), (), s32[]{:S(2)}) async-start(), calls=%async_computation.7 | async-start | bytes 7077888 | tf_op jit(solution)/shard_map/reduce_scatter | solution.py:967
  613.0 20.1 %collective-permute-start.4 = (f32[2,1024]{1,0:T(2,128)S(1)}, f32[2,1024]{1,0:T(2,128)S(1)}, u32[]{:S(2)}, u32[]{:S(2)}) collective-permute-start(f32[2,1024]{1,0:T(2,128)S(1)} %pad_add_fusion.1), channel_id=1, source_target_pairs={{4,0},{8,4},{12,8},{5,1},{9,5},{13,9},{6,2},{10,6},{14,10},{7,3},{... | collective-permute-start | bytes 24584 | tf_op jit(solution)/shard_map/ppermute | solution.py:20
  649.7 4.4 collective-permute-start.5
  (92 other events, 465.5 us)
Sparse Core Ops, SparseCore 0:
  10.5 94.2 all-gather.6
  107.3 32.0 all-gather.8
  141.9 34.5 all-gather.10
  178.2 26.5 all-gather.14
  206.5 33.9 all-gather.12
  242.2 27.8 all-gather.16
  520.2 144.4 all-reduce.7
  668.1 60.8 reduce-scatter.1

commit v3 on v2

--- a/solution.py
+++ b/solution.py
@@ -146,7 +146,9 @@
     gate_in,
     up_in,
     down_in,
-    attn_in,
+    query_in,
+    kv_in,
+    proj_in,
     conv_b_in,
     conv_c_in,
     conv_x_in,
@@ -204,11 +206,11 @@
     per_kind = n_fsdp * subs
     down_half = down_in.shape[0] // 2
     down_chunks = down_half // b_rows
-    attn_rows = attn_in.shape[0]
-    attn_chunks = attn_rows // b_rows
-    conv_start = down_chunks + attn_chunks
     c_rows = c_own.shape[1]
-    conv_chunks = c_rows // b_rows
+    mixers = (query_in, kv_in, proj_in, conv_b_in, conv_c_in, conv_x_in, conv_o_in)
+    n_mix = len(mixers)
+    cut = 3 * half // b_rows
+    c_parts = ((0, cut), (cut, c_rows // b_rows))
     ticks = a_chunks // 2
     tail = 2 * (n_ctx - 1)
 
@@ -278,29 +280,22 @@
                 device_id_type=MESH,
             )
         )
-    for chunk in range(attn_chunks):
-        local.append(
-            pltpu.make_async_copy(
-                attn_in.at[pl.ds(chunk * b_rows, b_rows)],
-                b_own.at[down_chunks + chunk],
-                own_sem.at[a_chunks + down_chunks + chunk],
-            )
-        )
     for copy in pair:
         copy.start()
     for copy in local:
         copy.start()
-    c_local, c_pair = [], []
-    for owner in range(n_fsdp):
-        for kind, source in enumerate((conv_b_in, conv_c_in, conv_x_in, conv_o_in)):
-            index = owner * 5 + kind
+    c_local, c_pair = ([], []), ([], [])
+    for kind, source in enumerate(mixers):
+        part = 0 if kind < 3 else 1
+        for owner in range(n_fsdp):
+            index = owner * (n_mix + 1) + kind
             place_at = pl.ds(kind * half, half)
-            c_local.append(
+            c_local[part].append(
                 pltpu.make_async_copy(
                     source.at[half_rows(owner, section)], c_own.at[owner, place_at], c_own_sem.at[index]
                 )
             )
-            c_pair.append(
+            c_pair[part].append(
                 pltpu.make_async_remote_copy(
                     src_ref=source.at[half_rows(owner, other)],
                     dst_ref=c_other.at[owner, place_at],
@@ -310,12 +305,13 @@
                     device_id_type=MESH,
                 )
             )
-        small_at = pl.ds(4 * half, c_rows - 4 * half)
-        index = owner * 5 + 4
-        c_local.append(
+    for owner in range(n_fsdp):
+        small_at = pl.ds(n_mix * half, c_rows - n_mix * half)
+        index = owner * (n_mix + 1) + n_mix
+        c_local[1].append(
             pltpu.make_async_copy(small_in.at[owner, section], c_own.at[owner, small_at], c_own_sem.at[index])
         )
-        c_pair.append(
+        c_pair[1].append(
             pltpu.make_async_remote_copy(
                 src_ref=small_in.at[owner, other],
                 dst_ref=c_other.at[owner, small_at],
@@ -325,56 +321,62 @@
                 device_id_type=MESH,
             )
         )
-    for copy in c_pair:
-        copy.start()
-    for copy in c_local:
-        copy.start()
+    for part in range(2):
+        for copy in c_pair[part]:
+            copy.start()
+        for copy in c_local[part]:
+            copy.start()
     b_own[b_chunks - 1] = jnp.zeros((b_rows, b_width), BF16)
     for copy in local:
         copy.wait()
     for copy in pair:
         copy.wait_recv()
 
-    def conv_copy(step):
+    def mixer_copy(part, step):
         target = lax.rem(group + step, n_fsdp)
+        first, last = c_parts[part]
+        at = pl.ds(first * b_rows, (last - first) * b_rows)
         return pltpu.make_async_remote_copy(
-            src_ref=c_own.at[target],
-            dst_ref=c_got.at[step - 1],
-            send_sem=c_send.at[step],
-            recv_sem=c_recv.at[step],
+            src_ref=c_own.at[target, at],
+            dst_ref=c_got.at[step - 1, at],
+            send_sem=c_send.at[part, step],
+            recv_sem=c_recv.at[part, step],
             device_id={"fsdp": target},
             device_id_type=MESH,
         )
 
-    def conv_out_step():
-        for copy in c_local:
+    def mixer_out(part):
+        for copy in c_local[part]:
             copy.wait()
-        for copy in c_pair:
+        for copy in c_pair[part]:
             copy.wait_recv()
+        first, last = c_parts[part]
+        size = last - first
 
         def add(index, carry):
-            owner = index // conv_chunks
-            at = pl.ds(pl.multiple_of(lax.rem(index, conv_chunks) * b_rows, b_rows), b_rows)
+            owner = index // size
+            at = pl.ds(pl.multiple_of((first + lax.rem(index, size)) * b_rows, b_rows), b_rows)
             c_own[owner, at] = (c_own[owner, at].astype(F32) + c_other[owner, at].astype(F32)).astype(BF16)
             return carry
 
-        lax.fori_loop(0, n_fsdp * conv_chunks, add, 0)
+        lax.fori_loop(0, n_fsdp * size, add, 0)
         for step in range(1, n_fsdp):
-            conv_copy(step).start()
-
-    def conv_in_step():
+            mixer_copy(part, step).start()
+
+    def mixer_in(part):
         for step in range(1, n_fsdp):
-            conv_copy(step).wait_recv()
+            mixer_copy(part, step).wait_recv()
+        first, last = c_parts[part]
 
         def add(index, carry):
             at = pl.ds(pl.multiple_of(index * b_rows, b_rows), b_rows)
             total = c_own[group, at].astype(F32)
             for step in range(1, n_fsdp):
                 total = total + c_got[step - 1, at].astype(F32)
-            b_own[conv_start + index] = total.astype(BF16)
+            b_own[down_chunks + index] = total.astype(BF16)
             return carry
 
-        lax.fori_loop(0, conv_chunks, add, 0)
+        lax.fori_loop(first, last, add, 0)
 
     def second_start():
         for kind in range(2):
@@ -538,17 +540,22 @@
         lanes.append((way, rank, ahead, behind))
 
     def tick_step(tick, carry):
-        @pl.when(tick == 1)
+        @pl.when(tick == 0)
         def _():
-            conv_out_step()
-
-        @pl.when(tick == ticks // 2)
+            mixer_out(0)
+
+        @pl.when(tick == 2)
         def _():
+            mixer_out(1)
+
+        @pl.when(tick == down_chunks // 2)
+        def _():
+            mixer_in(0)
+
+        @pl.when(tick == (down_chunks + cut) // 2)
+        def _():
+            mixer_in(1)
             second_start()
-
-        @pl.when(tick == conv_start // 2)
-        def _():
-            conv_in_step()
 
         for way, rank, ahead, behind in lanes:
             step = tick - rank
@@ -607,10 +614,11 @@
 
     for copy in pair:
         copy.wait_send()
-    for copy in c_pair:
-        copy.wait_send()
-    for step in range(1, n_fsdp):
-        conv_copy(step).wait_send()
+    for part in range(2):
+        for copy in c_pair[part]:
+            copy.wait_send()
+        for step in range(1, n_fsdp):
+            mixer_copy(part, step).wait_send()
 
     def settle(step, carry):
         for way, rank, ahead, behind in lanes:
@@ -660,22 +668,21 @@
     pltpu.make_async_copy(region, region, rest_recv).wait()
 
 
-def summed_gradients(first, attn_half, conv_grads, small, second_gu, second_down):
+def summed_gradients(first, mixers, small, second_gu, second_down):
     n_ctx, n_fsdp = lax.axis_size("ctx"), lax.axis_size("fsdp")
     gate, up, down = first
     half = gate.shape[0] // n_fsdp // 2
     a_rows, b_rows = half // 4, half * 3 // 8
     a_chunks = 2 * n_fsdp * 4
     a_width, b_width = gate.shape[1], down.shape[1]
-    c_rows = 4 * half + small.shape[2]
+    c_rows = len(mixers) * half + small.shape[2]
     down_chunks = down.shape[0] // 2 // b_rows
-    attn_chunks = attn_half.shape[0] // b_rows
-    conv_chunks = c_rows // b_rows
-    b_chunks = down_chunks + attn_chunks + conv_chunks + 1
+    b_chunks = down_chunks + c_rows // b_rows + 1
     assert a_chunks == b_chunks and c_rows % b_rows == 0
     rest = b_chunks - down_chunks
     dma = pltpu.SemaphoreType.DMA
-    loads = a_chunks + down_chunks + attn_chunks
+    loads = a_chunks + down_chunks
+    pieces = n_fsdp * (len(mixers) + 1)
     return pl.pallas_call(
         functools.partial(tail_kernel, (n_ctx, n_fsdp)),
         out_shape=(
@@ -683,7 +690,7 @@
             jax.ShapeDtypeStruct(down.shape, BF16),
             jax.ShapeDtypeStruct((2, rest * b_rows, b_width), BF16),
         ),
-        in_specs=[pl.BlockSpec(memory_space=pl.ANY)] * 11,
+        in_specs=[pl.BlockSpec(memory_space=pl.ANY)] * (6 + len(mixers)),
         out_specs=[pl.BlockSpec(memory_space=pl.ANY)] * 3,
         scratch_shapes=[
             pltpu.VMEM((a_chunks, a_rows, a_width), BF16),
@@ -700,11 +707,11 @@
             dma((loads,)),
             dma((loads,)),
             dma((loads,)),
-            dma((n_fsdp * 5,)),
-            dma((n_fsdp * 5,)),
-            dma((n_fsdp * 5,)),
-            dma((n_fsdp,)),
-            dma((n_fsdp,)),
+            dma((pieces,)),
+            dma((pieces,)),
+            dma((pieces,)),
+            dma((2, n_fsdp)),
+            dma((2, n_fsdp)),
             dma((a_chunks,)),
             dma((a_chunks,)),
             dma((a_chunks,)),
@@ -724,7 +731,265 @@
         compiler_params=pltpu.CompilerParams(
             collective_id=6, has_side_effects=True, vmem_limit_bytes=56 << 20
         ),
-    )(gate, up, down, attn_half, *conv_grads, small, second_gu, second_down)
+    )(gate, up, down, *mixers, small, second_gu, second_down)
+
+
+def mixer_weights_kernel(count, first_in, second_in, first_out, second_out, send_sem, recv_sem, pair_send, pair_recv, own_sem):
+    section = lax.axis_index("section")
+    me = lax.axis_index("fsdp")
+    other = 1 - section
+    beside = me + 1 - 2 * lax.rem(me, 2)
+    across = lax.rem(me + 2, count)
+    opposite = lax.rem(beside + 2, count)
+    rows = first_in.shape[0]
+    half = rows // 2
+    quarter = half // 2
+    barrier = pltpu.get_barrier_semaphore()
+    for target in ({"fsdp": beside}, {"fsdp": across}, {"section": other}):
+        pl.semaphore_signal(barrier, inc=1, device_id=target, device_id_type=MESH)
+    pl.semaphore_wait(barrier, 3)
+    arrays = ((first_in, first_out), (second_in, second_out))
+
+    def at_rows(owner, extra, size):
+        return pl.ds(pl.multiple_of(owner * rows + extra, quarter), size)
+
+    def remote(slot, sems, src, dst, target):
+        return pltpu.make_async_remote_copy(
+            src_ref=src,
+            dst_ref=dst,
+            send_sem=sems[0].at[slot],
+            recv_sem=sems[1].at[slot],
+            device_id=target,
+            device_id_type=MESH,
+        )
+
+    hop, pair = (send_sem, recv_sem), (pair_send, pair_recv)
+    waiting = []
+    direct = []
+    for index, (source, out) in enumerate(arrays):
+        mine = source.at[pl.ds(pl.multiple_of(section * half, half), half)]
+        spot = out.at[at_rows(me, section * half, half)]
+        copies = [
+            remote(index * 4, hop, mine, spot, {"fsdp": beside}),
+            remote(index * 4 + 1, hop, mine, spot, {"fsdp": across}),
+        ]
+        for copy in copies:
+            copy.start()
+        direct.append(copies)
+    own = [
+        pltpu.make_async_copy(source, out.at[at_rows(me, 0, rows)], own_sem.at[index])
+        for index, (source, out) in enumerate(arrays)
+    ]
+    for copy in own:
+        copy.start()
+
+    def arrived(owner, size, extra):
+        return lambda out: out.at[at_rows(owner, section * half + extra, size)]
+
+    onward = []
+    for index, (source, out) in enumerate(arrays):
+        direct[index][0].wait_recv()
+        part = arrived(beside, quarter, 0)(out)
+        onward.append(remote(index * 4 + 2, hop, part, part, {"fsdp": across}))
+        onward[-1].start()
+        whole = arrived(beside, half, 0)(out)
+        waiting.append(remote(index * 4, pair, whole, whole, {"section": other}))
+        waiting[-1].start()
+        direct[index][1].wait_recv()
+        part = arrived(across, quarter, quarter)(out)
+        onward.append(remote(index * 4 + 3, hop, part, part, {"fsdp": beside}))
+        onward[-1].start()
+        whole = arrived(across, half, 0)(out)
+        waiting.append(remote(index * 4 + 1, pair, whole, whole, {"section": other}))
+        waiting[-1].start()
+    for index, (source, out) in enumerate(arrays):
+        for turn in range(2):
+            onward[2 * index + turn].wait_recv()
+            part = arrived(opposite, quarter, turn * quarter)(out)
+            waiting.append(remote(index * 4 + 2 + turn, pair, part, part, {"section": other}))
+            waiting[-1].start()
+    for copy in own:
+        copy.wait()
+    for copies in direct:
+        for copy in copies:
+            copy.wait_send()
+    for copy in onward:
+        copy.wait_send()
+    for copy in waiting:
+        copy.wait()
+
+
+def mixer_weights(first, second, collective_id):
+    count = lax.axis_size("fsdp")
+    dma = pltpu.SemaphoreType.DMA
+    return pl.pallas_call(
+        functools.partial(mixer_weights_kernel, count),
+        out_shape=tuple(
+            jax.ShapeDtypeStruct((count * w.shape[0], w.shape[1]), w.dtype) for w in (first, second)
+        ),
+        in_specs=[pl.BlockSpec(memory_space=pl.ANY)] * 2,
+        out_specs=[pl.BlockSpec(memory_space=pl.ANY)] * 2,
+        scratch_shapes=[dma((8,)), dma((8,)), dma((8,)), dma((8,)), dma((2,))],
+        compiler_params=pltpu.CompilerParams(
+            collective_id=collective_id, has_side_effects=True, vmem_limit_bytes=8 << 20
+        ),
+    )(first, second)
+
+
+def column_weights_kernel(count, holder, n_ctx, *refs):
+    if n_ctx > 1:
+        kv_in, refs = refs[0], refs[1:]
+    gate_in, up_in, down_in, gate_out, up_out, down_out = refs[:6]
+    refs = refs[6:]
+    if n_ctx > 1:
+        kv_out, refs = refs[0], refs[1:]
+    send_sem, recv_sem, pair_send, pair_recv, own_sem = refs[:5]
+    section = lax.axis_index("section")
+    me = lax.axis_index("fsdp")
+    place = lax.axis_index("ctx")
+    other = 1 - section
+    rows = gate_in.shape[0]
+    wide = gate_out.shape[1]
+    barrier = pltpu.get_barrier_semaphore()
+    for step in range(1, count):
+        pl.semaphore_signal(
+            barrier, inc=1, device_id={"fsdp": lax.rem(me + step, count)}, device_id_type=MESH
+        )
+    pl.semaphore_signal(barrier, inc=1, device_id={"section": other}, device_id_type=MESH)
+    for step in range(1, n_ctx):
+        pl.semaphore_signal(
+            barrier, inc=1, device_id={"ctx": lax.rem(place + step, n_ctx)}, device_id_type=MESH
+        )
+    pl.semaphore_wait(barrier, count + n_ctx - 1)
+    kv_copies = []
+    if n_ctx > 1:
+        kv_send, kv_recv, kv_own = refs[5:]
+        kv_rows = kv_in.shape[0]
+        spot = kv_out.at[pl.ds(pl.multiple_of(place * kv_rows, kv_rows), kv_rows)]
+        for step in range(1, n_ctx):
+            kv_copies.append(
+                pltpu.make_async_remote_copy(
+                    src_ref=kv_in,
+                    dst_ref=spot,
+                    send_sem=kv_send.at[step],
+                    recv_sem=kv_recv.at[step],
+                    device_id={"ctx": lax.rem(place + step, n_ctx)},
+                    device_id_type=MESH,
+                )
+            )
+            kv_copies[-1].start()
+        kv_keep = pltpu.make_async_copy(kv_in, spot, kv_own)
+        kv_keep.start()
+    arrays = ((gate_in, gate_out), (up_in, up_out))
+
+    def at_rows(out, owner):
+        return out.at[pl.ds(pl.multiple_of(owner * rows, rows), rows)]
+
+    def crossing(kind, step):
+        source, out = arrays[kind]
+        target = lax.rem(me + step, count)
+        return pltpu.make_async_remote_copy(
+            src_ref=source.at[:, pl.ds(pl.multiple_of(target * wide, 128), wide)],
+            dst_ref=at_rows(out, me),
+            send_sem=send_sem.at[kind, step],
+            recv_sem=recv_sem.at[kind, step],
+            device_id={"fsdp": target},
+            device_id_type=MESH,
+        )
+
+    def handed(kind, step):
+        source, out = arrays[kind]
+        origin = lax.rem(me + count - step, count)
+        if step == 0:
+            src = source.at[:, pl.ds(pl.multiple_of(me * wide, 128), wide)]
+        else:
+            src = at_rows(out, origin)
+        return pltpu.make_async_remote_copy(
+            src_ref=src,
+            dst_ref=at_rows(out, origin),
+            send_sem=pair_send.at[kind, step],
+            recv_sem=pair_recv.at[kind, step],
+            device_id={"section": other},
+            device_id_type=MESH,
+        )
+
+    down_copy = pltpu.make_async_remote_copy(
+        src_ref=down_in,
+        dst_ref=down_out,
+        send_sem=pair_send.at[2, 0],
+        recv_sem=pair_recv.at[2, 0],
+        device_id={"section": other},
+        device_id_type=MESH,
+    )
+    kinds = range(2)
+
+    @pl.when(section == holder)
+    def _():
+        for step in range(1, count):
+            for kind in kinds:
+                crossing(kind, step).start()
+        for kind in kinds:
+            handed(kind, 0).start()
+        down_copy.start()
+        keep = [
+            pltpu.make_async_copy(
+                arrays[kind][0].at[:, pl.ds(pl.multiple_of(me * wide, 128), wide)],
+                at_rows(arrays[kind][1], me),
+                own_sem.at[kind],
+            )
+            for kind in kinds
+        ] + [pltpu.make_async_copy(down_in, down_out, own_sem.at[2])]
+        for copy in keep:
+            copy.start()
+        for step in range(1, count):
+            for kind in kinds:
+                crossing(kind, step).wait_recv()
+                handed(kind, step).start()
+        for copy in keep:
+            copy.wait()
+        for step in range(1, count):
+            for kind in kinds:
+                crossing(kind, step).wait_send()
+        for step in range(count):
+            for kind in kinds:
+                handed(kind, step).wait_send()
+        down_copy.wait_send()
+
+    @pl.when(section != holder)
+    def _():
+        for step in range(count):
+            for kind in kinds:
+                handed(kind, step).wait_recv()
+        down_copy.wait_recv()
+
+    if n_ctx > 1:
+        kv_keep.wait()
+        for copy in kv_copies:
+            copy.wait()
+
+
+def column_weights(gate, up, down, holder, collective_id, kv=None):
+    count = lax.axis_size("fsdp")
+    n_ctx = 1 if kv is None else lax.axis_size("ctx")
+    dma = pltpu.SemaphoreType.DMA
+    column = jax.ShapeDtypeStruct((count * gate.shape[0], gate.shape[1] // count), gate.dtype)
+    outs = [column, column, jax.ShapeDtypeStruct(down.shape, down.dtype)]
+    ins = [gate, up, down]
+    sems = [dma((2, count)), dma((2, count)), dma((3, count)), dma((3, count)), dma((3,))]
+    if kv is not None:
+        ins = [kv] + ins
+        outs.append(jax.ShapeDtypeStruct((n_ctx * kv.shape[0], kv.shape[1]), kv.dtype))
+        sems += [dma((n_ctx,)), dma((n_ctx,)), dma]
+    return pl.pallas_call(
+        functools.partial(column_weights_kernel, count, holder, n_ctx),
+        out_shape=tuple(outs),
+        in_specs=[pl.BlockSpec(memory_space=pl.ANY)] * len(ins),
+        out_specs=[pl.BlockSpec(memory_space=pl.ANY)] * len(outs),
+        scratch_shapes=sems,
+        compiler_params=pltpu.CompilerParams(
+            collective_id=collective_id, has_side_effects=True, vmem_limit_bytes=8 << 20
+        ),
+    )(*ins)
 
 
 def attend(query, key_all, value_all, allowed):
@@ -818,24 +1083,9 @@
         mine = lax.dynamic_slice_in_dim(weight, section * half, half, 0)
         return lax.all_gather(mine, ("fsdp", "section"), axis=0, tiled=True)
 
-    def to_columns(weight):
-        deep, wide = weight.shape
-        blocks = weight.reshape(deep, fsdp, wide // fsdp).transpose(1, 0, 2)
-        return swapped_blocks(blocks.reshape(fsdp * deep, wide // fsdp), "fsdp", 2)
-
-    def both(weight):
-        other = swapped(weight, "section")
-        first = section == 0
-        return jnp.where(first, weight, other), jnp.where(first, other, weight)
-
-    in_full = whole_rows(conv_in)
-    out_full = whole_rows(conv_out)
-    gate_up = to_columns(jnp.concatenate([ffn_gate[0], ffn_up[0]], axis=0))
     part = ffn_gate.shape[1]
-    gate_up = gate_up.reshape(fsdp, 2, part, -1)
-    gates = both(gate_up[:, 0].reshape(fsdp * part, -1))
-    ups = both(gate_up[:, 1].reshape(fsdp * part, -1))
-    downs = both(ffn_down[0])
+    in_full, out_full = mixer_weights(conv_in, conv_out, 2)
+    gate1, up1, down1 = column_weights(ffn_gate[0], ffn_up[0], ffn_down[0], 0, 7)
     query_full, key_full, value_full, proj_full = (
         whole_rows(attn_q),
         whole_rows(attn_k),
@@ -863,7 +1113,7 @@
     z_low = (c_gate * convolved).astype(BF16)
     mixed = matmul(z_low, out_full)
     res1 = x + mixed
-    ffn1, kept1 = ffn_forward(res1, norm_gains[1], gates[0], ups[0], downs[0])
+    ffn1, kept1 = ffn_forward(res1, norm_gains[1], gate1, up1, down1)
     h_low = (res1 + ffn1).astype(BF16)
 
     h = h_low.astype(F32)
@@ -874,7 +1124,14 @@
     query = (q_normed * head_gains[0]).astype(BF16)
     key = (k_normed * head_gains[1]).astype(BF16)
     value = matmul(act2, value_full).astype(BF16)
-    kv_all = gathered(jnp.concatenate([key.reshape(rows, kv_width), value], axis=1), "ctx", 3)
+    gate2, up2, down2, kv_all = column_weights(
+        ffn_gate[0],
+        ffn_up[0],
+        ffn_down[0],
+        1,
+        3,
+        jnp.concatenate([key.reshape(rows, kv_width), value], axis=1),
+    )
     key_all = kv_all[:, :kv_width].reshape(-1, kv_heads, head)
     value_all = kv_all[:, kv_width:].reshape(-1, kv_heads, head)
     key_pos = jnp.arange(kv_all.shape[0])
@@ -883,7 +1140,7 @@
     attended_low = attended.astype(BF16)
     attn_rows = matmul(attended_low, proj_full)
     res2 = h + attn_rows
-    ffn2, kept2 = ffn_forward(res2, norm_gains[3], gates[1], ups[1], downs[1])
+    ffn2, kept2 = ffn_forward(res2, norm_gains[3], gate2, up2, down2)
     result = (res2 + ffn2) * mask
 
     def square(values):
@@ -895,7 +1152,7 @@
 
     d_sum_low = (lax.dynamic_index_in_dim(cotangent, section, keepdims=False).astype(F32) * mask).astype(BF16)
     d_sum = d_sum_low.astype(F32)
-    d_ffn, gain3, grads2 = ffn_backward(d_sum_low, kept2, norm_gains[3], gates[1], ups[1], downs[1])
+    d_ffn, gain3, grads2 = ffn_backward(d_sum_low, kept2, norm_gains[3], gate2, up2, down2)
     d_res2 = d_sum + d_ffn
     d_attn = d_res2.astype(BF16)
     grad_proj = matmul_left(attended_low, d_attn)
@@ -917,9 +1174,6 @@
     grad_kgain = jnp.sum(d_kn * k_normed, axis=(0, 1))
     d_kpre = norm_back(d_kn * head_gains[1], k_normed, k_inv).reshape(rows, -1).astype(BF16)
     d_vpre = d_kv[:, kv_width:].astype(BF16)
-    grad_query = matmul_left(act2, d_qpre)
-    grad_key = matmul_left(act2, d_kpre)
-    grad_value = matmul_left(act2, d_vpre)
     d_act2 = (
         matmul_right(d_qpre, query_full)
         + matmul_right(d_kpre, key_full)
@@ -928,7 +1182,7 @@
     gain2 = jnp.sum(d_act2 * normed2, axis=0)
     d_h_low = (d_res2 + norm_back(d_act2 * norm_gains[2], normed2, inv2)).astype(BF16)
 
-    d_ffn1, gain1, grads1 = ffn_backward(d_h_low, kept1, norm_gains[1], gates[0], ups[0], downs[0])
+    d_ffn1, gain1, grads1 = ffn_backward(d_h_low, kept1, norm_gains[1], gate1, up1, down1)
     d_res1 = d_h_low.astype(F32) + d_ffn1
     d_mixed = d_res1.astype(BF16)
     grad_out = matmul_left(z_low, d_mixed)
@@ -964,15 +1218,11 @@
     grad_parts = [
         matmul_left(act1, d_projected[:, i * width : (i + 1) * width]).astype(BF16) for i in range(3)
     ]
-    attn_half = lax.psum_scatter(
-        jnp.concatenate([grad_query, grad_key, grad_value, grad_proj], axis=1).astype(BF16),
-        ("fsdp", "section"),
-        scatter_dimension=0,
-        tiled=True,
-    )
-    attn_half = jnp.concatenate(
-        [attn_half[:, i * width : (i + 1) * width] for i in range(attn_half.shape[1] // width)], axis=0
-    )
+    mixers = [
+        matmul_left(act2, d_qpre).astype(BF16),
+        matmul_left(act2, jnp.concatenate([d_kpre, d_vpre], axis=1)).astype(BF16),
+        grad_proj.astype(BF16),
+    ] + grad_parts + [grad_out.astype(BF16)]
 
     half = part // 2
 
@@ -1011,8 +1261,7 @@
     small = jnp.pad(by_owner, ((0, 0), (0, 1), (0, 16 - by_owner.shape[2]), (0, 0))).astype(BF16)
     gu_sum, down_sum, rest_sum = summed_gradients(
         grads1,
-        attn_half,
-        grad_parts + [grad_out.astype(BF16)],
+        mixers,
         small,
         jnp.stack([second[0], second[1]]),
         second[2],

time: 921 us -> 972 us (1.055)
  waiting for transfers between devices: 70.6 us -> 114 us
  Pallas kernels: 524 us -> 555 us
  matrix products: 173 us -> 145 us
    pallas_call x0 -> x3, Pallas kernels: none -> 126 us  [the longest x2 80.2 us: column_weights(): pl.pallas_call(functools.partial(column_weights_kernel, count, holder, n_...]
    pallas_call x11 -> x9, Pallas kernels: 369 us -> 253 us  [exchange(): pl.pallas_call(functools.partial(kernel, axis, count, rows), out_shape=ja...]
    psum x1, waiting for transfers between devices: 9.48 us -> 103 us  [shards(): lax.psum((shared_halves(grads2[0], fsdp), shared_halves(grads2[1], fsdp),...]
    reduce_scatter x1 -> x0, waiting for transfers between devices: 61 us -> none  [shards(): lax.psum_scatter(jnp.concatenate([grad_query, grad_key, grad_value, grad_...]
    pallas_call x1, Pallas kernels: 155 us -> 176 us  [summed_gradients(): pl.pallas_call(functools.partial(tail_kernel, (n_ctx, n_fsdp)), out_shape...]
    dot_general x12, matrix products: 54.3 us -> 35.9 us  [matmul(): return jnp.dot(left_op, right_op, preferred_element_type=F32)]
    unnamed x206 -> x244, local copies, waits for them, and re-layouts: 15.9 us -> 28.9 us
    dot_general x12, matrix products: 49.1 us -> 38.5 us  [matmul_right(): lax.dot_general(left_op, right_op, (((1,), (1,)), ((), ())), preferred_el...]
  transfers between devices with their start and end apart: 17 -> 11, of which waited for: 2 -> 2; matrix products, arithmetic and copies ran while one was open for 20% -> 10% of each run, Pallas kernels for 32% -> 22%
where the time goes in v3:
time: 972 us; the launch traced here: 960 us
  Pallas kernels  555 us (57%)
  matrix products  145 us (15%)
  waiting for transfers between devices  114 us (12%)
  local copies, waits for them, and re-layouts  65.3 us (7%)
  other arithmetic  58.3 us (6%)
  between operations  16.4 us (2%)
    pallas_call x9, Pallas kernels, exchange(): pl.pallas_call(functools.partial(kernel, axis, count, rows), out_shape=ja...  253 us
    pallas_call x1, Pallas kernels, summed_gradients(): pl.pallas_call(functools.partial(tail_kernel, (n_ctx, n_fsdp)), out_shape...  176 us
    psum x1, waiting for transfers between devices, shards(): lax.psum((shared_halves(grads2[0], fsdp), shared_halves(grads2[1], fsdp),...  103 us
    pallas_call x2, Pallas kernels, column_weights(): pl.pallas_call(functools.partial(column_weights_kernel, count, holder, n_...  80.2 us
    pallas_call x1, Pallas kernels, mixer_weights(): pl.pallas_call(functools.partial(mixer_weights_kernel, count), out_shape=...  45.7 us
    dot_general x13, matrix products, matmul_left(): lax.dot_general(left_op, right_op, (((0,), (0,)), ((), ())), preferred_el...  40 us
    dot_general x12, matrix products, matmul_right(): lax.dot_general(left_op, right_op, (((1,), (1,)), ((), ())), preferred_el...  38.5 us
    dot_general x12, matrix products, matmul(): return jnp.dot(left_op, right_op, preferred_element_type=F32)  35.9 us
  transfers between devices with their start and end apart: 11, of which 2 were waited for; matrix products, arithmetic and copies ran while one was open for 10% of the time, Pallas kernels for 22%

profile of v3, /device:TPU:0, one launch (start us, length us, event | category | flops | bytes accessed | tf_op | source)
XLA Modules:
  0.0 960.1 jit_solution(13472341487582524920)
XLA Ops:
  13.8 45.7 %shard_map.262 = (bf16[1024,3072]{1,0:T(8,128)(2,1)S(1)}, bf16[1024,1024]{1,0:T(8,128)(2,1)S(1)}) custom-call(bf16[256,3072]{1,0:T(8,128)(2,1)S(1)} %copy-done.14, bf16[256,1024]{1,0:T(8,128)(2,1)S(1)} %copy-done.15), custom_call_target="tpu_custom_call" | custom-call | tf_op jit(solution)/shard_map/pallas_call | solution.py:825
  73.6 30.5 %shard_map.267 = bf16[1024,1024]{1,0:T(8,128)(2,1)S(1)} custom-call(bf16[256,1024]{1,0:T(8,128)(2,1)S(1)} %get-tuple-element.135.block), custom_call_target="tpu_custom_call" | custom-call | tf_op jit(solution)/shard_map/pallas_call | solution.py:114
  108.8 42.3 %shard_map.264 = (bf16[1024,1152]{1,0:T(8,128)(2,1)S(1)}, bf16[1024,1152]{1,0:T(8,128)(2,1)S(1)}, bf16[1152,1024]{1,0:T(8,128)(2,1)S(1)}) custom-call(bf16[256,4608]{1,0:T(8,128)(2,1)S(1)} %bitcast.253, bf16[256,4608]{1,0:T(8,128)(2,1)S(1)} %bitcast.255, bf16[1152,1024]{1,0:T(8,128)(2,1)S(1)} %bitcast.257), custom_call_target="tpu_custom_call" | custom-call | tf_op jit(solution)/shard_map/pallas_call | solution.py:983
  158.5 26.7 %shard_map.263 = bf16[1024,1024]{1,0:T(8,128)(2,1)S(1)} custom-call(bf16[256,1024]{1,0:T(8,128)(2,1)S(1)} %multiply_convert_fusion.9.block), custom_call_target="tpu_custom_call" | custom-call | tf_op jit(solution)/shard_map/pallas_call | solution.py:114
  188.2 4.5 multiply_convert_fusion.5
  195.8 24.6 %shard_map.265 = bf16[1024,1024]{1,0:T(8,128)(2,1)S(1)} custom-call(bf16[1024,1024]{1,0:T(8,128)(2,1)S(1)} %convolution_convert_fusion.7.blocks), custom_call_target="tpu_custom_call" | custom-call | tf_op jit(solution)/shard_map/pallas_call | solution.py:114
  237.7 37.9 %shard_map.266 = (bf16[1024,1152]{1,0:T(8,128)(2,1)S(1)}, bf16[1024,1152]{1,0:T(8,128)(2,1)S(1)}, bf16[1152,1024]{1,0:T(8,128)(2,1)S(1)}, bf16[1024,1024]{1,0:T(8,128)(2,1)S(1)}) custom-call(bf16[256,1024]{1,0:T(8,128)(2,1)S(1)} %pad_maximum_fusion.3.refs_0_, bf16[256,4608]{1,0:T(8,128)(2,1)S(1)} %bitcast.254, bf16[256,4608]{1,0:T(8,128)(2,1)S(1)} %bitcast.256, ...), custom_call_target="tpu_custom_call" | custom-call | tf_op jit(solution)/shard_map/pallas_call | solution.py:983
  295.3 5.6 fusion.109
  303.7 25.8 %shard_map.268 = bf16[1024,1024]{1,0:T(8,128)(2,1)S(1)} custom-call(bf16[256,1024]{1,0:T(8,128)(2,1)S(1)} %multiply_convert_fusion.7.block), custom_call_target="tpu_custom_call" | custom-call | tf_op jit(solution)/shard_map/pallas_call | solution.py:114
  336.9 8.7 multiply_convert_fusion.3
  345.6 4.9 convolution_convert_fusion.6.blocks
  361.7 25.2 %shard_map.273 = bf16[1024,1024]{1,0:T(8,128)(2,1)S(1)} custom-call(bf16[1024,1024]{1,0:T(8,128)(2,1)S(1)} %convolution_convert_fusion.6.blocks), custom_call_target="tpu_custom_call" | custom-call | tf_op jit(solution)/shard_map/pallas_call | solution.py:114
  396.0 24.3 %shard_map.269 = bf16[1024,1024]{1,0:T(8,128)(2,1)S(1)} custom-call(bf16[1024,1024]{1,0:T(8,128)(2,1)S(1)} %add_convert_fusion.1.blocks), custom_call_target="tpu_custom_call" | custom-call | tf_op jit(solution)/shard_map/pallas_call | solution.py:114
  430.0 8.6 bitcast_convert_fusion.1
  438.6 8.9 fusion.1
  458.0 48.1 %shard_map.270 = bf16[1024,1024]{1,0:T(8,128)(2,1)S(1)} custom-call(bf16[1024,1024]{1,0:T(8,128)(2,1)S(1)} %pad_maximum_fusion.2.blocks), custom_call_target="tpu_custom_call" | custom-call | tf_op jit(solution)/shard_map/pallas_call | solution.py:114
  517.6 23.7 %shard_map.271 = bf16[1024,1024]{1,0:T(8,128)(2,1)S(1)} custom-call(bf16[256,1024]{1,0:T(8,128)(2,1)S(1)} %fusion.61.block), custom_call_target="tpu_custom_call" | custom-call | tf_op jit(solution)/shard_map/pallas_call | solution.py:114
  564.6 24.2 %shard_map.272 = bf16[1024,1024]{1,0:T(8,128)(2,1)S(1)} custom-call(bf16[1024,1024]{1,0:T(8,128)(2,1)S(1)} %add_convert_fusion.blocks), custom_call_target="tpu_custom_call" | custom-call | tf_op jit(solution)/shard_map/pallas_call | solution.py:114
  618.0 10.4 %collective-permute-done.1 = f32[2,1024]{1,0:T(2,128)S(1)} collective-permute-done((f32[2,1024]{1,0:T(2,128)S(1)}, f32[2,1024]{1,0:T(2,128)S(1)}, u32[]{:S(2)}, u32[]{:S(2)}) %collective-permute-start.1) | collective-permute-done | bytes 8224 | tf_op jit(solution)/shard_map/ppermute | solution.py:20
  631.6 6.5 fusion.56
  638.1 5.3 stack.93
  651.8 103.3 %all-reduce.8.cloned.1.call-done = (bf16[1,4,128,1152]{3,2,1,0:T(8,128)(2,1)}, bf16[1,4,128,1152]{3,2,1,0:T(8,128)(2,1)}, bf16[576,1024]{1,0:T(8,128)(2,1)}) async-done(((bf16[1,4,128,1152]{3,2,1,0:T(8,128)(2,1)}, bf16[1,4,128,1152]{3,2,1,0:T(8,128)(2,1)}, bf16[576,1024]{1,0:T(8,128)(2,1)}), (bf16[1,4,128,1152]{3,2,1,0:T(8,128)(2,1)}, bf16[1,4,128,1152]{3,2,1,0:T(8,128)(2,1)}, ...) | async-done | bytes 3538960 | tf_op jit(solution)/shard_map/psum | solution.py:1235
  758.4 175.9 %shard_map.274 = (bf16[2,256,4608]{2,1,0:T(8,128)(2,1)}, bf16[1152,1024]{1,0:T(8,128)(2,1)}, bf16[2,960,1024]{2,1,0:T(8,128)(2,1)}) custom-call(bf16[1024,1152]{1,0:T(8,128)(2,1)} %convolution_convert_fusion.5.gate_in, bf16[1024,1152]{1,0:T(8,128)(2,1)} %convolution_convert_fusion.4.up_in, bf16[1152,1024]{1,0:T(8,128)(2,1)} %convolution_convert_fusion.3.down_in, ...), custom_call_target="tpu_custom_call" | custom-call | tf_op jit(solution)/shard_map/pallas_call | solution.py:686
  944.3 5.0 slice_convert_fusion
  (425 shorter events, 217.0 us)
Async XLA Ops:
  7.2 214.6 %all-gather.5.cloned.1.call-start = ((), (), s32[]{:S(2)}) async-start(), calls=%async_computation | async-start | bytes 1179648 | tf_op jit(solution)/shard_map/all_gather | solution.py:1084
  9.0 224.2 %all-gather.7.cloned.1.call-start = ((), (), s32[]{:S(2)}) async-start(), calls=%async_computation.1 | async-start | bytes 1179648 | tf_op jit(solution)/shard_map/all_gather | solution.py:1084
  10.6 51.2 %copy-start.93 = (f32[4,1024]{1,0:T(4,128)S(1)}, f32[4,1024]{1,0:T(4,128)}, u32[]{:S(2)}) copy-start(f32[4,1024]{1,0:T(4,128)} %param.18) | copy-start | bytes 49156
  10.6 273.4 %all-gather.9.cloned.1.call-start = ((), (), s32[]{:S(2)}) async-start(), calls=%async_computation.2 | async-start | bytes 2359296 | tf_op jit(solution)/shard_map/all_gather | solution.py:1084
  11.5 289.4 %all-gather.11.cloned.1.call-start = ((), (), s32[]{:S(2)}) async-start(), calls=%async_computation.3 | async-start | bytes 2359296 | tf_op jit(solution)/shard_map/all_gather | solution.py:1084
  13.8 47.7 %copy-start.42 = (bf16[2,256,1024]{2,1,0:T(8,128)(2,1)S(1)}, bf16[2,256,1024]{2,1,0:T(8,128)(2,1)}, u32[]{:S(2)}) copy-start(bf16[2,256,1024]{2,1,0:T(8,128)(2,1)} %param.15) | copy-start | bytes 3145732
  13.8 47.7 %copy-start.72 = (bf16[2,256,1024]{2,1,0:T(8,128)(2,1)S(1)}, bf16[2,256,1024]{2,1,0:T(8,128)(2,1)}, u32[]{:S(2)}) copy-start(bf16[2,256,1024]{2,1,0:T(8,128)(2,1)} %param.16) | copy-start | bytes 3145732
  61.9 96.4 %copy-start.79 = (f32[1,1024]{1,0:T(1,128)}, f32[1,1024]{1,0:T(1,128)S(1)}, u32[]{:S(2)}) copy-start(f32[1,1024]{1,0:T(1,128)S(1)} %get-tuple-element.112) | copy-start | bytes 12292
  61.9 222.2 %copy-start.87 = (f32[1,1024]{1,0:T(1,128)}, f32[1,1024]{1,0:T(1,128)S(1)}, u32[]{:S(2)}) copy-start(f32[1,1024]{1,0:T(1,128)S(1)} %get-tuple-element.114) | copy-start | bytes 12292
  66.1 85.0 %collective-permute-start = (bf16[2,1024]{1,0:T(2,128)(2,1)S(1)}, bf16[2,1024]{1,0:T(2,128)(2,1)S(1)}, u32[]{:S(2)}, u32[]{:S(2)}) collective-permute-start(bf16[2,1024]{1,0:T(2,128)(2,1)S(1)} %slice.203), channel_id=1, source_target_pairs={{0,4},{4,8},{8,12},{1,5},{5,9},{9,13},{2,6},{6,10},{10,14},{3,7},{... | collective-permute-start | bytes 12296 | tf_op jit(solution)/shard_map/ppermute | solution.py:20
  70.5 684.6 %all-reduce.8.cloned.1.call-start = ((), (), s32[]{:S(2)}) async-start(), calls=%async_computation.4 | async-start | bytes 7077888 | tf_op jit(solution)/shard_map/psum | solution.py:1235
  71.3 80.0 %copy-start.81 = (f32[1,1024]{1,0:T(1,128)}, f32[1,1024]{1,0:T(1,128)S(1)}, u32[]{:S(2)}) copy-start(f32[1,1024]{1,0:T(1,128)S(1)} %get-tuple-element.115) | copy-start | bytes 12292
  71.3 80.0 %copy-start.83 = (f32[1,1024]{1,0:T(1,128)}, f32[1,1024]{1,0:T(1,128)S(1)}, u32[]{:S(2)}) copy-start(f32[1,1024]{1,0:T(1,128)S(1)} %get-tuple-element.116) | copy-start | bytes 12292
  71.3 80.0 %copy-start.85 = (f32[1,1024]{1,0:T(1,128)}, f32[1,1024]{1,0:T(1,128)S(1)}, u32[]{:S(2)}) copy-start(f32[1,1024]{1,0:T(1,128)S(1)} %get-tuple-element.117) | copy-start | bytes 12292
  73.6 157.4 %copy-start.91 = (f32[512]{0:T(512)}, f32[512]{0:T(512)S(1)}, u32[]{:S(2)}) copy-start(f32[512]{0:T(512)S(1)} %mul.645) | copy-start | bytes 6148
  158.3 62.5 %copy-start.35 = (f32[256,1024]{1,0:T(8,128)}, f32[256,1024]{1,0:T(8,128)S(1)}, u32[]{:S(2)}) copy-start(f32[256,1024]{1,0:T(8,128)S(1)} %get-tuple-element.74) | copy-start | bytes 3145732
  221.8 62.2 %copy-start.96 = (f32[256]{0:T(256)}, f32[256]{0:T(256)S(1)}, u32[]{:S(2)}) copy-start(f32[256]{0:T(256)S(1)} %add_rsqrt_fusion.3) | copy-start | bytes 3076
  286.7 162.4 %copy-start.32 = (f32[256,1024]{0,1:T(8,128)}, f32[256,1024]{0,1:T(8,128)S(1)}, u32[]{:S(2)}) copy-start(f32[256,1024]{0,1:T(8,128)S(1)} %get-tuple-element.126) | copy-start | bytes 3145732
  458.0 48.1 %copy-start.33 = (f32[256,1024]{0,1:T(8,128)S(1)}, f32[256,1024]{0,1:T(8,128)}, u32[]{:S(2)}) copy-start(f32[256,1024]{0,1:T(8,128)} %copy-done.32) | copy-start | bytes 3145732
  595.4 12.5 %collective-permute-start.5 = (bf16[1,576,1024]{2,1,0:T(8,128)(2,1)S(1)}, bf16[1,576,1024]{2,1,0:T(8,128)(2,1)S(1)}, u32[]{:S(2)}, u32[]{:S(2)}) collective-permute-start(bf16[1,576,1024]{2,1,0:T(8,128)(2,1)S(1)} %dynamic-slice_bitcast_fusion), channel_id=1, source_target_pairs={{0,16},{16,0},{1,17},{17,1},{2,18},{18,2},{3,19},{19,3},{4,20},{20... | collective-permute-start | bytes 3538952 | tf_op jit(solution)/shard_map/ppermute | solution.py:24
  597.1 12.3 %collective-permute-start.3 = (bf16[4,128,1152]{2,1,0:T(8,128)(2,1)S(1)}, bf16[4,128,1152]{2,1,0:T(8,128)(2,1)S(1)}, u32[]{:S(2)}, u32[]{:S(2)}) collective-permute-start(bf16[4,128,1152]{2,1,0:T(8,128)(2,1)S(1)} %dynamic-slice_bitcast_fusion.2), channel_id=1, source_target_pairs={{0,16},{16,0},{1,17},{17,1},{2,18},{18,2},{3,19},{19,3},{4,20},{20... | collective-permute-start | bytes 3538952 | tf_op jit(solution)/shard_map/ppermute | solution.py:24
  597.1 13.5 %collective-permute-start.4 = (bf16[4,128,1152]{2,1,0:T(8,128)(2,1)S(1)}, bf16[4,128,1152]{2,1,0:T(8,128)(2,1)S(1)}, u32[]{:S(2)}, u32[]{:S(2)}) collective-permute-start(bf16[4,128,1152]{2,1,0:T(8,128)(2,1)S(1)} %dynamic-slice_bitcast_fusion.1), channel_id=1, source_target_pairs={{0,16},{16,0},{1,17},{17,1},{2,18},{18,2},{3,19},{19,3},{4,20},{20... | collective-permute-start | bytes 3538952 | tf_op jit(solution)/shard_map/ppermute | solution.py:24
  613.1 15.3 %collective-permute-start.1 = (f32[2,1024]{1,0:T(2,128)S(1)}, f32[2,1024]{1,0:T(2,128)S(1)}, u32[]{:S(2)}, u32[]{:S(2)}) collective-permute-start(f32[2,1024]{1,0:T(2,128)S(1)} %pad_add_fusion.1), channel_id=1, source_target_pairs={{4,0},{8,4},{12,8},{5,1},{9,5},{13,9},{6,2},{10,6},{14,10},{7,3},{... | collective-permute-start | bytes 24584 | tf_op jit(solution)/shard_map/ppermute | solution.py:20
  646.2 4.4 collective-permute-start.2
  (105 other events, 629.0 us)
Sparse Core Ops, SparseCore 0:
  10.5 30.6 all-gather.4
  43.6 25.3 all-gather.6
  70.9 38.2 all-gather.8
  111.0 36.7 all-gather.10
  612.2 142.9 all-reduce.7

commit v4 on v3

--- a/solution.py
+++ b/solution.py
@@ -62,27 +62,8 @@
     pl.semaphore_wait(barrier, count - 1)
 
 
-def gather_kernel(axis, count, rows, block, whole, send_sem, recv_sem, own_sem):
-    me = lax.axis_index(axis)
-    greet(axis, count)
-    own_rows = pl.ds(pl.multiple_of(me * rows, rows), rows)
-    copies = []
-    for step in range(1, count):
-        copy = pltpu.make_async_remote_copy(
-            src_ref=block,
-            dst_ref=whole.at[own_rows],
-            send_sem=send_sem.at[step],
-            recv_sem=recv_sem.at[step],
-            device_id={axis: lax.rem(me + step, count)},
-            device_id_type=MESH,
-        )
-        copy.start()
-        copies.append(copy)
-    own = pltpu.make_async_copy(block, whole.at[own_rows], own_sem)
-    own.start()
-    own.wait()
-    for copy in copies:
-        copy.wait()
+def busy(microseconds):
+    return pl.CostEstimate(flops=int(microseconds), bytes_accessed=1 << 16, transcendentals=0)
 
 
 def swap_kernel(axis, count, rows, blocks, whole, send_sem, recv_sem, own_sem):
@@ -109,10 +90,11 @@
         copy.wait()
 
 
-def exchange(kernel, axis, array, rows, collective_id):
+def swapped_blocks(array, axis, collective_id):
     count = lax.axis_size(axis)
+    rows = array.shape[0] // count
     return pl.pallas_call(
-        functools.partial(kernel, axis, count, rows),
+        functools.partial(swap_kernel, axis, count, rows),
         out_shape=jax.ShapeDtypeStruct((count * rows,) + array.shape[1:], array.dtype),
         in_specs=[pl.BlockSpec(memory_space=pl.ANY)],
         out_specs=pl.BlockSpec(memory_space=pl.ANY),
@@ -124,21 +106,141 @@
         compiler_params=pltpu.CompilerParams(
             collective_id=collective_id, has_side_effects=True, vmem_limit_bytes=8 << 20
         ),
+        cost_estimate=busy(40),
     )(array)
 
 
-def gathered(array, axis, collective_id):
-    return exchange(gather_kernel, axis, array, array.shape[0], collective_id)
-
-
-def swapped_blocks(array, axis, collective_id):
-    return exchange(swap_kernel, axis, array, array.shape[0] // lax.axis_size(axis), collective_id)
-
-
-def reduced(partial, axis, collective_id):
-    count = lax.axis_size(axis)
-    terms = swapped_blocks(partial.astype(BF16), axis, collective_id)
-    return jnp.sum(terms.reshape(count, -1, partial.shape[1]).astype(F32), axis=0)
+def corners():
+    me = lax.axis_index("fsdp")
+    beside = me + 1 - 2 * lax.rem(me, 2)
+    across = lax.rem(me + 2, 4)
+    return me, beside, across, lax.rem(beside + 2, 4)
+
+
+def greet_sides():
+    _, beside, across, _ = corners()
+    barrier = pltpu.get_barrier_semaphore()
+    for target in (beside, across):
+        pl.semaphore_signal(barrier, inc=1, device_id={"fsdp": target}, device_id_type=MESH)
+    pl.semaphore_wait(barrier, 2)
+
+
+def to_side(src, dst, send_sem, recv_sem, target):
+    return pltpu.make_async_remote_copy(
+        src_ref=src,
+        dst_ref=dst,
+        send_sem=send_sem,
+        recv_sem=recv_sem,
+        device_id={"fsdp": target},
+        device_id_type=MESH,
+    )
+
+
+def gather_kernel(block, whole, send_sem, recv_sem, own_sem):
+    me, beside, across, _ = corners()
+    rows = block.shape[0]
+    half = rows // 2
+
+    def part(owner, start, size):
+        return whole.at[pl.ds(pl.multiple_of(owner * rows + start, half), size)]
+
+    greet_sides()
+    first = to_side(block, part(me, 0, rows), send_sem.at[0], recv_sem.at[0], beside)
+    second = to_side(block, part(me, 0, rows), send_sem.at[1], recv_sem.at[1], across)
+    first.start()
+    second.start()
+    own = pltpu.make_async_copy(block, part(me, 0, rows), own_sem)
+    own.start()
+    first.wait_recv()
+    at = part(beside, 0, half)
+    third = to_side(at, at, send_sem.at[2], recv_sem.at[2], across)
+    third.start()
+    second.wait_recv()
+    at = part(across, half, half)
+    fourth = to_side(at, at, send_sem.at[3], recv_sem.at[3], beside)
+    fourth.start()
+    own.wait()
+    for copy in (first, second):
+        copy.wait_send()
+    for copy in (third, fourth):
+        copy.wait()
+
+
+def gathered(array, collective_id):
+    rows, width = array.shape
+    assert lax.axis_size("fsdp") == 4
+    dma = pltpu.SemaphoreType.DMA
+    return pl.pallas_call(
+        gather_kernel,
+        out_shape=jax.ShapeDtypeStruct((4 * rows, width), array.dtype),
+        in_specs=[pl.BlockSpec(memory_space=pltpu.VMEM)],
+        out_specs=pl.BlockSpec(memory_space=pltpu.VMEM),
+        scratch_shapes=[dma((4,)), dma((4,)), dma],
+        compiler_params=pltpu.CompilerParams(
+            collective_id=collective_id, has_side_effects=True, vmem_limit_bytes=8 << 20
+        ),
+        cost_estimate=busy(25),
+    )(array)
+
+
+def reduce_kernel(blocks, total, beside_got, across_got, passed, passed_got, send_sem, recv_sem):
+    me, beside, across, opposite = corners()
+    rows = total.shape[0]
+    half = rows // 2
+
+    def part(owner, turn):
+        return pl.ds(pl.multiple_of(owner * rows + turn * half, half), half)
+
+    greet_sides()
+    copies = []
+    for index, (turn, target, got) in enumerate(((0, beside, beside_got), (1, across, across_got))):
+        for slot, owner in ((1, opposite), (0, target)):
+            copies.append(
+                to_side(
+                    blocks.at[part(owner, turn)],
+                    got.at[slot],
+                    send_sem.at[2 * index + slot],
+                    recv_sem.at[2 * index + slot],
+                    target,
+                )
+            )
+    for copy in (copies[0], copies[2], copies[1], copies[3]):
+        copy.start()
+    onward = []
+    for turn, owner, copy, got in ((0, across, copies[0], beside_got), (1, beside, copies[2], across_got)):
+        copy.wait_recv()
+        passed[turn] = (blocks[part(owner, turn)].astype(F32) + got[1].astype(F32)).astype(BF16)
+        onward.append(
+            to_side(passed.at[turn], passed_got.at[turn], send_sem.at[4 + turn], recv_sem.at[4 + turn], owner)
+        )
+        onward[-1].start()
+    for turn, copy, got in ((0, copies[1], beside_got), (1, copies[3], across_got)):
+        copy.wait_recv()
+        total[pl.ds(turn * half, half)] = blocks[part(me, turn)].astype(F32) + got[0].astype(F32)
+    for turn in range(2):
+        onward[turn].wait_recv()
+        at = pl.ds(turn * half, half)
+        total[at] = total[at] + passed_got[turn].astype(F32)
+    for copy in copies + onward:
+        copy.wait_send()
+
+
+def reduced(partial, collective_id):
+    rows, width = partial.shape[0] // 4, partial.shape[1]
+    assert lax.axis_size("fsdp") == 4
+    dma = pltpu.SemaphoreType.DMA
+    pair = pltpu.VMEM((2, rows // 2, width), BF16)
+    return pl.pallas_call(
+        reduce_kernel,
+        out_shape=jax.ShapeDtypeStruct((rows, width), F32),
+        in_specs=[pl.BlockSpec(memory_space=pltpu.VMEM)],
+        out_specs=pl.BlockSpec(memory_space=pltpu.VMEM),
+        scratch_shapes=[pair, pair, pair, pair, dma((6,)), dma((6,))],
+        compiler_params=pltpu.CompilerParams(
+            collective_id=collective_id, has_side_effects=True, vmem_limit_bytes=16 << 20
+        ),
+        cost_estimate=busy(25),
+    )(partial.astype(BF16))
 
 
 def tail_kernel(
@@ -731,6 +833,7 @@
         compiler_params=pltpu.CompilerParams(
             collective_id=6, has_side_effects=True, vmem_limit_bytes=56 << 20
         ),
+        cost_estimate=busy(160),
     )(gate, up, down, *mixers, small, second_gu, second_down)
 
 
@@ -833,6 +936,7 @@
         compiler_params=pltpu.CompilerParams(
             collective_id=collective_id, has_side_effects=True, vmem_limit_bytes=8 << 20
         ),
+        cost_estimate=busy(45),
     )(first, second)
 
 
@@ -989,6 +1093,7 @@
         compiler_params=pltpu.CompilerParams(
             collective_id=collective_id, has_side_effects=True, vmem_limit_bytes=8 << 20
         ),
+        cost_estimate=busy(40),
     )(*ins)
 
 
@@ -1026,27 +1131,29 @@
 
 def ffn_forward(residual, gain, w_gate, w_up, w_down):
     normed, inv_rms = norm_rows(residual)
-    act = gathered((normed * gain).astype(BF16), "fsdp", 0)
+    act = gathered((normed * gain).astype(BF16), 0)
     gate_pre = matmul(act, w_gate)
     up_pre = matmul(act, w_up)
     hidden = (jax.nn.silu(gate_pre) * up_pre).astype(BF16)
-    out = reduced(matmul(hidden, w_down), "fsdp", 1)
+    out = reduced(matmul(hidden, w_down), 1)
     return out, (normed, inv_rms, act, gate_pre, up_pre, hidden)
 
 
-def ffn_backward(d_low, kept, gain, w_gate, w_up, w_down):
+def ffn_backward(d_low, kept, gain, w_gate, w_up, w_down, settled=None):
     normed, inv_rms, act, gate_pre, up_pre, hidden = kept
-    d_all = gathered(d_low, "fsdp", 0)
+    d_all = gathered(d_low, 0)
+    if settled is not None:
+        d_all, settled = lax.optimization_barrier((d_all, settled))
     d_hidden = matmul_right(d_all, w_down)
     sigmoid = jax.nn.sigmoid(gate_pre)
     d_up = (d_hidden * gate_pre * sigmoid).astype(BF16)
     d_gate = (d_hidden * up_pre * sigmoid * (1.0 + gate_pre * (1.0 - sigmoid))).astype(BF16)
-    d_act = reduced(matmul_right(d_gate, w_gate) + matmul_right(d_up, w_up), "fsdp", 1)
+    d_act = reduced(matmul_right(d_gate, w_gate) + matmul_right(d_up, w_up), 1)
     grad_gate = matmul_left(act, d_gate).astype(BF16)
     grad_up = matmul_left(act, d_up).astype(BF16)
     grad_down = matmul_left(hidden, d_all).astype(BF16)
     grad_gain = jnp.sum(d_act * normed, axis=0)
-    return norm_back(d_act * gain, normed, inv_rms), grad_gain, (grad_gate, grad_up, grad_down)
+    return norm_back(d_act * gain, normed, inv_rms), grad_gain, (grad_gate, grad_up, grad_down), settled
 
 
 def shards(
@@ -1152,7 +1259,7 @@
 
     d_sum_low = (lax.dynamic_index_in_dim(cotangent, section, keepdims=False).astype(F32) * mask).astype(BF16)
     d_sum = d_sum_low.astype(F32)
-    d_ffn, gain3, grads2 = ffn_backward(d_sum_low, kept2, norm_gains[3], gate2, up2, down2)
+    d_ffn, gain3, grads2, _ = ffn_backward(d_sum_low, kept2, norm_gains[3], gate2, up2, down2)
     d_res2 = d_sum + d_ffn
     d_attn = d_res2.astype(BF16)
     grad_proj = matmul_left(attended_low, d_attn)
@@ -1160,12 +1267,32 @@
     d_query, d_key_all, d_value_all = attend_back(
         query, key_all, value_all, allowed, log_total, attended, d_att
     )
-    d_kv = reduced(
-        jnp.concatenate(
-            [d_key_all.reshape(-1, kv_width), d_value_all.reshape(-1, kv_width)], axis=1
-        ),
-        "ctx",
-        4,
+    half = part // 2
+
+    def shared_halves(grad, lead):
+        pieces = grad.reshape(lead, 2, -1, grad.shape[1])
+        mine = lax.dynamic_index_in_dim(pieces, section, 1, keepdims=False)
+        other = swapped(lax.dynamic_index_in_dim(pieces, 1 - section, 1, keepdims=False), "section")
+        return (mine.astype(F32) + other.astype(F32)).astype(BF16)
+
+    d_kv_terms = jnp.concatenate(
+        [d_key_all.reshape(-1, kv_width), d_value_all.reshape(-1, kv_width)], axis=1
+    ).astype(BF16)
+    d_kv_terms, second = lax.optimization_barrier(
+        (
+            d_kv_terms,
+            (
+                shared_halves(jnp.concatenate(grads2[:2], axis=0), 2 * fsdp),
+                shared_halves(grads2[2], 1)[0],
+            ),
+        )
+    )
+    second = tuple(
+        lax.psum_scatter(term.reshape(-1, term.shape[-1]), "ctx", scatter_dimension=0, tiled=True)
+        for term in second
+    )
+    d_kv = jnp.sum(
+        swapped_blocks(d_kv_terms, "ctx", 4).reshape(lax.axis_size("ctx"), rows, -1).astype(F32), axis=0
     )
     d_qn = rounded(d_query)
     grad_qgain = jnp.sum(d_qn * q_normed, axis=(0, 1))
@@ -1182,7 +1309,10 @@
     gain2 = jnp.sum(d_act2 * normed2, axis=0)
     d_h_low = (d_res2 + norm_back(d_act2 * norm_gains[2], normed2, inv2)).astype(BF16)
 
-    d_ffn1, gain1, grads1 = ffn_backward(d_h_low, kept1, norm_gains[1], gate1, up1, down1)
+    d_ffn1, gain1, grads1, second = ffn_backward(
+        d_h_low, kept1, norm_gains[1], gate1, up1, down1, second
+    )
+    second = tuple(lax.all_gather(term, "ctx", axis=0, tiled=True) for term in second)
     d_res1 = d_h_low.astype(F32) + d_ffn1
     d_mixed = d_res1.astype(BF16)
     grad_out = matmul_left(z_low, d_mixed)
@@ -1201,7 +1331,9 @@
         + jnp.pad(d_conv * conv_kernel[1], ((1, 1), (0, 0)))
         + jnp.pad(d_conv * conv_kernel[2], ((2, 0), (0, 0)))
     )
-    from_next = passed_along(d_extended[:2], "ctx", -1)
+    from_next, second_gu = lax.optimization_barrier(
+        (passed_along(d_extended[:2], "ctx", -1), second[0])
+    )
     d_bproduct = rounded(d_extended[2:] + jnp.pad(from_next, ((rows - 2, 0), (0, 0))))
     d_projected = jnp.concatenate(
         [d_bproduct * x_value, d_cgate, d_bproduct * b_gate], axis=1
@@ -1224,22 +1356,6 @@
         grad_proj.astype(BF16),
     ] + grad_parts + [grad_out.astype(BF16)]
 
-    half = part // 2
-
-    def shared_halves(grad, lead):
-        pieces = grad.reshape(lead, 2, -1, grad.shape[1])
-        mine = lax.dynamic_index_in_dim(pieces, section, 1, keepdims=False)
-        other = swapped(lax.dynamic_index_in_dim(pieces, 1 - section, 1, keepdims=False), "section")
-        return (mine.astype(F32) + other.astype(F32)).astype(BF16)
-
-    second = lax.psum(
-        (
-            shared_halves(grads2[0], fsdp),
-            shared_halves(grads2[1], fsdp),
-            shared_halves(grads2[2], 1)[0],
-        ),
-        "ctx",
-    )
     cut = width // fsdp
     head_cut = head // fsdp
     square_cut = squares.shape[0] // fsdp
@@ -1263,8 +1379,8 @@
         grads1,
         mixers,
         small,
-        jnp.stack([second[0], second[1]]),
-        second[2],
+        second_gu.reshape(2, fsdp, part // 2, -1),
+        second[1],
     )
     rest_sum = rest_sum.astype(F32)
 

time: 972 us -> 903 us (0.929)
  waiting for transfers between devices: 114 us -> 45.5 us
  Pallas kernels: 555 us -> 526 us
  local copies, waits for them, and re-layouts: 65.3 us -> 79.7 us
    psum x1 -> x0, waiting for transfers between devices: 103 us -> none  [shards(): lax.psum((shared_halves(grads2[0], fsdp), shared_halves(grads2[1], fsdp),...]
    all_gather x0 -> x2, waiting for transfers between devices: none -> 31.8 us  [shards(): lax.all_gather(term, 'ctx', axis=0, tiled=True)]
    pallas_call x9, Pallas kernels: 253 us -> 224 us  [the longest x4 90 us: gathered(): pl.pallas_call(gather_kernel, out_shape=jax.ShapeDtypeStruct((4 * rows, w...]
    reduce_scatter x0 -> x2, waiting for transfers between devices: none -> 13.5 us  [shards(): lax.psum_scatter(term.reshape(-1, term.shape[-1]), 'ctx', scatter_dimensi...]
    unnamed x244 -> x278, local copies, waits for them, and re-layouts: 28.9 us -> 42.2 us
    ppermute x2, waiting for transfers between devices: 10.4 us -> 0.01 us  [passed_along(): return lax.ppermute(block, axis, route)]
  transfers between devices with their start and end apart: 11 -> 13, of which waited for: 2 -> 3; matrix products, arithmetic and copies ran while one was open for 10% -> 21% of each run, Pallas kernels for 22% -> 35%
where the time goes in v4:
time: 903 us; the launch traced here: 890 us
  Pallas kernels  526 us (58%)
  matrix products  153 us (17%)
  local copies, waits for them, and re-layouts  79.7 us (9%)
  other arithmetic  64.3 us (7%)
  waiting for transfers between devices  45.5 us (5%)
  between operations  16.8 us (2%)
    pallas_call x1, Pallas kernels, summed_gradients(): pl.pallas_call(functools.partial(tail_kernel, (n_ctx, n_fsdp)), out_shape...  176 us
    pallas_call x4, Pallas kernels, gathered(): pl.pallas_call(gather_kernel, out_shape=jax.ShapeDtypeStruct((4 * rows, w...  90 us
    pallas_call x2, Pallas kernels, column_weights(): pl.pallas_call(functools.partial(column_weights_kernel, count, holder, n_...  79.9 us
    pallas_call x4, Pallas kernels, reduced(): pl.pallas_call(reduce_kernel, out_shape=jax.ShapeDtypeStruct((rows, width...  76.3 us
    pallas_call x1, Pallas kernels, swapped_blocks(): pl.pallas_call(functools.partial(swap_kernel, axis, count, rows), out_sha...  57.3 us
    pallas_call x1, Pallas kernels, mixer_weights(): pl.pallas_call(functools.partial(mixer_weights_kernel, count), out_shape=...  45.7 us
    unnamed x278, local copies, waits for them, and re-layouts  42.2 us
    dot_general x13, matrix products, matmul_left(): lax.dot_general(left_op, right_op, (((0,), (0,)), ((), ())), preferred_el...  40.8 us
  transfers between devices with their start and end apart: 13, of which 3 were waited for; matrix products, arithmetic and copies ran while one was open for 21% of the time, Pallas kernels for 35%

profile of v4, /device:TPU:0, one launch (start us, length us, event | category | flops | bytes accessed | tf_op | source)
XLA Modules:
  0.0 890.0 jit_solution(15080882201463774147)
XLA Ops:
  12.6 45.7 %shard_map.262 = (bf16[1024,3072]{1,0:T(8,128)(2,1)S(1)}, bf16[1024,1024]{1,0:T(8,128)(2,1)S(1)}) custom-call(bf16[256,3072]{1,0:T(8,128)(2,1)S(1)} %copy-done.20, bf16[256,1024]{1,0:T(8,128)(2,1)S(1)} %copy-done.21), custom_call_target="tpu_custom_call" | custom-call | flops 45 | bytes 65536 | tf_op jit(solution)/shard_map/pallas_call | solution.py:928
  78.2 27.8 %shard_map.267 = bf16[1024,1024]{1,0:T(8,128)(2,1)S(1)} custom-call(bf16[256,1024]{1,0:T(8,128)(2,1)S(1)} %get-tuple-element.148.block), custom_call_target="tpu_custom_call" | custom-call | flops 25 | bytes 65536 | tf_op jit(solution)/shard_map/pallas_call | solution.py:173
  110.7 41.7 %shard_map.264 = (bf16[1024,1152]{1,0:T(8,128)(2,1)S(1)}, bf16[1024,1152]{1,0:T(8,128)(2,1)S(1)}, bf16[1152,1024]{1,0:T(8,128)(2,1)S(1)}) custom-call(bf16[256,4608]{1,0:T(8,128)(2,1)S(1)} %bitcast.233, bf16[256,4608]{1,0:T(8,128)(2,1)S(1)} %bitcast.235, bf16[1152,1024]{1,0:T(8,128)(2,1)S(1)} %bitcast.237), custom_call_target="tpu_custom_call" | custom-call | flops 40 | bytes 65536 | tf_op jit(solution)/shard_map/pallas_call | solution.py:1087
  162.7 21.2 %shard_map.263 = bf16[1024,1024]{1,0:T(8,128)(2,1)S(1)} custom-call(bf16[256,1024]{1,0:T(8,128)(2,1)S(1)} %multiply_convert_fusion.9.block), custom_call_target="tpu_custom_call" | custom-call | flops 25 | bytes 65536 | tf_op jit(solution)/shard_map/pallas_call | solution.py:173
  197.1 18.6 %shard_map.265 = f32[256,1024]{1,0:T(8,128)S(1)} custom-call(bf16[1024,1024]{1,0:T(8,128)(2,1)S(1)} %copy-done.18), custom_call_target="tpu_custom_call" | custom-call | flops 25 | bytes 65536 | tf_op jit(solution)/shard_map/pallas_call | solution.py:233
  236.6 38.3 %shard_map.266 = (bf16[1024,1152]{1,0:T(8,128)(2,1)S(1)}, bf16[1024,1152]{1,0:T(8,128)(2,1)S(1)}, bf16[1152,1024]{1,0:T(8,128)(2,1)S(1)}, bf16[1024,1024]{1,0:T(8,128)(2,1)S(1)}) custom-call(bf16[256,1024]{1,0:T(8,128)(2,1)S(1)} %copy-done.19, bf16[256,4608]{1,0:T(8,128)(2,1)S(1)} %bitcast.234, bf16[256,4608]{1,0:T(8,128)(2,1)S(1)} %bitcast.236, ...), custom_call_target="tpu_custom_call" | custom-call | flops 40 | bytes 65536 | tf_op jit(solution)/shard_map/pallas_call | solution.py:1087
  294.4 5.7 fusion.106
  304.8 20.0 %shard_map.268 = bf16[1024,1024]{1,0:T(8,128)(2,1)S(1)} custom-call(bf16[256,1024]{1,0:T(8,128)(2,1)S(1)} %multiply_convert_fusion.7.block), custom_call_target="tpu_custom_call" | custom-call | flops 25 | bytes 65536 | tf_op jit(solution)/shard_map/pallas_call | solution.py:173
  330.6 6.4 multiply_convert_fusion.3
  352.0 17.6 %shard_map.273 = f32[256,1024]{1,0:T(8,128)S(1)} custom-call(bf16[1024,1024]{1,0:T(8,128)(2,1)S(1)} %convolution_convert_fusion.6.blocks), custom_call_target="tpu_custom_call" | custom-call | flops 25 | bytes 65536 | tf_op jit(solution)/shard_map/pallas_call | solution.py:233
  378.4 20.2 %shard_map.269 = f32[256,1024]{1,0:T(8,128)S(1)} custom-call(bf16[1024,1024]{1,0:T(8,128)(2,1)S(1)} %add_convert_fusion.1.blocks), custom_call_target="tpu_custom_call" | custom-call | flops 25 | bytes 65536 | tf_op jit(solution)/shard_map/pallas_call | solution.py:233
  410.0 8.7 fusion.1
  423.5 7.6 bitcast_convert_fusion.1
  443.7 5.2 fusion.31
  456.0 57.3 %shard_map.270 = bf16[1024,1024]{1,0:T(8,128)(2,1)S(1)} custom-call(bf16[1024,1024]{1,0:T(8,128)(2,1)S(1)} %pad_maximum_fusion.2.blocks), custom_call_target="tpu_custom_call" | custom-call | flops 40 | bytes 65536 | tf_op jit(solution)/shard_map/pallas_call | solution.py:96
  524.0 21.1 %shard_map.271 = bf16[1024,1024]{1,0:T(8,128)(2,1)S(1)} custom-call(bf16[256,1024]{1,0:T(8,128)(2,1)S(1)} %fusion.58.block), custom_call_target="tpu_custom_call" | custom-call | flops 25 | bytes 65536 | tf_op jit(solution)/shard_map/pallas_call | solution.py:173
  548.5 13.5 %reduce-scatter.3.cloned.1.call-done = bf16[256,1152]{1,0:T(8,128)(2,1)} async-done(((bf16[1024,1152]{1,0:T(8,128)(2,1)}), bf16[256,1152]{1,0:T(8,128)(2,1)}) %reduce-scatter.3.cloned.1.call-update) | async-done | bytes 589840 | tf_op jit(solution)/shard_map/reduce_scatter | solution.py:1291
  562.0 7.4 multiply_convert_fusion
  578.6 19.9 %shard_map.272 = f32[256,1024]{1,0:T(8,128)S(1)} custom-call(bf16[1024,1024]{1,0:T(8,128)(2,1)S(1)} %copy-done.17), custom_call_target="tpu_custom_call" | custom-call | flops 25 | bytes 65536 | tf_op jit(solution)/shard_map/pallas_call | solution.py:233
  624.5 21.1 %all-gather.15.cloned.1.call-done = bf16[1024,1152]{1,0:T(8,128)(2,1)} async-done(((bf16[256,1152]{1,0:T(8,128)(2,1)}), bf16[1024,1152]{1,0:T(8,128)(2,1)}) %all-gather.15.cloned.1.call-update) | async-done | bytes 2359312 | tf_op jit(solution)/shard_map/all_gather | solution.py:1315
  647.4 6.7 fusion.53
  654.1 5.2 stack.84
  665.7 10.8 %all-gather.17.cloned.1.call-done.second_down_in = bf16[576,1024]{1,0:T(8,128)(2,1)} async-done(((bf16[144,1024]{1,0:T(8,128)(2,1)}), bf16[576,1024]{1,0:T(8,128)(2,1)}) %all-gather.17.cloned.1.call-update) | async-done | bytes 1179664 | tf_op jit(solution)/shard_map/all_gather | solution.py:1315
  676.4 176.5 %shard_map.274 = (bf16[2,256,4608]{2,1,0:T(8,128)(2,1)}, bf16[1152,1024]{1,0:T(8,128)(2,1)}, bf16[2,960,1024]{2,1,0:T(8,128)(2,1)}) custom-call(bf16[1024,1152]{1,0:T(8,128)(2,1)} %convolution_convert_fusion.2.gate_in, bf16[1024,1152]{1,0:T(8,128)(2,1)} %convolution_convert_fusion.1.up_in, bf16[1152,1024]{1,0:T(8,128)(2,1)} %convolution_convert_fusion.down_in, ...), custom_call_target="tpu_custom_call" | custom-call | flops 160 | bytes 65536 | tf_op jit(solution)/shard_map/pallas_call | solution.py:788
  (457 shorter events, 249.2 us)
Async XLA Ops:
  7.2 55.0 %copy-start.123 = (s32[8]{0:T(128)S(1)}, s32[8]{0:T(128)}, u32[]{:S(2)}) copy-start(s32[8]{0:T(128)} %param.17) | copy-start | bytes 100
  7.2 210.7 %all-gather.7.cloned.1.call-start = ((), (), s32[]{:S(2)}) async-start(), calls=%async_computation.2 | async-start | bytes 1179648 | tf_op jit(solution)/shard_map/all_gather | solution.py:1191
  9.0 220.4 %all-gather.9.cloned.1.call-start = ((), (), s32[]{:S(2)}) async-start(), calls=%async_computation.3 | async-start | bytes 1179648 | tf_op jit(solution)/shard_map/all_gather | solution.py:1191
  10.6 54.1 %copy-start.111 = (f32[4,1024]{1,0:T(4,128)S(1)}, f32[4,1024]{1,0:T(4,128)}, u32[]{:S(2)}) copy-start(f32[4,1024]{1,0:T(4,128)} %param.18) | copy-start | bytes 49156
  10.7 272.4 %all-gather.11.cloned.1.call-start = ((), (), s32[]{:S(2)}) async-start(), calls=%async_computation.4 | async-start | bytes 2359296 | tf_op jit(solution)/shard_map/all_gather | solution.py:1191
  11.5 288.7 %all-gather.13.cloned.1.call-start = ((), (), s32[]{:S(2)}) async-start(), calls=%async_computation.5 | async-start | bytes 2359296 | tf_op jit(solution)/shard_map/all_gather | solution.py:1191
  12.6 50.9 %copy-start.55 = (bf16[2,256,1024]{2,1,0:T(8,128)(2,1)S(1)}, bf16[2,256,1024]{2,1,0:T(8,128)(2,1)}, u32[]{:S(2)}) copy-start(bf16[2,256,1024]{2,1,0:T(8,128)(2,1)} %param.15) | copy-start | bytes 3145732
  64.8 96.8 %copy-start.97 = (f32[1,1024]{1,0:T(1,128)}, f32[1,1024]{1,0:T(1,128)S(1)}, u32[]{:S(2)}) copy-start(f32[1,1024]{1,0:T(1,128)S(1)} %get-tuple-element.125) | copy-start | bytes 12292
  64.8 218.2 %copy-start.105 = (f32[1,1024]{1,0:T(1,128)}, f32[1,1024]{1,0:T(1,128)S(1)}, u32[]{:S(2)}) copy-start(f32[1,1024]{1,0:T(1,128)S(1)} %get-tuple-element.127) | copy-start | bytes 12292
  72.0 35.4 %copy-start.2 = (bf16[1,256,4608]{2,1,0:T(8,128)(2,1)S(1)}, bf16[1,256,4608]{2,1,0:T(8,128)(2,1)}, u32[]{:S(2)}) copy-start(bf16[1,256,4608]{2,1,0:T(8,128)(2,1)} %param.27) | copy-start | bytes 7077892
  72.1 84.6 %collective-permute-start = (bf16[2,1024]{1,0:T(2,128)(2,1)S(1)}, bf16[2,1024]{1,0:T(2,128)(2,1)S(1)}, u32[]{:S(2)}, u32[]{:S(2)}) collective-permute-start(bf16[2,1024]{1,0:T(2,128)(2,1)S(1)} %slice.203), channel_id=1, source_target_pairs={{0,4},{4,8},{8,12},{1,5},{5,9},{9,13},{2,6},{6,10},{10,14},{3,7},{... | collective-permute-start | bytes 12296 | tf_op jit(solution)/shard_map/ppermute | solution.py:20
  76.5 472.0 %reduce-scatter.5.cloned.1.call-start = ((), (), s32[]{:S(2)}) async-start(), calls=%async_computation.7 | async-start | bytes 1474560 | tf_op jit(solution)/shard_map/reduce_scatter | solution.py:1291
  77.2 79.6 %copy-start.99 = (f32[1,1024]{1,0:T(1,128)}, f32[1,1024]{1,0:T(1,128)S(1)}, u32[]{:S(2)}) copy-start(f32[1,1024]{1,0:T(1,128)S(1)} %get-tuple-element.128) | copy-start | bytes 12292
  77.2 79.6 %copy-start.101 = (f32[1,1024]{1,0:T(1,128)}, f32[1,1024]{1,0:T(1,128)S(1)}, u32[]{:S(2)}) copy-start(f32[1,1024]{1,0:T(1,128)S(1)} %get-tuple-element.129) | copy-start | bytes 12292
  77.2 79.6 %copy-start.103 = (f32[1,1024]{1,0:T(1,128)}, f32[1,1024]{1,0:T(1,128)S(1)}, u32[]{:S(2)}) copy-start(f32[1,1024]{1,0:T(1,128)S(1)} %get-tuple-element.130) | copy-start | bytes 12292
  78.2 117.2 %copy-start.119 = (f32[64]{0:T(128)}, f32[64]{0:T(128)S(1)}, u32[]{:S(2)}) copy-start(f32[64]{0:T(128)S(1)} %get-tuple-element.134) | copy-start | bytes 772
  217.9 65.2 %copy-start.114 = (f32[256]{0:T(256)}, f32[256]{0:T(256)S(1)}, u32[]{:S(2)}) copy-start(f32[256]{0:T(256)S(1)} %add_rsqrt_fusion.3) | copy-start | bytes 3076
  378.4 56.3 %collective-permute-start.2 = (bf16[1,576,1024]{2,1,0:T(8,128)(2,1)}, bf16[1,576,1024]{2,1,0:T(8,128)(2,1)}, u32[]{:S(2)}, u32[]{:S(2)}) collective-permute-start(bf16[1,576,1024]{2,1,0:T(8,128)(2,1)} %dynamic-slice_bitcast_fusion.1), channel_id=1, source_target_pairs={{0,16},{16,0},{1,17},{17,1},{2,18},{18,2},{3,19},{19,3},{4,20},{20... | collective-permute-start | bytes 3538952 | tf_op jit(solution)/shard_map/ppermute | solution.py:24
  409.8 28.0 %collective-permute-start.1 = (bf16[8,128,1152]{2,1,0:T(8,128)(2,1)}, bf16[8,128,1152]{2,1,0:T(8,128)(2,1)}, u32[]{:S(2)}, u32[]{:S(2)}) collective-permute-start(bf16[8,128,1152]{2,1,0:T(8,128)(2,1)} %dynamic-slice_bitcast_fusion), channel_id=1, source_target_pairs={{0,16},{16,0},{1,17},{17,1},{2,18},{18,2},{3,19},{19,3},{4,20},{20... | collective-permute-start | bytes 7077896 | tf_op jit(solution)/shard_map/ppermute | solution.py:24
  442.2 119.8 %reduce-scatter.3.cloned.1.call-start = ((), (), s32[]{:S(2)}) async-start(), calls=%async_computation.6 | async-start | bytes 2949120 | tf_op jit(solution)/shard_map/reduce_scatter | solution.py:1291
  443.6 201.9 %all-gather.15.cloned.1.call-start = ((), (), s32[]{:S(2)}) async-start(), calls=%async_computation.8 | async-start | bytes 2949120 | tf_op jit(solution)/shard_map/all_gather | solution.py:1315
  576.9 99.5 %all-gather.17.cloned.1.call-start = ((), (), s32[]{:S(2)}) async-start(), calls=%async_computation.9 | async-start | bytes 1474560 | tf_op jit(solution)/shard_map/all_gather | solution.py:1315
  604.8 19.6 %collective-permute-start.3 = (f32[2,1024]{1,0:T(2,128)S(1)}, f32[2,1024]{1,0:T(2,128)S(1)}, u32[]{:S(2)}, u32[]{:S(2)}) collective-permute-start(f32[2,1024]{1,0:T(2,128)S(1)} %pad_add_fusion.1), channel_id=1, source_target_pairs={{4,0},{8,4},{12,8},{5,1},{9,5},{13,9},{6,2},{10,6},{14,10},{7,3},{... | collective-permute-start | bytes 24584 | tf_op jit(solution)/shard_map/ppermute | solution.py:20
  864.1 17.7 %collective-permute-start.4 = (bf16[256,1024]{1,0:T(8,128)(2,1)}, bf16[256,1024]{1,0:T(8,128)(2,1)S(1)}, u32[]{:S(2)}, u32[]{:S(2)}) collective-permute-start(bf16[256,1024]{1,0:T(8,128)(2,1)} %get-tuple-element.78), channel_id=1, source_target_pairs={{0,16},{16,0},{1,17},{17,1},{2,18},{18,2},{3,19},{19,3},{4,20},{20... | collective-permute-start | bytes 1572872 | tf_op jit(solution)/shard_map/ppermute | solution.py:24
  (124 other events, 667.8 us)
Sparse Core Ops, SparseCore 0:
  10.5 31.3 all-gather.6
  43.8 24.6 all-gather.8
  70.4 34.5 all-gather.10
  106.7 42.4 all-gather.12
  442.3 54.3 reduce-scatter.4
  498.9 63.0 reduce-scatter.2
  577.1 68.4 all-gather.14
  647.1 29.2 all-gather.16

commit v5 on v4

--- a/solution.py
+++ b/solution.py
@@ -49,65 +49,8 @@
     return inv_rms * dnormed - normed * inv_rms * jnp.mean(dnormed * normed, axis=-1, keepdims=True)
 
 
-def greet(axis, count):
-    me = lax.axis_index(axis)
-    barrier = pltpu.get_barrier_semaphore()
-    for step in range(1, count):
-        pl.semaphore_signal(
-            barrier,
-            inc=1,
-            device_id={axis: lax.rem(me + step, count)},
-            device_id_type=MESH,
-        )
-    pl.semaphore_wait(barrier, count - 1)
-
-
 def busy(microseconds):
     return pl.CostEstimate(flops=int(microseconds), bytes_accessed=1 << 16, transcendentals=0)
-
-
-def swap_kernel(axis, count, rows, blocks, whole, send_sem, recv_sem, own_sem):
-    me = lax.axis_index(axis)
-    greet(axis, count)
-    own_rows = pl.ds(pl.multiple_of(me * rows, rows), rows)
-    copies = []
-    for step in range(1, count):
-        target = lax.rem(me + step, count)
-        copy = pltpu.make_async_remote_copy(
-            src_ref=blocks.at[pl.ds(pl.multiple_of(target * rows, rows), rows)],
-            dst_ref=whole.at[own_rows],
-            send_sem=send_sem.at[step],
-            recv_sem=recv_sem.at[step],
-            device_id={axis: target},
-            device_id_type=MESH,
-        )
-        copy.start()
-        copies.append(copy)
-    own = pltpu.make_async_copy(blocks.at[own_rows], whole.at[own_rows], own_sem)
-    own.start()
-    own.wait()
-    for copy in copies:
-        copy.wait()
-
-
-def swapped_blocks(array, axis, collective_id):
-    count = lax.axis_size(axis)
-    rows = array.shape[0] // count
-    return pl.pallas_call(
-        functools.partial(swap_kernel, axis, count, rows),
-        out_shape=jax.ShapeDtypeStruct((count * rows,) + array.shape[1:], array.dtype),
-        in_specs=[pl.BlockSpec(memory_space=pl.ANY)],
-        out_specs=pl.BlockSpec(memory_space=pl.ANY),
-        scratch_shapes=[
-            pltpu.SemaphoreType.DMA((count,)),
-            pltpu.SemaphoreType.DMA((count,)),
-            pltpu.SemaphoreType.DMA,
-        ],
-        compiler_params=pltpu.CompilerParams(
-            collective_id=collective_id, has_side_effects=True, vmem_limit_bytes=8 << 20
-        ),
-        cost_estimate=busy(40),
-    )(array)
 
 
 def corners():
@@ -136,34 +79,48 @@
     )
 
 
+class SideGather:
+    def __init__(self, block, whole, send_sem, recv_sem, own_sem):
+        me, beside, across, _ = corners()
+        rows = block.shape[0]
+        half = rows // 2
+
+        def part(owner, start, size):
+            return whole.at[pl.ds(pl.multiple_of(owner * rows + start, half), size)]
+
+        self.first = to_side(block, part(me, 0, rows), send_sem.at[0], recv_sem.at[0], beside)
+        self.second = to_side(block, part(me, 0, rows), send_sem.at[1], recv_sem.at[1], across)
+        at = part(beside, 0, half)
+        self.third = to_side(at, at, send_sem.at[2], recv_sem.at[2], across)
+        at = part(across, half, half)
+        self.fourth = to_side(at, at, send_sem.at[3], recv_sem.at[3], beside)
+        self.own = pltpu.make_async_copy(block, part(me, 0, rows), own_sem)
+
+    def start(self):
+        self.first.start()
+        self.second.start()
+        self.own.start()
+
+    def relay(self):
+        self.first.wait_recv()
+        self.third.start()
+        self.second.wait_recv()
+        self.fourth.start()
+
+    def finish(self):
+        self.own.wait()
+        self.first.wait_send()
+        self.second.wait_send()
+        self.third.wait()
+        self.fourth.wait()
+
+
 def gather_kernel(block, whole, send_sem, recv_sem, own_sem):
-    me, beside, across, _ = corners()
-    rows = block.shape[0]
-    half = rows // 2
-
-    def part(owner, start, size):
-        return whole.at[pl.ds(pl.multiple_of(owner * rows + start, half), size)]
-
     greet_sides()
-    first = to_side(block, part(me, 0, rows), send_sem.at[0], recv_sem.at[0], beside)
-    second = to_side(block, part(me, 0, rows), send_sem.at[1], recv_sem.at[1], across)
-    first.start()
-    second.start()
-    own = pltpu.make_async_copy(block, part(me, 0, rows), own_sem)
-    own.start()
-    first.wait_recv()
-    at = part(beside, 0, half)
-    third = to_side(at, at, send_sem.at[2], recv_sem.at[2], across)
-    third.start()
-    second.wait_recv()
-    at = part(across, half, half)
-    fourth = to_side(at, at, send_sem.at[3], recv_sem.at[3], beside)
-    fourth.start()
-    own.wait()
-    for copy in (first, second):
-        copy.wait_send()
-    for copy in (third, fourth):
-        copy.wait()
+    gather = SideGather(block, whole, send_sem, recv_sem, own_sem)
+    gather.start()
+    gather.relay()
+    gather.finish()
 
 
 def gathered(array, collective_id):
@@ -183,46 +140,63 @@
     )(array)
 
 
+class SideReduce:
+    def __init__(self, blocks, total, beside_got, across_got, passed, passed_got, send_sem, recv_sem):
+        self.refs = blocks, total, beside_got, across_got, passed, passed_got
+        me, beside, across, opposite = corners()
+        self.me, self.beside, self.across = me, beside, across
+        self.copies = []
+        for index, (turn, target, got) in enumerate(((0, beside, beside_got), (1, across, across_got))):
+            for slot, owner in ((1, opposite), (0, target)):
+                self.copies.append(
+                    to_side(
+                        blocks.at[self.part(owner, turn)],
+                        got.at[slot],
+                        send_sem.at[2 * index + slot],
+                        recv_sem.at[2 * index + slot],
+                        target,
+                    )
+                )
+        self.onward = [
+            to_side(passed.at[turn], passed_got.at[turn], send_sem.at[4 + turn], recv_sem.at[4 + turn], owner)
+            for turn, owner in ((0, across), (1, beside))
+        ]
+
+    def part(self, owner, turn):
+        half = self.refs[1].shape[0] // 2
+        return pl.ds(pl.multiple_of(owner * 2 * half + turn * half, half), half)
+
+    def start(self):
+        for index in (0, 2, 1, 3):
+            self.copies[index].start()
+
+    def relay(self):
+        blocks, _, beside_got, across_got, passed, _ = self.refs
+        for turn, owner, index, got in ((0, self.across, 0, beside_got), (1, self.beside, 2, across_got)):
+            self.copies[index].wait_recv()
+            passed[turn] = (blocks[self.part(owner, turn)].astype(F32) + got[1].astype(F32)).astype(BF16)
+            self.onward[turn].start()
+
+    def finish(self):
+        blocks, total, beside_got, across_got, _, passed_got = self.refs
+        half = total.shape[0] // 2
+        for turn, index, got in ((0, 1, beside_got), (1, 3, across_got)):
+            self.copies[index].wait_recv()
+            total[pl.ds(turn * half, half)] = blocks[self.part(self.me, turn)].astype(F32) + got[0].astype(F32)
+        for turn in range(2):
+            self.onward[turn].wait_recv()
+            at = pl.ds(turn * half, half)
+            total[at] = total[at] + passed_got[turn].astype(F32)
+        for copy in self.copies + self.onward:
+            copy.wait_send()
+
+
 def reduce_kernel(blocks, total, beside_got, across_got, passed, passed_got, send_sem, recv_sem):
-    me, beside, across, opposite = corners()
-    rows = total.shape[0]
-    half = rows // 2
-
-    def part(owner, turn):
-        return pl.ds(pl.multiple_of(owner * rows + turn * half, half), half)
-
     greet_sides()
-    copies = []
-    for index, (turn, target, got) in enumerate(((0, beside, beside_got), (1, across, across_got))):
-        for slot, owner in ((1, opposite), (0, target)):
-            copies.append(
-                to_side(
-                    blocks.at[part(owner, turn)],
-                    got.at[slot],
-                    send_sem.at[2 * index + slot],
-                    recv_sem.at[2 * index + slot],
-                    target,
-                )
-            )
-    for copy in (copies[0], copies[2], copies[1], copies[3]):
-        copy.start()
-    onward = []
-    for turn, owner, copy, got in ((0, across, copies[0], beside_got), (1, beside, copies[2], across_got)):
-        copy.wait_recv()
-        passed[turn] = (blocks[part(owner, turn)].astype(F32) + got[1].astype(F32)).astype(BF16)
-        onward.append(
-            to_side(passed.at[turn], passed_got.at[turn], send_sem.at[4 + turn], recv_sem.at[4 + turn], owner)
-        )
-        onward[-1].start()
-    for turn, copy, got in ((0, copies[1], beside_got), (1, copies[3], across_got)):
-        copy.wait_recv()
-        total[pl.ds(turn * half, half)] = blocks[part(me, turn)].astype(F32) + got[0].astype(F32)
-    for turn in range(2):
-        onward[turn].wait_recv()
-        at = pl.ds(turn * half, half)
-        total[at] = total[at] + passed_got[turn].astype(F32)
-    for copy in copies + onward:
-        copy.wait_send()
+    reduction = SideReduce(blocks, total, beside_got, across_got, passed, passed_got, send_sem, recv_sem)
+    reduction.start()
+    reduction.relay()
+    reduction.finish()
 
 
 def reduced(partial, collective_id):
@@ -940,193 +914,517 @@
     )(first, second)
 
 
-def column_weights_kernel(count, holder, n_ctx, *refs):
-    if n_ctx > 1:
-        kv_in, refs = refs[0], refs[1:]
-    gate_in, up_in, down_in, gate_out, up_out, down_out = refs[:6]
-    refs = refs[6:]
-    if n_ctx > 1:
-        kv_out, refs = refs[0], refs[1:]
-    send_sem, recv_sem, pair_send, pair_recv, own_sem = refs[:5]
-    section = lax.axis_index("section")
-    me = lax.axis_index("fsdp")
-    place = lax.axis_index("ctx")
-    other = 1 - section
-    rows = gate_in.shape[0]
-    wide = gate_out.shape[1]
-    barrier = pltpu.get_barrier_semaphore()
-    for step in range(1, count):
-        pl.semaphore_signal(
-            barrier, inc=1, device_id={"fsdp": lax.rem(me + step, count)}, device_id_type=MESH
+class Columns:
+    def __init__(self, holder, sources, targets, send_sem, recv_sem, pair_send, pair_recv, own_sem):
+        self.count = 4
+        self.holder = holder
+        self.section = lax.axis_index("section")
+        self.me = lax.axis_index("fsdp")
+        self.sources, self.targets = sources, targets
+        self.sems = send_sem, recv_sem, pair_send, pair_recv, own_sem
+        self.rows = sources[0].shape[0]
+        self.wide = targets[0].shape[1]
+        self.steps = [(step, kind) for step in range(1, self.count) for kind in range(2)]
+
+    def at_rows(self, out, owner):
+        return out.at[pl.ds(pl.multiple_of(owner * self.rows, self.rows), self.rows)]
+
+    def at_columns(self, source, owner):
+        return source.at[:, pl.ds(pl.multiple_of(owner * self.wide, 128), self.wide)]
+
+    def crossing(self, step, kind):
+        target = lax.rem(self.me + step, self.count)
+        return to_side(
+            self.at_columns(self.sources[kind], target),
+            self.at_rows(self.targets[kind], self.me),
+            self.sems[0].at[kind, step],
+            self.sems[1].at[kind, step],
+            target,
         )
-    pl.semaphore_signal(barrier, inc=1, device_id={"section": other}, device_id_type=MESH)
-    for step in range(1, n_ctx):
-        pl.semaphore_signal(
-            barrier, inc=1, device_id={"ctx": lax.rem(place + step, n_ctx)}, device_id_type=MESH
-        )
-    pl.semaphore_wait(barrier, count + n_ctx - 1)
-    kv_copies = []
-    if n_ctx > 1:
-        kv_send, kv_recv, kv_own = refs[5:]
-        kv_rows = kv_in.shape[0]
-        spot = kv_out.at[pl.ds(pl.multiple_of(place * kv_rows, kv_rows), kv_rows)]
-        for step in range(1, n_ctx):
-            kv_copies.append(
-                pltpu.make_async_remote_copy(
-                    src_ref=kv_in,
-                    dst_ref=spot,
-                    send_sem=kv_send.at[step],
-                    recv_sem=kv_recv.at[step],
-                    device_id={"ctx": lax.rem(place + step, n_ctx)},
-                    device_id_type=MESH,
-                )
-            )
-            kv_copies[-1].start()
-        kv_keep = pltpu.make_async_copy(kv_in, spot, kv_own)
-        kv_keep.start()
-    arrays = ((gate_in, gate_out), (up_in, up_out))
-
-    def at_rows(out, owner):
-        return out.at[pl.ds(pl.multiple_of(owner * rows, rows), rows)]
-
-    def crossing(kind, step):
-        source, out = arrays[kind]
-        target = lax.rem(me + step, count)
+
+    def handed(self, step, kind):
+        if kind == 2:
+            src, dst = self.sources[2], self.targets[2]
+        else:
+            origin = lax.rem(self.me + self.count - step, self.count)
+            dst = self.at_rows(self.targets[kind], origin)
+            src = self.at_columns(self.sources[kind], self.me) if step == 0 else dst
         return pltpu.make_async_remote_copy(
-            src_ref=source.at[:, pl.ds(pl.multiple_of(target * wide, 128), wide)],
-            dst_ref=at_rows(out, me),
-            send_sem=send_sem.at[kind, step],
-            recv_sem=recv_sem.at[kind, step],
-            device_id={"fsdp": target},
+            src_ref=src,
+            dst_ref=dst,
+            send_sem=self.sems[2].at[kind, step],
+            recv_sem=self.sems[3].at[kind, step],
+            device_id={"section": 1 - self.section},
             device_id_type=MESH,
         )
 
-    def handed(kind, step):
-        source, out = arrays[kind]
-        origin = lax.rem(me + count - step, count)
-        if step == 0:
-            src = source.at[:, pl.ds(pl.multiple_of(me * wide, 128), wide)]
-        else:
-            src = at_rows(out, origin)
-        return pltpu.make_async_remote_copy(
-            src_ref=src,
-            dst_ref=at_rows(out, origin),
-            send_sem=pair_send.at[kind, step],
-            recv_sem=pair_recv.at[kind, step],
-            device_id={"section": other},
-            device_id_type=MESH,
+    def kept(self, kind):
+        if kind == 2:
+            return pltpu.make_async_copy(self.sources[2], self.targets[2], self.sems[4].at[2])
+        return pltpu.make_async_copy(
+            self.at_columns(self.sources[kind], self.me),
+            self.at_rows(self.targets[kind], self.me),
+            self.sems[4].at[kind],
         )
 
-    down_copy = pltpu.make_async_remote_copy(
-        src_ref=down_in,
-        dst_ref=down_out,
-        send_sem=pair_send.at[2, 0],
-        recv_sem=pair_recv.at[2, 0],
-        device_id={"section": other},
-        device_id_type=MESH,
-    )
-    kinds = range(2)
-
-    @pl.when(section == holder)
-    def _():
-        for step in range(1, count):
-            for kind in kinds:
-                crossing(kind, step).start()
-        for kind in kinds:
-            handed(kind, 0).start()
-        down_copy.start()
-        keep = [
-            pltpu.make_async_copy(
-                arrays[kind][0].at[:, pl.ds(pl.multiple_of(me * wide, 128), wide)],
-                at_rows(arrays[kind][1], me),
-                own_sem.at[kind],
-            )
-            for kind in kinds
-        ] + [pltpu.make_async_copy(down_in, down_out, own_sem.at[2])]
-        for copy in keep:
-            copy.start()
-        for step in range(1, count):
-            for kind in kinds:
-                crossing(kind, step).wait_recv()
-                handed(kind, step).start()
-        for copy in keep:
-            copy.wait()
-        for step in range(1, count):
-            for kind in kinds:
-                crossing(kind, step).wait_send()
-        for step in range(count):
-            for kind in kinds:
-                handed(kind, step).wait_send()
-        down_copy.wait_send()
-
-    @pl.when(section != holder)
-    def _():
-        for step in range(count):
-            for kind in kinds:
-                handed(kind, step).wait_recv()
-        down_copy.wait_recv()
-
-    if n_ctx > 1:
-        kv_keep.wait()
-        for copy in kv_copies:
-            copy.wait()
-
-
-def column_weights(gate, up, down, holder, collective_id, kv=None):
+    def start(self):
+        @pl.when(self.section == self.holder)
+        def _():
+            for step, kind in self.steps:
+                self.crossing(step, kind).start()
+            for kind in range(3):
+                self.handed(0, kind).start()
+            for kind in range(3):
+                self.kept(kind).start()
+
+    def relay(self):
+        @pl.when(self.section == self.holder)
+        def _():
+            for step, kind in self.steps:
+                self.crossing(step, kind).wait_recv()
+                self.handed(step, kind).start()
+
+    def finish(self):
+        every = [(0, kind) for kind in range(3)] + self.steps
+
+        @pl.when(self.section == self.holder)
+        def _():
+            for kind in range(3):
+                self.kept(kind).wait()
+            for step, kind in self.steps:
+                self.crossing(step, kind).wait_send()
+            for step, kind in every:
+                self.handed(step, kind).wait_send()
+
+        @pl.when(self.section != self.holder)
+        def _():
+            for step, kind in every:
+                self.handed(step, kind).wait_recv()
+
+
+def column_weights_kernel(holder, *refs):
+    section = lax.axis_index("section")
+    _, beside, across, opposite = corners()
+    barrier = pltpu.get_barrier_semaphore()
+    for target in ({"fsdp": beside}, {"fsdp": across}, {"fsdp": opposite}, {"section": 1 - section}):
+        pl.semaphore_signal(barrier, inc=1, device_id=target, device_id_type=MESH)
+    pl.semaphore_wait(barrier, 4)
+    columns = Columns(holder, refs[:3], refs[3:6], *refs[6:])
+    columns.start()
+    columns.relay()
+    columns.finish()
+
+
+def column_weights(gate, up, down, holder, collective_id):
     count = lax.axis_size("fsdp")
-    n_ctx = 1 if kv is None else lax.axis_size("ctx")
+    assert count == 4
     dma = pltpu.SemaphoreType.DMA
     column = jax.ShapeDtypeStruct((count * gate.shape[0], gate.shape[1] // count), gate.dtype)
-    outs = [column, column, jax.ShapeDtypeStruct(down.shape, down.dtype)]
-    ins = [gate, up, down]
-    sems = [dma((2, count)), dma((2, count)), dma((3, count)), dma((3, count)), dma((3,))]
-    if kv is not None:
-        ins = [kv] + ins
-        outs.append(jax.ShapeDtypeStruct((n_ctx * kv.shape[0], kv.shape[1]), kv.dtype))
-        sems += [dma((n_ctx,)), dma((n_ctx,)), dma]
     return pl.pallas_call(
-        functools.partial(column_weights_kernel, count, holder, n_ctx),
-        out_shape=tuple(outs),
-        in_specs=[pl.BlockSpec(memory_space=pl.ANY)] * len(ins),
-        out_specs=[pl.BlockSpec(memory_space=pl.ANY)] * len(outs),
-        scratch_shapes=sems,
+        functools.partial(column_weights_kernel, holder),
+        out_shape=(column, column, jax.ShapeDtypeStruct(down.shape, down.dtype)),
+        in_specs=[pl.BlockSpec(memory_space=pl.ANY)] * 3,
+        out_specs=[pl.BlockSpec(memory_space=pl.ANY)] * 3,
+        scratch_shapes=[dma((2, count)), dma((2, count)), dma((3, count)), dma((3, count)), dma((3,))],
         compiler_params=pltpu.CompilerParams(
             collective_id=collective_id, has_side_effects=True, vmem_limit_bytes=8 << 20
         ),
         cost_estimate=busy(40),
-    )(*ins)
-
-
-def attend(query, key_all, value_all, allowed):
-    kv_heads = key_all.shape[1]
-    rows, q_heads, head = query.shape
-    grouped = query.reshape(rows, kv_heads, q_heads // kv_heads, head)
-    scores = jnp.einsum("qghd,kgd->ghqk", grouped, key_all, preferred_element_type=F32) * head ** (-0.5)
-    scores = jnp.where(allowed, scores, NEGATIVE)
-    peak = jnp.max(scores, axis=-1, keepdims=True)
-    weights = jnp.where(allowed, jnp.exp(scores - peak), 0.0)
-    total = jnp.sum(weights, axis=-1, keepdims=True)
-    log_total = peak + jnp.log(total)
-    prob = (weights / total).astype(BF16)
-    out = jnp.einsum("ghqk,kgd->qghd", prob, value_all, preferred_element_type=F32)
-    return out.reshape(rows, q_heads * head), log_total
-
-
-def attend_back(query, key_all, value_all, allowed, log_total, attended, d_out):
-    kv_heads = key_all.shape[1]
-    rows, q_heads, head = query.shape
-    scale = head ** (-0.5)
-    grouped = query.reshape(rows, kv_heads, q_heads // kv_heads, head)
-    d_group = d_out.reshape(rows, kv_heads, q_heads // kv_heads, head)
-    delta = jnp.sum(d_group.astype(F32) * attended.reshape(d_group.shape), axis=-1)
-    scores = jnp.einsum("qghd,kgd->ghqk", grouped, key_all, preferred_element_type=F32) * scale
-    prob = jnp.where(allowed, jnp.exp(scores - log_total), 0.0)
-    d_prob = jnp.einsum("qghd,kgd->ghqk", d_group, value_all, preferred_element_type=F32)
-    d_scores = (prob * (d_prob - delta.transpose(1, 2, 0)[..., None])).astype(BF16)
-    d_query = jnp.einsum("ghqk,kgd->qghd", d_scores, key_all, preferred_element_type=F32) * scale
-    d_key = jnp.einsum("ghqk,qghd->kgd", d_scores, grouped, preferred_element_type=F32) * scale
-    d_value = jnp.einsum("ghqk,qghd->kgd", prob.astype(BF16), d_group, preferred_element_type=F32)
-    return d_query.reshape(rows, q_heads, head), d_key, d_value
+    )(gate, up, down)
+
+
+class Chain:
+    def __init__(self, count):
+        self.count = count
+        self.place = lax.axis_index("ctx")
+        self.has_next = self.place < count - 1
+        self.has_last = self.place > 0
+
+
+def greet_mixed(chain, targets):
+    barrier = pltpu.get_barrier_semaphore()
+    for target in targets:
+        pl.semaphore_signal(barrier, inc=1, device_id=target, device_id_type=MESH)
+
+    @pl.when(chain.has_last)
+    def _():
+        pl.semaphore_signal(barrier, inc=1, device_id={"ctx": chain.place - 1}, device_id_type=MESH)
+
+    @pl.when(chain.has_next)
+    def _():
+        pl.semaphore_signal(barrier, inc=1, device_id={"ctx": chain.place + 1}, device_id_type=MESH)
+
+    inner = chain.has_last & chain.has_next
+
+    @pl.when(inner)
+    def _():
+        pl.semaphore_wait(barrier, len(targets) + 2)
+
+    @pl.when(jnp.logical_not(inner))
+    def _():
+        pl.semaphore_wait(barrier, len(targets) + 1)
+
+
+def along(src, dst, send_sem, recv_sem, place):
+    return pltpu.make_async_remote_copy(
+        src_ref=src,
+        dst_ref=dst,
+        send_sem=send_sem,
+        recv_sem=recv_sem,
+        device_id={"ctx": place},
+        device_id_type=MESH,
+    )
+
+
+def spread_heads(source, spread):
+    rows = source.shape[0]
+    low = lax.broadcasted_iota(jnp.int32, (rows, 128), 1) < 64
+    for pair in range(source.shape[1] // 256):
+        first = source[:, pair * 256 : pair * 256 + 128].astype(F32)
+        second = source[:, pair * 256 + 128 : pair * 256 + 256].astype(F32)
+        spread[4 * pair] = jnp.where(low, first, 0.0).astype(BF16)
+        spread[4 * pair + 1] = jnp.where(low, pltpu.roll(first, 64, 1), 0.0).astype(BF16)
+        spread[4 * pair + 2] = jnp.where(low, 0.0, pltpu.roll(second, 64, 1)).astype(BF16)
+        spread[4 * pair + 3] = jnp.where(low, 0.0, second).astype(BF16)
+
+
+def join_heads(spread, target):
+    rows = target.shape[0]
+    low = lax.broadcasted_iota(jnp.int32, (rows, 128), 1) < 64
+    for pair in range(target.shape[1] // 256):
+        parts = [spread(4 * pair + i).T for i in range(4)]
+        target[:, pair * 256 : pair * 256 + 128] = jnp.where(low, parts[0], pltpu.roll(parts[1], 64, 1))
+        target[:, pair * 256 + 128 : pair * 256 + 256] = jnp.where(low, pltpu.roll(parts[2], 64, 1), parts[3])
+
+
+def mask_block(bias, length, place, block):
+    rows = bias.shape[0]
+    key_at = block * rows + lax.broadcasted_iota(jnp.int32, bias.shape, 0)
+    query_at = place * rows + lax.broadcasted_iota(jnp.int32, bias.shape, 1)
+    bias[...] = jnp.where((key_at <= query_at) & (key_at < length), 0.0, NEGATIVE)
+
+
+def dot_right(left, right):
+    return lax.dot_general(left, right, (((1,), (1,)), ((), ())), preferred_element_type=F32)
+
+
+def dot_plain(left, right):
+    return jnp.dot(left, right, preferred_element_type=F32)
+
+
+def attend_kernel(
+    n_ctx,
+    length_ref,
+    query,
+    kv,
+    d_block,
+    gate_in,
+    up_in,
+    down_in,
+    attended,
+    log_total,
+    kv_all,
+    d_all,
+    gate_out,
+    up_out,
+    down_out,
+    spread,
+    bias,
+    peak,
+    total,
+    out_t,
+    kv_send,
+    kv_recv,
+    d_send,
+    d_recv,
+    d_own,
+    send_sem,
+    recv_sem,
+    pair_send,
+    pair_recv,
+    own_sem,
+):
+    chain = Chain(n_ctx)
+    place = chain.place
+    section = lax.axis_index("section")
+    me, beside, across, opposite = corners()
+    greet_mixed(
+        chain,
+        [{"fsdp": beside}, {"fsdp": across}, {"fsdp": opposite}, {"section": 1 - section}],
+    )
+    rows = query.shape[0]
+    half_width = kv.shape[1] // 2
+
+    def block_rows(block):
+        return pl.ds(pl.multiple_of(block * rows, rows), rows)
+
+    def upward(step, src):
+        return along(
+            src,
+            kv_all.at[block_rows(place - step)],
+            kv_send.at[step],
+            kv_recv.at[step + 1],
+            place + 1,
+        )
+
+    def arriving(step):
+        at = kv_all.at[block_rows(place - step)]
+        return along(at, at, kv_send.at[step], kv_recv.at[step], place)
+
+    @pl.when(chain.has_next)
+    def _():
+        upward(0, kv).start()
+
+    gather = SideGather(d_block, d_all, d_send, d_recv, d_own)
+    gather.start()
+    columns = Columns(
+        1, (gate_in, up_in, down_in), (gate_out, up_out, down_out), send_sem, recv_sem, pair_send, pair_recv, own_sem
+    )
+    columns.start()
+    kv_all[block_rows(place)] = kv[...]
+    spread_heads(query, spread)
+    peak[...] = jnp.full(peak.shape, NEGATIVE, F32)
+    total[...] = jnp.zeros(total.shape, F32)
+    out_t[...] = jnp.zeros(out_t.shape, F32)
+    length = length_ref[0]
+    scale = 64 ** (-0.5)
+
+    def attend_block(block):
+        mask_block(bias, length, place, block)
+        for pair in range(half_width // 128):
+            key = kv_all[block_rows(block), pair * 128 : pair * 128 + 128]
+            value_t = kv_all[block_rows(block), half_width + pair * 128 : half_width + pair * 128 + 128].T
+            for index in range(4):
+                head = 4 * pair + index
+                scores = dot_right(key, spread[head]) * scale + bias[...]
+                before = peak[head]
+                now = jnp.maximum(before, jnp.max(scores, axis=0, keepdims=True))
+                weights = jnp.exp(scores - now)
+                fade = jnp.exp(before - now)
+                peak[head] = now
+                total[head] = total[head] * fade + jnp.sum(weights, axis=0, keepdims=True)
+                out_t[head] = out_t[head] * fade + dot_plain(value_t, weights.astype(BF16))
+
+    attend_block(place)
+    gather.relay()
+
+    def step_on(step, carry):
+        @pl.when(step <= place)
+        def _():
+            arriving(step).wait_recv()
+
+            @pl.when(chain.has_next)
+            def _():
+                upward(step, kv_all.at[block_rows(place - step)]).start()
+
+            attend_block(place - step)
+
+        return carry
+
+    lax.fori_loop(1, n_ctx, step_on, 0)
+    join_heads(lambda head: out_t[head] / total[head], attended)
+    for head in range(spread.shape[0]):
+        log_total[head] = peak[head] + jnp.log(total[head])
+    columns.relay()
+    gather.finish()
+    columns.finish()
+
+    def settle(step, carry):
+        @pl.when((step <= place) & chain.has_next)
+        def _():
+            upward(step, kv_all.at[block_rows(place - step)]).wait_send()
+
+        return carry
+
+    lax.fori_loop(0, n_ctx, settle, 0)
+
+
+def attend(length, query, kv, d_block, gate, up, down, collective_id):
+    n_ctx, count = lax.axis_size("ctx"), lax.axis_size("fsdp")
+    rows, width = query.shape
+    heads = width // 64
+    dma = pltpu.SemaphoreType.DMA
+    vmem = pl.BlockSpec(memory_space=pltpu.VMEM)
+    hbm = pl.BlockSpec(memory_space=pl.ANY)
+    column = jax.ShapeDtypeStruct((count * gate.shape[0], gate.shape[1] // count), gate.dtype)
+    return pl.pallas_call(
+        functools.partial(attend_kernel, n_ctx),
+        out_shape=(
+            jax.ShapeDtypeStruct((rows, width), F32),
+            jax.ShapeDtypeStruct((heads, 1, rows), F32),
+            jax.ShapeDtypeStruct((n_ctx * rows, kv.shape[1]), BF16),
+            jax.ShapeDtypeStruct((count * rows, d_block.shape[1]), BF16),
+            column,
+            column,
+            jax.ShapeDtypeStruct(down.shape, down.dtype),
+        ),
+        in_specs=[pl.BlockSpec(memory_space=pltpu.SMEM), vmem, vmem, vmem, hbm, hbm, hbm],
+        out_specs=[vmem, vmem, vmem, vmem, hbm, hbm, hbm],
+        scratch_shapes=[
+            pltpu.VMEM((heads, rows, 128), BF16),
+            pltpu.VMEM((rows, rows), F32),
+            pltpu.VMEM((heads, 1, rows), F32),
+            pltpu.VMEM((heads, 1, rows), F32),
+            pltpu.VMEM((heads, 128, rows), F32),
+            dma((n_ctx + 1,)),
+            dma((n_ctx + 1,)),
+            dma((4,)),
+            dma((4,)),
+            dma,
+            dma((2, count)),
+            dma((2, count)),
+            dma((3, count)),
+            dma((3, count)),
+            dma((3,)),
+        ],
+        compiler_params=pltpu.CompilerParams(
+            collective_id=collective_id, has_side_effects=True, vmem_limit_bytes=40 << 20
+        ),
+        cost_estimate=busy(50),
+    )(length, query, kv, d_block, gate, up, down)
+
+
+def attend_back_kernel(
+    n_ctx,
+    length_ref,
+    query,
+    kv_all,
+    d_out,
+    log_total,
+    delta,
+    blocks,
+    d_query,
+    d_kv,
+    reduced_out,
+    spread,
+    d_spread,
+    bias,
+    d_query_t,
+    term,
+    leaving,
+    coming,
+    kv_send,
+    kv_recv,
+    beside_got,
+    across_got,
+    passed,
+    passed_got,
+    send_sem,
+    recv_sem,
+):
+    chain = Chain(n_ctx)
+    place = chain.place
+    _, beside, across, _ = corners()
+    greet_mixed(chain, [{"fsdp": beside}, {"fsdp": across}])
+    rows = query.shape[0]
+    half_width = kv_all.shape[1] // 2
+    reduction = SideReduce(blocks, reduced_out, beside_got, across_got, passed, passed_got, send_sem, recv_sem)
+    reduction.start()
+    spread_heads(query, spread)
+    spread_heads(d_out, d_spread)
+    d_query_t[...] = jnp.zeros(d_query_t.shape, F32)
+    length = length_ref[0]
+    scale = 64 ** (-0.5)
+
+    def downward(block):
+        return along(leaving.at[block], coming.at[block], kv_send.at[block], kv_recv.at[block], place - 1)
+
+    def step_on(block, carry):
+        @pl.when(block <= place)
+        def _():
+            mask_block(bias, length, place, block)
+            at = pl.ds(pl.multiple_of(block * rows, rows), rows)
+            for pair in range(half_width // 128):
+                lanes = slice(pair * 128, pair * 128 + 128)
+                more = slice(half_width + pair * 128, half_width + pair * 128 + 128)
+                key = kv_all[at, lanes]
+                value = kv_all[at, more]
+                key_t = key.T
+                d_key = jnp.zeros((rows, 128), F32)
+                d_value = jnp.zeros((rows, 128), F32)
+                for index in range(4):
+                    head = 4 * pair + index
+                    scores = dot_right(key, spread[head]) * scale + bias[...]
+                    prob = jnp.exp(scores - log_total[head])
+                    d_prob = dot_right(value, d_spread[head])
+                    d_scores = (prob * (d_prob - delta[head])).astype(BF16)
+                    d_value = d_value + dot_plain(prob.astype(BF16), d_spread[head])
+                    d_key = d_key + dot_plain(d_scores, spread[head])
+                    d_query_t[head] = d_query_t[head] + dot_plain(key_t, d_scores)
+                term[:, lanes] = d_key * scale
+                term[:, more] = d_value
+
+            @pl.when(chain.has_next)
+            def _():
+                along(
+                    leaving.at[block], coming.at[block], kv_send.at[block], kv_recv.at[block], place
+                ).wait_recv()
+                term[...] = term[...] + coming[block].astype(F32)
+
+            @pl.when(block < place)
+            def _():
+                leaving[block] = term[...].astype(BF16)
+                downward(block).start()
+
+            @pl.when(block == place)
+            def _():
+                d_kv[...] = term[...]
+
+        @pl.when(block == 0)
+        def _():
+            reduction.relay()
+
+        return carry
+
+    lax.fori_loop(0, n_ctx, step_on, 0)
+    join_heads(lambda head: d_query_t[head] * scale, d_query)
+    reduction.finish()
+
+    def settle(block, carry):
+        @pl.when(block < place)
+        def _():
+            downward(block).wait_send()
+
+        return carry
+
+    lax.fori_loop(0, n_ctx, settle, 0)
+
+
+def attend_back(length, query, kv_all, d_out, log_total, delta, blocks, collective_id):
+    n_ctx = lax.axis_size("ctx")
+    rows, width = query.shape
+    heads = width // 64
+    dma = pltpu.SemaphoreType.DMA
+    vmem = pl.BlockSpec(memory_space=pltpu.VMEM)
+    wide = jax.ShapeDtypeStruct((rows, width), F32)
+    pair = pltpu.VMEM((2, rows // 2, blocks.shape[1]), BF16)
+    return pl.pallas_call(
+        functools.partial(attend_back_kernel, n_ctx),
+        out_shape=(wide, jax.ShapeDtypeStruct((rows, kv_all.shape[1]), F32), wide),
+        in_specs=[pl.BlockSpec(memory_space=pltpu.SMEM)] + [vmem] * 6,
+        out_specs=[vmem] * 3,
+        scratch_shapes=[
+            pltpu.VMEM((heads, rows, 128), BF16),
+            pltpu.VMEM((heads, rows, 128), BF16),
+            pltpu.VMEM((rows, rows), F32),
+            pltpu.VMEM((heads, 128, rows), F32),
+            pltpu.VMEM((rows, kv_all.shape[1]), F32),
+            pltpu.VMEM((n_ctx, rows, kv_all.shape[1]), BF16),
+            pltpu.VMEM((n_ctx, rows, kv_all.shape[1]), BF16),
+            dma((n_ctx,)),
+            dma((n_ctx,)),
+            pair,
+            pair,
+            pair,
+            pair,
+            dma((6,)),
+            dma((6,)),
+        ],
+        compiler_params=pltpu.CompilerParams(
+            collective_id=collective_id, has_side_effects=True, vmem_limit_bytes=56 << 20
+        ),
+        cost_estimate=busy(50),
+    )(length, query, kv_all, d_out, log_total, delta, blocks)
 
 
 def ffn_forward(residual, gain, w_gate, w_up, w_down):
@@ -1135,15 +1433,11 @@
     gate_pre = matmul(act, w_gate)
     up_pre = matmul(act, w_up)
     hidden = (jax.nn.silu(gate_pre) * up_pre).astype(BF16)
-    out = reduced(matmul(hidden, w_down), 1)
-    return out, (normed, inv_rms, act, gate_pre, up_pre, hidden)
-
-
-def ffn_backward(d_low, kept, gain, w_gate, w_up, w_down, settled=None):
+    return matmul(hidden, w_down).astype(BF16), (normed, inv_rms, act, gate_pre, up_pre, hidden)
+
+
+def ffn_backward(d_all, kept, gain, w_gate, w_up, w_down):
     normed, inv_rms, act, gate_pre, up_pre, hidden = kept
-    d_all = gathered(d_low, 0)
-    if settled is not None:
-        d_all, settled = lax.optimization_barrier((d_all, settled))
     d_hidden = matmul_right(d_all, w_down)
     sigmoid = jax.nn.sigmoid(gate_pre)
     d_up = (d_hidden * gate_pre * sigmoid).astype(BF16)
@@ -1153,7 +1447,7 @@
     grad_up = matmul_left(act, d_up).astype(BF16)
     grad_down = matmul_left(hidden, d_all).astype(BF16)
     grad_gain = jnp.sum(d_act * normed, axis=0)
-    return norm_back(d_act * gain, normed, inv_rms), grad_gain, (grad_gate, grad_up, grad_down), settled
+    return norm_back(d_act * gain, normed, inv_rms), grad_gain, (grad_gate, grad_up, grad_down)
 
 
 def shards(
@@ -1220,7 +1514,8 @@
     z_low = (c_gate * convolved).astype(BF16)
     mixed = matmul(z_low, out_full)
     res1 = x + mixed
-    ffn1, kept1 = ffn_forward(res1, norm_gains[1], gate1, up1, down1)
+    terms1, kept1 = ffn_forward(res1, norm_gains[1], gate1, up1, down1)
+    ffn1 = reduced(terms1, 1)
     h_low = (res1 + ffn1).astype(BF16)
 
     h = h_low.astype(F32)
@@ -1228,45 +1523,31 @@
     act2 = (normed2 * norm_gains[2]).astype(BF16)
     q_normed, q_inv = norm_rows(matmul(act2, query_full).reshape(rows, q_heads, head))
     k_normed, k_inv = norm_rows(matmul(act2, key_full).reshape(rows, kv_heads, head))
-    query = (q_normed * head_gains[0]).astype(BF16)
-    key = (k_normed * head_gains[1]).astype(BF16)
+    query = (q_normed * head_gains[0]).astype(BF16).reshape(rows, q_width)
+    key = (k_normed * head_gains[1]).astype(BF16).reshape(rows, kv_width)
     value = matmul(act2, value_full).astype(BF16)
-    gate2, up2, down2, kv_all = column_weights(
+    d_sum_low = (lax.dynamic_index_in_dim(cotangent, section, keepdims=False).astype(F32) * mask).astype(BF16)
+    attended, log_total, kv_all, d_sum_all, gate2, up2, down2 = attend(
+        length.reshape(1),
+        query,
+        jnp.concatenate([key, value], axis=1),
+        d_sum_low,
         ffn_gate[0],
         ffn_up[0],
         ffn_down[0],
-        1,
         3,
-        jnp.concatenate([key.reshape(rows, kv_width), value], axis=1),
-    )
-    key_all = kv_all[:, :kv_width].reshape(-1, kv_heads, head)
-    value_all = kv_all[:, kv_width:].reshape(-1, kv_heads, head)
-    key_pos = jnp.arange(kv_all.shape[0])
-    allowed = (key_pos[None, :] <= positions[:, None]) & (key_pos[None, :] < length)
-    attended, log_total = attend(query, key_all, value_all, allowed)
+    )
     attended_low = attended.astype(BF16)
     attn_rows = matmul(attended_low, proj_full)
     res2 = h + attn_rows
-    ffn2, kept2 = ffn_forward(res2, norm_gains[3], gate2, up2, down2)
-    result = (res2 + ffn2) * mask
-
-    def square(values):
-        return jnp.sum(mask * values * values)
-
-    squares = jnp.stack(
-        [square(v) for v in (x, mixed, ffn1, h, attn_rows, res2, ffn2, result)]
-    )
-
-    d_sum_low = (lax.dynamic_index_in_dim(cotangent, section, keepdims=False).astype(F32) * mask).astype(BF16)
+    terms2, kept2 = ffn_forward(res2, norm_gains[3], gate2, up2, down2)
+
     d_sum = d_sum_low.astype(F32)
-    d_ffn, gain3, grads2, _ = ffn_backward(d_sum_low, kept2, norm_gains[3], gate2, up2, down2)
+    d_ffn, gain3, grads2 = ffn_backward(d_sum_all, kept2, norm_gains[3], gate2, up2, down2)
     d_res2 = d_sum + d_ffn
     d_attn = d_res2.astype(BF16)
     grad_proj = matmul_left(attended_low, d_attn)
     d_att = matmul_right(d_attn, proj_full).astype(BF16)
-    d_query, d_key_all, d_value_all = attend_back(
-        query, key_all, value_all, allowed, log_total, attended, d_att
-    )
     half = part // 2
 
     def shared_halves(grad, lead):
@@ -1275,26 +1556,27 @@
         other = swapped(lax.dynamic_index_in_dim(pieces, 1 - section, 1, keepdims=False), "section")
         return (mine.astype(F32) + other.astype(F32)).astype(BF16)
 
-    d_kv_terms = jnp.concatenate(
-        [d_key_all.reshape(-1, kv_width), d_value_all.reshape(-1, kv_width)], axis=1
-    ).astype(BF16)
-    d_kv_terms, second = lax.optimization_barrier(
-        (
-            d_kv_terms,
-            (
-                shared_halves(jnp.concatenate(grads2[:2], axis=0), 2 * fsdp),
-                shared_halves(grads2[2], 1)[0],
-            ),
-        )
+    delta = jnp.sum((d_att.astype(F32) * attended).reshape(rows, q_heads, head), axis=-1)
+    d_query, d_kv, ffn2 = attend_back(
+        length.reshape(1), query, kv_all, d_att, log_total, delta.T.reshape(q_heads, 1, rows), terms2, 4
+    )
+    result = (res2 + ffn2) * mask
+
+    def square(values):
+        return jnp.sum(mask * values * values)
+
+    squares = jnp.stack(
+        [square(v) for v in (x, mixed, ffn1, h, attn_rows, res2, ffn2, result)]
+    )
+    second = (
+        shared_halves(jnp.concatenate(grads2[:2], axis=0), 2 * fsdp),
+        shared_halves(grads2[2], 1)[0],
     )
     second = tuple(
         lax.psum_scatter(term.reshape(-1, term.shape[-1]), "ctx", scatter_dimension=0, tiled=True)
         for term in second
     )
-    d_kv = jnp.sum(
-        swapped_blocks(d_kv_terms, "ctx", 4).reshape(lax.axis_size("ctx"), rows, -1).astype(F32), axis=0
-    )
-    d_qn = rounded(d_query)
+    d_qn = rounded(d_query).reshape(rows, q_heads, head)
     grad_qgain = jnp.sum(d_qn * q_normed, axis=(0, 1))
     d_qpre = norm_back(d_qn * head_gains[0], q_normed, q_inv).reshape(rows, -1).astype(BF16)
     d_kn = rounded(d_kv[:, :kv_width]).reshape(rows, kv_heads, head)
@@ -1309,9 +1591,8 @@
     gain2 = jnp.sum(d_act2 * normed2, axis=0)
     d_h_low = (d_res2 + norm_back(d_act2 * norm_gains[2], normed2, inv2)).astype(BF16)
 
-    d_ffn1, gain1, grads1, second = ffn_backward(
-        d_h_low, kept1, norm_gains[1], gate1, up1, down1, second
-    )
+    d_h_all, second = lax.optimization_barrier((gathered(d_h_low, 0), second))
+    d_ffn1, gain1, grads1 = ffn_backward(d_h_all, kept1, norm_gains[1], gate1, up1, down1)
     second = tuple(lax.all_gather(term, "ctx", axis=0, tiled=True) for term in second)
     d_res1 = d_h_low.astype(F32) + d_ffn1
     d_mixed = d_res1.astype(BF16)

time: 903 us -> 846 us (0.937)
  matrix products: 153 us -> 131 us
  Pallas kernels: 526 us -> 506 us
  waiting for transfers between devices: 45.5 us -> 31.4 us
    dot_general x6 -> x0, matrix products: 32.6 us -> none  [the longest x1 8.74 us: attend_back(): jnp.einsum('qghd,kgd->ghqk', d_group, value_all, preferred_element_type=F32)]
    pallas_call x3, Pallas kernels: 137 us -> 161 us  [the longest x1 76.8 us: attend_back(): pl.pallas_call(functools.partial(attend_back_kernel, n_ctx), out_shape=(w...]
    pallas_call x4 -> x3, Pallas kernels: 76.3 us -> 52.9 us  [reduced(): pl.pallas_call(reduce_kernel, out_shape=jax.ShapeDtypeStruct((rows, width...]
    pallas_call x4 -> x3, Pallas kernels: 90 us -> 70 us  [gathered(): pl.pallas_call(gather_kernel, out_shape=jax.ShapeDtypeStruct((4 * rows, w...]
    reduce_scatter x2, waiting for transfers between devices: 13.5 us -> 0.01 us  [shards(): lax.psum_scatter(term.reshape(-1, term.shape[-1]), 'ctx', scatter_dimensi...]
    unnamed x278 -> x230, local copies, waits for them, and re-layouts: 42.2 us -> 41.6 us
  transfers between devices with their start and end apart: 13 -> 13, of which waited for: 3 -> 2; matrix products, arithmetic and copies ran while one was open for 21% -> 21% of each run, Pallas kernels for 35% -> 35%
where the time goes in v5:
time: 846 us; the launch traced here: 839 us
  Pallas kernels  506 us (60%)
  matrix products  131 us (15%)
  local copies, waits for them, and re-layouts  86.4 us (10%)
  other arithmetic  61.2 us (7%)
  waiting for transfers between devices  31.4 us (4%)
  between operations  16.4 us (2%)
    pallas_call x1, Pallas kernels, summed_gradients(): pl.pallas_call(functools.partial(tail_kernel, (n_ctx, n_fsdp)), out_shape...  176 us
    pallas_call x1, Pallas kernels, attend_back(): pl.pallas_call(functools.partial(attend_back_kernel, n_ctx), out_shape=(w...  76.8 us
    pallas_call x3, Pallas kernels, gathered(): pl.pallas_call(gather_kernel, out_shape=jax.ShapeDtypeStruct((4 * rows, w...  70 us
    pallas_call x3, Pallas kernels, reduced(): pl.pallas_call(reduce_kernel, out_shape=jax.ShapeDtypeStruct((rows, width...  52.9 us
    dot_general x12, matrix products, matmul_right(): lax.dot_general(left_op, right_op, (((1,), (1,)), ((), ())), preferred_el...  47.4 us
    pallas_call x1, Pallas kernels, mixer_weights(): pl.pallas_call(functools.partial(mixer_weights_kernel, count), out_shape=...  45.7 us
    pallas_call x1, Pallas kernels, attend(): pl.pallas_call(functools.partial(attend_kernel, n_ctx), out_shape=(jax.Sh...  45.2 us
    dot_general x12, matrix products, matmul(): return jnp.dot(left_op, right_op, preferred_element_type=F32)  44.2 us
  transfers between devices with their start and end apart: 13, of which 2 were waited for; matrix products, arithmetic and copies ran while one was open for 21% of the time, Pallas kernels for 35%

profile of v5, /device:TPU:0, one launch (start us, length us, event | category | flops | bytes accessed | tf_op | source)
XLA Modules:
  0.0 838.5 jit_solution(7274994592987637580)
XLA Ops:
  12.6 45.7 %shard_map.262 = (bf16[1024,3072]{1,0:T(8,128)(2,1)S(1)}, bf16[1024,1024]{1,0:T(8,128)(2,1)S(1)}) custom-call(bf16[256,3072]{1,0:T(8,128)(2,1)S(1)} %copy-done.24, bf16[256,1024]{1,0:T(8,128)(2,1)S(1)} %copy-done.25), custom_call_target="tpu_custom_call" | custom-call | flops 45 | bytes 65536 | tf_op jit(solution)/shard_map/pallas_call | solution.py:902
  65.5 4.8 fusion.63
  80.1 38.8 %shard_map.264 = (bf16[1024,1152]{1,0:T(8,128)(2,1)S(1)}, bf16[1024,1152]{1,0:T(8,128)(2,1)S(1)}, bf16[1152,1024]{1,0:T(8,128)(2,1)S(1)}) custom-call(bf16[256,4608]{1,0:T(8,128)(2,1)S(1)} %bitcast.156, bf16[256,4608]{1,0:T(8,128)(2,1)S(1)} %bitcast.158, bf16[1152,1024]{1,0:T(8,128)(2,1)S(1)} %bitcast.160), custom_call_target="tpu_custom_call" | custom-call | flops 40 | bytes 65536 | tf_op jit(solution)/shard_map/pallas_call | solution.py:1023
  130.0 25.9 %shard_map.263 = bf16[1024,1024]{1,0:T(8,128)(2,1)S(1)} custom-call(bf16[256,1024]{1,0:T(8,128)(2,1)S(1)} %multiply_convert_fusion.9.block), custom_call_target="tpu_custom_call" | custom-call | flops 25 | bytes 65536 | tf_op jit(solution)/shard_map/pallas_call | solution.py:130
  158.9 4.5 multiply_convert_fusion.5
  170.6 17.4 %shard_map.265 = f32[256,1024]{1,0:T(8,128)S(1)} custom-call(bf16[1024,1024]{1,0:T(8,128)(2,1)S(1)} %copy-done.21), custom_call_target="tpu_custom_call" | custom-call | flops 25 | bytes 65536 | tf_op jit(solution)/shard_map/pallas_call | solution.py:207
  212.5 45.2 %shard_map.266 = (f32[256,1024]{1,0:T(8,128)S(1)}, f32[16,1,256]{2,1,0:T(1,128)S(1)}, bf16[1024,1024]{1,0:T(8,128)(2,1)S(1)}, bf16[1024,1024]{1,0:T(8,128)(2,1)S...) custom-call(s32[1]{0:T(128)} %dynamic_slice.38.length_ref, ...), custom_call_target="tpu_custom_call" | custom-call | flops 50 | bytes 65536 | tf_op jit(solution)/shard_map/pallas_call | solution.py:1250
  272.5 21.6 %shard_map.267 = bf16[1024,1024]{1,0:T(8,128)(2,1)S(1)} custom-call(bf16[256,1024]{1,0:T(8,128)(2,1)S(1)} %copy-done.23), custom_call_target="tpu_custom_call" | custom-call | flops 25 | bytes 65536 | tf_op jit(solution)/shard_map/pallas_call | solution.py:130
  294.0 4.7 fusion.80
  301.6 5.6 multiply_convert_fusion.2
  326.8 7.8 add_convert_fusion.1.blocks
  336.9 19.7 %shard_map.268 = f32[256,1024]{1,0:T(8,128)S(1)} custom-call(bf16[1024,1024]{1,0:T(8,128)(2,1)S(1)} %copy-done.19), custom_call_target="tpu_custom_call" | custom-call | flops 25 | bytes 65536 | tf_op jit(solution)/shard_map/pallas_call | solution.py:207
  370.4 6.6 convolution_convert_fusion.6.blocks
  377.0 76.8 %shard_map.269 = (f32[256,1024]{1,0:T(8,128)}, f32[256,1024]{1,0:T(8,128)}, f32[256,1024]{1,0:T(8,128)}) custom-call(s32[1]{0:T(128)} %dynamic_slice.38.length_ref, bf16[256,1024]{1,0:T(8,128)(2,1)} %copy-done.11, bf16[1024,1024]{1,0:T(8,128)(2,1)} %copy-done.22, bf16[256,1024]{1,0:T(8,128)(2,1)} %get-tuple-element.146.d_out, f32[16,1,256]{2,1,0:T(1,128)} %copy-done.26, ...), custom_call_target="tpu_custom_call" | custom-call | flops 50 | bytes 65536 | tf_op jit(solution)/shard_map/pallas_call | solution.py:1401
  481.5 22.5 %shard_map.270 = bf16[1024,1024]{1,0:T(8,128)(2,1)S(1)} custom-call(bf16[256,1024]{1,0:T(8,128)(2,1)S(1)} %copy-done.9), custom_call_target="tpu_custom_call" | custom-call | flops 25 | bytes 65536 | tf_op jit(solution)/shard_map/pallas_call | solution.py:130
  513.5 9.0 %multiply_convert_fusion = (bf16[1024,1152]{1,0:T(8,128)(2,1)S(1)}, bf16[1024,1152]{1,0:T(8,128)(2,1)S(1)}) fusion(f32[1024,1152]{1,0:T(8,128)} %copy-done.102, f32[1024,1152]{1,0:T(8,128)} %get-tuple-element.143, bf16[1024,1024]{1,0:T(8,128)(2,1)} %copy-done.16, bf16[1152,1024]{1,0:T(8,128)(2,1)} %copy-done.34), kind=kOutput, calls=%fused_computation.3 | convolution fusion | flops 2431254528 | bytes 18612224 | tf_op jit(solution)/shard_map/dot_general | solution.py:40
  531.7 15.8 %shard_map.271 = f32[256,1024]{1,0:T(8,128)S(1)} custom-call(bf16[1024,1024]{1,0:T(8,128)(2,1)S(1)} %copy-done.20), custom_call_target="tpu_custom_call" | custom-call | flops 25 | bytes 65536 | tf_op jit(solution)/shard_map/pallas_call | solution.py:207
  574.7 23.7 %all-gather.15.cloned.1.call-done = bf16[1024,1152]{1,0:T(8,128)(2,1)} async-done(((bf16[256,1152]{1,0:T(8,128)(2,1)}), bf16[1024,1152]{1,0:T(8,128)(2,1)}) %all-gather.15.cloned.1.call-update) | async-done | bytes 2359312 | tf_op jit(solution)/shard_map/all_gather | solution.py:1596
  601.8 7.9 fusion.31
  609.7 5.4 stack.84
  621.6 7.6 all-gather.17.cloned.1.call-done.second_down_in
  629.2 176.5 %shard_map.272 = (bf16[2,256,4608]{2,1,0:T(8,128)(2,1)}, bf16[1152,1024]{1,0:T(8,128)(2,1)}, bf16[2,960,1024]{2,1,0:T(8,128)(2,1)}) custom-call(bf16[1024,1152]{1,0:T(8,128)(2,1)} %convolution_convert_fusion.2.gate_in, bf16[1024,1152]{1,0:T(8,128)(2,1)} %convolution_convert_fusion.1.up_in, bf16[1152,1024]{1,0:T(8,128)(2,1)} %convolution_convert_fusion.down_in, ...), custom_call_target="tpu_custom_call" | custom-call | flops 160 | bytes 65536 | tf_op jit(solution)/shard_map/pallas_call | solution.py:762
  805.7 4.7 fusion.73
  812.7 5.0 slice_convert_fusion
  (403 shorter events, 219.1 us)
Async XLA Ops:
  7.2 55.0 %copy-start.101 = (s32[8]{0:T(128)S(1)}, s32[8]{0:T(128)}, u32[]{:S(2)}) copy-start(s32[8]{0:T(128)} %param.17) | copy-start | bytes 100
  7.2 182.0 %all-gather.9.cloned.1.call-start = ((), (), s32[]{:S(2)}) async-start(), calls=%async_computation.3 | async-start | bytes 1179648 | tf_op jit(solution)/shard_map/all_gather | solution.py:1485
  9.0 189.3 %all-gather.11.cloned.1.call-start = ((), (), s32[]{:S(2)}) async-start(), calls=%async_computation.4 | async-start | bytes 1179648 | tf_op jit(solution)/shard_map/all_gather | solution.py:1485
  10.6 54.8 %copy-start.97 = (f32[4,1024]{1,0:T(4,128)S(1)}, f32[4,1024]{1,0:T(4,128)}, u32[]{:S(2)}) copy-start(f32[4,1024]{1,0:T(4,128)} %param.18) | copy-start | bytes 49156
  10.7 190.2 %all-gather.7.cloned.1.call-start = ((), (), s32[]{:S(2)}) async-start(), calls=%async_computation.2 | async-start | bytes 2359296 | tf_op jit(solution)/shard_map/all_gather | solution.py:1485
  11.5 254.6 %all-gather.13.cloned.1.call-start = ((), (), s32[]{:S(2)}) async-start(), calls=%async_computation.5 | async-start | bytes 2359296 | tf_op jit(solution)/shard_map/all_gather | solution.py:1485
  12.6 50.9 %copy-start.61 = (bf16[2,256,1024]{2,1,0:T(8,128)(2,1)S(1)}, bf16[2,256,1024]{2,1,0:T(8,128)(2,1)}, u32[]{:S(2)}) copy-start(bf16[2,256,1024]{2,1,0:T(8,128)(2,1)} %param.15) | copy-start | bytes 3145732
  72.2 51.7 %collective-permute-start = (bf16[2,1024]{1,0:T(2,128)(2,1)S(1)}, bf16[2,1024]{1,0:T(2,128)(2,1)S(1)}, u32[]{:S(2)}, u32[]{:S(2)}) collective-permute-start(bf16[2,1024]{1,0:T(2,128)(2,1)S(1)} %slice.195), channel_id=1, source_target_pairs={{0,4},{4,8},{8,12},{1,5},{5,9},{9,13},{2,6},{6,10},{10,14},{3,7},{... | collective-permute-start | bytes 12296 | tf_op jit(solution)/shard_map/ppermute | solution.py:20
  76.6 436.9 %reduce-scatter.5.cloned.1.call-start = ((), (), s32[]{:S(2)}) async-start(), calls=%async_computation.7 | async-start | bytes 1474560 | tf_op jit(solution)/shard_map/reduce_scatter | solution.py:1576
  130.0 26.0 %copy-start.32 = (bf16[1024,1152]{1,0:T(8,128)(2,1)S(1)}, bf16[1024,1152]{1,0:T(8,128)(2,1)}, u32[]{:S(2)}) copy-start(bf16[1024,1152]{1,0:T(8,128)(2,1)} %copy-done.31) | copy-start | bytes 7077892
  272.5 21.6 %copy-start.37 = (bf16[1152,1024]{1,0:T(8,128)(2,1)S(1)}, bf16[1152,1024]{1,0:T(8,128)(2,1)}, u32[]{:S(2)}) copy-start(bf16[1152,1024]{1,0:T(8,128)(2,1)} %copy-done.36) | copy-start | bytes 7077892
  310.4 14.8 %collective-permute-start.2 = (bf16[1,576,1024]{2,1,0:T(8,128)(2,1)S(1)}, bf16[1,576,1024]{2,1,0:T(8,128)(2,1)S(1)}, u32[]{:S(2)}, u32[]{:S(2)}) collective-permute-start(bf16[1,576,1024]{2,1,0:T(8,128)(2,1)S(1)} %dynamic-slice_bitcast_fusion.1), channel_id=1, source_target_pairs={{0,16},{16,0},{1,17},{17,1},{2,18},{18,2},{3,19},{19,3},{4,20},{20... | collective-permute-start | bytes 3538952 | tf_op jit(solution)/shard_map/ppermute | solution.py:24
  320.3 45.4 %collective-permute-start.1 = (bf16[8,128,1152]{2,1,0:T(8,128)(2,1)}, bf16[8,128,1152]{2,1,0:T(8,128)(2,1)}, u32[]{:S(2)}, u32[]{:S(2)}) collective-permute-start(bf16[8,128,1152]{2,1,0:T(8,128)(2,1)} %dynamic-slice_bitcast_fusion), channel_id=1, source_target_pairs={{0,16},{16,0},{1,17},{17,1},{2,18},{18,2},{3,19},{19,3},{4,20},{20... | collective-permute-start | bytes 7077896 | tf_op jit(solution)/shard_map/ppermute | solution.py:24
  326.8 186.7 %reduce-scatter.3.cloned.1.call-start = ((), (), s32[]{:S(2)}) async-start(), calls=%async_computation.6 | async-start | bytes 2949120 | tf_op jit(solution)/shard_map/reduce_scatter | solution.py:1576
  336.9 19.7 %copy-start.52 = (f32[256,1024]{1,0:T(8,128)S(1)}, f32[256,1024]{1,0:T(8,128)}, u32[]{:S(2)}) copy-start(f32[256,1024]{1,0:T(8,128)} %copy-done.51) | copy-start | bytes 3145732
  336.9 20.8 %copy-start.8 = (bf16[256,1024]{1,0:T(8,128)(2,1)S(1)}, bf16[256,1024]{1,0:T(8,128)(2,1)}, u32[]{:S(2)}) copy-start(bf16[256,1024]{1,0:T(8,128)(2,1)} %get-tuple-element.150.d_block) | copy-start | bytes 1572868
  370.1 228.2 %all-gather.15.cloned.1.call-start = ((), (), s32[]{:S(2)}) async-start(), calls=%async_computation.8 | async-start | bytes 2949120 | tf_op jit(solution)/shard_map/all_gather | solution.py:1596
  479.3 26.6 %copy-start.91 = (bf16[256,512]{1,0:T(8,128)(2,1)S(1)}, bf16[256,512]{1,0:T(8,128)(2,1)}, u32[]{:S(2)}) copy-start(bf16[256,512]{1,0:T(8,128)(2,1)} %copy-done.90) | copy-start | bytes 786436
  525.9 21.6 %copy-start.48 = (f32[256,1024]{1,0:T(8,128)S(1)}, f32[256,1024]{1,0:T(8,128)}, u32[]{:S(2)}) copy-start(f32[256,1024]{1,0:T(8,128)} %copy-done.46) | copy-start | bytes 3145732
  549.3 80.0 %all-gather.17.cloned.1.call-start = ((), (), s32[]{:S(2)}) async-start(), calls=%async_computation.9 | async-start | bytes 1474560 | tf_op jit(solution)/shard_map/all_gather | solution.py:1596
  554.8 19.9 %collective-permute-start.3 = (f32[2,1024]{1,0:T(2,128)S(1)}, f32[2,1024]{1,0:T(2,128)S(1)}, u32[]{:S(2)}, u32[]{:S(2)}) collective-permute-start(f32[2,1024]{1,0:T(2,128)S(1)} %pad_add_fusion.1), channel_id=1, source_target_pairs={{4,0},{8,4},{12,8},{5,1},{9,5},{13,9},{6,2},{10,6},{14,10},{7,3},{... | collective-permute-start | bytes 24584 | tf_op jit(solution)/shard_map/ppermute | solution.py:20
  574.6 27.1 %copy-start.13 = (f32[256,1024]{1,0:T(8,128)S(1)}, f32[256,1024]{1,0:T(8,128)}, u32[]{:S(2)}) copy-start(f32[256,1024]{1,0:T(8,128)} %copy-done.12) | copy-start | bytes 3145732
  574.6 27.1 %copy-start.53 = (f32[256,1024]{1,0:T(8,128)S(1)}, f32[256,1024]{1,0:T(8,128)}, u32[]{:S(2)}) copy-start(f32[256,1024]{1,0:T(8,128)} %copy-done.51) | copy-start | bytes 3145732
  824.9 5.4 collective-permute-start.4
  (100 other events, 348.7 us)
Sparse Core Ops, SparseCore 0:
  10.5 31.3 all-gather.8
  43.8 24.6 all-gather.10
  70.4 43.3 all-gather.6
  115.5 35.5 all-gather.12
  326.9 29.4 reduce-scatter.4
  370.3 75.4 reduce-scatter.2
  549.4 48.9 all-gather.14
  599.9 29.2 all-gather.16

commit v6 on v5

--- a/solution.py
+++ b/solution.py
@@ -47,6 +47,22 @@
 
 def norm_back(dnormed, normed, inv_rms):
     return inv_rms * dnormed - normed * inv_rms * jnp.mean(dnormed * normed, axis=-1, keepdims=True)
+
+
+def head_sums(values, head):
+    heads = values.shape[1] // head
+    owner = (jnp.arange(values.shape[1])[:, None] // head == jnp.arange(heads)[None, :]).astype(F32)
+    sums = jnp.dot(values, owner, precision=lax.Precision.HIGHEST, preferred_element_type=F32)
+    return jnp.dot(sums, owner.T, precision=lax.Precision.HIGHEST, preferred_element_type=F32)
+
+
+def norm_heads(values, head):
+    inv_rms = lax.rsqrt(head_sums(values * values, head) / head + EPSILON)
+    return (values * inv_rms, inv_rms)
+
+
+def norm_heads_back(dnormed, normed, inv_rms, head):
+    return inv_rms * dnormed - normed * inv_rms * (head_sums(dnormed * normed, head) / head)
 
 
 def busy(microseconds):
@@ -138,6 +154,51 @@
         ),
         cost_estimate=busy(25),
     )(array)
+
+
+def gather_swap_kernel(block, pieces, whole, swapped_out, send_sem, recv_sem, own_sem, cross_send, cross_recv, keep_sem):
+    me, beside, across, opposite = corners()
+    barrier = pltpu.get_barrier_semaphore()
+    for target in (beside, across, opposite):
+        pl.semaphore_signal(barrier, inc=1, device_id={"fsdp": target}, device_id_type=MESH)
+    pl.semaphore_wait(barrier, 3)
+    gather = SideGather(block, whole, send_sem, recv_sem, own_sem)
+    gather.start()
+    crossing = []
+    for step in range(1, 4):
+        target = lax.rem(me + step, 4)
+        crossing.append(
+            to_side(pieces.at[target], swapped_out.at[me], cross_send.at[step], cross_recv.at[step], target)
+        )
+        crossing[-1].start()
+    keep = pltpu.make_async_copy(pieces.at[me], swapped_out.at[me], keep_sem)
+    keep.start()
+    gather.relay()
+    gather.finish()
+    keep.wait()
+    for copy in crossing:
+        copy.wait()
+
+
+def gathered_swapped(array, pieces, collective_id):
+    rows, width = array.shape
+    dma = pltpu.SemaphoreType.DMA
+    vmem = pl.BlockSpec(memory_space=pltpu.VMEM)
+    hbm = pl.BlockSpec(memory_space=pl.ANY)
+    return pl.pallas_call(
+        gather_swap_kernel,
+        out_shape=(
+            jax.ShapeDtypeStruct((4 * rows, width), array.dtype),
+            jax.ShapeDtypeStruct(pieces.shape, pieces.dtype),
+        ),
+        in_specs=[vmem, hbm],
+        out_specs=[vmem, hbm],
+        scratch_shapes=[dma((4,)), dma((4,)), dma, dma((4,)), dma((4,)), dma],
+        compiler_params=pltpu.CompilerParams(
+            collective_id=collective_id, has_side_effects=True, vmem_limit_bytes=56 << 20
+        ),
+        cost_estimate=busy(25),
+    )(array, pieces)
 
 
 class SideReduce:
@@ -269,6 +330,7 @@
     down_recv,
     rest_recv,
     second_send,
+    second_recv,
 ):
     n_ctx, n_fsdp = counts
     section = lax.axis_index("section")
@@ -356,10 +418,11 @@
                 device_id_type=MESH,
             )
         )
-    for copy in pair:
-        copy.start()
-    for copy in local:
-        copy.start()
+    for index in range(a_chunks):
+        order = [index] + ([a_chunks + index] if index < down_chunks else [])
+        for spot in order:
+            pair[spot].start()
+            local[spot].start()
     c_local, c_pair = ([], []), ([], [])
     for kind, source in enumerate(mixers):
         part = 0 if kind < 3 else 1
@@ -385,11 +448,11 @@
         small_at = pl.ds(n_mix * half, c_rows - n_mix * half)
         index = owner * (n_mix + 1) + n_mix
         c_local[1].append(
-            pltpu.make_async_copy(small_in.at[owner, section], c_own.at[owner, small_at], c_own_sem.at[index])
+            pltpu.make_async_copy(small_in.at[section], c_own.at[owner, small_at], c_own_sem.at[index])
         )
         c_pair[1].append(
             pltpu.make_async_remote_copy(
-                src_ref=small_in.at[owner, other],
+                src_ref=small_in.at[other],
                 dst_ref=c_other.at[owner, small_at],
                 send_sem=c_pair_send.at[index],
                 recv_sem=c_pair_recv.at[index],
@@ -403,23 +466,40 @@
         for copy in c_local[part]:
             copy.start()
     b_own[b_chunks - 1] = jnp.zeros((b_rows, b_width), BF16)
-    for copy in local:
-        copy.wait()
-    for copy in pair:
-        copy.wait_recv()
-
-    def mixer_copy(part, step):
-        target = lax.rem(group + step, n_fsdp)
+    _, beside, across, opposite = corners()
+
+    def span(first, last):
+        return pl.ds(first * b_rows, (last - first) * b_rows)
+
+    def mixer_spans(part):
         first, last = c_parts[part]
-        at = pl.ds(first * b_rows, (last - first) * b_rows)
-        return pltpu.make_async_remote_copy(
-            src_ref=c_own.at[target, at],
-            dst_ref=c_got.at[step - 1, at],
-            send_sem=c_send.at[part, step],
-            recv_sem=c_recv.at[part, step],
-            device_id={"fsdp": target},
-            device_id_type=MESH,
-        )
+        middle = (first + last) // 2
+        return (first, middle, beside, across), (middle, last, across, beside)
+
+    def mixer_copies(part):
+        opening, onward = [], []
+        for turn, (first, last, near, far) in enumerate(mixer_spans(part)):
+            at = span(first, last)
+            for slot, owner in ((0, opposite), (1, near)):
+                opening.append(
+                    to_side(
+                        c_own.at[owner, at],
+                        c_got.at[slot, at],
+                        c_send.at[part, 3 * turn + slot],
+                        c_recv.at[part, 3 * turn + slot],
+                        near,
+                    )
+                )
+            onward.append(
+                to_side(
+                    c_own.at[far, at],
+                    c_got.at[2, at],
+                    c_send.at[part, 3 * turn + 2],
+                    c_recv.at[part, 3 * turn + 2],
+                    far,
+                )
+            )
+        return opening, onward
 
     def mixer_out(part):
         for copy in c_local[part]:
@@ -436,63 +516,77 @@
             return carry
 
         lax.fori_loop(0, n_fsdp * size, add, 0)
-        for step in range(1, n_fsdp):
-            mixer_copy(part, step).start()
+        opening, _ = mixer_copies(part)
+        for index in (0, 2, 1, 3):
+            opening[index].start()
+
+    def mixer_on(part):
+        opening, onward = mixer_copies(part)
+        for turn, (first, last, near, far) in enumerate(mixer_spans(part)):
+            opening[2 * turn].wait_recv()
+
+            def add(index, carry, far=far):
+                at = pl.ds(pl.multiple_of(index * b_rows, b_rows), b_rows)
+                c_own[far, at] = (c_own[far, at].astype(F32) + c_got[0, at].astype(F32)).astype(BF16)
+                return carry
+
+            lax.fori_loop(first, last, add, 0)
+            onward[turn].start()
 
     def mixer_in(part):
-        for step in range(1, n_fsdp):
-            mixer_copy(part, step).wait_recv()
+        opening, onward = mixer_copies(part)
+        for turn in range(2):
+            opening[2 * turn + 1].wait_recv()
+            onward[turn].wait_recv()
         first, last = c_parts[part]
 
         def add(index, carry):
             at = pl.ds(pl.multiple_of(index * b_rows, b_rows), b_rows)
-            total = c_own[group, at].astype(F32)
-            for step in range(1, n_fsdp):
-                total = total + c_got[step - 1, at].astype(F32)
+            total = c_own[group, at].astype(F32) + c_got[1, at].astype(F32) + c_got[2, at].astype(F32)
             b_own[down_chunks + index] = total.astype(BF16)
             return carry
 
         lax.fori_loop(first, last, add, 0)
 
+    strip = half // n_ctx
+
+    def second_copies(remote):
+        for index in range(n_ctx * n_fsdp * 2):
+            source, kind = index // 2, index % 2
+            turn, owner = source // n_fsdp, source % n_fsdp
+            src = second_gu_in.at[turn, owner, kind]
+            dst = gu_out.at[
+                kind,
+                pl.ds(pl.multiple_of(section * half + turn * strip, strip), strip),
+                pl.ds(owner * a_width, a_width),
+            ]
+            if remote:
+                pltpu.make_async_remote_copy(
+                    src_ref=src,
+                    dst_ref=dst,
+                    send_sem=second_send.at[0],
+                    recv_sem=second_recv,
+                    device_id={"section": 1},
+                    device_id_type=MESH,
+                ).start()
+            else:
+                pltpu.make_async_copy(src, dst, second_send.at[0]).start()
+
     def second_start():
-        for kind in range(2):
-            for owner in range(n_fsdp):
-                index = kind * n_fsdp + owner
-                src = second_gu_in.at[kind, owner]
-                dst = gu_out.at[
-                    kind,
-                    pl.ds(pl.multiple_of(section * half, half), half),
-                    pl.ds(pl.multiple_of(group * a_width, 128), a_width),
-                ]
-                is_mine = (section == 1) & (group == owner)
-
-                @pl.when(is_mine)
-                def _(src=src, dst=dst, index=index):
-                    pltpu.make_async_copy(src, dst, second_send.at[index]).start()
-
-                @pl.when(jnp.logical_not(is_mine))
-                def _(src=src, dst=dst, index=index, kind=kind, owner=owner):
-                    pltpu.make_async_remote_copy(
-                        src_ref=src,
-                        dst_ref=dst,
-                        send_sem=second_send.at[index],
-                        recv_sem=gu_recv.at[kind, section * n_fsdp + group],
-                        device_id={"section": 1, "fsdp": owner},
-                        device_id_type=MESH,
-                    ).start()
-
         down_at = down_out.at[pl.ds(pl.multiple_of(section * down_half, b_rows), down_half)]
 
         @pl.when(section == 1)
         def _():
-            pltpu.make_async_copy(second_down_in, down_at, second_send.at[2 * n_fsdp]).start()
+            second_copies(False)
+            pltpu.make_async_copy(second_down_in, down_at, second_send.at[1]).start()
 
         @pl.when(section == 0)
         def _():
+            second_copies(True)
             pltpu.make_async_remote_copy(
                 src_ref=second_down_in,
                 dst_ref=down_at,
-                send_sem=second_send.at[2 * n_fsdp],
+                send_sem=second_send.at[1],
                 recv_sem=down_recv,
                 device_id={"section": 1},
                 device_id_type=MESH,
@@ -602,8 +696,13 @@
         )
 
     def own_term(k):
+        pltpu.make_async_copy(a_own.at[k], a_other.at[k], own_sem.at[k]).wait()
+        pltpu.make_async_copy(a_own.at[k], a_other.at[k], pair_recv.at[k]).wait()
+
         @pl.when(k < down_chunks)
         def _():
+            pltpu.make_async_copy(b_own.at[k], b_sum.at[k], own_sem.at[a_chunks + k]).wait()
+            pltpu.make_async_copy(b_own.at[k], b_sum.at[k], pair_recv.at[a_chunks + k]).wait()
             b_own[k] = (b_own[k].astype(F32) + b_other[k].astype(F32)).astype(BF16)
 
         return a_own[k].astype(F32) + a_other[k].astype(F32)
@@ -616,21 +715,22 @@
         lanes.append((way, rank, ahead, behind))
 
     def tick_step(tick, carry):
-        @pl.when(tick == 0)
+        events = (
+            (1, mixer_out, 0),
+            (2, mixer_out, 1),
+            (3, mixer_on, 0),
+            (down_chunks // 2 - 1, mixer_on, 1),
+            (down_chunks // 2, mixer_in, 0),
+            ((down_chunks + cut) // 2, mixer_in, 1),
+        )
+        for moment, action, part in events:
+
+            @pl.when(tick == moment)
+            def _(action=action, part=part):
+                action(part)
+
+        @pl.when(tick == 4)
         def _():
-            mixer_out(0)
-
-        @pl.when(tick == 2)
-        def _():
-            mixer_out(1)
-
-        @pl.when(tick == down_chunks // 2)
-        def _():
-            mixer_in(0)
-
-        @pl.when(tick == (down_chunks + cut) // 2)
-        def _():
-            mixer_in(1)
             second_start()
 
         for way, rank, ahead, behind in lanes:
@@ -693,8 +793,9 @@
     for part in range(2):
         for copy in c_pair[part]:
             copy.wait_send()
-        for step in range(1, n_fsdp):
-            mixer_copy(part, step).wait_send()
+        opening, onward = mixer_copies(part)
+        for copy in opening + onward:
+            copy.wait_send()
 
     def settle(step, carry):
         for way, rank, ahead, behind in lanes:
@@ -721,22 +822,26 @@
         return carry
 
     lax.fori_loop(0, ticks, settle, 0)
-    for kind in range(2):
-        for owner in range(n_fsdp):
-            src = second_gu_in.at[kind, owner]
-            pltpu.make_async_copy(src, src, second_send.at[kind * n_fsdp + owner]).wait()
-    pltpu.make_async_copy(second_down_in, second_down_in, second_send.at[2 * n_fsdp]).wait()
-    for kind in range(2):
-        for source in range(2 * n_fsdp):
-
-            @pl.when(section * n_fsdp + group != source)
-            def _(kind=kind, source=source):
-                region = gu_out.at[
-                    kind,
-                    pl.ds((source // n_fsdp) * half, half),
-                    pl.ds((source % n_fsdp) * a_width, a_width),
-                ]
-                pltpu.make_async_copy(region, region, gu_recv.at[kind, source]).wait()
+    pltpu.make_async_copy(second_gu_in, second_gu_in, second_send.at[0]).wait()
+    pltpu.make_async_copy(second_down_in, second_down_in, second_send.at[1]).wait()
+
+    @pl.when(section == 0)
+    def _():
+        for kind in range(2):
+            for source in range(2 * n_fsdp):
+
+                @pl.when(group != source)
+                def _(kind=kind, source=source):
+                    region = gu_out.at[
+                        kind,
+                        pl.ds((source // n_fsdp) * half, half),
+                        pl.ds((source % n_fsdp) * a_width, a_width),
+                    ]
+                    pltpu.make_async_copy(region, region, gu_recv.at[kind, source]).wait()
+
+    @pl.when(section == 1)
+    def _():
+        pltpu.make_async_copy(second_gu_in, second_gu_in, second_recv).wait()
 
     region = down_out.at[pl.ds(pl.multiple_of(other * down_half, b_rows), down_half)]
     pltpu.make_async_copy(region, region, down_recv).wait()
@@ -751,7 +856,7 @@
     a_rows, b_rows = half // 4, half * 3 // 8
     a_chunks = 2 * n_fsdp * 4
     a_width, b_width = gate.shape[1], down.shape[1]
-    c_rows = len(mixers) * half + small.shape[2]
+    c_rows = len(mixers) * half + small.shape[1]
     down_chunks = down.shape[0] // 2 // b_rows
     b_chunks = down_chunks + c_rows // b_rows + 1
     assert a_chunks == b_chunks and c_rows % b_rows == 0
@@ -786,8 +891,8 @@
             dma((pieces,)),
             dma((pieces,)),
             dma((pieces,)),
-            dma((2, n_fsdp)),
-            dma((2, n_fsdp)),
+            dma((2, 6)),
+            dma((2, 6)),
             dma((a_chunks,)),
             dma((a_chunks,)),
             dma((a_chunks,)),
@@ -802,7 +907,8 @@
             dma((2, 2 * n_fsdp)),
             dma,
             dma,
-            dma((2 * n_fsdp + 1,)),
+            dma((2,)),
+            dma,
         ],
         compiler_params=pltpu.CompilerParams(
             collective_id=6, has_side_effects=True, vmem_limit_bytes=56 << 20
@@ -908,7 +1014,7 @@
         out_specs=[pl.BlockSpec(memory_space=pl.ANY)] * 2,
         scratch_shapes=[dma((8,)), dma((8,)), dma((8,)), dma((8,)), dma((2,))],
         compiler_params=pltpu.CompilerParams(
-            collective_id=collective_id, has_side_effects=True, vmem_limit_bytes=8 << 20
+            collective_id=collective_id, has_side_effects=True, vmem_limit_bytes=56 << 20
         ),
         cost_estimate=busy(45),
     )(first, second)
@@ -1027,7 +1133,7 @@
         out_specs=[pl.BlockSpec(memory_space=pl.ANY)] * 3,
         scratch_shapes=[dma((2, count)), dma((2, count)), dma((3, count)), dma((3, count)), dma((3,))],
         compiler_params=pltpu.CompilerParams(
-            collective_id=collective_id, has_side_effects=True, vmem_limit_bytes=8 << 20
+            collective_id=collective_id, has_side_effects=True, vmem_limit_bytes=56 << 20
         ),
         cost_estimate=busy(40),
     )(gate, up, down)
@@ -1278,7 +1384,7 @@
             dma((3,)),
         ],
         compiler_params=pltpu.CompilerParams(
-            collective_id=collective_id, has_side_effects=True, vmem_limit_bytes=40 << 20
+            collective_id=collective_id, has_side_effects=True, vmem_limit_bytes=56 << 20
         ),
         cost_estimate=busy(50),
     )(length, query, kv, d_block, gate, up, down)
@@ -1521,10 +1627,12 @@
     h = h_low.astype(F32)
     normed2, inv2 = norm_rows(h)
     act2 = (normed2 * norm_gains[2]).astype(BF16)
-    q_normed, q_inv = norm_rows(matmul(act2, query_full).reshape(rows, q_heads, head))
-    k_normed, k_inv = norm_rows(matmul(act2, key_full).reshape(rows, kv_heads, head))
-    query = (q_normed * head_gains[0]).astype(BF16).reshape(rows, q_width)
-    key = (k_normed * head_gains[1]).astype(BF16).reshape(rows, kv_width)
+    q_normed, q_inv = norm_heads(matmul(act2, query_full), head)
+    k_normed, k_inv = norm_heads(matmul(act2, key_full), head)
+    q_gain = jnp.tile(head_gains[0], q_heads)
+    k_gain = jnp.tile(head_gains[1], kv_heads)
+    query = (q_normed * q_gain).astype(BF16)
+    key = (k_normed * k_gain).astype(BF16)
     value = matmul(act2, value_full).astype(BF16)
     d_sum_low = (lax.dynamic_index_in_dim(cotangent, section, keepdims=False).astype(F32) * mask).astype(BF16)
     attended, log_total, kv_all, d_sum_all, gate2, up2, down2 = attend(
@@ -1549,12 +1657,19 @@
     grad_proj = matmul_left(attended_low, d_attn)
     d_att = matmul_right(d_attn, proj_full).astype(BF16)
     half = part // 2
-
-    def shared_halves(grad, lead):
-        pieces = grad.reshape(lead, 2, -1, grad.shape[1])
-        mine = lax.dynamic_index_in_dim(pieces, section, 1, keepdims=False)
-        other = swapped(lax.dynamic_index_in_dim(pieces, 1 - section, 1, keepdims=False), "section")
-        return (mine.astype(F32) + other.astype(F32)).astype(BF16)
+    strip = half // lax.axis_size("ctx")
+
+    def shared(mine, theirs):
+        return (mine.astype(F32) + swapped(theirs, "section").astype(F32)).astype(BF16)
+
+    def column_half(which):
+        pieces = jnp.stack(grads2[:2]).reshape(2, fsdp, 2, half // strip, strip, -1)
+        pieces = lax.dynamic_index_in_dim(pieces, which, 2, keepdims=False)
+        return pieces.transpose(2, 1, 0, 3, 4).reshape(2 * fsdp * half, -1)
+
+    def down_half(which):
+        size = grads2[2].shape[0] // 2
+        return lax.dynamic_slice_in_dim(grads2[2], which * size, size, 0)
 
     delta = jnp.sum((d_att.astype(F32) * attended).reshape(rows, q_heads, head), axis=-1)
     d_query, d_kv, ffn2 = attend_back(
@@ -1568,20 +1683,18 @@
     squares = jnp.stack(
         [square(v) for v in (x, mixed, ffn1, h, attn_rows, res2, ffn2, result)]
     )
-    second = (
-        shared_halves(jnp.concatenate(grads2[:2], axis=0), 2 * fsdp),
-        shared_halves(grads2[2], 1)[0],
-    )
-    second = tuple(
-        lax.psum_scatter(term.reshape(-1, term.shape[-1]), "ctx", scatter_dimension=0, tiled=True)
-        for term in second
-    )
-    d_qn = rounded(d_query).reshape(rows, q_heads, head)
-    grad_qgain = jnp.sum(d_qn * q_normed, axis=(0, 1))
-    d_qpre = norm_back(d_qn * head_gains[0], q_normed, q_inv).reshape(rows, -1).astype(BF16)
-    d_kn = rounded(d_kv[:, :kv_width]).reshape(rows, kv_heads, head)
-    grad_kgain = jnp.sum(d_kn * k_normed, axis=(0, 1))
-    d_kpre = norm_back(d_kn * head_gains[1], k_normed, k_inv).reshape(rows, -1).astype(BF16)
+    second_gu, second_down = (
+        lax.psum_scatter(
+            shared(pick(section), pick(1 - section)), "ctx", scatter_dimension=0, tiled=True
+        )
+        for pick in (column_half, down_half)
+    )
+    d_qn = rounded(d_query)
+    grad_qgain = jnp.sum(jnp.sum(d_qn * q_normed, axis=0).reshape(q_heads, head), axis=0)
+    d_qpre = norm_heads_back(d_qn * q_gain, q_normed, q_inv, head).astype(BF16)
+    d_kn = rounded(d_kv[:, :kv_width])
+    grad_kgain = jnp.sum(jnp.sum(d_kn * k_normed, axis=0).reshape(kv_heads, head), axis=0)
+    d_kpre = norm_heads_back(d_kn * k_gain, k_normed, k_inv, head).astype(BF16)
     d_vpre = d_kv[:, kv_width:].astype(BF16)
     d_act2 = (
         matmul_right(d_qpre, query_full)
@@ -1591,9 +1704,11 @@
     gain2 = jnp.sum(d_act2 * normed2, axis=0)
     d_h_low = (d_res2 + norm_back(d_act2 * norm_gains[2], normed2, inv2)).astype(BF16)
 
-    d_h_all, second = lax.optimization_barrier((gathered(d_h_low, 0), second))
+    d_h_all, second_gu = gathered_swapped(d_h_low, second_gu.reshape(fsdp, 2 * strip, -1), 5)
+    second_gu = lax.all_gather(second_gu, "ctx", axis=0)
+    second_down = lax.all_gather(second_down, "ctx", axis=0, tiled=True)
     d_ffn1, gain1, grads1 = ffn_backward(d_h_all, kept1, norm_gains[1], gate1, up1, down1)
-    second = tuple(lax.all_gather(term, "ctx", axis=0, tiled=True) for term in second)
+    d_ffn1, second_gu = lax.optimization_barrier((d_ffn1, second_gu))
     d_res1 = d_h_low.astype(F32) + d_ffn1
     d_mixed = d_res1.astype(BF16)
     grad_out = matmul_left(z_low, d_mixed)
@@ -1612,8 +1727,8 @@
         + jnp.pad(d_conv * conv_kernel[1], ((1, 1), (0, 0)))
         + jnp.pad(d_conv * conv_kernel[2], ((2, 0), (0, 0)))
     )
-    from_next, second_gu = lax.optimization_barrier(
-        (passed_along(d_extended[:2], "ctx", -1), second[0])
+    from_next, second_down = lax.optimization_barrier(
+        (passed_along(d_extended[:2], "ctx", -1), second_down)
     )
     d_bproduct = rounded(d_extended[2:] + jnp.pad(from_next, ((rows - 2, 0), (0, 0))))
     d_projected = jnp.concatenate(
@@ -1637,31 +1752,24 @@
         grad_proj.astype(BF16),
     ] + grad_parts + [grad_out.astype(BF16)]
 
-    cut = width // fsdp
-    head_cut = head // fsdp
-    square_cut = squares.shape[0] // fsdp
-    by_owner = jnp.concatenate(
+    last_row = jnp.concatenate(
+        [grad_qgain, grad_kgain, squares, jnp.zeros((width - 2 * head - squares.shape[0],), F32)]
+    )
+    small = jnp.concatenate(
         [
-            jnp.concatenate([jnp.stack([gain0, gain1, gain2, gain3]), grad_kernel])
-            .reshape(7, fsdp, cut)
-            .transpose(1, 0, 2)
-            .reshape(fsdp, 7 * cut),
-            jnp.stack([grad_qgain, grad_kgain])
-            .reshape(2, fsdp, head_cut)
-            .transpose(1, 0, 2)
-            .reshape(fsdp, 2 * head_cut),
-            squares.reshape(fsdp, square_cut),
-            jnp.zeros((fsdp, cut - 2 * head_cut - square_cut), F32),
-        ],
-        axis=1,
-    ).reshape(fsdp, 1, -1, width)
-    small = jnp.pad(by_owner, ((0, 0), (0, 1), (0, 16 - by_owner.shape[2]), (0, 0))).astype(BF16)
+            jnp.stack([gain0, gain1, gain2, gain3]),
+            grad_kernel,
+            last_row[None],
+            jnp.zeros((24, width), F32),
+        ]
+    ).astype(BF16)
+    small = small.reshape(2, 16, width)
     gu_sum, down_sum, rest_sum = summed_gradients(
         grads1,
         mixers,
         small,
-        second_gu.reshape(2, fsdp, part // 2, -1),
-        second[1],
+        second_gu.reshape(-1, fsdp, 2, strip, second_gu.shape[-1]),
+        second_down,
     )
     rest_sum = rest_sum.astype(F32)
 
@@ -1671,10 +1779,15 @@
 
     attn_blocks = [block(i) for i in range(3)]
     conv_blocks = [block(3 + i) for i in range(4)]
-    small_sum = rest_sum[0, 7 * half : 7 * half + 2].reshape(-1)
-    mine = small_sum[: 7 * cut].reshape(7, cut)
-    heads = small_sum[7 * cut : 7 * cut + 2 * head_cut].reshape(2, head_cut)
-    square_sum = small_sum[7 * cut + 2 * head_cut : 7 * cut + 2 * head_cut + square_cut]
+    small_sum = rest_sum[0, 7 * half : 7 * half + 8]
+    cut = width // fsdp
+    mine = lax.dynamic_slice_in_dim(small_sum[:7], group * cut, cut, 1)
+    head_cut = head // fsdp
+    heads = lax.dynamic_slice_in_dim(
+        small_sum[7, : 2 * head].reshape(2, head), group * head_cut, head_cut, 1
+    )
+    square_cut = squares.shape[0] // fsdp
+    square_sum = lax.dynamic_slice_in_dim(small_sum[7], 2 * head + group * square_cut, square_cut)
     token_total = jnp.sum(lengths).astype(F32) * width
     rms = jnp.sqrt(square_sum / token_total)
     return (

time: 846 us -> 887 us (1.048)
  starting transfers between devices: 6.42 us -> 68.2 us
  Pallas kernels: 506 us -> 556 us
  local copies, waits for them, and re-layouts: 86.4 us -> 42.6 us
  other arithmetic: 61.2 us -> 45.4 us
  waiting for transfers between devices: 31.4 us -> 17.1 us
    pallas_call x1, Pallas kernels: 38.8 us -> 110 us  [column_weights(): pl.pallas_call(functools.partial(column_weights_kernel, holder), out_shap...]
    ppermute x3, starting transfers between devices: 0.54 us -> 62.2 us  [swapped(): return lax.ppermute(block, axis, [(0, 1), (1, 0)])]
    pallas_call x3 -> x2, Pallas kernels: 70 us -> 29.9 us  [gathered(): pl.pallas_call(gather_kernel, out_shape=jax.ShapeDtypeStruct((4 * rows, w...]
    pallas_call x1, Pallas kernels: 76.8 us -> 51.2 us  [attend_back(): pl.pallas_call(functools.partial(attend_back_kernel, n_ctx), out_shape=(w...]
    unnamed x230 -> x197, local copies, waits for them, and re-layouts: 41.6 us -> 16.8 us
    pallas_call x0 -> x1, Pallas kernels: none -> 23.5 us  [gathered_swapped(): pl.pallas_call(gather_swap_kernel, out_shape=(jax.ShapeDtypeStruct((4 * r...]
    pallas_call x1, Pallas kernels: 45.7 us -> 68 us  [mixer_weights(): pl.pallas_call(functools.partial(mixer_weights_kernel, count), out_shape=...]
    all_gather x2, waiting for transfers between devices: 31.3 us -> 13.3 us  [the longest x1 13.3 us: shards(): second_down = lax.all_gather(second_down, 'ctx', axis=0, tiled=True)]
  transfers between devices with their start and end apart: 13 -> 13, of which waited for: 2 -> 2; matrix products, arithmetic and copies ran while one was open for 21% -> 15% of each run, Pallas kernels for 35% -> 41%
where the time goes in v6:
time: 887 us; the launch traced here: 880 us
  Pallas kernels  556 us (63%)
  matrix products  135 us (15%)
  starting transfers between devices  68.2 us (8%)
  other arithmetic  45.4 us (5%)
  local copies, waits for them, and re-layouts  42.6 us (5%)
  waiting for transfers between devices  17.1 us (2%)
  between operations  16.4 us (2%)
    pallas_call x1, Pallas kernels, summed_gradients(): pl.pallas_call(functools.partial(tail_kernel, (n_ctx, n_fsdp)), out_shape...  177 us
    pallas_call x1, Pallas kernels, column_weights(): pl.pallas_call(functools.partial(column_weights_kernel, holder), out_shap...  110 us
    pallas_call x1, Pallas kernels, mixer_weights(): pl.pallas_call(functools.partial(mixer_weights_kernel, count), out_shape=...  68 us
    ppermute x3, starting transfers between devices, swapped(): return lax.ppermute(block, axis, [(0, 1), (1, 0)])  62.2 us
    pallas_call x1, Pallas kernels, attend_back(): pl.pallas_call(functools.partial(attend_back_kernel, n_ctx), out_shape=(w...  51.2 us
    pallas_call x1, Pallas kernels, attend(): pl.pallas_call(functools.partial(attend_kernel, n_ctx), out_shape=(jax.Sh...  49.9 us
    pallas_call x3, Pallas kernels, reduced(): pl.pallas_call(reduce_kernel, out_shape=jax.ShapeDtypeStruct((rows, width...  45.7 us
    dot_general x12, matrix products, matmul(): return jnp.dot(left_op, right_op, preferred_element_type=F32)  44.9 us
  transfers between devices with their start and end apart: 13, of which 2 were waited for; matrix products, arithmetic and copies ran while one was open for 15% of the time, Pallas kernels for 41%

profile of v6, /device:TPU:0, one launch (start us, length us, event | category | flops | bytes accessed | tf_op | source)
XLA Modules:
  0.0 880.2 jit_solution(17926352067460516768)
XLA Ops:
  11.5 68.0 %shard_map.262 = (bf16[1024,3072]{1,0:T(8,128)(2,1)}, bf16[1024,1024]{1,0:T(8,128)(2,1)}) custom-call(bf16[256,3072]{1,0:T(8,128)(2,1)} %first_in.1, bf16[256,1024]{1,0:T(8,128)(2,1)} %second_in.1), custom_call_target="tpu_custom_call" | custom-call | flops 45 | bytes 65536 | tf_op jit(solution)/shard_map/pallas_call | solution.py:1008
  81.9 4.9 fusion.107
  92.2 110.4 %shard_map.264 = (bf16[1024,1152]{1,0:T(8,128)(2,1)}, bf16[1024,1152]{1,0:T(8,128)(2,1)}, bf16[1152,1024]{1,0:T(8,128)(2,1)}) custom-call(bf16[256,4608]{1,0:T(8,128)(2,1)} %bitcast.150, bf16[256,4608]{1,0:T(8,128)(2,1)} %bitcast.152, bf16[1152,1024]{1,0:T(8,128)(2,1)} %bitcast.154), custom_call_target="tpu_custom_call" | custom-call | flops 40 | bytes 65536 | tf_op jit(solution)/shard_map/pallas_call | solution.py:1129
  209.7 15.1 %shard_map.263 = bf16[1024,1024]{1,0:T(8,128)(2,1)S(1)} custom-call(bf16[256,1024]{1,0:T(8,128)(2,1)S(1)} %multiply_convert_fusion.9.block), custom_call_target="tpu_custom_call" | custom-call | flops 25 | bytes 65536 | tf_op jit(solution)/shard_map/pallas_call | solution.py:146
  224.8 4.7 fusion.122
  241.1 12.2 %shard_map.265 = f32[256,1024]{1,0:T(8,128)S(1)} custom-call(bf16[1024,1024]{1,0:T(8,128)(2,1)S(1)} %copy-done.2), custom_call_target="tpu_custom_call" | custom-call | flops 25 | bytes 65536 | tf_op jit(solution)/shard_map/pallas_call | solution.py:268
  267.6 49.9 %shard_map.266 = (f32[256,1024]{1,0:T(8,128)}, f32[16,1,256]{2,1,0:T(1,128)}, bf16[1024,1024]{1,0:T(8,128)(2,1)}, bf16[1024,1024]{1,0:T(8,128)(2,1)}, bf16[1024,...) custom-call(s32[1]{0:T(128)} %dynamic_slice.46.length_ref, ...), custom_call_target="tpu_custom_call" | custom-call | flops 50 | bytes 65536 | tf_op jit(solution)/shard_map/pallas_call | solution.py:1356
  324.2 14.8 %shard_map.267 = bf16[1024,1024]{1,0:T(8,128)(2,1)S(1)} custom-call(bf16[256,1024]{1,0:T(8,128)(2,1)S(1)} %copy-done.3), custom_call_target="tpu_custom_call" | custom-call | flops 25 | bytes 65536 | tf_op jit(solution)/shard_map/pallas_call | solution.py:146
  346.6 5.6 multiply_convert_fusion.2
  359.5 61.7 %collective-permute-start.1 = (bf16[1024,1152]{1,0:T(8,128)(2,1)S(1)}, bf16[1024,1152]{1,0:T(8,128)(2,1)S(1)}, u32[]{:S(2)}, u32[]{:S(2)}) collective-permute-start(bf16[1024,1152]{1,0:T(8,128)(2,1)S(1)} %bitcast.165), channel_id=1, source_target_pairs={{0,16},{16,0},{1,17},{17,1},{2,18},{18,2},{3,19},{19,3},{4,20},{20... | collective-permute-start | bytes 7077896 | tf_op jit(solution)/shard_map/ppermute | solution.py:24
  427.5 5.1 convolution_convert_fusion.3
  442.7 19.8 %shard_map.268 = f32[256,1024]{1,0:T(8,128)S(1)} custom-call(bf16[1024,1024]{1,0:T(8,128)(2,1)S(1)} %add_convert_fusion.1.blocks), custom_call_target="tpu_custom_call" | custom-call | flops 25 | bytes 65536 | tf_op jit(solution)/shard_map/pallas_call | solution.py:268
  472.1 6.5 convolution_convert_fusion.6.blocks
  478.6 51.2 %shard_map.269 = (f32[256,1024]{1,0:T(8,128)}, f32[256,1024]{1,0:T(8,128)}, f32[256,1024]{1,0:T(8,128)}) custom-call(s32[1]{0:T(128)} %dynamic_slice.46.length_ref, bf16[256,1024]{1,0:T(8,128)(2,1)} %get-tuple-element.90.query, bf16[1024,1024]{1,0:T(8,128)(2,1)} %get-tuple-element.49.kv_all, bf16[256,1024]{1,0:T(8,128)(2,1)} %get-tuple-element.148.d_out, ...), custom_call_target="tpu_custom_call" | custom-call | flops 50 | bytes 65536 | tf_op jit(solution)/shard_map/pallas_call | solution.py:1507
  546.5 23.5 %shard_map.270 = (bf16[1024,1024]{1,0:T(8,128)(2,1)}, bf16[4,64,1152]{2,1,0:T(8,128)(2,1)}) custom-call(bf16[256,1024]{1,0:T(8,128)(2,1)} %fusion.52.block, bf16[4,64,1152]{2,1,0:T(8,128)(2,1)} %bitcast.171), custom_call_target="tpu_custom_call" | custom-call | flops 25 | bytes 65536 | tf_op jit(solution)/shard_map/pallas_call | solution.py:188
  582.4 6.5 convolution_convert_fusion.down_in
  589.0 6.7 multiply_convert_fusion
  610.2 13.7 %shard_map.271 = f32[256,1024]{1,0:T(8,128)S(1)} custom-call(bf16[1024,1024]{1,0:T(8,128)(2,1)S(1)} %add_convert_fusion.blocks), custom_call_target="tpu_custom_call" | custom-call | flops 25 | bytes 65536 | tf_op jit(solution)/shard_map/pallas_call | solution.py:268
  637.3 13.3 %all-gather.16.cloned.1.call-done.second_down_in = bf16[576,1024]{1,0:T(8,128)(2,1)} async-done(((bf16[144,1024]{1,0:T(8,128)(2,1)}), bf16[576,1024]{1,0:T(8,128)(2,1)}) %all-gather.16.cloned.1.call-update) | async-done | bytes 1179664 | tf_op jit(solution)/shard_map/all_gather | solution.py:1709
  658.3 7.0 fusion.47
  665.3 5.3 concatenate.43
  671.9 177.5 %shard_map.272 = (bf16[2,256,4608]{2,1,0:T(8,128)(2,1)}, bf16[1152,1024]{1,0:T(8,128)(2,1)}, bf16[2,960,1024]{2,1,0:T(8,128)(2,1)}) custom-call(bf16[1024,1152]{1,0:T(8,128)(2,1)} %convolution_convert_fusion.2.gate_in, bf16[1024,1152]{1,0:T(8,128)(2,1)} %convolution_convert_fusion.1.up_in, bf16[1152,1024]{1,0:T(8,128)(2,1)} %convolution_convert_fusion.down_in, ...), custom_call_target="tpu_custom_call" | custom-call | flops 160 | bytes 65536 | tf_op jit(solution)/shard_map/pallas_call | solution.py:867
  849.4 5.4 fusion.117
  856.2 5.0 slice_convert_fusion
  (354 shorter events, 170.2 us)
Async XLA Ops:
  7.2 72.3 %copy-start.89 = (s32[8]{0:T(128)S(1)}, s32[8]{0:T(128)}, u32[]{:S(2)}) copy-start(s32[8]{0:T(128)} %param.17) | copy-start | bytes 100
  7.2 73.6 %copy-start.21 = (bf16[2,256,1024]{2,1,0:T(8,128)(2,1)S(1)}, bf16[2,256,1024]{2,1,0:T(8,128)(2,1)}, u32[]{:S(2)}) copy-start(bf16[2,256,1024]{2,1,0:T(8,128)(2,1)} %param.15) | copy-start | bytes 3145732
  7.2 73.6 %copy-start.57 = (bf16[2,256,1024]{2,1,0:T(8,128)(2,1)S(1)}, bf16[2,256,1024]{2,1,0:T(8,128)(2,1)}, u32[]{:S(2)}) copy-start(bf16[2,256,1024]{2,1,0:T(8,128)(2,1)} %param.16) | copy-start | bytes 3145732
  7.2 247.0 %all-gather.10.cloned.1.call-start = ((), (), s32[]{:S(2)}) async-start(), calls=%async_computation.3 | async-start | bytes 1179648 | tf_op jit(solution)/shard_map/all_gather | solution.py:1591
  9.0 248.3 %all-gather.12.cloned.1.call-start = ((), (), s32[]{:S(2)}) async-start(), calls=%async_computation.4 | async-start | bytes 1179648 | tf_op jit(solution)/shard_map/all_gather | solution.py:1591
  10.6 71.2 %copy-start.71 = (f32[4,1024]{1,0:T(4,128)S(1)}, f32[4,1024]{1,0:T(4,128)}, u32[]{:S(2)}) copy-start(f32[4,1024]{1,0:T(4,128)} %param.18) | copy-start | bytes 49156
  10.7 251.1 %all-gather.8.cloned.1.call-start = ((), (), s32[]{:S(2)}) async-start(), calls=%async_computation.2 | async-start | bytes 2359296 | tf_op jit(solution)/shard_map/all_gather | solution.py:1591
  11.5 306.0 %all-gather.14.cloned.1.call-start = ((), (), s32[]{:S(2)}) async-start(), calls=%async_computation.5 | async-start | bytes 2359296 | tf_op jit(solution)/shard_map/all_gather | solution.py:1591
  81.9 126.7 %copy-start.61 = (f32[1,1024]{1,0:T(1,128)}, f32[1,1024]{1,0:T(1,128)S(1)}, u32[]{:S(2)}) copy-start(f32[1,1024]{1,0:T(1,128)S(1)} %get-tuple-element.127) | copy-start | bytes 12292
  86.7 118.6 %copy-start.20 = (f32[256,3072]{1,0:T(8,128)}, f32[256,3072]{1,0:T(8,128)S(1)}, u32[]{:S(2)}) copy-start(f32[256,3072]{1,0:T(8,128)S(1)} %fusion.107) | copy-start | bytes 9437188
  87.7 115.0 %collective-permute-start = (bf16[2,1024]{1,0:T(2,128)(2,1)S(1)}, bf16[2,1024]{1,0:T(2,128)(2,1)S(1)}, u32[]{:S(2)}, u32[]{:S(2)}) collective-permute-start(bf16[2,1024]{1,0:T(2,128)(2,1)S(1)} %slice.192), channel_id=1, source_target_pairs={{0,4},{4,8},{8,12},{1,5},{5,9},{9,13},{2,6},{6,10},{10,14},{3,7},{... | collective-permute-start | bytes 12296 | tf_op jit(solution)/shard_map/ppermute | solution.py:20
  92.0 454.5 %reduce-scatter.3.cloned.1.call-start = ((), (), s32[]{:S(2)}) async-start(), calls=%async_computation.6 | async-start | bytes 2949120 | tf_op jit(solution)/shard_map/reduce_scatter | solution.py:1687
  92.1 111.9 %copy-start.63 = (f32[1,1024]{1,0:T(1,128)}, f32[1,1024]{1,0:T(1,128)S(1)}, u32[]{:S(2)}) copy-start(f32[1,1024]{1,0:T(1,128)S(1)} %get-tuple-element.130) | copy-start | bytes 12292
  92.1 111.9 %copy-start.65 = (f32[1,1024]{1,0:T(1,128)}, f32[1,1024]{1,0:T(1,128)S(1)}, u32[]{:S(2)}) copy-start(f32[1,1024]{1,0:T(1,128)S(1)} %get-tuple-element.131) | copy-start | bytes 12292
  92.1 111.9 %copy-start.67 = (f32[1,1024]{1,0:T(1,128)}, f32[1,1024]{1,0:T(1,128)S(1)}, u32[]{:S(2)}) copy-start(f32[1,1024]{1,0:T(1,128)S(1)} %get-tuple-element.132) | copy-start | bytes 12292
  208.6 21.0 %copy-start.72 = (f32[256]{0:T(256)}, f32[256]{0:T(256)S(1)}, u32[]{:S(2)}) copy-start(f32[256]{0:T(256)S(1)} %add_rsqrt_fusion.2) | copy-start | bytes 3076
  359.5 65.9 %collective-permute-start.1 = (bf16[1024,1152]{1,0:T(8,128)(2,1)S(1)}, bf16[1024,1152]{1,0:T(8,128)(2,1)S(1)}, u32[]{:S(2)}, u32[]{:S(2)}) collective-permute-start(bf16[1024,1152]{1,0:T(8,128)(2,1)S(1)} %bitcast.165), channel_id=1, source_target_pairs={{0,16},{16,0},{1,17},{17,1},{2,18},{18,2},{3,19},{19,3},{4,20},{20... | collective-permute-start | bytes 7077896 | tf_op jit(solution)/shard_map/ppermute | solution.py:24
  427.3 155.1 %reduce-scatter.5.cloned.1.call-start = ((), (), s32[]{:S(2)}) async-start(), calls=%async_computation.7 | async-start | bytes 1474560 | tf_op jit(solution)/shard_map/reduce_scatter | solution.py:1687
  442.3 21.4 %copy-start.33 = (bf16[256,1024]{1,0:T(8,128)(2,1)S(1)}, bf16[256,1024]{1,0:T(8,128)(2,1)}, u32[]{:S(2)}) copy-start(bf16[256,1024]{1,0:T(8,128)(2,1)} %get-tuple-element.152.d_block) | copy-start | bytes 1572868
  442.3 90.5 %collective-permute-start.3 = (bf16[576,1024]{1,0:T(8,128)(2,1)}, bf16[576,1024]{1,0:T(8,128)(2,1)}, u32[]{:S(2)}, u32[]{:S(2)}) collective-permute-start(bf16[576,1024]{1,0:T(8,128)(2,1)} %constant_dynamic-slice_fusion.4), channel_id=1, source_target_pairs={{0,16},{16,0},{1,17},{17,1},{2,18},{18,2},{3,19},{19,3},{4,20},{20... | collective-permute-start | bytes 3538952 | tf_op jit(solution)/shard_map/ppermute | solution.py:24
  535.5 89.1 %all-gather.18.cloned.1.call-start = ((), (), s32[]{:S(2)}) async-start(), calls=%async_computation.9 | async-start | bytes 2949120 | tf_op jit(solution)/shard_map/all_gather | solution.py:1708
  570.1 80.5 %all-gather.16.cloned.1.call-start = ((), (), s32[]{:S(2)}) async-start(), calls=%async_computation.8 | async-start | bytes 1474560 | tf_op jit(solution)/shard_map/all_gather | solution.py:1709
  629.9 20.7 %collective-permute-start.2 = (f32[2,1024]{1,0:T(2,128)S(1)}, f32[2,1024]{1,0:T(2,128)S(1)}, u32[]{:S(2)}, u32[]{:S(2)}) collective-permute-start(f32[2,1024]{1,0:T(2,128)S(1)} %pad_add_fusion.1), channel_id=1, source_target_pairs={{4,0},{8,4},{12,8},{5,1},{9,5},{13,9},{6,2},{10,6},{14,10},{7,3},{... | collective-permute-start | bytes 24584 | tf_op jit(solution)/shard_map/ppermute | solution.py:20
  868.7 3.3 collective-permute-start.4
  (87 other events, 333.9 us)
Sparse Core Ops, SparseCore 0:
  10.5 31.0 all-gather.9
  43.5 24.6 all-gather.11
  70.1 30.1 all-gather.7
  102.1 35.2 all-gather.13
  427.4 47.3 reduce-scatter.2
  535.7 26.4 reduce-scatter.4
  570.2 49.3 all-gather.17
  621.2 29.4 all-gather.15

commit v7 on v6

--- a/solution.py
+++ b/solution.py
@@ -195,7 +195,7 @@
         out_specs=[vmem, hbm],
         scratch_shapes=[dma((4,)), dma((4,)), dma, dma((4,)), dma((4,)), dma],
         compiler_params=pltpu.CompilerParams(
-            collective_id=collective_id, has_side_effects=True, vmem_limit_bytes=56 << 20
+            collective_id=collective_id, has_side_effects=True, vmem_limit_bytes=8 << 20
         ),
         cost_estimate=busy(25),
     )(array, pieces)
@@ -258,6 +258,72 @@
     reduction.start()
     reduction.relay()
     reduction.finish()
+
+
+def reduce_pair_kernel(
+    blocks,
+    give_a,
+    give_b,
+    total,
+    got_a,
+    got_b,
+    beside_got,
+    across_got,
+    passed,
+    passed_got,
+    send_sem,
+    recv_sem,
+    pair_send,
+    pair_recv,
+):
+    other = {"section": 1 - lax.axis_index("section")}
+    _, beside, across, _ = corners()
+    barrier = pltpu.get_barrier_semaphore()
+    for target in ({"fsdp": beside}, {"fsdp": across}, other):
+        pl.semaphore_signal(barrier, inc=1, device_id=target, device_id_type=MESH)
+    pl.semaphore_wait(barrier, 3)
+    reduction = SideReduce(blocks, total, beside_got, across_got, passed, passed_got, send_sem, recv_sem)
+    reduction.start()
+    pairs = [
+        pltpu.make_async_remote_copy(
+            src_ref=src,
+            dst_ref=dst,
+            send_sem=pair_send.at[index],
+            recv_sem=pair_recv.at[index],
+            device_id=other,
+            device_id_type=MESH,
+        )
+        for index, (src, dst) in enumerate(((give_a, got_a), (give_b, got_b)))
+    ]
+    for copy in pairs:
+        copy.start()
+    reduction.relay()
+    reduction.finish()
+    for copy in pairs:
+        copy.wait()
+
+
+def reduced_swapping(partial, give_a, give_b, collective_id):
+    rows, width = partial.shape[0] // 4, partial.shape[1]
+    dma = pltpu.SemaphoreType.DMA
+    pair = pltpu.VMEM((2, rows // 2, width), BF16)
+    vmem = pl.BlockSpec(memory_space=pltpu.VMEM)
+    hbm = pl.BlockSpec(memory_space=pl.ANY)
+    return pl.pallas_call(
+        reduce_pair_kernel,
+        out_shape=(
+            jax.ShapeDtypeStruct((rows, width), F32),
+            jax.ShapeDtypeStruct(give_a.shape, BF16),
+            jax.ShapeDtypeStruct(give_b.shape, BF16),
+        ),
+        in_specs=[vmem, hbm, hbm],
+        out_specs=[vmem, hbm, hbm],
+        scratch_shapes=[pair, pair, pair, pair, dma((6,)), dma((6,)), dma((2,)), dma((2,))],
+        compiler_params=pltpu.CompilerParams(
+            collective_id=collective_id, has_side_effects=True, vmem_limit_bytes=16 << 20
+        ),
+        cost_estimate=busy(25),
+    )(partial.astype(BF16), give_a, give_b)
 
 
 def reduced(partial, collective_id):
@@ -349,7 +415,7 @@
     n_mix = len(mixers)
     cut = 3 * half // b_rows
     c_parts = ((0, cut), (cut, c_rows // b_rows))
-    ticks = a_chunks // 2
+    ticks = a_chunks
     tail = 2 * (n_ctx - 1)
 
     barrier = pltpu.get_barrier_semaphore()
@@ -383,46 +449,48 @@
     def half_rows(owner, which):
         return pl.ds(pl.multiple_of(owner * (2 * half) + which * half, half), half)
 
-    local, pair = [], []
-    for kind, source in enumerate((gate_in, up_in)):
-        for owner in range(n_fsdp):
-            index = kind * n_fsdp + owner
-            slot = pl.ds(index * subs, subs)
-            for sub in range(subs):
-                src_own = source.at[pl.ds(pl.multiple_of(owner * (2 * half) + section * half + sub * a_rows, a_rows), a_rows)]
-                src_other = source.at[pl.ds(pl.multiple_of(owner * (2 * half) + other * half + sub * a_rows, a_rows), a_rows)]
-                spot = index * subs + sub
-                local.append(pltpu.make_async_copy(src_own, a_own.at[spot], own_sem.at[spot]))
-                pair.append(
-                    pltpu.make_async_remote_copy(
-                        src_ref=src_other,
-                        dst_ref=a_other.at[spot],
-                        send_sem=pair_send.at[spot],
-                        recv_sem=pair_recv.at[spot],
-                        device_id={"section": other},
-                        device_id_type=MESH,
-                    )
-                )
-    for chunk in range(down_chunks):
-        spot = a_chunks + chunk
-        src_own = down_in.at[pl.ds(pl.multiple_of(section * down_half + chunk * b_rows, b_rows), b_rows)]
-        src_other = down_in.at[pl.ds(pl.multiple_of(other * down_half + chunk * b_rows, b_rows), b_rows)]
-        local.append(pltpu.make_async_copy(src_own, b_own.at[chunk], own_sem.at[spot]))
-        pair.append(
+    a_part, b_part = a_rows // 2, b_width // 2
+
+    def a_at(buffer, k, way):
+        return buffer.at[k, pl.ds(way * a_part, a_part)]
+
+    def b_at(buffer, k, way):
+        return buffer.at[k, :, pl.ds(way * b_part, b_part)]
+
+    def opening(k, way):
+        copies = []
+        kind, rest = divmod(k, per_kind)
+        owner, sub = divmod(rest, subs)
+        source = (gate_in, up_in)[kind]
+        spots = []
+        for which in (section, other):
+            start = owner * (2 * half) + which * half + sub * a_rows + way * a_part
+            spots.append(source.at[pl.ds(pl.multiple_of(start, a_part), a_part)])
+        spot = 2 * k + way
+        copies.append((spots, a_at(a_own, k, way), a_at(a_other, k, way), spot))
+        if k < down_chunks:
+            spots = [
+                down_in.at[
+                    pl.ds(pl.multiple_of(which * down_half + k * b_rows, b_rows), b_rows),
+                    pl.ds(way * b_part, b_part),
+                ]
+                for which in (section, other)
+            ]
+            copies.append((spots, b_at(b_own, k, way), b_at(b_other, k, way), 2 * a_chunks + spot))
+        for (mine, theirs), own_dst, other_dst, spot in copies:
+            pltpu.make_async_copy(mine, own_dst, own_sem.at[spot]).start()
             pltpu.make_async_remote_copy(
-                src_ref=src_other,
-                dst_ref=b_other.at[chunk],
+                src_ref=theirs,
+                dst_ref=other_dst,
                 send_sem=pair_send.at[spot],
                 recv_sem=pair_recv.at[spot],
                 device_id={"section": other},
                 device_id_type=MESH,
-            )
-        )
-    for index in range(a_chunks):
-        order = [index] + ([a_chunks + index] if index < down_chunks else [])
-        for spot in order:
-            pair[spot].start()
-            local[spot].start()
+            ).start()
+
+    for k in range(a_chunks):
+        for way in range(2):
+            opening(k, way)
     c_local, c_pair = ([], []), ([], [])
     for kind, source in enumerate(mixers):
         part = 0 if kind < 3 else 1
@@ -592,32 +660,36 @@
                 device_id_type=MESH,
             ).start()
 
-    def a_target(k):
+    def a_target(k, way):
         kind = k // per_kind
         rest = lax.rem(k, per_kind)
         owner = rest // subs
         sub = lax.rem(rest, subs)
+        start = section * half + sub * a_rows + way * a_part
         spot = gu_out.at[
             kind,
-            pl.ds(pl.multiple_of(section * half + sub * a_rows, a_rows), a_rows),
+            pl.ds(pl.multiple_of(start, a_part), a_part),
             pl.ds(pl.multiple_of(group * a_width, 128), a_width),
         ]
         return kind, owner, spot
 
-    def hand_out(k):
-        kind, owner, spot = a_target(k)
+    def hand_out(k, way):
+        kind, owner, spot = a_target(k, way)
         is_mine = (section == 0) & (group == owner)
+        slot = 2 * k + way
+        a_ref, b_ref = a_at(a_done, k, way), b_at(b_done, k, way)
+        lanes_at = pl.ds(way * b_part, b_part)
 
         @pl.when(is_mine)
         def _():
-            pltpu.make_async_copy(a_done.at[k], spot, a_out_send.at[k]).start()
+            pltpu.make_async_copy(a_ref, spot, a_out_send.at[slot]).start()
 
         @pl.when(jnp.logical_not(is_mine))
         def _():
             pltpu.make_async_remote_copy(
-                src_ref=a_done.at[k],
+                src_ref=a_ref,
                 dst_ref=spot,
-                send_sem=a_out_send.at[k],
+                send_sem=a_out_send.at[slot],
                 recv_sem=gu_recv.at[kind, section * n_fsdp + group],
                 device_id={"section": 0, "fsdp": owner},
                 device_id_type=MESH,
@@ -625,18 +697,18 @@
 
         @pl.when(k < down_chunks)
         def _():
-            at = down_out.at[pl.ds(pl.multiple_of(section * down_half + k * b_rows, b_rows), b_rows)]
+            at = down_out.at[pl.ds(pl.multiple_of(section * down_half + k * b_rows, b_rows), b_rows), lanes_at]
 
             @pl.when(section == 0)
             def _():
-                pltpu.make_async_copy(b_done.at[k], at, b_out_send.at[k]).start()
+                pltpu.make_async_copy(b_ref, at, b_out_send.at[slot]).start()
 
             @pl.when(section == 1)
             def _():
                 pltpu.make_async_remote_copy(
-                    src_ref=b_done.at[k],
+                    src_ref=b_ref,
                     dst_ref=at,
-                    send_sem=b_out_send.at[k],
+                    send_sem=b_out_send.at[slot],
                     recv_sem=down_recv,
                     device_id={"section": 0},
                     device_id_type=MESH,
@@ -644,68 +716,69 @@
 
         @pl.when(k >= down_chunks)
         def _():
-            at = rest_out.at[section, pl.ds(pl.multiple_of((k - down_chunks) * b_rows, b_rows), b_rows)]
-            pltpu.make_async_copy(b_done.at[k], at, b_keep_sem.at[k]).start()
+            at = rest_out.at[
+                section, pl.ds(pl.multiple_of((k - down_chunks) * b_rows, b_rows), b_rows), lanes_at
+            ]
+            pltpu.make_async_copy(b_ref, at, b_keep_sem.at[slot]).start()
             pltpu.make_async_remote_copy(
-                src_ref=b_done.at[k],
+                src_ref=b_ref,
                 dst_ref=at,
-                send_sem=b_out_send.at[k],
+                send_sem=b_out_send.at[slot],
                 recv_sem=rest_recv,
                 device_id={"section": other},
                 device_id_type=MESH,
             ).start()
 
-    def up_copies(k, target):
-        return (
+    def chain_copies(k, way, target, buffers, sems):
+        slot = 2 * k + way
+        return [
             pltpu.make_async_remote_copy(
-                src_ref=a_sum.at[k],
-                dst_ref=a_sum.at[k],
-                send_sem=a_up_send.at[k],
-                recv_sem=a_up_recv.at[k],
+                src_ref=at,
+                dst_ref=at,
+                send_sem=send.at[slot],
+                recv_sem=recv.at[slot],
                 device_id={"ctx": target},
                 device_id_type=MESH,
-            ),
-            pltpu.make_async_remote_copy(
-                src_ref=b_sum.at[k],
-                dst_ref=b_sum.at[k],
-                send_sem=b_up_send.at[k],
-                recv_sem=b_up_recv.at[k],
-                device_id={"ctx": target},
-                device_id_type=MESH,
-            ),
+            )
+            for at, (send, recv) in zip((a_at(buffers[0], k, way), b_at(buffers[1], k, way)), sems)
+        ]
+
+    def up_copies(k, way, target):
+        return chain_copies(
+            k, way, target, (a_sum, b_sum), ((a_up_send, a_up_recv), (b_up_send, b_up_recv))
         )
 
-    def back_copies(k, target):
-        return (
-            pltpu.make_async_remote_copy(
-                src_ref=a_done.at[k],
-                dst_ref=a_done.at[k],
-                send_sem=a_back_send.at[k],
-                recv_sem=a_back_recv.at[k],
-                device_id={"ctx": target},
-                device_id_type=MESH,
-            ),
-            pltpu.make_async_remote_copy(
-                src_ref=b_done.at[k],
-                dst_ref=b_done.at[k],
-                send_sem=b_back_send.at[k],
-                recv_sem=b_back_recv.at[k],
-                device_id={"ctx": target},
-                device_id_type=MESH,
-            ),
+    def back_copies(k, way, target):
+        return chain_copies(
+            k, way, target, (a_done, b_done), ((a_back_send, a_back_recv), (b_back_send, b_back_recv))
         )
 
-    def own_term(k):
-        pltpu.make_async_copy(a_own.at[k], a_other.at[k], own_sem.at[k]).wait()
-        pltpu.make_async_copy(a_own.at[k], a_other.at[k], pair_recv.at[k]).wait()
+    def a_load(buffer, k, way):
+        return buffer[k, pl.ds(way * a_part, a_part)].astype(F32)
+
+    def b_load(buffer, k, way):
+        return buffer[k, :, pl.ds(way * b_part, b_part)].astype(F32)
+
+    def a_store(buffer, k, way, value):
+        buffer[k, pl.ds(way * a_part, a_part)] = value.astype(BF16)
+
+    def b_store(buffer, k, way, value):
+        buffer[k, :, pl.ds(way * b_part, b_part)] = value.astype(BF16)
+
+    def own_terms(k, way):
+        slot = 2 * k + way
+        at = a_at(a_own, k, way)
+        pltpu.make_async_copy(at, at, own_sem.at[slot]).wait()
+        pltpu.make_async_copy(at, at, pair_recv.at[slot]).wait()
 
         @pl.when(k < down_chunks)
         def _():
-            pltpu.make_async_copy(b_own.at[k], b_sum.at[k], own_sem.at[a_chunks + k]).wait()
-            pltpu.make_async_copy(b_own.at[k], b_sum.at[k], pair_recv.at[a_chunks + k]).wait()
-            b_own[k] = (b_own[k].astype(F32) + b_other[k].astype(F32)).astype(BF16)
-
-        return a_own[k].astype(F32) + a_other[k].astype(F32)
+            at = b_at(b_own, k, way)
+            pltpu.make_async_copy(at, at, own_sem.at[2 * a_chunks + slot]).wait()
+            pltpu.make_async_copy(at, at, pair_recv.at[2 * a_chunks + slot]).wait()
+            b_store(b_own, k, way, b_load(b_own, k, way) + b_load(b_other, k, way))
+
+        return a_load(a_own, k, way) + a_load(a_other, k, way), b_load(b_own, k, way)
 
     lanes = []
     for way in range(2):
@@ -717,11 +790,11 @@
     def tick_step(tick, carry):
         events = (
             (1, mixer_out, 0),
-            (2, mixer_out, 1),
-            (3, mixer_on, 0),
-            (down_chunks // 2 - 1, mixer_on, 1),
-            (down_chunks // 2, mixer_in, 0),
-            ((down_chunks + cut) // 2, mixer_in, 1),
+            (3, mixer_out, 1),
+            (6, mixer_on, 0),
+            (down_chunks - 1, mixer_on, 1),
+            (down_chunks, mixer_in, 0),
+            (down_chunks + cut, mixer_in, 1),
         )
         for moment, action, part in events:
 
@@ -729,67 +802,65 @@
             def _(action=action, part=part):
                 action(part)
 
-        @pl.when(tick == 4)
+        @pl.when(tick == 8)
         def _():
             second_start()
 
         for way, rank, ahead, behind in lanes:
             step = tick - rank
-            k = 2 * jnp.clip(step, 0, ticks - 1) + way
+            k = jnp.clip(step, 0, ticks - 1)
 
             @pl.when((step >= 0) & (step < ticks))
-            def _(k=k, rank=rank, ahead=ahead, behind=behind):
-                term = own_term(k)
+            def _(k=k, way=way, rank=rank, ahead=ahead, behind=behind):
+                a_term, b_term = own_terms(k, way)
 
                 @pl.when(rank == 0)
                 def _():
-                    a_sum[k] = term.astype(BF16)
-                    b_sum[k] = b_own[k]
+                    a_store(a_sum, k, way, a_term)
+                    b_store(b_sum, k, way, b_term)
 
                 @pl.when(rank > 0)
                 def _():
-                    for copy in up_copies(k, behind):
+                    for copy in up_copies(k, way, behind):
                         copy.wait_recv()
 
                 @pl.when((rank > 0) & (rank < n_ctx - 1))
                 def _():
-                    a_sum[k] = (term + a_sum[k].astype(F32)).astype(BF16)
-                    b_sum[k] = (b_own[k].astype(F32) + b_sum[k].astype(F32)).astype(BF16)
+                    a_store(a_sum, k, way, a_term + a_load(a_sum, k, way))
+                    b_store(b_sum, k, way, b_term + b_load(b_sum, k, way))
 
                 @pl.when(rank < n_ctx - 1)
                 def _():
-                    for copy in up_copies(k, ahead):
+                    for copy in up_copies(k, way, ahead):
                         copy.start()
 
                 @pl.when(rank == n_ctx - 1)
                 def _():
-                    a_done[k] = (term + a_sum[k].astype(F32)).astype(BF16)
-                    b_done[k] = (b_own[k].astype(F32) + b_sum[k].astype(F32)).astype(BF16)
-                    for copy in back_copies(k, behind):
+                    a_store(a_done, k, way, a_term + a_load(a_sum, k, way))
+                    b_store(b_done, k, way, b_term + b_load(b_sum, k, way))
+                    for copy in back_copies(k, way, behind):
                         copy.start()
-                    hand_out(k)
+                    hand_out(k, way)
 
             late = tick - (tail - rank)
-            j = 2 * jnp.clip(late, 0, ticks - 1) + way
+            j = jnp.clip(late, 0, ticks - 1)
 
             @pl.when((late >= 0) & (late < ticks) & (rank < n_ctx - 1))
-            def _(j=j, rank=rank, ahead=ahead, behind=behind):
-                for copy in back_copies(j, ahead):
+            def _(j=j, way=way, rank=rank, ahead=ahead, behind=behind):
+                for copy in back_copies(j, way, ahead):
                     copy.wait_recv()
 
                 @pl.when(rank > 0)
                 def _():
-                    for copy in back_copies(j, behind):
+                    for copy in back_copies(j, way, behind):
                         copy.start()
 
-                hand_out(j)
+                hand_out(j, way)
 
         return carry
 
     lax.fori_loop(0, ticks + tail, tick_step, 0)
 
-    for copy in pair:
-        copy.wait_send()
     for part in range(2):
         for copy in c_pair[part]:
             copy.wait_send()
@@ -797,27 +868,32 @@
         for copy in opening + onward:
             copy.wait_send()
 
-    def settle(step, carry):
+    def settle(k, carry):
         for way, rank, ahead, behind in lanes:
-            k = 2 * step + way
+            slot = 2 * k + way
+            a_ref, b_ref = a_at(a_own, k, way), b_at(b_own, k, way)
+            pltpu.make_async_copy(a_ref, a_ref, pair_send.at[slot]).wait()
+
+            @pl.when(k < down_chunks)
+            def _(b_ref=b_ref, slot=slot):
+                pltpu.make_async_copy(b_ref, b_ref, pair_send.at[2 * a_chunks + slot]).wait()
 
             @pl.when(rank < n_ctx - 1)
-            def _(k=k, ahead=ahead):
-                for copy in up_copies(k, ahead):
+            def _(k=k, way=way, ahead=ahead):
+                for copy in up_copies(k, way, ahead):
                     copy.wait_send()
 
             @pl.when(rank > 0)
-            def _(k=k, behind=behind):
-                for copy in back_copies(k, behind):
+            def _(k=k, way=way, behind=behind):
+                for copy in back_copies(k, way, behind):
                     copy.wait_send()
 
-            _, _, spot = a_target(k)
-            pltpu.make_async_copy(a_done.at[k], spot, a_out_send.at[k]).wait()
-            pltpu.make_async_copy(b_done.at[k], b_own.at[k], b_out_send.at[k]).wait()
+            pltpu.make_async_copy(a_ref, a_ref, a_out_send.at[slot]).wait()
+            pltpu.make_async_copy(b_ref, b_ref, b_out_send.at[slot]).wait()
 
             @pl.when(k >= down_chunks)
-            def _(k=k):
-                pltpu.make_async_copy(b_done.at[k], b_own.at[k], b_keep_sem.at[k]).wait()
+            def _(b_ref=b_ref, slot=slot):
+                pltpu.make_async_copy(b_ref, b_ref, b_keep_sem.at[slot]).wait()
 
         return carry
 
@@ -862,7 +938,7 @@
     assert a_chunks == b_chunks and c_rows % b_rows == 0
     rest = b_chunks - down_chunks
     dma = pltpu.SemaphoreType.DMA
-    loads = a_chunks + down_chunks
+    loads = 2 * (a_chunks + down_chunks)
     pieces = n_fsdp * (len(mixers) + 1)
     return pl.pallas_call(
         functools.partial(tail_kernel, (n_ctx, n_fsdp)),
@@ -893,17 +969,17 @@
             dma((pieces,)),
             dma((2, 6)),
             dma((2, 6)),
-            dma((a_chunks,)),
-            dma((a_chunks,)),
-            dma((a_chunks,)),
-            dma((a_chunks,)),
-            dma((a_chunks,)),
-            dma((b_chunks,)),
-            dma((b_chunks,)),
-            dma((b_chunks,)),
-            dma((b_chunks,)),
-            dma((b_chunks,)),
-            dma((b_chunks,)),
+            dma((2 * a_chunks,)),
+            dma((2 * a_chunks,)),
+            dma((2 * a_chunks,)),
+            dma((2 * a_chunks,)),
+            dma((2 * a_chunks,)),
+            dma((2 * b_chunks,)),
+            dma((2 * b_chunks,)),
+            dma((2 * b_chunks,)),
+            dma((2 * b_chunks,)),
+            dma((2 * b_chunks,)),
+            dma((2 * b_chunks,)),
             dma((2, 2 * n_fsdp)),
             dma,
             dma,
@@ -1014,7 +1090,7 @@
         out_specs=[pl.BlockSpec(memory_space=pl.ANY)] * 2,
         scratch_shapes=[dma((8,)), dma((8,)), dma((8,)), dma((8,)), dma((2,))],
         compiler_params=pltpu.CompilerParams(
-            collective_id=collective_id, has_side_effects=True, vmem_limit_bytes=56 << 20
+            collective_id=collective_id, has_side_effects=True, vmem_limit_bytes=8 << 20
         ),
         cost_estimate=busy(45),
     )(first, second)
@@ -1133,7 +1209,7 @@
         out_specs=[pl.BlockSpec(memory_space=pl.ANY)] * 3,
         scratch_shapes=[dma((2, count)), dma((2, count)), dma((3, count)), dma((3, count)), dma((3,))],
         compiler_params=pltpu.CompilerParams(
-            collective_id=collective_id, has_side_effects=True, vmem_limit_bytes=56 << 20
+            collective_id=collective_id, has_side_effects=True, vmem_limit_bytes=8 << 20
         ),
         cost_estimate=busy(40),
     )(gate, up, down)
@@ -1384,7 +1460,7 @@
             dma((3,)),
         ],
         compiler_params=pltpu.CompilerParams(
-            collective_id=collective_id, has_side_effects=True, vmem_limit_bytes=56 << 20
+            collective_id=collective_id, has_side_effects=True, vmem_limit_bytes=40 << 20
         ),
         cost_estimate=busy(50),
     )(length, query, kv, d_block, gate, up, down)
@@ -1542,18 +1618,24 @@
     return matmul(hidden, w_down).astype(BF16), (normed, inv_rms, act, gate_pre, up_pre, hidden)
 
 
-def ffn_backward(d_all, kept, gain, w_gate, w_up, w_down):
-    normed, inv_rms, act, gate_pre, up_pre, hidden = kept
+def ffn_backward(d_all, kept, w_gate, w_up, w_down):
+    _, _, act, gate_pre, up_pre, hidden = kept
     d_hidden = matmul_right(d_all, w_down)
     sigmoid = jax.nn.sigmoid(gate_pre)
     d_up = (d_hidden * gate_pre * sigmoid).astype(BF16)
     d_gate = (d_hidden * up_pre * sigmoid * (1.0 + gate_pre * (1.0 - sigmoid))).astype(BF16)
-    d_act = reduced(matmul_right(d_gate, w_gate) + matmul_right(d_up, w_up), 1)
-    grad_gate = matmul_left(act, d_gate).astype(BF16)
-    grad_up = matmul_left(act, d_up).astype(BF16)
-    grad_down = matmul_left(hidden, d_all).astype(BF16)
-    grad_gain = jnp.sum(d_act * normed, axis=0)
-    return norm_back(d_act * gain, normed, inv_rms), grad_gain, (grad_gate, grad_up, grad_down)
+    terms = (matmul_right(d_gate, w_gate) + matmul_right(d_up, w_up)).astype(BF16)
+    grads = (
+        matmul_left(act, d_gate).astype(BF16),
+        matmul_left(act, d_up).astype(BF16),
+        matmul_left(hidden, d_all).astype(BF16),
+    )
+    return terms, grads
+
+
+def ffn_norm_back(d_act, kept, gain):
+    normed, inv_rms = kept[:2]
+    return norm_back(d_act * gain, normed, inv_rms), jnp.sum(d_act * normed, axis=0)
 
 
 def shards(
@@ -1651,26 +1733,27 @@
     terms2, kept2 = ffn_forward(res2, norm_gains[3], gate2, up2, down2)
 
     d_sum = d_sum_low.astype(F32)
-    d_ffn, gain3, grads2 = ffn_backward(d_sum_all, kept2, norm_gains[3], gate2, up2, down2)
+    d_terms2, grads2 = ffn_backward(d_sum_all, kept2, gate2, up2, down2)
+    half = part // 2
+    strip = half // lax.axis_size("ctx")
+
+    def column_half(which):
+        pieces = jnp.stack(grads2[:2]).reshape(2, fsdp, 2, half // strip, strip, -1)
+        pieces = lax.dynamic_index_in_dim(pieces, which, 2, keepdims=False)
+        return pieces.transpose(2, 1, 0, 3, 4).reshape(2 * fsdp * half, -1)
+
+    def down_half(which):
+        size = grads2[2].shape[0] // 2
+        return lax.dynamic_slice_in_dim(grads2[2], which * size, size, 0)
+
+    d_act3, got_gu, got_down = reduced_swapping(
+        d_terms2, column_half(1 - section), down_half(1 - section), 8
+    )
+    d_ffn, gain3 = ffn_norm_back(d_act3, kept2, norm_gains[3])
     d_res2 = d_sum + d_ffn
     d_attn = d_res2.astype(BF16)
     grad_proj = matmul_left(attended_low, d_attn)
     d_att = matmul_right(d_attn, proj_full).astype(BF16)
-    half = part // 2
-    strip = half // lax.axis_size("ctx")
-
-    def shared(mine, theirs):
-        return (mine.astype(F32) + swapped(theirs, "section").astype(F32)).astype(BF16)
-
-    def column_half(which):
-        pieces = jnp.stack(grads2[:2]).reshape(2, fsdp, 2, half // strip, strip, -1)
-        pieces = lax.dynamic_index_in_dim(pieces, which, 2, keepdims=False)
-        return pieces.transpose(2, 1, 0, 3, 4).reshape(2 * fsdp * half, -1)
-
-    def down_half(which):
-        size = grads2[2].shape[0] // 2
-        return lax.dynamic_slice_in_dim(grads2[2], which * size, size, 0)
-
     delta = jnp.sum((d_att.astype(F32) * attended).reshape(rows, q_heads, head), axis=-1)
     d_query, d_kv, ffn2 = attend_back(
         length.reshape(1), query, kv_all, d_att, log_total, delta.T.reshape(q_heads, 1, rows), terms2, 4
@@ -1678,16 +1761,14 @@
     result = (res2 + ffn2) * mask
 
     def square(values):
-        return jnp.sum(mask * values * values)
-
-    squares = jnp.stack(
-        [square(v) for v in (x, mixed, ffn1, h, attn_rows, res2, ffn2, result)]
-    )
+        return jnp.sum(mask * values * values, axis=0, keepdims=True)
+
+    squares = [square(v) for v in (x, mixed, ffn1, h, attn_rows, res2, ffn2, result)]
     second_gu, second_down = (
         lax.psum_scatter(
-            shared(pick(section), pick(1 - section)), "ctx", scatter_dimension=0, tiled=True
+            (mine.astype(F32) + got.astype(F32)).astype(BF16), "ctx", scatter_dimension=0, tiled=True
         )
-        for pick in (column_half, down_half)
+        for mine, got in ((column_half(section), got_gu), (down_half(section), got_down))
     )
     d_qn = rounded(d_query)
     grad_qgain = jnp.sum(jnp.sum(d_qn * q_normed, axis=0).reshape(q_heads, head), axis=0)
@@ -1707,7 +1788,8 @@
     d_h_all, second_gu = gathered_swapped(d_h_low, second_gu.reshape(fsdp, 2 * strip, -1), 5)
     second_gu = lax.all_gather(second_gu, "ctx", axis=0)
     second_down = lax.all_gather(second_down, "ctx", axis=0, tiled=True)
-    d_ffn1, gain1, grads1 = ffn_backward(d_h_all, kept1, norm_gains[1], gate1, up1, down1)
+    d_terms1, grads1 = ffn_backward(d_h_all, kept1, gate1, up1, down1)
+    d_ffn1, gain1 = ffn_norm_back(reduced(d_terms1, 1), kept1, norm_gains[1])
     d_ffn1, second_gu = lax.optimization_barrier((d_ffn1, second_gu))
     d_res1 = d_h_low.astype(F32) + d_ffn1
     d_mixed = d_res1.astype(BF16)
@@ -1752,16 +1834,12 @@
         grad_proj.astype(BF16),
     ] + grad_parts + [grad_out.astype(BF16)]
 
-    last_row = jnp.concatenate(
-        [grad_qgain, grad_kgain, squares, jnp.zeros((width - 2 * head - squares.shape[0],), F32)]
-    )
     small = jnp.concatenate(
-        [
-            jnp.stack([gain0, gain1, gain2, gain3]),
-            grad_kernel,
-            last_row[None],
-            jnp.zeros((24, width), F32),
-        ]
+        [gain0[None], gain1[None], gain2[None], gain3[None], grad_kernel]
+        + [jnp.pad(grad[None], ((0, 0), (0, width - head))) for grad in (grad_qgain, grad_kgain)]
+        + [jnp.zeros((7, width), F32)]
+        + squares
+        + [jnp.zeros((8, width), F32)]
     ).astype(BF16)
     small = small.reshape(2, 16, width)
     gu_sum, down_sum, rest_sum = summed_gradients(
@@ -1779,15 +1857,15 @@
 
     attn_blocks = [block(i) for i in range(3)]
     conv_blocks = [block(3 + i) for i in range(4)]
-    small_sum = rest_sum[0, 7 * half : 7 * half + 8]
+    small_sum = rest_sum[0, 7 * half : 7 * half + 9]
     cut = width // fsdp
     mine = lax.dynamic_slice_in_dim(small_sum[:7], group * cut, cut, 1)
     head_cut = head // fsdp
-    heads = lax.dynamic_slice_in_dim(
-        small_sum[7, : 2 * head].reshape(2, head), group * head_cut, head_cut, 1
+    heads = lax.dynamic_slice_in_dim(small_sum[7:9], group * head_cut, head_cut, 1)
+    square_cut = len(squares) // fsdp
+    square_sum = jnp.sum(
+        lax.dynamic_slice_in_dim(rest_sum[1, 7 * half : 7 * half + 8], group * square_cut, square_cut, 0), axis=1
     )
-    square_cut = squares.shape[0] // fsdp
-    square_sum = lax.dynamic_slice_in_dim(small_sum[7], 2 * head + group * square_cut, square_cut)
     token_total = jnp.sum(lengths).astype(F32) * width
     rms = jnp.sqrt(square_sum / token_total)
     return (

time: 887 us -> 768 us (0.87)
  starting transfers between devices: 68.2 us -> 6.02 us
  Pallas kernels: 556 us -> 514 us
  matrix products: 135 us -> 121 us
  local copies, waits for them, and re-layouts: 42.6 us -> 54.8 us
    pallas_call x1, Pallas kernels: 110 us -> 39.4 us  [column_weights(): pl.pallas_call(functools.partial(column_weights_kernel, holder), out_shap...]
    ppermute x3 -> x1, starting transfers between devices: 62.2 us -> 0.07 us  [swapped(): return lax.ppermute(block, axis, [(0, 1), (1, 0)])]
    pallas_call x1, Pallas kernels: 68 us -> 45.3 us  [mixer_weights(): pl.pallas_call(functools.partial(mixer_weights_kernel, count), out_shape=...]
    pallas_call x1, Pallas kernels: 51.2 us -> 70.8 us  [attend_back(): pl.pallas_call(functools.partial(attend_back_kernel, n_ctx), out_shape=(w...]
    pallas_call x0 -> x1, Pallas kernels: none -> 18.8 us  [reduced_swapping(): pl.pallas_call(reduce_pair_kernel, out_shape=(jax.ShapeDtypeStruct((rows,...]
    unnamed x197 -> x225, local copies, waits for them, and re-layouts: 16.8 us -> 34 us
    pallas_call x2, Pallas kernels: 29.9 us -> 47 us  [gathered(): pl.pallas_call(gather_kernel, out_shape=jax.ShapeDtypeStruct((4 * rows, w...]
    pallas_call x3 -> x2, Pallas kernels: 45.7 us -> 36 us  [reduced(): pl.pallas_call(reduce_kernel, out_shape=jax.ShapeDtypeStruct((rows, width...]
  transfers between devices with their start and end apart: 13 -> 11, of which waited for: 2 -> 1; matrix products, arithmetic and copies ran while one was open for 15% -> 15% of each run, Pallas kernels for 41% -> 37%
where the time goes in v7:
time: 768 us; the launch traced here: 764 us
  Pallas kernels  514 us (67%)
  matrix products  121 us (16%)
  local copies, waits for them, and re-layouts  54.8 us (7%)
  other arithmetic  39.1 us (5%)
  between operations  16.8 us (2%)
  waiting for transfers between devices  12.7 us (2%)
    pallas_call x1, Pallas kernels, summed_gradients(): pl.pallas_call(functools.partial(tail_kernel, (n_ctx, n_fsdp)), out_shape...  187 us
    pallas_call x1, Pallas kernels, attend_back(): pl.pallas_call(functools.partial(attend_back_kernel, n_ctx), out_shape=(w...  70.8 us
    pallas_call x2, Pallas kernels, gathered(): pl.pallas_call(gather_kernel, out_shape=jax.ShapeDtypeStruct((4 * rows, w...  47 us
    pallas_call x1, Pallas kernels, mixer_weights(): pl.pallas_call(functools.partial(mixer_weights_kernel, count), out_shape=...  45.3 us
    pallas_call x1, Pallas kernels, attend(): pl.pallas_call(functools.partial(attend_kernel, n_ctx), out_shape=(jax.Sh...  45.2 us
    dot_general x13, matrix products, matmul_left(): lax.dot_general(left_op, right_op, (((0,), (0,)), ((), ())), preferred_el...  40.7 us
    dot_general x12, matrix products, matmul(): return jnp.dot(left_op, right_op, preferred_element_type=F32)  40 us
    pallas_call x1, Pallas kernels, column_weights(): pl.pallas_call(functools.partial(column_weights_kernel, holder), out_shap...  39.4 us
  transfers between devices with their start and end apart: 11, of which 1 were waited for; matrix products, arithmetic and copies ran while one was open for 15% of the time, Pallas kernels for 37%

profile of v7, /device:TPU:0, one launch (start us, length us, event | category | flops | bytes accessed | tf_op | source)
XLA Modules:
  0.0 764.2 jit_solution(6527554636351937795)
XLA Ops:
  12.6 45.3 %shard_map.262 = (bf16[1024,3072]{1,0:T(8,128)(2,1)S(1)}, bf16[1024,1024]{1,0:T(8,128)(2,1)S(1)}) custom-call(bf16[256,3072]{1,0:T(8,128)(2,1)S(1)} %copy-done.14, bf16[256,1024]{1,0:T(8,128)(2,1)S(1)} %copy-done.18), custom_call_target="tpu_custom_call" | custom-call | flops 45 | bytes 65536 | tf_op jit(solution)/shard_map/pallas_call | solution.py:1084
  65.0 4.8 fusion.107
  71.6 3.8 collective-permute-start
  79.8 39.4 %shard_map.264 = (bf16[1024,1152]{1,0:T(8,128)(2,1)S(1)}, bf16[1024,1152]{1,0:T(8,128)(2,1)S(1)}, bf16[1152,1024]{1,0:T(8,128)(2,1)S(1)}) custom-call(bf16[256,4608]{1,0:T(8,128)(2,1)S(1)} %bitcast.147, bf16[256,4608]{1,0:T(8,128)(2,1)S(1)} %bitcast.149, bf16[1152,1024]{1,0:T(8,128)(2,1)S(1)} %bitcast.151), custom_call_target="tpu_custom_call" | custom-call | flops 40 | bytes 65536 | tf_op jit(solution)/shard_map/pallas_call | solution.py:1205
  129.7 25.4 %shard_map.263 = bf16[1024,1024]{1,0:T(8,128)(2,1)S(1)} custom-call(bf16[256,1024]{1,0:T(8,128)(2,1)S(1)} %multiply_convert_fusion.9.block), custom_call_target="tpu_custom_call" | custom-call | flops 25 | bytes 65536 | tf_op jit(solution)/shard_map/pallas_call | solution.py:146
  158.1 4.5 multiply_convert_fusion.5
  167.1 19.4 %shard_map.265 = f32[256,1024]{1,0:T(8,128)S(1)} custom-call(bf16[1024,1024]{1,0:T(8,128)(2,1)S(1)} %convolution_convert_fusion.7.blocks), custom_call_target="tpu_custom_call" | custom-call | flops 25 | bytes 65536 | tf_op jit(solution)/shard_map/pallas_call | solution.py:334
  198.7 45.2 %shard_map.266 = (f32[256,1024]{1,0:T(8,128)S(1)}, f32[16,1,256]{2,1,0:T(1,128)S(1)}, bf16[1024,1024]{1,0:T(8,128)(2,1)S(1)}, bf16[1024,1024]{1,0:T(8,128)(2,1)S...) custom-call(s32[1]{0:T(128)} %dynamic_slice.48.length_ref, ...), custom_call_target="tpu_custom_call" | custom-call | flops 50 | bytes 65536 | tf_op jit(solution)/shard_map/pallas_call | solution.py:1432
  255.8 21.6 %shard_map.267 = bf16[1024,1024]{1,0:T(8,128)(2,1)S(1)} custom-call(bf16[256,1024]{1,0:T(8,128)(2,1)S(1)} %multiply_convert_fusion.7.block), custom_call_target="tpu_custom_call" | custom-call | flops 25 | bytes 65536 | tf_op jit(solution)/shard_map/pallas_call | solution.py:146
  277.5 4.7 fusion.123
  285.0 4.6 multiply_convert_fusion.2
  306.8 18.8 %shard_map.268 = (f32[256,1024]{1,0:T(8,128)S(1)}, bf16[1024,1152]{1,0:T(8,128)(2,1)S(1)}, bf16[576,1024]{1,0:T(8,128)(2,1)S(1)}) custom-call(bf16[1024,1024]{1,0:T(8,128)(2,1)S(1)} %add_convert_fusion.1.blocks, bf16[1024,1152]{1,0:T(8,128)(2,1)S(1)} %bitcast.152, bf16[576,1024]{1,0:T(8,128)(2,1)S(1)} %constant_dynamic-slice_fusion.3.give_b), custom_call_target="tpu_custom_call" | custom-call | flops 25 | bytes 65536 | tf_op jit(solution)/shard_map/pallas_call | solution.py:312
  336.3 6.5 convolution_convert_fusion.6.blocks
  342.8 70.8 %shard_map.269 = (f32[256,1024]{1,0:T(8,128)}, f32[256,1024]{1,0:T(8,128)}, f32[256,1024]{1,0:T(8,128)}) custom-call(s32[1]{0:T(128)} %dynamic_slice.48.length_ref, bf16[256,1024]{1,0:T(8,128)(2,1)} %copy-done.8, bf16[1024,1024]{1,0:T(8,128)(2,1)} %copy-done.13, bf16[256,1024]{1,0:T(8,128)(2,1)} %get-tuple-element.154.d_out, f32[16,1,256]{2,1,0:T(1,128)} %copy-done.19, ...), custom_call_target="tpu_custom_call" | custom-call | flops 50 | bytes 65536 | tf_op jit(solution)/shard_map/pallas_call | solution.py:1583
  427.4 24.4 %shard_map.270 = (bf16[1024,1024]{1,0:T(8,128)(2,1)S(1)}, bf16[4,64,1152]{2,1,0:T(8,128)(2,1)}) custom-call(bf16[256,1024]{1,0:T(8,128)(2,1)S(1)} %fusion.52.block, bf16[4,64,1152]{2,1,0:T(8,128)(2,1)S(1)} %bitcast.153), custom_call_target="tpu_custom_call" | custom-call | flops 25 | bytes 65536 | tf_op jit(solution)/shard_map/pallas_call | solution.py:188
  464.8 6.5 convolution_convert_fusion.down_in
  471.3 6.0 multiply_convert_fusion
  480.3 4.2 convolution_convert_fusion.1.up_in
  487.7 4.2 convolution_convert_fusion.2.gate_in
  491.9 16.6 %shard_map.271 = f32[256,1024]{1,0:T(8,128)S(1)} custom-call(bf16[1024,1024]{1,0:T(8,128)(2,1)S(1)} %add_convert_fusion.blocks), custom_call_target="tpu_custom_call" | custom-call | flops 25 | bytes 65536 | tf_op jit(solution)/shard_map/pallas_call | solution.py:334
  522.1 12.5 %all-gather.16.cloned.1.call-done.second_down_in = bf16[576,1024]{1,0:T(8,128)(2,1)} async-done(((bf16[144,1024]{1,0:T(8,128)(2,1)}), bf16[576,1024]{1,0:T(8,128)(2,1)}) %all-gather.16.cloned.1.call-update) | async-done | bytes 1179664 | tf_op jit(solution)/shard_map/all_gather | solution.py:1790
  548.9 186.7 %shard_map.272 = (bf16[2,256,4608]{2,1,0:T(8,128)(2,1)}, bf16[1152,1024]{1,0:T(8,128)(2,1)}, bf16[2,960,1024]{2,1,0:T(8,128)(2,1)}) custom-call(bf16[1024,1152]{1,0:T(8,128)(2,1)} %convolution_convert_fusion.2.gate_in, bf16[1024,1152]{1,0:T(8,128)(2,1)} %convolution_convert_fusion.1.up_in, bf16[1152,1024]{1,0:T(8,128)(2,1)} %convolution_convert_fusion.down_in, ...), custom_call_target="tpu_custom_call" | custom-call | flops 160 | bytes 65536 | tf_op jit(solution)/shard_map/pallas_call | solution.py:943
  735.6 4.2 fusion.117
  742.1 5.0 slice_convert_fusion
  (386 shorter events, 162.4 us)
Async XLA Ops:
  7.2 54.7 %copy-start.102 = (s32[8]{0:T(128)S(1)}, s32[8]{0:T(128)}, u32[]{:S(2)}) copy-start(s32[8]{0:T(128)} %param.17) | copy-start | bytes 100
  7.2 180.5 %all-gather.10.cloned.1.call-start = ((), (), s32[]{:S(2)}) async-start(), calls=%async_computation.3 | async-start | bytes 1179648 | tf_op jit(solution)/shard_map/all_gather | solution.py:1673
  9.0 180.9 %all-gather.12.cloned.1.call-start = ((), (), s32[]{:S(2)}) async-start(), calls=%async_computation.4 | async-start | bytes 1179648 | tf_op jit(solution)/shard_map/all_gather | solution.py:1673
  10.6 53.8 %copy-start.95 = (f32[4,1024]{1,0:T(4,128)S(1)}, f32[4,1024]{1,0:T(4,128)}, u32[]{:S(2)}) copy-start(f32[4,1024]{1,0:T(4,128)} %param.18) | copy-start | bytes 49156
  10.7 182.6 %all-gather.8.cloned.1.call-start = ((), (), s32[]{:S(2)}) async-start(), calls=%async_computation.2 | async-start | bytes 2359296 | tf_op jit(solution)/shard_map/all_gather | solution.py:1673
  11.5 239.9 %all-gather.14.cloned.1.call-start = ((), (), s32[]{:S(2)}) async-start(), calls=%async_computation.5 | async-start | bytes 2359296 | tf_op jit(solution)/shard_map/all_gather | solution.py:1673
  12.6 50.6 %copy-start.55 = (bf16[2,256,1024]{2,1,0:T(8,128)(2,1)S(1)}, bf16[2,256,1024]{2,1,0:T(8,128)(2,1)}, u32[]{:S(2)}) copy-start(bf16[2,256,1024]{2,1,0:T(8,128)(2,1)} %param.15) | copy-start | bytes 3145732
  64.5 64.2 %copy-start.85 = (f32[1,1024]{1,0:T(1,128)}, f32[1,1024]{1,0:T(1,128)S(1)}, u32[]{:S(2)}) copy-start(f32[1,1024]{1,0:T(1,128)S(1)} %get-tuple-element.133) | copy-start | bytes 12292
  71.6 52.0 %collective-permute-start = (bf16[2,1024]{1,0:T(2,128)(2,1)S(1)}, bf16[2,1024]{1,0:T(2,128)(2,1)S(1)}, u32[]{:S(2)}, u32[]{:S(2)}) collective-permute-start(bf16[2,1024]{1,0:T(2,128)(2,1)S(1)} %slice.189), channel_id=1, source_target_pairs={{0,4},{4,8},{8,12},{1,5},{5,9},{9,13},{2,6},{6,10},{10,14},{3,7},{... | collective-permute-start | bytes 12296 | tf_op jit(solution)/shard_map/ppermute | solution.py:20
  76.2 350.1 %reduce-scatter.3.cloned.1.call-start = ((), (), s32[]{:S(2)}) async-start(), calls=%async_computation.6 | async-start | bytes 2949120 | tf_op jit(solution)/shard_map/reduce_scatter | solution.py:1768
  76.3 47.5 %copy-start.87 = (f32[1,1024]{1,0:T(1,128)}, f32[1,1024]{1,0:T(1,128)S(1)}, u32[]{:S(2)}) copy-start(f32[1,1024]{1,0:T(1,128)S(1)} %get-tuple-element.136) | copy-start | bytes 12292
  76.3 47.5 %copy-start.89 = (f32[1,1024]{1,0:T(1,128)}, f32[1,1024]{1,0:T(1,128)S(1)}, u32[]{:S(2)}) copy-start(f32[1,1024]{1,0:T(1,128)S(1)} %get-tuple-element.137) | copy-start | bytes 12292
  76.3 47.5 %copy-start.91 = (f32[1,1024]{1,0:T(1,128)}, f32[1,1024]{1,0:T(1,128)S(1)}, u32[]{:S(2)}) copy-start(f32[1,1024]{1,0:T(1,128)S(1)} %get-tuple-element.138) | copy-start | bytes 12292
  128.6 26.5 %copy-start.25 = (bf16[1024,1152]{1,0:T(8,128)(2,1)S(1)}, bf16[1024,1152]{1,0:T(8,128)(2,1)}, u32[]{:S(2)}) copy-start(bf16[1024,1152]{1,0:T(8,128)(2,1)} %copy-done.24) | copy-start | bytes 7077892
  128.6 29.4 %copy-start.96 = (f32[256]{0:T(256)}, f32[256]{0:T(256)S(1)}, u32[]{:S(2)}) copy-start(f32[256]{0:T(256)S(1)} %add_rsqrt_fusion.2) | copy-start | bytes 3076
  198.7 45.3 %copy-start.8 = (bf16[256,1024]{1,0:T(8,128)(2,1)}, bf16[256,1024]{1,0:T(8,128)(2,1)S(1)}, u32[]{:S(2)}) copy-start(bf16[256,1024]{1,0:T(8,128)(2,1)S(1)} %get-tuple-element.96.query) | copy-start | bytes 1572868
  255.8 21.6 %copy-start.31 = (bf16[1152,1024]{1,0:T(8,128)(2,1)S(1)}, bf16[1152,1024]{1,0:T(8,128)(2,1)}, u32[]{:S(2)}) copy-start(bf16[1152,1024]{1,0:T(8,128)(2,1)} %copy-done.30) | copy-start | bytes 7077892
  328.6 136.1 %reduce-scatter.5.cloned.1.call-start = ((), (), s32[]{:S(2)}) async-start(), calls=%async_computation.7 | async-start | bytes 1474560 | tf_op jit(solution)/shard_map/reduce_scatter | solution.py:1768
  342.8 73.1 %copy-start.72 = (bf16[1152,1024]{1,0:T(8,128)(2,1)S(1)}, bf16[1152,1024]{1,0:T(8,128)(2,1)}, u32[]{:S(2)}) copy-start(bf16[1152,1024]{1,0:T(8,128)(2,1)} %copy-done.71) | copy-start | bytes 7077892
  417.4 92.8 %all-gather.18.cloned.1.call-start = ((), (), s32[]{:S(2)}) async-start(), calls=%async_computation.9 | async-start | bytes 2949120 | tf_op jit(solution)/shard_map/all_gather | solution.py:1789
  453.0 81.5 %all-gather.16.cloned.1.call-start = ((), (), s32[]{:S(2)}) async-start(), calls=%async_computation.8 | async-start | bytes 1474560 | tf_op jit(solution)/shard_map/all_gather | solution.py:1790
  514.7 19.8 %collective-permute-start.1 = (f32[2,1024]{1,0:T(2,128)S(1)}, f32[2,1024]{1,0:T(2,128)S(1)}, u32[]{:S(2)}, u32[]{:S(2)}) collective-permute-start(f32[2,1024]{1,0:T(2,128)S(1)} %pad_add_fusion.1), channel_id=1, source_target_pairs={{4,0},{8,4},{12,8},{5,1},{9,5},{13,9},{6,2},{10,6},{14,10},{7,3},{... | collective-permute-start | bytes 24584 | tf_op jit(solution)/shard_map/ppermute | solution.py:20
  520.7 21.7 %slice-start = ((s8[6291456]{0:T(1024)(128)(4,1)}), s8[2097152]{0:T(1024)(128)(4,1)S(1)}, s32[]{:S(2)}) async-start(s8[6291456]{0:T(1024)(128)(4,1)} %bitcast.154), calls=%async_computation.10 | async-start | bytes 4194304
  752.7 3.3 collective-permute-start.2
  (99 other events, 356.4 us)
Sparse Core Ops, SparseCore 0:
  10.5 31.3 all-gather.9
  44.4 24.4 all-gather.11
  71.4 43.9 all-gather.7
  117.1 34.8 all-gather.13
  328.7 67.4 reduce-scatter.2
  417.5 28.9 reduce-scatter.4
  453.2 50.3 all-gather.17
  505.1 29.3 all-gather.15

commit v8 on v7

--- a/solution.py
+++ b/solution.py
@@ -569,21 +569,24 @@
             )
         return opening, onward
 
-    def mixer_out(part):
-        for copy in c_local[part]:
-            copy.wait()
-        for copy in c_pair[part]:
-            copy.wait_recv()
+    def mixer_sum(part, owner):
+        kinds = range(3) if part == 0 else range(3, n_mix + 1)
         first, last = c_parts[part]
-        size = last - first
+        for kind in kinds:
+            size = half if kind < n_mix else c_rows - n_mix * half
+            at = c_own.at[owner, pl.ds(kind * half, size)]
+            index = owner * (n_mix + 1) + kind
+            pltpu.make_async_copy(at, at, c_own_sem.at[index]).wait()
+            pltpu.make_async_copy(at, at, c_pair_recv.at[index]).wait()
 
         def add(index, carry):
-            owner = index // size
-            at = pl.ds(pl.multiple_of((first + lax.rem(index, size)) * b_rows, b_rows), b_rows)
+            at = pl.ds(pl.multiple_of(index * b_rows, b_rows), b_rows)
             c_own[owner, at] = (c_own[owner, at].astype(F32) + c_other[owner, at].astype(F32)).astype(BF16)
             return carry
 
-        lax.fori_loop(0, n_fsdp * size, add, 0)
+        lax.fori_loop(first, last, add, 0)
+
+    def mixer_out(part):
         opening, _ = mixer_copies(part)
         for index in (0, 2, 1, 3):
             opening[index].start()
@@ -788,12 +791,19 @@
         lanes.append((way, rank, ahead, behind))
 
     def tick_step(tick, carry):
+        for part, start in ((0, 2), (1, 6)):
+            for owner in range(n_fsdp):
+
+                @pl.when(tick == start + owner)
+                def _(part=part, owner=owner):
+                    mixer_sum(part, owner)
+
         events = (
-            (1, mixer_out, 0),
-            (3, mixer_out, 1),
-            (6, mixer_on, 0),
-            (down_chunks - 1, mixer_on, 1),
+            (5, mixer_out, 0),
+            (9, mixer_out, 1),
+            (10, mixer_on, 0),
             (down_chunks, mixer_in, 0),
+            (16, mixer_on, 1),
             (down_chunks + cut, mixer_in, 1),
         )
         for moment, action, part in events:
@@ -802,12 +812,8 @@
             def _(action=action, part=part):
                 action(part)
 
-        @pl.when(tick == 8)
-        def _():
-            second_start()
-
         for way, rank, ahead, behind in lanes:
-            step = tick - rank
+            step = tick - 2 * rank
             k = jnp.clip(step, 0, ticks - 1)
 
             @pl.when((step >= 0) & (step < ticks))
@@ -842,7 +848,7 @@
                         copy.start()
                     hand_out(k, way)
 
-            late = tick - (tail - rank)
+            late = tick - 2 * (tail - rank)
             j = jnp.clip(late, 0, ticks - 1)
 
             @pl.when((late >= 0) & (late < ticks) & (rank < n_ctx - 1))
@@ -859,7 +865,8 @@
 
         return carry
 
-    lax.fori_loop(0, ticks + tail, tick_step, 0)
+    second_start()
+    lax.fori_loop(0, ticks + 2 * tail, tick_step, 0)
 
     for part in range(2):
         for copy in c_pair[part]:
@@ -993,109 +1000,6 @@
     )(gate, up, down, *mixers, small, second_gu, second_down)
 
 
-def mixer_weights_kernel(count, first_in, second_in, first_out, second_out, send_sem, recv_sem, pair_send, pair_recv, own_sem):
-    section = lax.axis_index("section")
-    me = lax.axis_index("fsdp")
-    other = 1 - section
-    beside = me + 1 - 2 * lax.rem(me, 2)
-    across = lax.rem(me + 2, count)
-    opposite = lax.rem(beside + 2, count)
-    rows = first_in.shape[0]
-    half = rows // 2
-    quarter = half // 2
-    barrier = pltpu.get_barrier_semaphore()
-    for target in ({"fsdp": beside}, {"fsdp": across}, {"section": other}):
-        pl.semaphore_signal(barrier, inc=1, device_id=target, device_id_type=MESH)
-    pl.semaphore_wait(barrier, 3)
-    arrays = ((first_in, first_out), (second_in, second_out))
-
-    def at_rows(owner, extra, size):
-        return pl.ds(pl.multiple_of(owner * rows + extra, quarter), size)
-
-    def remote(slot, sems, src, dst, target):
-        return pltpu.make_async_remote_copy(
-            src_ref=src,
-            dst_ref=dst,
-            send_sem=sems[0].at[slot],
-            recv_sem=sems[1].at[slot],
-            device_id=target,
-            device_id_type=MESH,
-        )
-
-    hop, pair = (send_sem, recv_sem), (pair_send, pair_recv)
-    waiting = []
-    direct = []
-    for index, (source, out) in enumerate(arrays):
-        mine = source.at[pl.ds(pl.multiple_of(section * half, half), half)]
-        spot = out.at[at_rows(me, section * half, half)]
-        copies = [
-            remote(index * 4, hop, mine, spot, {"fsdp": beside}),
-            remote(index * 4 + 1, hop, mine, spot, {"fsdp": across}),
-        ]
-        for copy in copies:
-            copy.start()
-        direct.append(copies)
-    own = [
-        pltpu.make_async_copy(source, out.at[at_rows(me, 0, rows)], own_sem.at[index])
-        for index, (source, out) in enumerate(arrays)
-    ]
-    for copy in own:
-        copy.start()
-
-    def arrived(owner, size, extra):
-        return lambda out: out.at[at_rows(owner, section * half + extra, size)]
-
-    onward = []
-    for index, (source, out) in enumerate(arrays):
-        direct[index][0].wait_recv()
-        part = arrived(beside, quarter, 0)(out)
-        onward.append(remote(index * 4 + 2, hop, part, part, {"fsdp": across}))
-        onward[-1].start()
-        whole = arrived(beside, half, 0)(out)
-        waiting.append(remote(index * 4, pair, whole, whole, {"section": other}))
-        waiting[-1].start()
-        direct[index][1].wait_recv()
-        part = arrived(across, quarter, quarter)(out)
-        onward.append(remote(index * 4 + 3, hop, part, part, {"fsdp": beside}))
-        onward[-1].start()
-        whole = arrived(across, half, 0)(out)
-        waiting.append(remote(index * 4 + 1, pair, whole, whole, {"section": other}))
-        waiting[-1].start()
-    for index, (source, out) in enumerate(arrays):
-        for turn in range(2):
-            onward[2 * index + turn].wait_recv()
-            part = arrived(opposite, quarter, turn * quarter)(out)
-            waiting.append(remote(index * 4 + 2 + turn, pair, part, part, {"section": other}))
-            waiting[-1].start()
-    for copy in own:
-        copy.wait()
-    for copies in direct:
-        for copy in copies:
-            copy.wait_send()
-    for copy in onward:
-        copy.wait_send()
-    for copy in waiting:
-        copy.wait()
-
-
-def mixer_weights(first, second, collective_id):
-    count = lax.axis_size("fsdp")
-    dma = pltpu.SemaphoreType.DMA
-    return pl.pallas_call(
-        functools.partial(mixer_weights_kernel, count),
-        out_shape=tuple(
-            jax.ShapeDtypeStruct((count * w.shape[0], w.shape[1]), w.dtype) for w in (first, second)
-        ),
-        in_specs=[pl.BlockSpec(memory_space=pl.ANY)] * 2,
-        out_specs=[pl.BlockSpec(memory_space=pl.ANY)] * 2,
-        scratch_shapes=[dma((8,)), dma((8,)), dma((8,)), dma((8,)), dma((2,))],
-        compiler_params=pltpu.CompilerParams(
-            collective_id=collective_id, has_side_effects=True, vmem_limit_bytes=8 << 20
-        ),
-        cost_estimate=busy(45),
-    )(first, second)
-
-
 class Columns:
     def __init__(self, holder, sources, targets, send_sem, recv_sem, pair_send, pair_recv, own_sem):
         self.count = 4
@@ -1166,53 +1070,28 @@
                 self.crossing(step, kind).wait_recv()
                 self.handed(step, kind).start()
 
-    def finish(self):
+    def arrive(self):
         every = [(0, kind) for kind in range(3)] + self.steps
 
         @pl.when(self.section == self.holder)
         def _():
             for kind in range(3):
                 self.kept(kind).wait()
+
+        @pl.when(self.section != self.holder)
+        def _():
+            for step, kind in every:
+                self.handed(step, kind).wait_recv()
+
+    def finish(self):
+        every = [(0, kind) for kind in range(3)] + self.steps
+
+        @pl.when(self.section == self.holder)
+        def _():
             for step, kind in self.steps:
                 self.crossing(step, kind).wait_send()
             for step, kind in every:
                 self.handed(step, kind).wait_send()
-
-        @pl.when(self.section != self.holder)
-        def _():
-            for step, kind in every:
-                self.handed(step, kind).wait_recv()
-
-
-def column_weights_kernel(holder, *refs):
-    section = lax.axis_index("section")
-    _, beside, across, opposite = corners()
-    barrier = pltpu.get_barrier_semaphore()
-    for target in ({"fsdp": beside}, {"fsdp": across}, {"fsdp": opposite}, {"section": 1 - section}):
-        pl.semaphore_signal(barrier, inc=1, device_id=target, device_id_type=MESH)
-    pl.semaphore_wait(barrier, 4)
-    columns = Columns(holder, refs[:3], refs[3:6], *refs[6:])
-    columns.start()
-    columns.relay()
-    columns.finish()
-
-
-def column_weights(gate, up, down, holder, collective_id):
-    count = lax.axis_size("fsdp")
-    assert count == 4
-    dma = pltpu.SemaphoreType.DMA
-    column = jax.ShapeDtypeStruct((count * gate.shape[0], gate.shape[1] // count), gate.dtype)
-    return pl.pallas_call(
-        functools.partial(column_weights_kernel, holder),
-        out_shape=(column, column, jax.ShapeDtypeStruct(down.shape, down.dtype)),
-        in_specs=[pl.BlockSpec(memory_space=pl.ANY)] * 3,
-        out_specs=[pl.BlockSpec(memory_space=pl.ANY)] * 3,
-        scratch_shapes=[dma((2, count)), dma((2, count)), dma((3, count)), dma((3, count)), dma((3,))],
-        compiler_params=pltpu.CompilerParams(
-            collective_id=collective_id, has_side_effects=True, vmem_limit_bytes=8 << 20
-        ),
-        cost_estimate=busy(40),
-    )(gate, up, down)
 
 
 class Chain:
@@ -1310,6 +1189,10 @@
     gate_out,
     up_out,
     down_out,
+    w_gate,
+    w_up,
+    w_down,
+    keep_sem,
     spread,
     bias,
     peak,
@@ -1360,7 +1243,7 @@
     gather = SideGather(d_block, d_all, d_send, d_recv, d_own)
     gather.start()
     columns = Columns(
-        1, (gate_in, up_in, down_in), (gate_out, up_out, down_out), send_sem, recv_sem, pair_send, pair_recv, own_sem
+        1, (gate_in, up_in, down_in), (w_gate, w_up, w_down), send_sem, recv_sem, pair_send, pair_recv, own_sem
     )
     columns.start()
     kv_all[block_rows(place)] = kv[...]
@@ -1408,8 +1291,17 @@
     for head in range(spread.shape[0]):
         log_total[head] = peak[head] + jnp.log(total[head])
     columns.relay()
+    columns.arrive()
+    keeping = [
+        pltpu.make_async_copy(src, dst, keep_sem.at[index])
+        for index, (src, dst) in enumerate(((w_gate, gate_out), (w_up, up_out), (w_down, down_out)))
+    ]
+    for copy in keeping:
+        copy.start()
     gather.finish()
     columns.finish()
+    for copy in keeping:
+        copy.wait()
 
     def settle(step, carry):
         @pl.when((step <= place) & chain.has_next)
@@ -1443,6 +1335,10 @@
         in_specs=[pl.BlockSpec(memory_space=pltpu.SMEM), vmem, vmem, vmem, hbm, hbm, hbm],
         out_specs=[vmem, vmem, vmem, vmem, hbm, hbm, hbm],
         scratch_shapes=[
+            pltpu.VMEM(column.shape, BF16),
+            pltpu.VMEM(column.shape, BF16),
+            pltpu.VMEM(down.shape, BF16),
+            dma((3,)),
             pltpu.VMEM((heads, rows, 128), BF16),
             pltpu.VMEM((rows, rows), F32),
             pltpu.VMEM((heads, 1, rows), F32),
@@ -1460,7 +1356,7 @@
             dma((3,)),
         ],
         compiler_params=pltpu.CompilerParams(
-            collective_id=collective_id, has_side_effects=True, vmem_limit_bytes=40 << 20
+            collective_id=collective_id, has_side_effects=True, vmem_limit_bytes=58 << 20
         ),
         cost_estimate=busy(50),
     )(length, query, kv, d_block, gate, up, down)
@@ -1609,17 +1505,316 @@
     )(length, query, kv_all, d_out, log_total, delta, blocks)
 
 
-def ffn_forward(residual, gain, w_gate, w_up, w_down):
-    normed, inv_rms = norm_rows(residual)
-    act = gathered((normed * gain).astype(BF16), 0)
+class MixerGather:
+    def __init__(self, sources, targets, send_sem, recv_sem, pair_send, pair_recv, own_sem):
+        self.section = section = lax.axis_index("section")
+        me, beside, across, opposite = corners()
+        rows = sources[0].shape[0]
+        half = rows // 2
+        quarter = half // 2
+
+        def at_rows(out, owner, extra, size):
+            return out.at[pl.ds(pl.multiple_of(owner * rows + extra, quarter), size)]
+
+        def pair(slot, at):
+            return pltpu.make_async_remote_copy(
+                src_ref=at,
+                dst_ref=at,
+                send_sem=pair_send.at[slot],
+                recv_sem=pair_recv.at[slot],
+                device_id={"section": 1 - section},
+                device_id_type=MESH,
+            )
+
+        self.direct, self.onward, self.early, self.late, self.own = [], [], [], [], []
+        start = section * half
+        for index, (source, out) in enumerate(zip(sources, targets)):
+            mine = source.at[pl.ds(pl.multiple_of(start, half), half)]
+            spot = at_rows(out, me, start, half)
+            slot = 4 * index
+            self.direct.append(
+                [
+                    to_side(mine, spot, send_sem.at[slot], recv_sem.at[slot], beside),
+                    to_side(mine, spot, send_sem.at[slot + 1], recv_sem.at[slot + 1], across),
+                ]
+            )
+            passing = at_rows(out, beside, start, quarter), at_rows(out, across, start + quarter, quarter)
+            self.onward.append(
+                [
+                    to_side(passing[0], passing[0], send_sem.at[slot + 2], recv_sem.at[slot + 2], across),
+                    to_side(passing[1], passing[1], send_sem.at[slot + 3], recv_sem.at[slot + 3], beside),
+                ]
+            )
+            self.early.append(
+                [
+                    pair(slot, at_rows(out, beside, start, half)),
+                    pair(slot + 1, at_rows(out, across, start, half)),
+                ]
+            )
+            self.late.append(
+                [
+                    pair(slot + 2, at_rows(out, opposite, start, quarter)),
+                    pair(slot + 3, at_rows(out, opposite, start + quarter, quarter)),
+                ]
+            )
+            self.own.append(pltpu.make_async_copy(source, at_rows(out, me, 0, rows), own_sem.at[index]))
+
+    def start(self):
+        for copies in self.direct:
+            for copy in copies:
+                copy.start()
+        for copy in self.own:
+            copy.start()
+
+    def relay(self):
+        for direct, onward, early in zip(self.direct, self.onward, self.early):
+            for turn in range(2):
+                direct[turn].wait_recv()
+                onward[turn].start()
+                early[turn].start()
+
+    def relay_last(self):
+        for onward, late in zip(self.onward, self.late):
+            for turn in range(2):
+                onward[turn].wait_recv()
+                late[turn].start()
+
+    def arrive(self, index):
+        self.own[index].wait()
+        for copy in self.early[index] + self.late[index]:
+            copy.wait_recv()
+
+    def finish(self):
+        for group in (self.direct, self.onward, self.early, self.late):
+            for copies in group:
+                for copy in copies:
+                    copy.wait_send()
+
+
+def front_kernel(
+    n_ctx,
+    x_ref,
+    gains,
+    taps,
+    conv_in,
+    conv_out,
+    gate_in,
+    up_in,
+    down_in,
+    in_out,
+    out_out,
+    gate_out,
+    up_out,
+    down_out,
+    projected,
+    convolved,
+    z_low,
+    mixed,
+    rim,
+    act_all,
+    w_in,
+    w_out,
+    w_gate,
+    w_up,
+    w_down,
+    act1,
+    act2,
+    last_rows,
+    rim_sem,
+    mix_send,
+    mix_recv,
+    mix_pair_send,
+    mix_pair_recv,
+    mix_own,
+    send_sem,
+    recv_sem,
+    pair_send,
+    pair_recv,
+    own_sem,
+    act_send,
+    act_recv,
+    act_own,
+    keep_sem,
+):
+    chain = Chain(n_ctx)
+    section = lax.axis_index("section")
+    _, beside, across, opposite = corners()
+    greet_mixed(
+        chain,
+        [{"fsdp": beside}, {"fsdp": across}, {"fsdp": opposite}, {"section": 1 - section}],
+    )
+    mixers = MixerGather(
+        (conv_in, conv_out), (w_in, w_out), mix_send, mix_recv, mix_pair_send, mix_pair_recv, mix_own
+    )
+    mixers.start()
+    columns = Columns(
+        0, (gate_in, up_in, down_in), (w_gate, w_up, w_down), send_sem, recv_sem, pair_send, pair_recv, own_sem
+    )
+    gather = SideGather(act2, act_all, act_send, act_recv, act_own)
+    keeping = [
+        pltpu.make_async_copy(src, dst, keep_sem.at[index])
+        for index, (src, dst) in enumerate(
+            ((w_in, in_out), (w_out, out_out), (w_gate, gate_out), (w_up, up_out), (w_down, down_out))
+        )
+    ]
+    rows, width = x_ref.shape
+    strip = 64
+
+    def normalize(values, gain):
+        inv_rms = lax.rsqrt(jnp.mean(values * values, axis=-1, keepdims=True) + EPSILON)
+        return (values * inv_rms * gain).astype(BF16)
+
+    def first_norm(index, carry):
+        at = pl.ds(pl.multiple_of(index * strip, strip), strip)
+        act1[at] = normalize(x_ref[at].astype(F32), gains[0:1])
+        return carry
+
+    lax.fori_loop(0, rows // strip, first_norm, 0)
+    mixers.relay()
+    columns.start()
+    mixers.relay_last()
+    mixers.arrive(0)
+    keeping[0].start()
+    wide = 512
+
+    def project(index, carry):
+        at = pl.ds(pl.multiple_of(index * wide, wide), wide)
+        projected[:, at] = dot_plain(act1[...], w_in[:, at])
+        return carry
+
+    lax.fori_loop(0, projected.shape[1] // wide, project, 0)
+    tail_at = pl.ds(rows - 16, 16)
+    last_rows[...] = (projected[tail_at, :width] * projected[tail_at, 2 * width :]).astype(BF16)
+    to_next = along(last_rows, rim, rim_sem.at[0], rim_sem.at[1], chain.place + 1)
+
+    @pl.when(chain.has_next)
+    def _():
+        to_next.start()
+
+    @pl.when(chain.has_last)
+    def _():
+        along(last_rows, rim, rim_sem.at[0], rim_sem.at[1], chain.place).wait_recv()
+
+    @pl.when(jnp.logical_not(chain.has_last))
+    def _():
+        rim[...] = jnp.zeros(rim.shape, BF16)
+
+    part = 128
+    row_at = lax.broadcasted_iota(jnp.int32, (rows, part), 0)
+
+    def convolve(index, carry):
+        def lanes(offset):
+            return pl.ds(pl.multiple_of(offset * width + index * part, part), part)
+
+        product = (projected[:, lanes(0)] * projected[:, lanes(2)]).astype(BF16).astype(F32)
+        edge = rim[:, lanes(0)].astype(F32)
+        near, far = edge[15:16], edge[14:15]
+        one = jnp.where(row_at >= 1, pltpu.roll(product, 1, 0), near)
+        two = jnp.where(row_at >= 2, pltpu.roll(product, 2, 0), jnp.where(row_at == 1, near, far))
+        tap = taps[:, lanes(0)]
+        value = tap[0:1] * two + tap[1:2] * one + tap[2:3] * product
+        convolved[:, lanes(0)] = value
+        z_low[:, lanes(0)] = (projected[:, lanes(1)] * value).astype(BF16)
+        return carry
+
+    lax.fori_loop(0, width // part, convolve, 0)
+    mixers.arrive(1)
+    keeping[1].start()
+
+    def mix(index, carry):
+        at = pl.ds(pl.multiple_of(index * wide, wide), wide)
+        mixed[:, at] = dot_plain(z_low[...], w_out[:, at])
+        return carry
+
+    lax.fori_loop(0, width // wide, mix, 0)
+
+    def second_norm(index, carry):
+        at = pl.ds(pl.multiple_of(index * strip, strip), strip)
+        act2[at] = normalize(x_ref[at].astype(F32) + mixed[at], gains[1:2])
+        return carry
+
+    lax.fori_loop(0, rows // strip, second_norm, 0)
+    gather.start()
+    gather.relay()
+    columns.relay()
+    columns.arrive()
+    for copy in keeping[2:]:
+        copy.start()
+    gather.finish()
+    columns.finish()
+    mixers.finish()
+
+    @pl.when(chain.has_next)
+    def _():
+        to_next.wait_send()
+
+    for copy in keeping:
+        copy.wait()
+
+
+def front(x_low, gains, taps, conv_in, conv_out, gate, up, down, collective_id):
+    n_ctx, count = lax.axis_size("ctx"), lax.axis_size("fsdp")
+    assert count == 4
+    rows, width = x_low.shape
+    dma = pltpu.SemaphoreType.DMA
+    vmem = pl.BlockSpec(memory_space=pltpu.VMEM)
+    hbm = pl.BlockSpec(memory_space=pl.ANY)
+
+    def whole(weight):
+        return (count * weight.shape[0], weight.shape[1])
+
+    column = (count * gate.shape[0], gate.shape[1] // count)
+    weights = [whole(conv_in), whole(conv_out), column, column, down.shape]
+    return pl.pallas_call(
+        functools.partial(front_kernel, n_ctx),
+        out_shape=tuple(jax.ShapeDtypeStruct(shape, BF16) for shape in weights)
+        + (
+            jax.ShapeDtypeStruct((rows, conv_in.shape[1]), F32),
+            jax.ShapeDtypeStruct((rows, width), F32),
+            jax.ShapeDtypeStruct((rows, width), BF16),
+            jax.ShapeDtypeStruct((rows, width), F32),
+            jax.ShapeDtypeStruct((16, width), BF16),
+            jax.ShapeDtypeStruct((count * rows, width), BF16),
+        ),
+        in_specs=[vmem] * 3 + [hbm] * 5,
+        out_specs=[hbm] * 5 + [vmem] * 6,
+        scratch_shapes=[pltpu.VMEM(shape, BF16) for shape in weights]
+        + [
+            pltpu.VMEM((rows, width), BF16),
+            pltpu.VMEM((rows, width), BF16),
+            pltpu.VMEM((16, width), BF16),
+            dma((2,)),
+            dma((8,)),
+            dma((8,)),
+            dma((8,)),
+            dma((8,)),
+            dma((2,)),
+            dma((2, count)),
+            dma((2, count)),
+            dma((3, count)),
+            dma((3, count)),
+            dma((3,)),
+            dma((4,)),
+            dma((4,)),
+            dma,
+            dma((5,)),
+        ],
+        compiler_params=pltpu.CompilerParams(
+            collective_id=collective_id, has_side_effects=True, vmem_limit_bytes=58 << 20
+        ),
+        cost_estimate=busy(70),
+    )(x_low, gains, taps, conv_in, conv_out, gate, up, down)
+
+
+def ffn_forward(act, w_gate, w_up, w_down):
     gate_pre = matmul(act, w_gate)
     up_pre = matmul(act, w_up)
     hidden = (jax.nn.silu(gate_pre) * up_pre).astype(BF16)
-    return matmul(hidden, w_down).astype(BF16), (normed, inv_rms, act, gate_pre, up_pre, hidden)
+    return matmul(hidden, w_down).astype(BF16), (act, gate_pre, up_pre, hidden)
 
 
 def ffn_backward(d_all, kept, w_gate, w_up, w_down):
-    _, _, act, gate_pre, up_pre, hidden = kept
+    act, gate_pre, up_pre, hidden = kept
     d_hidden = matmul_right(d_all, w_down)
     sigmoid = jax.nn.sigmoid(gate_pre)
     d_up = (d_hidden * gate_pre * sigmoid).astype(BF16)
@@ -1633,8 +1828,8 @@
     return terms, grads
 
 
-def ffn_norm_back(d_act, kept, gain):
-    normed, inv_rms = kept[:2]
+def ffn_norm_back(d_act, residual, gain):
+    normed, inv_rms = norm_rows(residual)
     return norm_back(d_act * gain, normed, inv_rms), jnp.sum(d_act * normed, axis=0)
 
 
@@ -1673,8 +1868,6 @@
         return lax.all_gather(mine, ("fsdp", "section"), axis=0, tiled=True)
 
     part = ffn_gate.shape[1]
-    in_full, out_full = mixer_weights(conv_in, conv_out, 2)
-    gate1, up1, down1 = column_weights(ffn_gate[0], ffn_up[0], ffn_down[0], 0, 7)
     query_full, key_full, value_full, proj_full = (
         whole_rows(attn_q),
         whole_rows(attn_k),
@@ -1682,27 +1875,13 @@
         whole_rows(attn_out),
     )
 
-    x = lax.dynamic_index_in_dim(inputs, section, keepdims=False).astype(F32)
-    normed0, inv0 = norm_rows(x)
-    act1 = (normed0 * norm_gains[0]).astype(BF16)
-    projected = matmul(act1, in_full)
-    b_gate, c_gate, x_value = (
-        projected[:, :width],
-        projected[:, width : 2 * width],
-        projected[:, 2 * width :],
-    )
-    b_product = (b_gate * x_value).astype(BF16)
-    rim = passed_along(b_product[-2:], "ctx", 1)
-    extended = jnp.concatenate([rim, b_product], axis=0).astype(F32)
-    convolved = (
-        conv_kernel[0] * extended[:-2]
-        + conv_kernel[1] * extended[1:-1]
-        + conv_kernel[2] * extended[2:]
-    )
-    z_low = (c_gate * convolved).astype(BF16)
-    mixed = matmul(z_low, out_full)
+    x_low = lax.dynamic_index_in_dim(inputs, section, keepdims=False)
+    in_full, out_full, gate1, up1, down1, projected, convolved, z_low, mixed, rim, act_all1 = front(
+        x_low, norm_gains, conv_kernel, conv_in, conv_out, ffn_gate[0], ffn_up[0], ffn_down[0], 2
+    )
+    x = x_low.astype(F32)
     res1 = x + mixed
-    terms1, kept1 = ffn_forward(res1, norm_gains[1], gate1, up1, down1)
+    terms1, kept1 = ffn_forward(act_all1, gate1, up1, down1)
     ffn1 = reduced(terms1, 1)
     h_low = (res1 + ffn1).astype(BF16)
 
@@ -1730,7 +1909,9 @@
     attended_low = attended.astype(BF16)
     attn_rows = matmul(attended_low, proj_full)
     res2 = h + attn_rows
-    terms2, kept2 = ffn_forward(res2, norm_gains[3], gate2, up2, down2)
+    normed3, _ = norm_rows(res2)
+    act_all2 = gathered((normed3 * norm_gains[3]).astype(BF16), 0)
+    terms2, kept2 = ffn_forward(act_all2, gate2, up2, down2)
 
     d_sum = d_sum_low.astype(F32)
     d_terms2, grads2 = ffn_backward(d_sum_all, kept2, gate2, up2, down2)
@@ -1749,12 +1930,17 @@
     d_act3, got_gu, got_down = reduced_swapping(
         d_terms2, column_half(1 - section), down_half(1 - section), 8
     )
-    d_ffn, gain3 = ffn_norm_back(d_act3, kept2, norm_gains[3])
+    d_ffn, gain3 = ffn_norm_back(d_act3, res2, norm_gains[3])
     d_res2 = d_sum + d_ffn
     d_attn = d_res2.astype(BF16)
     grad_proj = matmul_left(attended_low, d_attn)
     d_att = matmul_right(d_attn, proj_full).astype(BF16)
     delta = jnp.sum((d_att.astype(F32) * attended).reshape(rows, q_heads, head), axis=-1)
+    shared_terms = tuple(
+        (mine.astype(F32) + got.astype(F32)).astype(BF16)
+        for mine, got in ((column_half(section), got_gu), (down_half(section), got_down))
+    )
+    d_att, shared_terms = lax.optimization_barrier((d_att, shared_terms))
     d_query, d_kv, ffn2 = attend_back(
         length.reshape(1), query, kv_all, d_att, log_total, delta.T.reshape(q_heads, 1, rows), terms2, 4
     )
@@ -1765,10 +1951,7 @@
 
     squares = [square(v) for v in (x, mixed, ffn1, h, attn_rows, res2, ffn2, result)]
     second_gu, second_down = (
-        lax.psum_scatter(
-            (mine.astype(F32) + got.astype(F32)).astype(BF16), "ctx", scatter_dimension=0, tiled=True
-        )
-        for mine, got in ((column_half(section), got_gu), (down_half(section), got_down))
+        lax.psum_scatter(term, "ctx", scatter_dimension=0, tiled=True) for term in shared_terms
     )
     d_qn = rounded(d_query)
     grad_qgain = jnp.sum(jnp.sum(d_qn * q_normed, axis=0).reshape(q_heads, head), axis=0)
@@ -1789,11 +1972,19 @@
     second_gu = lax.all_gather(second_gu, "ctx", axis=0)
     second_down = lax.all_gather(second_down, "ctx", axis=0, tiled=True)
     d_terms1, grads1 = ffn_backward(d_h_all, kept1, gate1, up1, down1)
-    d_ffn1, gain1 = ffn_norm_back(reduced(d_terms1, 1), kept1, norm_gains[1])
+    d_ffn1, gain1 = ffn_norm_back(reduced(d_terms1, 1), res1, norm_gains[1])
     d_ffn1, second_gu = lax.optimization_barrier((d_ffn1, second_gu))
     d_res1 = d_h_low.astype(F32) + d_ffn1
     d_mixed = d_res1.astype(BF16)
     grad_out = matmul_left(z_low, d_mixed)
+    normed0, inv0 = norm_rows(x)
+    act1 = (normed0 * norm_gains[0]).astype(BF16)
+    b_gate, c_gate, x_value = (
+        projected[:, :width],
+        projected[:, width : 2 * width],
+        projected[:, 2 * width :],
+    )
+    extended = jnp.concatenate([rim[14:], (b_gate * x_value).astype(BF16)], axis=0).astype(F32)
     d_z = matmul_right(d_mixed, out_full)
     d_cgate = d_z * convolved
     d_conv = d_z * c_gate

time: 768 us -> 761 us (level)
  local copies, waits for them, and re-layouts: 54.8 us -> 28.5 us
  Pallas kernels: 514 us -> 528 us
    pallas_call x2 -> x1, Pallas kernels: 47 us -> 18.7 us  [gathered(): pl.pallas_call(gather_kernel, out_shape=jax.ShapeDtypeStruct((4 * rows, w...]
    unnamed x225 -> x129, local copies, waits for them, and re-layouts: 34 us -> 6.39 us
    pallas_call x2 -> x1, Pallas kernels: 84.7 us -> 106 us  [front(): pl.pallas_call(functools.partial(front_kernel, n_ctx), out_shape=tuple((j...]
    pallas_call x1, Pallas kernels: 70.8 us -> 80 us  [attend_back(): pl.pallas_call(functools.partial(attend_back_kernel, n_ctx), out_shape=(w...]
    pallas_call x1, Pallas kernels: 45.2 us -> 53.1 us  [attend(): pl.pallas_call(functools.partial(attend_kernel, n_ctx), out_shape=(jax.Sh...]
    dot_general x12 -> x10, matrix products: 40 us -> 36.3 us  [matmul(): return jnp.dot(left_op, right_op, preferred_element_type=F32)]
  transfers between devices with their start and end apart: 11 -> 10, of which waited for: 1 -> 1; matrix products, arithmetic and copies ran while one was open for 15% -> 15% of each run, Pallas kernels for 37% -> 41%
where the time goes in v8:
time: 761 us; the launch traced here: 752 us
  Pallas kernels  528 us (69%)
  matrix products  126 us (17%)
  other arithmetic  43.3 us (6%)
  local copies, waits for them, and re-layouts  28.5 us (4%)
  between operations  16.5 us (2%)
    pallas_call x1, Pallas kernels, summed_gradients(): pl.pallas_call(functools.partial(tail_kernel, (n_ctx, n_fsdp)), out_shape...  185 us
    pallas_call x1, Pallas kernels, front(): pl.pallas_call(functools.partial(front_kernel, n_ctx), out_shape=tuple((j...  106 us
    pallas_call x1, Pallas kernels, attend_back(): pl.pallas_call(functools.partial(attend_back_kernel, n_ctx), out_shape=(w...  80 us
    pallas_call x1, Pallas kernels, attend(): pl.pallas_call(functools.partial(attend_kernel, n_ctx), out_shape=(jax.Sh...  53.1 us
    pallas_call x2, Pallas kernels, reduced(): pl.pallas_call(reduce_kernel, out_shape=jax.ShapeDtypeStruct((rows, width...  41.7 us
    dot_general x13, matrix products, matmul_left(): lax.dot_general(left_op, right_op, (((0,), (0,)), ((), ())), preferred_el...  40.2 us
    dot_general x12, matrix products, matmul_right(): lax.dot_general(left_op, right_op, (((1,), (1,)), ((), ())), preferred_el...  40 us
    dot_general x10, matrix products, matmul(): return jnp.dot(left_op, right_op, preferred_element_type=F32)  36.3 us
  transfers between devices with their start and end apart: 10, of which 1 were waited for; matrix products, arithmetic and copies ran while one was open for 15% of the time, Pallas kernels for 41%

profile of v8, /device:TPU:0, one launch (start us, length us, event | category | flops | bytes accessed | tf_op | source)
XLA Modules:
  0.0 752.3 jit_solution(16124205975732450575)
XLA Ops:
  14.1 105.7 %shard_map.262 = (bf16[1024,3072]{1,0:T(8,128)(2,1)}, bf16[1024,1024]{1,0:T(8,128)(2,1)}, bf16[1024,1152]{1,0:T(8,128)(2,1)}, bf16[1024,1152]{1,0:T(8,128)(2,1)}...) custom-call(bf16[256,1024]{1,0:T(8,128)(2,1)} %dynamic-slice_bitcast, ...), custom_call_target="tpu_custom_call" | custom-call | flops 70 | bytes 65536 | tf_op jit(solution)/shard_map/pallas_call | solution.py:1768
  119.8 5.3 fusion.123
  125.2 4.5 multiply_convert_fusion.5
  132.8 24.1 %shard_map.263 = f32[256,1024]{1,0:T(8,128)S(1)} custom-call(bf16[1024,1024]{1,0:T(8,128)(2,1)S(1)} %convolution_convert_fusion.7.blocks), custom_call_target="tpu_custom_call" | custom-call | flops 25 | bytes 65536 | tf_op jit(solution)/shard_map/pallas_call | solution.py:334
  173.9 53.1 %shard_map.264 = (f32[256,1024]{1,0:T(8,128)}, f32[16,1,256]{2,1,0:T(1,128)}, bf16[1024,1024]{1,0:T(8,128)(2,1)}, bf16[1024,1024]{1,0:T(8,128)(2,1)}, bf16[1024,...) custom-call(s32[1]{0:T(128)} %dynamic_slice.48.length_ref, ...), custom_call_target="tpu_custom_call" | custom-call | flops 50 | bytes 65536 | tf_op jit(solution)/shard_map/pallas_call | solution.py:1324
  231.9 18.7 %shard_map.265 = bf16[1024,1024]{1,0:T(8,128)(2,1)S(1)} custom-call(bf16[256,1024]{1,0:T(8,128)(2,1)S(1)} %multiply_convert_fusion.8.block), custom_call_target="tpu_custom_call" | custom-call | flops 25 | bytes 65536 | tf_op jit(solution)/shard_map/pallas_call | solution.py:146
  250.6 4.7 fusion.124
  258.2 4.6 multiply_convert_fusion.2
  282.1 18.3 %shard_map.266 = (f32[256,1024]{1,0:T(8,128)S(1)}, bf16[1024,1152]{1,0:T(8,128)(2,1)S(1)}, bf16[576,1024]{1,0:T(8,128)(2,1)S(1)}) custom-call(bf16[1024,1024]{1,0:T(8,128)(2,1)S(1)} %add_convert_fusion.1.blocks, bf16[1024,1152]{1,0:T(8,128)(2,1)S(1)} %bitcast.139, bf16[576,1024]{1,0:T(8,128)(2,1)S(1)} %constant_dynamic-slice_fusion.3.give_b), custom_call_target="tpu_custom_call" | custom-call | flops 25 | bytes 65536 | tf_op jit(solution)/shard_map/pallas_call | solution.py:312
  304.6 4.2 fusion
  314.0 6.6 convolution_convert_fusion.6.blocks
  320.6 80.0 %shard_map.267 = (f32[256,1024]{1,0:T(8,128)}, f32[256,1024]{1,0:T(8,128)}, f32[256,1024]{1,0:T(8,128)}) custom-call(s32[1]{0:T(128)} %dynamic_slice.48.length_ref, bf16[256,1024]{1,0:T(8,128)(2,1)} %get-tuple-element.117.query, bf16[1024,1024]{1,0:T(8,128)(2,1)} %get-tuple-element.62.kv_all, bf16[256,1024]{1,0:T(8,128)(2,1)} %get-tuple-element.65.d_out, ...), custom_call_target="tpu_custom_call" | custom-call | flops 50 | bytes 65536 | tf_op jit(solution)/shard_map/pallas_call | solution.py:1479
  417.4 25.5 %shard_map.268 = (bf16[1024,1024]{1,0:T(8,128)(2,1)S(1)}, bf16[4,64,1152]{2,1,0:T(8,128)(2,1)}) custom-call(bf16[256,1024]{1,0:T(8,128)(2,1)S(1)} %fusion.45.block, bf16[4,64,1152]{2,1,0:T(8,128)(2,1)S(1)} %bitcast.140), custom_call_target="tpu_custom_call" | custom-call | flops 25 | bytes 65536 | tf_op jit(solution)/shard_map/pallas_call | solution.py:188
  457.6 5.9 convolution_convert_fusion.down_in
  463.6 6.7 multiply_convert_fusion
  473.2 4.2 convolution_convert_fusion.1.up_in
  480.6 4.2 convolution_convert_fusion.2.gate_in
  484.8 17.6 %shard_map.269 = f32[256,1024]{1,0:T(8,128)S(1)} custom-call(bf16[1024,1024]{1,0:T(8,128)(2,1)S(1)} %add_convert_fusion.blocks), custom_call_target="tpu_custom_call" | custom-call | flops 25 | bytes 65536 | tf_op jit(solution)/shard_map/pallas_call | solution.py:334
  503.3 4.3 fusion.59
  515.4 6.5 all-gather.16.cloned.1.call-done.second_down_in
  529.5 5.7 fusion.54
  537.8 185.5 %shard_map.270 = (bf16[2,256,4608]{2,1,0:T(8,128)(2,1)}, bf16[1152,1024]{1,0:T(8,128)(2,1)}, bf16[2,960,1024]{2,1,0:T(8,128)(2,1)}) custom-call(bf16[1024,1152]{1,0:T(8,128)(2,1)} %convolution_convert_fusion.2.gate_in, bf16[1024,1152]{1,0:T(8,128)(2,1)} %convolution_convert_fusion.1.up_in, bf16[1152,1024]{1,0:T(8,128)(2,1)} %convolution_convert_fusion.down_in, ...), custom_call_target="tpu_custom_call" | custom-call | flops 160 | bytes 65536 | tf_op jit(solution)/shard_map/pallas_call | solution.py:950
  723.3 4.2 fusion.118
  729.8 5.0 slice_convert_fusion
  (281 shorter events, 130.8 us)
Async XLA Ops:
  7.2 6.0 copy-start.22
  7.2 154.8 %all-gather.10.cloned.1.call-start = ((), (), s32[]{:S(2)}) async-start(), calls=%async_computation.3 | async-start | bytes 1179648 | tf_op jit(solution)/shard_map/all_gather | solution.py:1868
  9.0 155.2 %all-gather.12.cloned.1.call-start = ((), (), s32[]{:S(2)}) async-start(), calls=%async_computation.4 | async-start | bytes 1179648 | tf_op jit(solution)/shard_map/all_gather | solution.py:1868
  10.6 157.7 %all-gather.8.cloned.1.call-start = ((), (), s32[]{:S(2)}) async-start(), calls=%async_computation.2 | async-start | bytes 2359296 | tf_op jit(solution)/shard_map/all_gather | solution.py:1868
  11.4 215.7 %all-gather.14.cloned.1.call-start = ((), (), s32[]{:S(2)}) async-start(), calls=%async_computation.5 | async-start | bytes 2359296 | tf_op jit(solution)/shard_map/all_gather | solution.py:1868
  13.2 403.2 %reduce-scatter.3.cloned.1.call-start = ((), (), s32[]{:S(2)}) async-start(), calls=%async_computation.6 | async-start | bytes 2949120 | tf_op jit(solution)/shard_map/reduce_scatter | solution.py:1954
  132.8 24.2 %copy-start.45 = (f32[2,64]{1,0:T(2,128)S(1)}, f32[2,64]{1,0:T(2,128)}, u32[]{:S(2)}) copy-start(f32[2,64]{1,0:T(2,128)} %param.26) | copy-start | bytes 1540
  132.8 24.4 %copy-start.58 = (s32[8]{0:T(128)S(1)}, s32[8]{0:T(128)}, u32[]{:S(2)}) copy-start(s32[8]{0:T(128)} %param.17) | copy-start | bytes 100
  132.8 25.6 %copy-start.13 = (f32[256,1024]{1,0:T(8,128)S(1)}, f32[256,1024]{1,0:T(8,128)}, u32[]{:S(2)}) copy-start(f32[256,1024]{1,0:T(8,128)} %get-tuple-element.51) | copy-start | bytes 3145732
  159.8 67.3 %copy-start.9 = (bf16[256,1024]{1,0:T(8,128)(2,1)}, bf16[256,1024]{1,0:T(8,128)(2,1)S(1)}, u32[]{:S(2)}) copy-start(bf16[256,1024]{1,0:T(8,128)(2,1)S(1)} %get-tuple-element.120) | copy-start | bytes 1572868
  231.9 18.7 %copy-start.51 = (bf16[1152,1024]{1,0:T(8,128)(2,1)S(1)}, bf16[1152,1024]{1,0:T(8,128)(2,1)}, u32[]{:S(2)}) copy-start(bf16[1152,1024]{1,0:T(8,128)(2,1)} %get-tuple-element.58) | copy-start | bytes 7077892
  262.7 6.4 copy-start.61
  282.1 18.3 %copy-start.4 = (f32[256,1024]{1,0:T(8,128)S(1)}, f32[256,1024]{1,0:T(8,128)}, u32[]{:S(2)}) copy-start(f32[256,1024]{1,0:T(8,128)} %copy-done.3) | copy-start | bytes 3145732
  312.5 145.1 %reduce-scatter.5.cloned.1.call-start = ((), (), s32[]{:S(2)}) async-start(), calls=%async_computation.7 | async-start | bytes 1474560 | tf_op jit(solution)/shard_map/reduce_scatter | solution.py:1954
  404.7 98.6 %all-gather.18.cloned.1.call-start = ((), (), s32[]{:S(2)}) async-start(), calls=%async_computation.9 | async-start | bytes 2949120 | tf_op jit(solution)/shard_map/all_gather | solution.py:1972
  443.0 78.9 %all-gather.16.cloned.1.call-start = ((), (), s32[]{:S(2)}) async-start(), calls=%async_computation.8 | async-start | bytes 1474560 | tf_op jit(solution)/shard_map/all_gather | solution.py:1973
  463.6 6.7 copy-start.48
  484.8 17.6 %copy-start.15 = (f32[256,1024]{1,0:T(8,128)S(1)}, f32[256,1024]{1,0:T(8,128)}, u32[]{:S(2)}) copy-start(f32[256,1024]{1,0:T(8,128)} %get-tuple-element.51) | copy-start | bytes 3145732
  484.8 17.6 %copy-start.23 = (bf16[2,256,1024]{2,1,0:T(8,128)(2,1)S(1)}, bf16[2,256,1024]{2,1,0:T(8,128)(2,1)}, u32[]{:S(2)}) copy-start(bf16[2,256,1024]{2,1,0:T(8,128)(2,1)} %param.15) | copy-start | bytes 3145732
  508.0 13.9 %collective-permute-start = (f32[2,1024]{1,0:T(2,128)S(1)}, f32[2,1024]{1,0:T(2,128)S(1)}, u32[]{:S(2)}, u32[]{:S(2)}) collective-permute-start(f32[2,1024]{1,0:T(2,128)S(1)} %pad_add_fusion.1), channel_id=1, source_target_pairs={{4,0},{8,4},{12,8},{5,1},{9,5},{13,9},{6,2},{10,6},{14,10},{7,3},{... | collective-permute-start | bytes 24584 | tf_op jit(solution)/shard_map/ppermute | solution.py:20
  723.3 6.5 slice-start
  723.3 6.5 slice-start.1
  729.7 6.0 copy-start.29
  740.3 3.5 collective-permute-start.1
  (50 other events, 143.1 us)
Sparse Core Ops, SparseCore 0:
  10.5 30.6 all-gather.9
  43.6 31.7 all-gather.11
  77.8 39.7 all-gather.7
  120.0 33.7 all-gather.13
  312.6 73.9 reduce-scatter.2
  404.8 26.4 reduce-scatter.4
  443.1 47.7 all-gather.17
  492.4 29.4 all-gather.15

commit v9 on v8

--- a/solution.py
+++ b/solution.py
@@ -415,7 +415,9 @@
     n_mix = len(mixers)
     cut = 3 * half // b_rows
     c_parts = ((0, cut), (cut, c_rows // b_rows))
-    ticks = a_chunks
+    paired = a_chunks // 2
+    mix_chunks = b_chunks - down_chunks
+    ticks = paired + mix_chunks // 2
     tail = 2 * (n_ctx - 1)
 
     barrier = pltpu.get_barrier_semaphore()
@@ -676,12 +678,11 @@
         ]
         return kind, owner, spot
 
-    def hand_out(k, way):
+    def a_hand_out(k, way):
         kind, owner, spot = a_target(k, way)
         is_mine = (section == 0) & (group == owner)
         slot = 2 * k + way
-        a_ref, b_ref = a_at(a_done, k, way), b_at(b_done, k, way)
-        lanes_at = pl.ds(way * b_part, b_part)
+        a_ref = a_at(a_done, k, way)
 
         @pl.when(is_mine)
         def _():
@@ -698,90 +699,157 @@
                 device_id_type=MESH,
             ).start()
 
-        @pl.when(k < down_chunks)
+    def down_hand_out(k, way):
+        slot = 2 * k + way
+        b_ref = b_at(b_done, k, way)
+        at = down_out.at[
+            pl.ds(pl.multiple_of(section * down_half + k * b_rows, b_rows), b_rows),
+            pl.ds(way * b_part, b_part),
+        ]
+
+        @pl.when(section == 0)
         def _():
-            at = down_out.at[pl.ds(pl.multiple_of(section * down_half + k * b_rows, b_rows), b_rows), lanes_at]
-
-            @pl.when(section == 0)
-            def _():
-                pltpu.make_async_copy(b_ref, at, b_out_send.at[slot]).start()
-
-            @pl.when(section == 1)
-            def _():
-                pltpu.make_async_remote_copy(
-                    src_ref=b_ref,
-                    dst_ref=at,
-                    send_sem=b_out_send.at[slot],
-                    recv_sem=down_recv,
-                    device_id={"section": 0},
-                    device_id_type=MESH,
-                ).start()
-
-        @pl.when(k >= down_chunks)
+            pltpu.make_async_copy(b_ref, at, b_out_send.at[slot]).start()
+
+        @pl.when(section == 1)
         def _():
-            at = rest_out.at[
-                section, pl.ds(pl.multiple_of((k - down_chunks) * b_rows, b_rows), b_rows), lanes_at
-            ]
-            pltpu.make_async_copy(b_ref, at, b_keep_sem.at[slot]).start()
             pltpu.make_async_remote_copy(
                 src_ref=b_ref,
                 dst_ref=at,
                 send_sem=b_out_send.at[slot],
-                recv_sem=rest_recv,
-                device_id={"section": other},
+                recv_sem=down_recv,
+                device_id={"section": 0},
                 device_id_type=MESH,
             ).start()
 
-    def chain_copies(k, way, target, buffers, sems):
+    def mix_hand_out(k, way):
         slot = 2 * k + way
-        return [
-            pltpu.make_async_remote_copy(
-                src_ref=at,
-                dst_ref=at,
-                send_sem=send.at[slot],
-                recv_sem=recv.at[slot],
-                device_id={"ctx": target},
-                device_id_type=MESH,
-            )
-            for at, (send, recv) in zip((a_at(buffers[0], k, way), b_at(buffers[1], k, way)), sems)
+        b_ref = b_at(b_done, k, way)
+        at = rest_out.at[
+            section,
+            pl.ds(pl.multiple_of((k - down_chunks) * b_rows, b_rows), b_rows),
+            pl.ds(way * b_part, b_part),
         ]
-
-    def up_copies(k, way, target):
-        return chain_copies(
-            k, way, target, (a_sum, b_sum), ((a_up_send, a_up_recv), (b_up_send, b_up_recv))
+        pltpu.make_async_copy(b_ref, at, b_keep_sem.at[slot]).start()
+        pltpu.make_async_remote_copy(
+            src_ref=b_ref,
+            dst_ref=at,
+            send_sem=b_out_send.at[slot],
+            recv_sem=rest_recv,
+            device_id={"section": other},
+            device_id_type=MESH,
+        ).start()
+
+    def chain_copy(at, sems, slot, target):
+        return pltpu.make_async_remote_copy(
+            src_ref=at,
+            dst_ref=at,
+            send_sem=sems[0].at[slot],
+            recv_sem=sems[1].at[slot],
+            device_id={"ctx": target},
+            device_id_type=MESH,
         )
 
-    def back_copies(k, way, target):
-        return chain_copies(
-            k, way, target, (a_done, b_done), ((a_back_send, a_back_recv), (b_back_send, b_back_recv))
-        )
-
-    def a_load(buffer, k, way):
-        return buffer[k, pl.ds(way * a_part, a_part)].astype(F32)
-
-    def b_load(buffer, k, way):
-        return buffer[k, :, pl.ds(way * b_part, b_part)].astype(F32)
-
-    def a_store(buffer, k, way, value):
-        buffer[k, pl.ds(way * a_part, a_part)] = value.astype(BF16)
-
-    def b_store(buffer, k, way, value):
-        buffer[k, :, pl.ds(way * b_part, b_part)] = value.astype(BF16)
-
-    def own_terms(k, way):
+    class Gates:
+        hand_out = staticmethod(a_hand_out)
+
+        @staticmethod
+        def view(buffer, k, way):
+            return a_at(buffer, k, way)
+
+        own, sums, done = a_own, a_sum, a_done
+        up, back = (a_up_send, a_up_recv), (a_back_send, a_back_recv)
+
+        @staticmethod
+        def term(k, way):
+            slot = 2 * k + way
+            at = a_at(a_own, k, way)
+            pltpu.make_async_copy(at, at, own_sem.at[slot]).wait()
+            pltpu.make_async_copy(at, at, pair_recv.at[slot]).wait()
+            return at[...].astype(F32) + a_at(a_other, k, way)[...].astype(F32)
+
+    class Downs:
+        hand_out = staticmethod(down_hand_out)
+
+        @staticmethod
+        def view(buffer, k, way):
+            return b_at(buffer, k, way)
+
+        own, sums, done = b_own, b_sum, b_done
+        up, back = (b_up_send, b_up_recv), (b_back_send, b_back_recv)
+
+        @staticmethod
+        def term(k, way):
+            slot = 2 * a_chunks + 2 * k + way
+            at = b_at(b_own, k, way)
+            pltpu.make_async_copy(at, at, own_sem.at[slot]).wait()
+            pltpu.make_async_copy(at, at, pair_recv.at[slot]).wait()
+            return at[...].astype(F32) + b_at(b_other, k, way)[...].astype(F32)
+
+    class Mixed(Downs):
+        hand_out = staticmethod(mix_hand_out)
+
+        @staticmethod
+        def term(k, way):
+            return b_at(b_own, k, way)[...].astype(F32)
+
+    def upward(item, k, way, rank, ahead, behind):
         slot = 2 * k + way
-        at = a_at(a_own, k, way)
-        pltpu.make_async_copy(at, at, own_sem.at[slot]).wait()
-        pltpu.make_async_copy(at, at, pair_recv.at[slot]).wait()
-
-        @pl.when(k < down_chunks)
+        term = item.term(k, way)
+        sums = item.view(item.sums, k, way)
+
+        @pl.when(rank == 0)
         def _():
-            at = b_at(b_own, k, way)
-            pltpu.make_async_copy(at, at, own_sem.at[2 * a_chunks + slot]).wait()
-            pltpu.make_async_copy(at, at, pair_recv.at[2 * a_chunks + slot]).wait()
-            b_store(b_own, k, way, b_load(b_own, k, way) + b_load(b_other, k, way))
-
-        return a_load(a_own, k, way) + a_load(a_other, k, way), b_load(b_own, k, way)
+            sums[...] = term.astype(BF16)
+
+        @pl.when(rank > 0)
+        def _():
+            chain_copy(sums, item.up, slot, behind).wait_recv()
+
+        @pl.when((rank > 0) & (rank < n_ctx - 1))
+        def _():
+            sums[...] = (term + sums[...].astype(F32)).astype(BF16)
+
+        @pl.when(rank < n_ctx - 1)
+        def _():
+            chain_copy(sums, item.up, slot, ahead).start()
+
+        @pl.when(rank == n_ctx - 1)
+        def _():
+            done = item.view(item.done, k, way)
+            done[...] = (term + sums[...].astype(F32)).astype(BF16)
+            chain_copy(done, item.back, slot, behind).start()
+            item.hand_out(k, way)
+
+    def backward(item, k, way, rank, ahead, behind):
+        slot = 2 * k + way
+        done = item.view(item.done, k, way)
+        chain_copy(done, item.back, slot, ahead).wait_recv()
+
+        @pl.when(rank > 0)
+        def _():
+            chain_copy(done, item.back, slot, behind).start()
+
+        item.hand_out(k, way)
+
+    def on_step(action, step, active, *where):
+        early = active & (step < paired)
+
+        @pl.when(early)
+        def _():
+            at = jnp.clip(step, 0, paired - 1)
+            for index in range(2):
+                action(Gates, 2 * at + index, *where)
+
+            @pl.when(lax.rem(at, 4) < 3)
+            def _():
+                action(Downs, 3 * (at // 4) + lax.rem(at, 4), *where)
+
+        @pl.when(active & jnp.logical_not(early))
+        def _():
+            at = jnp.clip(step - paired, 0, mix_chunks // 2 - 1)
+            for index in range(2):
+                action(Mixed, down_chunks + 2 * at + index, *where)
 
     lanes = []
     for way in range(2):
@@ -791,7 +859,7 @@
         lanes.append((way, rank, ahead, behind))
 
     def tick_step(tick, carry):
-        for part, start in ((0, 2), (1, 6)):
+        for part, start in ((0, 1), (1, 5)):
             for owner in range(n_fsdp):
 
                 @pl.when(tick == start + owner)
@@ -799,12 +867,12 @@
                     mixer_sum(part, owner)
 
         events = (
-            (5, mixer_out, 0),
-            (9, mixer_out, 1),
-            (10, mixer_on, 0),
-            (down_chunks, mixer_in, 0),
-            (16, mixer_on, 1),
-            (down_chunks + cut, mixer_in, 1),
+            (4, mixer_out, 0),
+            (8, mixer_out, 1),
+            (9, mixer_on, 0),
+            (13, mixer_on, 1),
+            (paired - 1, mixer_in, 0),
+            (paired + 3, mixer_in, 1),
         )
         for moment, action, part in events:
 
@@ -814,54 +882,17 @@
 
         for way, rank, ahead, behind in lanes:
             step = tick - 2 * rank
-            k = jnp.clip(step, 0, ticks - 1)
-
-            @pl.when((step >= 0) & (step < ticks))
-            def _(k=k, way=way, rank=rank, ahead=ahead, behind=behind):
-                a_term, b_term = own_terms(k, way)
-
-                @pl.when(rank == 0)
-                def _():
-                    a_store(a_sum, k, way, a_term)
-                    b_store(b_sum, k, way, b_term)
-
-                @pl.when(rank > 0)
-                def _():
-                    for copy in up_copies(k, way, behind):
-                        copy.wait_recv()
-
-                @pl.when((rank > 0) & (rank < n_ctx - 1))
-                def _():
-                    a_store(a_sum, k, way, a_term + a_load(a_sum, k, way))
-                    b_store(b_sum, k, way, b_term + b_load(b_sum, k, way))
-
-                @pl.when(rank < n_ctx - 1)
-                def _():
-                    for copy in up_copies(k, way, ahead):
-                        copy.start()
-
-                @pl.when(rank == n_ctx - 1)
-                def _():
-                    a_store(a_done, k, way, a_term + a_load(a_sum, k, way))
-                    b_store(b_done, k, way, b_term + b_load(b_sum, k, way))
-                    for copy in back_copies(k, way, behind):
-                        copy.start()
-                    hand_out(k, way)
-
+            on_step(upward, step, (step >= 0) & (step < ticks), way, rank, ahead, behind)
             late = tick - 2 * (tail - rank)
-            j = jnp.clip(late, 0, ticks - 1)
-
-            @pl.when((late >= 0) & (late < ticks) & (rank < n_ctx - 1))
-            def _(j=j, way=way, rank=rank, ahead=ahead, behind=behind):
-                for copy in back_copies(j, way, ahead):
-                    copy.wait_recv()
-
-                @pl.when(rank > 0)
-                def _():
-                    for copy in back_copies(j, way, behind):
-                        copy.start()
-
-                hand_out(j, way)
+            on_step(
+                backward,
+                late,
+                (late >= 0) & (late < ticks) & (rank < n_ctx - 1),
+                way,
+                rank,
+                ahead,
+                behind,
+            )
 
         return carry
 
@@ -885,15 +916,15 @@
             def _(b_ref=b_ref, slot=slot):
                 pltpu.make_async_copy(b_ref, b_ref, pair_send.at[2 * a_chunks + slot]).wait()
 
-            @pl.when(rank < n_ctx - 1)
-            def _(k=k, way=way, ahead=ahead):
-                for copy in up_copies(k, way, ahead):
-                    copy.wait_send()
-
-            @pl.when(rank > 0)
-            def _(k=k, way=way, behind=behind):
-                for copy in back_copies(k, way, behind):
-                    copy.wait_send()
+            for item in (Gates, Mixed):
+
+                @pl.when(rank < n_ctx - 1)
+                def _(item=item, slot=slot, k=k, way=way, ahead=ahead):
+                    chain_copy(item.view(item.sums, k, way), item.up, slot, ahead).wait_send()
+
+                @pl.when(rank > 0)
+                def _(item=item, slot=slot, k=k, way=way, behind=behind):
+                    chain_copy(item.view(item.done, k, way), item.back, slot, behind).wait_send()
 
             pltpu.make_async_copy(a_ref, a_ref, a_out_send.at[slot]).wait()
             pltpu.make_async_copy(b_ref, b_ref, b_out_send.at[slot]).wait()
@@ -904,7 +935,7 @@
 
         return carry
 
-    lax.fori_loop(0, ticks, settle, 0)
+    lax.fori_loop(0, a_chunks, settle, 0)
     pltpu.make_async_copy(second_gu_in, second_gu_in, second_send.at[0]).wait()
     pltpu.make_async_copy(second_down_in, second_down_in, second_send.at[1]).wait()
 
@@ -943,6 +974,7 @@
     down_chunks = down.shape[0] // 2 // b_rows
     b_chunks = down_chunks + c_rows // b_rows + 1
     assert a_chunks == b_chunks and c_rows % b_rows == 0
+    assert down_chunks * 8 == a_chunks * 3 and (b_chunks - down_chunks) % 2 == 0
     rest = b_chunks - down_chunks
     dma = pltpu.SemaphoreType.DMA
     loads = 2 * (a_chunks + down_chunks)
@@ -1806,6 +1838,292 @@
     )(x_low, gains, taps, conv_in, conv_out, gate, up, down)
 
 
+def back_kernel(
+    n_ctx,
+    blocks,
+    d_gate,
+    d_up,
+    x_ref,
+    mixed,
+    d_h,
+    gains,
+    taps,
+    z_low,
+    rim,
+    act_in,
+    hidden_in,
+    d_all_in,
+    w_in_in,
+    w_out_in,
+    projected_in,
+    convolved_in,
+    gate_grad,
+    up_grad,
+    down_grad,
+    b_grad,
+    c_grad,
+    x_grad,
+    o_grad,
+    d_x,
+    small,
+    act,
+    hidden,
+    d_all,
+    w_in,
+    w_out,
+    projected,
+    convolved,
+    load_sem,
+    stage_wide,
+    stage,
+    stage_sem,
+    beside_got,
+    across_got,
+    passed,
+    passed_got,
+    send_sem,
+    recv_sem,
+    d_act,
+    d_res,
+    d_mixed,
+    d_conv,
+    d_proj,
+    act1,
+    edge,
+    next_edge,
+    edge_sem,
+):
+    chain = Chain(n_ctx)
+    _, beside, across, _ = corners()
+    greet_mixed(chain, [{"fsdp": beside}, {"fsdp": across}])
+    reduction = SideReduce(blocks, d_act, beside_got, across_got, passed, passed_got, send_sem, recv_sem)
+    reduction.start()
+    loads = [
+        pltpu.make_async_copy(src, dst, load_sem.at[index])
+        for index, (src, dst) in enumerate(
+            (
+                (act_in, act),
+                (hidden_in, hidden),
+                (d_all_in, d_all),
+                (convolved_in, convolved),
+                (projected_in, projected),
+                (w_out_in, w_out),
+                (w_in_in, w_in),
+            )
+        )
+    ]
+    for copy in loads:
+        copy.start()
+    rows, width = x_ref.shape
+    wide = d_gate.shape[1]
+    tile = 256
+    small[...] = jnp.zeros(small.shape, F32)
+
+    def weight_grad(left, right, at_right, target, staging, slot):
+        count = left.shape[1] // tile
+
+        def leaving(index, at):
+            return pltpu.make_async_copy(staging.at[at], target.at[index], stage_sem.at[slot + at])
+
+        def step(index, carry):
+            at = lax.rem(index, 2)
+            lanes = pl.ds(pl.multiple_of(index * tile, tile), tile)
+
+            @pl.when(index >= 2)
+            def _():
+                leaving(lanes, at).wait()
+
+            staging[at] = dot_plain(left[:, lanes].T, right[:, at_right]).astype(BF16)
+            leaving(lanes, at).start()
+            return carry
+
+        lax.fori_loop(0, count, step, 0)
+        for index in range(min(2, count)):
+            leaving(pl.ds(0, tile), index).wait()
+
+    loads[0].wait()
+    weight_grad(act, d_gate, slice(None), gate_grad, stage_wide, 0)
+    weight_grad(act, d_up, slice(None), up_grad, stage_wide, 0)
+    reduction.relay()
+    loads[1].wait()
+    loads[2].wait()
+    odd = hidden.shape[1] % tile
+
+    weight_grad(hidden, d_all, slice(None), down_grad, stage, 2)
+    if odd:
+        last = hidden.shape[1] - odd
+        stage[0, :odd] = dot_plain(hidden[:, last:].T, d_all[...]).astype(BF16)
+        copy = pltpu.make_async_copy(stage.at[0, pl.ds(0, odd)], down_grad.at[pl.ds(last, odd)], stage_sem.at[2])
+        copy.start()
+        copy.wait()
+    reduction.finish()
+    strip = 64
+
+    def norm_strip(at, values, gain, d_values, row):
+        inv_rms = lax.rsqrt(jnp.mean(values * values, axis=-1, keepdims=True) + EPSILON)
+        normed = values * inv_rms
+        small[row : row + 1] = small[row : row + 1] + jnp.sum(d_values * normed, axis=0, keepdims=True)
+        d_normed = d_values * gain
+        return inv_rms * d_normed - normed * inv_rms * jnp.mean(d_normed * normed, axis=-1, keepdims=True)
+
+    def second_norm(index, carry):
+        at = pl.ds(pl.multiple_of(index * strip, strip), strip)
+        x_rows = x_ref[at].astype(F32)
+        value = d_h[at].astype(F32) + norm_strip(at, x_rows + mixed[at], gains[1:2], d_act[at], 1)
+        d_res[at] = value
+        d_mixed[at] = value.astype(BF16)
+        inv_rms = lax.rsqrt(jnp.mean(x_rows * x_rows, axis=-1, keepdims=True) + EPSILON)
+        act1[at] = (x_rows * inv_rms * gains[0:1]).astype(BF16)
+        return carry
+
+    lax.fori_loop(0, rows // strip, second_norm, 0)
+    for index in range(3, 6):
+        loads[index].wait()
+
+    def to_z(index, carry):
+        at = pl.ds(pl.multiple_of(index * tile, tile), tile)
+        d_conv[:, at] = dot_right(d_mixed[...], w_out[at])
+        return carry
+
+    lax.fori_loop(0, width // tile, to_z, 0)
+    part = 128
+    row_at = lax.broadcasted_iota(jnp.int32, (rows, part), 0)
+
+    def lanes_of(offset, index):
+        return pl.ds(pl.multiple_of(offset * width + index * part, part), part)
+
+    def convolve_back(index, carry):
+        lanes = lanes_of(0, index)
+        product = (projected[:, lanes] * projected[:, lanes_of(2, index)]).astype(BF16).astype(F32)
+        before = rim[:, lanes].astype(F32)
+        near, far = before[15:16], before[14:15]
+        one = jnp.where(row_at >= 1, pltpu.roll(product, 1, 0), near)
+        two = jnp.where(row_at >= 2, pltpu.roll(product, 2, 0), jnp.where(row_at == 1, near, far))
+        d_z = d_conv[:, lanes]
+        d_proj[:, lanes_of(1, index)] = (d_z * convolved[:, lanes]).astype(BF16)
+        d_value = d_z * projected[:, lanes_of(1, index)]
+        d_conv[:, lanes] = d_value
+        for row, source in ((2, two), (3, one), (4, product)):
+            small[row : row + 1, lanes] = jnp.sum(d_value * source, axis=0, keepdims=True)
+        tap = taps[:, lanes]
+        edge[0:1, lanes] = tap[0:1] * d_value[0:1]
+        edge[1:2, lanes] = tap[0:1] * d_value[1:2] + tap[1:2] * d_value[0:1]
+        return carry
+
+    lax.fori_loop(0, width // part, convolve_back, 0)
+    edge[2:8] = jnp.zeros((6, width), F32)
+    to_last = along(edge, next_edge, edge_sem.at[0], edge_sem.at[1], chain.place - 1)
+
+    @pl.when(chain.has_last)
+    def _():
+        to_last.start()
+
+    weight_grad(z_low, d_mixed, slice(None), o_grad, stage, 2)
+
+    @pl.when(chain.has_next)
+    def _():
+        along(edge, next_edge, edge_sem.at[0], edge_sem.at[1], chain.place).wait_recv()
+
+    @pl.when(jnp.logical_not(chain.has_next))
+    def _():
+        next_edge[...] = jnp.zeros(next_edge.shape, F32)
+
+    def products_back(index, carry):
+        lanes = lanes_of(0, index)
+        d_value = d_conv[:, lanes]
+        tap = taps[:, lanes]
+        after = next_edge[:, lanes]
+        one = jnp.where(row_at < rows - 1, pltpu.roll(d_value, rows - 1, 0), 0.0)
+        two = jnp.where(row_at < rows - 2, pltpu.roll(d_value, rows - 2, 0), 0.0)
+        joined = tap[2:3] * d_value + tap[1:2] * one + tap[0:1] * two
+        joined = joined + jnp.where(row_at == rows - 2, after[0:1], 0.0)
+        joined = joined + jnp.where(row_at == rows - 1, after[1:2], 0.0)
+        joined = joined.astype(BF16).astype(F32)
+        d_proj[:, lanes] = (joined * projected[:, lanes_of(2, index)]).astype(BF16)
+        d_proj[:, lanes_of(2, index)] = (joined * projected[:, lanes]).astype(BF16)
+        return carry
+
+    lax.fori_loop(0, width // part, products_back, 0)
+    loads[6].wait()
+
+    def to_act(index, carry):
+        at = pl.ds(pl.multiple_of(index * tile, tile), tile)
+        d_act[:, at] = dot_right(d_proj[...], w_in[at])
+        return carry
+
+    lax.fori_loop(0, width // tile, to_act, 0)
+    for offset, target in enumerate((b_grad, c_grad, x_grad)):
+        weight_grad(act1, d_proj, slice(offset * width, (offset + 1) * width), target, stage, 2)
+
+    def first_norm(index, carry):
+        at = pl.ds(pl.multiple_of(index * strip, strip), strip)
+        value = d_res[at] + norm_strip(at, x_ref[at].astype(F32), gains[0:1], d_act[at], 0)
+        d_x[at] = value.astype(BF16)
+        return carry
+
+    lax.fori_loop(0, rows // strip, first_norm, 0)
+
+    @pl.when(chain.has_last)
+    def _():
+        to_last.wait_send()
+
+
+def conv_back(blocks, d_gate, d_up, local, kept, collective_id):
+    n_ctx = lax.axis_size("ctx")
+    x_low = local[0]
+    act, hidden = kept[0], kept[1]
+    rows, width = x_low.shape
+    wide = d_gate.shape[1]
+    dma = pltpu.SemaphoreType.DMA
+    vmem = pl.BlockSpec(memory_space=pltpu.VMEM)
+    hbm = pl.BlockSpec(memory_space=pl.ANY)
+    pair = pltpu.VMEM((2, rows // 2, width), BF16)
+    square = jax.ShapeDtypeStruct((width, width), BF16)
+    column = jax.ShapeDtypeStruct((width, wide), BF16)
+    return pl.pallas_call(
+        functools.partial(back_kernel, n_ctx),
+        out_shape=(
+            column,
+            column,
+            jax.ShapeDtypeStruct((wide, width), BF16),
+            square,
+            square,
+            square,
+            square,
+            jax.ShapeDtypeStruct((rows, width), BF16),
+            jax.ShapeDtypeStruct((8, width), F32),
+        ),
+        in_specs=[vmem] * (3 + len(local)) + [hbm] * len(kept),
+        out_specs=[hbm] * 7 + [vmem] * 2,
+        scratch_shapes=[pltpu.VMEM(k.shape, k.dtype) for k in kept]
+        + [
+            dma((7,)),
+            pltpu.VMEM((2, 256, wide), BF16),
+            pltpu.VMEM((2, 256, width), BF16),
+            dma((4,)),
+            pair,
+            pair,
+            pair,
+            pair,
+            dma((6,)),
+            dma((6,)),
+            pltpu.VMEM((rows, width), F32),
+            pltpu.VMEM((rows, width), F32),
+            pltpu.VMEM((rows, width), BF16),
+            pltpu.VMEM((rows, width), F32),
+            pltpu.VMEM((rows, 3 * width), BF16),
+            pltpu.VMEM((rows, width), BF16),
+            pltpu.VMEM((8, width), F32),
+            pltpu.VMEM((8, width), F32),
+            dma((2,)),
+        ],
+        compiler_params=pltpu.CompilerParams(
+            collective_id=collective_id, has_side_effects=True, vmem_limit_bytes=58 << 20
+        ),
+        cost_estimate=busy(35),
+    )(blocks, d_gate, d_up, *local, *kept)
+
+
 def ffn_forward(act, w_gate, w_up, w_down):
     gate_pre = matmul(act, w_gate)
     up_pre = matmul(act, w_up)
@@ -1820,12 +2138,16 @@
     d_up = (d_hidden * gate_pre * sigmoid).astype(BF16)
     d_gate = (d_hidden * up_pre * sigmoid * (1.0 + gate_pre * (1.0 - sigmoid))).astype(BF16)
     terms = (matmul_right(d_gate, w_gate) + matmul_right(d_up, w_up)).astype(BF16)
-    grads = (
+    return terms, d_gate, d_up
+
+
+def ffn_weight_grads(d_all, kept, d_gate, d_up):
+    act, _, _, hidden = kept
+    return (
         matmul_left(act, d_gate).astype(BF16),
         matmul_left(act, d_up).astype(BF16),
         matmul_left(hidden, d_all).astype(BF16),
     )
-    return terms, grads
 
 
 def ffn_norm_back(d_act, residual, gain):
@@ -1868,11 +2190,12 @@
         return lax.all_gather(mine, ("fsdp", "section"), axis=0, tiled=True)
 
     part = ffn_gate.shape[1]
+    attn_full = whole_rows(jnp.concatenate([attn_q, attn_k, attn_v, attn_out], axis=1))
     query_full, key_full, value_full, proj_full = (
-        whole_rows(attn_q),
-        whole_rows(attn_k),
-        whole_rows(attn_v),
-        whole_rows(attn_out),
+        attn_full[:, :q_width],
+        attn_full[:, q_width : q_width + kv_width],
+        attn_full[:, q_width + kv_width : q_width + 2 * kv_width],
+        attn_full[:, q_width + 2 * kv_width :],
     )
 
     x_low = lax.dynamic_index_in_dim(inputs, section, keepdims=False)
@@ -1914,7 +2237,8 @@
     terms2, kept2 = ffn_forward(act_all2, gate2, up2, down2)
 
     d_sum = d_sum_low.astype(F32)
-    d_terms2, grads2 = ffn_backward(d_sum_all, kept2, gate2, up2, down2)
+    d_terms2, d_gate2, d_up2 = ffn_backward(d_sum_all, kept2, gate2, up2, down2)
+    grads2 = ffn_weight_grads(d_sum_all, kept2, d_gate2, d_up2)
     half = part // 2
     strip = half // lax.axis_size("ctx")
 
@@ -1971,62 +2295,28 @@
     d_h_all, second_gu = gathered_swapped(d_h_low, second_gu.reshape(fsdp, 2 * strip, -1), 5)
     second_gu = lax.all_gather(second_gu, "ctx", axis=0)
     second_down = lax.all_gather(second_down, "ctx", axis=0, tiled=True)
-    d_terms1, grads1 = ffn_backward(d_h_all, kept1, gate1, up1, down1)
-    d_ffn1, gain1 = ffn_norm_back(reduced(d_terms1, 1), res1, norm_gains[1])
-    d_ffn1, second_gu = lax.optimization_barrier((d_ffn1, second_gu))
-    d_res1 = d_h_low.astype(F32) + d_ffn1
-    d_mixed = d_res1.astype(BF16)
-    grad_out = matmul_left(z_low, d_mixed)
-    normed0, inv0 = norm_rows(x)
-    act1 = (normed0 * norm_gains[0]).astype(BF16)
-    b_gate, c_gate, x_value = (
-        projected[:, :width],
-        projected[:, width : 2 * width],
-        projected[:, 2 * width :],
+    d_terms1, d_gate1, d_up1 = ffn_backward(d_h_all, kept1, gate1, up1, down1)
+    attn_mixers = [
+        matmul_left(act2, d_qpre).astype(BF16),
+        matmul_left(act2, jnp.concatenate([d_kpre, d_vpre], axis=1)).astype(BF16),
+        grad_proj.astype(BF16),
+    ]
+    *grads, d_x, conv_small = conv_back(
+        d_terms1,
+        d_gate1,
+        d_up1,
+        (x_low, mixed, d_h_low, norm_gains, conv_kernel, z_low, rim),
+        (act_all1, kept1[3], d_h_all, in_full, out_full, projected, convolved),
+        9,
     )
-    extended = jnp.concatenate([rim[14:], (b_gate * x_value).astype(BF16)], axis=0).astype(F32)
-    d_z = matmul_right(d_mixed, out_full)
-    d_cgate = d_z * convolved
-    d_conv = d_z * c_gate
-    grad_kernel = jnp.stack(
-        [
-            jnp.sum(d_conv * extended[:-2], axis=0),
-            jnp.sum(d_conv * extended[1:-1], axis=0),
-            jnp.sum(d_conv * extended[2:], axis=0),
-        ]
-    )
-    d_extended = (
-        jnp.pad(d_conv * conv_kernel[0], ((0, 2), (0, 0)))
-        + jnp.pad(d_conv * conv_kernel[1], ((1, 1), (0, 0)))
-        + jnp.pad(d_conv * conv_kernel[2], ((2, 0), (0, 0)))
-    )
-    from_next, second_down = lax.optimization_barrier(
-        (passed_along(d_extended[:2], "ctx", -1), second_down)
-    )
-    d_bproduct = rounded(d_extended[2:] + jnp.pad(from_next, ((rows - 2, 0), (0, 0))))
-    d_projected = jnp.concatenate(
-        [d_bproduct * x_value, d_cgate, d_bproduct * b_gate], axis=1
-    ).astype(BF16)
-    d_act1 = matmul_right(d_projected, in_full)
-    gain0 = jnp.sum(d_act1 * normed0, axis=0)
-    d_x = (d_res1 + norm_back(d_act1 * norm_gains[0], normed0, inv0)).astype(BF16)
 
     y_low = result.astype(BF16)
     is_first = section == 0
     other_end = swapped(jnp.where(is_first, y_low, d_x), "section")
     ends = jnp.where(is_first, jnp.stack([d_x, other_end]), jnp.stack([other_end, y_low]))[None]
 
-    grad_parts = [
-        matmul_left(act1, d_projected[:, i * width : (i + 1) * width]).astype(BF16) for i in range(3)
-    ]
-    mixers = [
-        matmul_left(act2, d_qpre).astype(BF16),
-        matmul_left(act2, jnp.concatenate([d_kpre, d_vpre], axis=1)).astype(BF16),
-        grad_proj.astype(BF16),
-    ] + grad_parts + [grad_out.astype(BF16)]
-
     small = jnp.concatenate(
-        [gain0[None], gain1[None], gain2[None], gain3[None], grad_kernel]
+        [conv_small[:2], gain2[None], gain3[None], conv_small[2:5]]
         + [jnp.pad(grad[None], ((0, 0), (0, width - head))) for grad in (grad_qgain, grad_kgain)]
         + [jnp.zeros((7, width), F32)]
         + squares
@@ -2034,8 +2324,8 @@
     ).astype(BF16)
     small = small.reshape(2, 16, width)
     gu_sum, down_sum, rest_sum = summed_gradients(
-        grads1,
-        mixers,
+        grads[:3],
+        attn_mixers + grads[3:],
         small,
         second_gu.reshape(-1, fsdp, 2, strip, second_gu.shape[-1]),
         second_down,

time: 761 us -> 733 us (0.963)
  matrix products: 126 us -> 99.4 us
  Pallas kernels: 528 us -> 553 us
  other arithmetic: 43.3 us -> 31.9 us
    pallas_call x0 -> x1, Pallas kernels: none -> 47.6 us  [conv_back(): pl.pallas_call(functools.partial(back_kernel, n_ctx), out_shape=(column,...]
    dot_general x13 -> x6, matrix products: 40.2 us -> 15.8 us  [matmul_left(): lax.dot_general(left_op, right_op, (((0,), (0,)), ((), ())), preferred_el...]
    pallas_call x2 -> x1, Pallas kernels: 41.7 us -> 18.3 us  [reduced(): pl.pallas_call(reduce_kernel, out_shape=jax.ShapeDtypeStruct((rows, width...]
    pallas_call x1, Pallas kernels: 185 us -> 164 us  [summed_gradients(): pl.pallas_call(functools.partial(tail_kernel, (n_ctx, n_fsdp)), out_shape...]
    pallas_call x1, Pallas kernels: 80 us -> 96.4 us  [attend_back(): pl.pallas_call(functools.partial(attend_back_kernel, n_ctx), out_shape=(w...]
    pallas_call x1, Pallas kernels: 106 us -> 114 us  [front(): pl.pallas_call(functools.partial(front_kernel, n_ctx), out_shape=tuple((j...]
    dot_general x12 -> x10, matrix products: 40 us -> 38.1 us  [matmul_right(): lax.dot_general(left_op, right_op, (((1,), (1,)), ((), ())), preferred_el...]
  transfers between devices with their start and end apart: 10 -> 6, of which waited for: 1 -> 0; matrix products, arithmetic and copies ran while one was open for 15% -> 10% of each run, Pallas kernels for 41% -> 41%
where the time goes in v9:
time: 733 us; the launch traced here: 724 us
  Pallas kernels  553 us (75%)
  matrix products  99.4 us (14%)
  other arithmetic  31.9 us (4%)
  local copies, waits for them, and re-layouts  22.5 us (3%)
  between operations  16 us (2%)
    pallas_call x1, Pallas kernels, summed_gradients(): pl.pallas_call(functools.partial(tail_kernel, (n_ctx, n_fsdp)), out_shape...  164 us
    pallas_call x1, Pallas kernels, front(): pl.pallas_call(functools.partial(front_kernel, n_ctx), out_shape=tuple((j...  114 us
    pallas_call x1, Pallas kernels, attend_back(): pl.pallas_call(functools.partial(attend_back_kernel, n_ctx), out_shape=(w...  96.4 us
    pallas_call x1, Pallas kernels, attend(): pl.pallas_call(functools.partial(attend_kernel, n_ctx), out_shape=(jax.Sh...  55.3 us
    pallas_call x1, Pallas kernels, conv_back(): pl.pallas_call(functools.partial(back_kernel, n_ctx), out_shape=(column,...  47.6 us
    dot_general x10, matrix products, matmul_right(): lax.dot_general(left_op, right_op, (((1,), (1,)), ((), ())), preferred_el...  38.1 us
    dot_general x10, matrix products, matmul(): return jnp.dot(left_op, right_op, preferred_element_type=F32)  36.7 us
    pallas_call x1, Pallas kernels, gathered_swapped(): pl.pallas_call(gather_swap_kernel, out_shape=(jax.ShapeDtypeStruct((4 * r...  19.4 us
  transfers between devices with their start and end apart: 6, of which 0 were waited for; matrix products, arithmetic and copies ran while one was open for 10% of the time, Pallas kernels for 41%

profile of v9, /device:TPU:0, one launch (start us, length us, event | category | flops | bytes accessed | tf_op | source)
XLA Modules:
  0.0 723.9 jit_solution(15045517263648377425)
XLA Ops:
  10.3 114.5 %shard_map.262 = (bf16[1024,3072]{1,0:T(8,128)(2,1)}, bf16[1024,1024]{1,0:T(8,128)(2,1)}, bf16[1024,1152]{1,0:T(8,128)(2,1)}, bf16[1024,1152]{1,0:T(8,128)(2,1)}...) custom-call(bf16[256,1024]{1,0:T(8,128)(2,1)} %dynamic-slice_bitcast, ...), custom_call_target="tpu_custom_call" | custom-call | flops 70 | bytes 65536 | tf_op jit(solution)/shard_map/pallas_call | solution.py:1800
  124.8 5.3 fusion.108
  130.2 4.5 multiply_convert_fusion.5
  137.9 18.3 %shard_map.263 = f32[256,1024]{1,0:T(8,128)S(1)} custom-call(bf16[1024,1024]{1,0:T(8,128)(2,1)S(1)} %convolution_convert_fusion.4.blocks), custom_call_target="tpu_custom_call" | custom-call | flops 25 | bytes 65536 | tf_op jit(solution)/shard_map/pallas_call | solution.py:334
  173.1 55.3 %shard_map.264 = (f32[256,1024]{1,0:T(8,128)}, f32[16,1,256]{2,1,0:T(1,128)}, bf16[1024,1024]{1,0:T(8,128)(2,1)}, bf16[1024,1024]{1,0:T(8,128)(2,1)}, bf16[1024,...) custom-call(s32[1]{0:T(128)} %dynamic_slice.39.length_ref, ...), custom_call_target="tpu_custom_call" | custom-call | flops 50 | bytes 65536 | tf_op jit(solution)/shard_map/pallas_call | solution.py:1356
  228.5 3.6 multiply_reduce_fusion.2
  232.3 18.5 %shard_map.265 = bf16[1024,1024]{1,0:T(8,128)(2,1)S(1)} custom-call(bf16[256,1024]{1,0:T(8,128)(2,1)S(1)} %multiply_convert_fusion.6.block), custom_call_target="tpu_custom_call" | custom-call | flops 25 | bytes 65536 | tf_op jit(solution)/shard_map/pallas_call | solution.py:146
  256.7 5.0 multiply_convert_fusion.2
  264.6 3.2 convolution_convert_fusion.2
  267.8 3.2 convolution_convert_fusion.1
  271.0 3.2 add_convert_fusion.1.blocks
  279.4 18.6 %shard_map.266 = (f32[256,1024]{1,0:T(8,128)S(1)}, bf16[1024,1152]{1,0:T(8,128)(2,1)S(1)}, bf16[576,1024]{1,0:T(8,128)(2,1)S(1)}) custom-call(bf16[1024,1024]{1,0:T(8,128)(2,1)S(1)} %add_convert_fusion.1.blocks, bf16[1024,1152]{1,0:T(8,128)(2,1)S(1)} %bitcast.108, bf16[576,1024]{1,0:T(8,128)(2,1)S(1)} %constant_dynamic-slice_fusion.3.give_b), custom_call_target="tpu_custom_call" | custom-call | flops 25 | bytes 65536 | tf_op jit(solution)/shard_map/pallas_call | solution.py:312
  305.8 4.1 convert_multiply_fusion.7
  314.5 6.6 convolution_convert_fusion.3.blocks
  321.0 96.4 %shard_map.267 = (f32[256,1024]{1,0:T(8,128)}, f32[256,1024]{1,0:T(8,128)}, f32[256,1024]{1,0:T(8,128)}) custom-call(s32[1]{0:T(128)} %dynamic_slice.39.length_ref, bf16[256,1024]{1,0:T(8,128)(2,1)} %get-tuple-element.114.query, bf16[1024,1024]{1,0:T(8,128)(2,1)} %get-tuple-element.67.kv_all, bf16[256,1024]{1,0:T(8,128)(2,1)} %get-tuple-element.70.d_out, ...), custom_call_target="tpu_custom_call" | custom-call | flops 50 | bytes 65536 | tf_op jit(solution)/shard_map/pallas_call | solution.py:1511
  425.6 3.3 fusion.8
  431.7 4.4 fusion.42
  442.0 19.4 %shard_map.268 = (bf16[1024,1024]{1,0:T(8,128)(2,1)S(1)}, bf16[4,64,1152]{2,1,0:T(8,128)(2,1)}) custom-call(bf16[256,1024]{1,0:T(8,128)(2,1)S(1)} %fusion.47.block.d_h, bf16[4,64,1152]{2,1,0:T(8,128)(2,1)S(1)} %bitcast.109), custom_call_target="tpu_custom_call" | custom-call | flops 25 | bytes 65536 | tf_op jit(solution)/shard_map/pallas_call | solution.py:188
  461.4 8.1 %multiply_convert_fusion = (bf16[1024,1152]{1,0:T(8,128)(2,1)S(1)}, bf16[1024,1152]{1,0:T(8,128)(2,1)S(1)}) fusion(f32[1024,1152]{1,0:T(8,128)} %copy-done.48, f32[1024,1152]{1,0:T(8,128)} %get-tuple-element.148, bf16[1024,1024]{1,0:T(8,128)(2,1)S(1)} %get-tuple-element.75.d_all_in, bf16[1152,1024]{1,0:T(8,128)(2,1)} %get-tuple-element.60), kind=kOutput, calls=%fused_computation.6 | convolution fusion | flops 2431254528 | bytes 18612224 | tf_op jit(solution)/shard_map/dot_general | solution.py:40
  472.9 4.1 add_convert_fusion.blocks
  477.0 47.6 %shard_map.269 = (bf16[1024,1152]{1,0:T(8,128)(2,1)}, bf16[1024,1152]{1,0:T(8,128)(2,1)}, bf16[1152,1024]{1,0:T(8,128)(2,1)}, bf16[1024,1024]{1,0:T(8,128)(2,1)}...) custom-call(bf16[1024,1024]{1,0:T(8,128)(2,1)} %add_convert_fusion.b, ...), custom_call_target="tpu_custom_call" | custom-call | flops 35 | bytes 65536 | tf_op jit(solution)/shard_map/pallas_call | solution.py:2083
  532.8 164.1 %shard_map.270 = (bf16[2,256,4608]{2,1,0:T(8,128)(2,1)}, bf16[1152,1024]{1,0:T(8,128)(2,1)}, bf16[2,960,1024]{2,1,0:T(8,128)(2,1)}) custom-call(bf16[1024,1152]{1,0:T(8,128)(2,1)} %get-tuple-element.84.gate_in, bf16[1024,1152]{1,0:T(8,128)(2,1)} %get-tuple-element.85.up_in, bf16[1152,1024]{1,0:T(8,128)(2,1)} %get-tuple-element.86.down_in, ...), custom_call_target="tpu_custom_call" | custom-call | flops 160 | bytes 65536 | tf_op jit(solution)/shard_map/pallas_call | solution.py:982
  697.8 4.5 fusion.104
  706.1 5.0 slice_convert_fusion
  (216 shorter events, 87.2 us)
Async XLA Ops:
  7.2 154.0 %all-gather.5.cloned.1.call-start = ((), (), s32[]{:S(2)}) async-start(), calls=%async_computation.2 | async-start | bytes 7077888 | tf_op jit(solution)/shard_map/all_gather | solution.py:2190
  9.4 419.4 %reduce-scatter.5.cloned.1.call-start = ((), (), s32[]{:S(2)}) async-start(), calls=%async_computation.4 | async-start | bytes 1474560 | tf_op jit(solution)/shard_map/reduce_scatter | solution.py:2278
  124.8 5.4 copy-start.27
  124.8 5.4 copy-start.39
  137.8 18.4 %copy-start.38 = (f32[2,64]{1,0:T(2,128)S(1)}, f32[2,64]{1,0:T(2,128)}, u32[]{:S(2)}) copy-start(f32[2,64]{1,0:T(2,128)} %param.26) | copy-start | bytes 1540
  137.9 18.6 %copy-start.47 = (s32[8]{0:T(128)S(1)}, s32[8]{0:T(128)}, u32[]{:S(2)}) copy-start(s32[8]{0:T(128)} %param.17) | copy-start | bytes 100
  137.9 19.8 %copy-start.10 = (f32[256,1024]{1,0:T(8,128)S(1)}, f32[256,1024]{1,0:T(8,128)}, u32[]{:S(2)}) copy-start(f32[256,1024]{1,0:T(8,128)} %get-tuple-element.56.mixed) | copy-start | bytes 3145732
  159.0 69.4 %copy-start.6 = (bf16[256,1024]{1,0:T(8,128)(2,1)}, bf16[256,1024]{1,0:T(8,128)(2,1)S(1)}, u32[]{:S(2)}) copy-start(bf16[256,1024]{1,0:T(8,128)(2,1)S(1)} %get-tuple-element.117) | copy-start | bytes 1572868
  232.3 18.5 %copy-start.45 = (bf16[1024,1152]{1,0:T(8,128)(2,1)S(1)}, bf16[1024,1152]{1,0:T(8,128)(2,1)}, u32[]{:S(2)}) copy-start(bf16[1024,1152]{1,0:T(8,128)(2,1)} %get-tuple-element.65) | copy-start | bytes 7077892
  261.6 13.4 %copy-start.49 = (bf16[1024,1152]{1,0:T(8,128)(2,1)}, bf16[1024,1152]{1,0:T(8,128)(2,1)S(1)}, u32[]{:S(2)}) copy-start(bf16[1024,1152]{1,0:T(8,128)(2,1)S(1)} %get-tuple-element.120) | copy-start | bytes 7077892
  309.9 130.8 %reduce-scatter.3.cloned.1.call-start = ((), (), s32[]{:S(2)}) async-start(), calls=%async_computation.3 | async-start | bytes 2949120 | tf_op jit(solution)/shard_map/reduce_scatter | solution.py:2278
  310.7 222.1 %all-gather.7.cloned.1.call-start = ((), (), s32[]{:S(2)}) async-start(), calls=%async_computation.5 | async-start | bytes 1474560 | tf_op jit(solution)/shard_map/all_gather | solution.py:2297
  428.9 103.9 %all-gather.9.cloned.1.call-start = ((), (), s32[]{:S(2)}) async-start(), calls=%async_computation.6 | async-start | bytes 2949120 | tf_op jit(solution)/shard_map/all_gather | solution.py:2296
  440.7 28.8 %copy-start = (bf16[256,1024]{1,0:T(8,128)(2,1)}, bf16[256,1024]{1,0:T(8,128)(2,1)S(1)}, u32[]{:S(2)}) copy-start(bf16[256,1024]{1,0:T(8,128)(2,1)S(1)} %fusion.47.block.d_h) | copy-start | bytes 1572868
  461.3 8.1 %copy-start.1 = (bf16[1024,1024]{1,0:T(8,128)(2,1)}, bf16[1024,1024]{1,0:T(8,128)(2,1)S(1)}, u32[]{:S(2)}) copy-start(bf16[1024,1024]{1,0:T(8,128)(2,1)S(1)} %get-tuple-element.75.d_all_in) | copy-start | bytes 6291460
  461.4 8.1 %copy-start.41 = (bf16[1024,1152]{1,0:T(8,128)(2,1)S(1)}, bf16[1024,1152]{1,0:T(8,128)(2,1)}, u32[]{:S(2)}) copy-start(bf16[1024,1152]{1,0:T(8,128)(2,1)} %get-tuple-element.58) | copy-start | bytes 7077892
  477.0 47.6 %copy-start.17 = (bf16[256,1024]{1,0:T(8,128)(2,1)S(1)}, bf16[256,1024]{1,0:T(8,128)(2,1)}, u32[]{:S(2)}) copy-start(bf16[256,1024]{1,0:T(8,128)(2,1)} %get-tuple-element.109) | copy-start | bytes 1572868
  477.0 47.8 %copy-start.9 = (bf16[256,1024]{1,0:T(8,128)(2,1)S(1)}, bf16[256,1024]{1,0:T(8,128)(2,1)}, u32[]{:S(2)}) copy-start(bf16[256,1024]{1,0:T(8,128)(2,1)} %copy-done.6) | copy-start | bytes 1572868
  477.0 47.8 %copy-start.34 = (bf16[256,512]{1,0:T(8,128)(2,1)S(1)}, bf16[256,512]{1,0:T(8,128)(2,1)}, u32[]{:S(2)}) copy-start(bf16[256,512]{1,0:T(8,128)(2,1)} %fusion.30) | copy-start | bytes 786436
  477.0 47.8 %copy-start.35 = (bf16[256,512]{1,0:T(8,128)(2,1)S(1)}, bf16[256,512]{1,0:T(8,128)(2,1)}, u32[]{:S(2)}) copy-start(bf16[256,512]{1,0:T(8,128)(2,1)} %get-tuple-element.136) | copy-start | bytes 786436
  524.7 6.9 collective-permute-start
  696.9 9.2 %slice-start = ((s8[4718592]{0:T(1024)(128)(4,1)}), s8[4194304]{0:T(1024)(128)(4,1)S(1)}, s32[]{:S(2)}) async-start(s8[4718592]{0:T(1024)(128)(4,1)} %bitcast.116), calls=%async_computation.7 | async-start | bytes 8388608
  697.8 8.3 %slice-start.1 = ((s8[4718592]{0:T(1024)(128)(4,1)}), s8[524288]{0:T(1024)(128)(4,1)S(1)}, s32[]{:S(2)}) async-start(s8[4718592]{0:T(1024)(128)(4,1)} %bitcast.116), calls=%async_computation.8 | async-start | bytes 1048576
  706.1 5.0 copy-start.25
  (34 other events, 100.6 us)
Sparse Core Ops, SparseCore 0:
  10.5 75.5 all-gather.4
  310.1 39.5 reduce-scatter.4
  352.6 63.3 reduce-scatter.2
  429.0 31.1 all-gather.6
  461.6 54.7 all-gather.8

commit v10 on v9

--- a/solution.py
+++ b/solution.py
@@ -258,72 +258,6 @@
     reduction.start()
     reduction.relay()
     reduction.finish()
-
-
-def reduce_pair_kernel(
-    blocks,
-    give_a,
-    give_b,
-    total,
-    got_a,
-    got_b,
-    beside_got,
-    across_got,
-    passed,
-    passed_got,
-    send_sem,
-    recv_sem,
-    pair_send,
-    pair_recv,
-):
-    other = {"section": 1 - lax.axis_index("section")}
-    _, beside, across, _ = corners()
-    barrier = pltpu.get_barrier_semaphore()
-    for target in ({"fsdp": beside}, {"fsdp": across}, other):
-        pl.semaphore_signal(barrier, inc=1, device_id=target, device_id_type=MESH)
-    pl.semaphore_wait(barrier, 3)
-    reduction = SideReduce(blocks, total, beside_got, across_got, passed, passed_got, send_sem, recv_sem)
-    reduction.start()
-    pairs = [
-        pltpu.make_async_remote_copy(
-            src_ref=src,
-            dst_ref=dst,
-            send_sem=pair_send.at[index],
-            recv_sem=pair_recv.at[index],
-            device_id=other,
-            device_id_type=MESH,
-        )
-        for index, (src, dst) in enumerate(((give_a, got_a), (give_b, got_b)))
-    ]
-    for copy in pairs:
-        copy.start()
-    reduction.relay()
-    reduction.finish()
-    for copy in pairs:
-        copy.wait()
-
-
-def reduced_swapping(partial, give_a, give_b, collective_id):
-    rows, width = partial.shape[0] // 4, partial.shape[1]
-    dma = pltpu.SemaphoreType.DMA
-    pair = pltpu.VMEM((2, rows // 2, width), BF16)
-    vmem = pl.BlockSpec(memory_space=pltpu.VMEM)
-    hbm = pl.BlockSpec(memory_space=pl.ANY)
-    return pl.pallas_call(
-        reduce_pair_kernel,
-        out_shape=(
-            jax.ShapeDtypeStruct((rows, width), F32),
-            jax.ShapeDtypeStruct(give_a.shape, BF16),
-            jax.ShapeDtypeStruct(give_b.shape, BF16),
-        ),
-        in_specs=[vmem, hbm, hbm],
-        out_specs=[vmem, hbm, hbm],
-        scratch_shapes=[pair, pair, pair, pair, dma((6,)), dma((6,)), dma((2,)), dma((2,))],
-        compiler_params=pltpu.CompilerParams(
-            collective_id=collective_id, has_side_effects=True, vmem_limit_bytes=16 << 20
-        ),
-        cost_estimate=busy(25),
-    )(partial.astype(BF16), give_a, give_b)
 
 
 def reduced(partial, collective_id):
@@ -416,8 +350,10 @@
     cut = 3 * half // b_rows
     c_parts = ((0, cut), (cut, c_rows // b_rows))
     paired = a_chunks // 2
-    mix_chunks = b_chunks - down_chunks
-    ticks = paired + mix_chunks // 2
+    mix_start = 2 * down_chunks
+    mix_chunks = b_chunks - mix_start
+    second = paired + down_chunks // 2
+    ticks = second + mix_chunks // 2
     tail = 2 * (n_ctx - 1)
 
     barrier = pltpu.get_barrier_semaphore()
@@ -493,6 +429,13 @@
     for k in range(a_chunks):
         for way in range(2):
             opening(k, way)
+    for k in range(down_chunks):
+        for way in range(2):
+            pltpu.make_async_copy(
+                second_down_in.at[pl.ds(k * b_rows, b_rows), pl.ds(way * b_part, b_part)],
+                b_at(b_own, down_chunks + k, way),
+                own_sem.at[2 * (a_chunks + down_chunks + k) + way],
+            ).start()
     c_local, c_pair = ([], []), ([], [])
     for kind, source in enumerate(mixers):
         part = 0 if kind < 3 else 1
@@ -616,7 +559,7 @@
         def add(index, carry):
             at = pl.ds(pl.multiple_of(index * b_rows, b_rows), b_rows)
             total = c_own[group, at].astype(F32) + c_got[1, at].astype(F32) + c_got[2, at].astype(F32)
-            b_own[down_chunks + index] = total.astype(BF16)
+            b_own[mix_start + index] = total.astype(BF16)
             return carry
 
         lax.fori_loop(first, last, add, 0)
@@ -646,24 +589,13 @@
                 pltpu.make_async_copy(src, dst, second_send.at[0]).start()
 
     def second_start():
-        down_at = down_out.at[pl.ds(pl.multiple_of(section * down_half, b_rows), down_half)]
-
         @pl.when(section == 1)
         def _():
             second_copies(False)
-            pltpu.make_async_copy(second_down_in, down_at, second_send.at[1]).start()
 
         @pl.when(section == 0)
         def _():
             second_copies(True)
-            pltpu.make_async_remote_copy(
-                src_ref=second_down_in,
-                dst_ref=down_at,
-                send_sem=second_send.at[1],
-                recv_sem=down_recv,
-                device_id={"section": 1},
-                device_id_type=MESH,
-            ).start()
 
     def a_target(k, way):
         kind = k // per_kind
@@ -699,26 +631,27 @@
                 device_id_type=MESH,
             ).start()
 
-    def down_hand_out(k, way):
+    def down_hand_out(k, way, keeper):
         slot = 2 * k + way
         b_ref = b_at(b_done, k, way)
+        index = k - keeper * down_chunks
         at = down_out.at[
-            pl.ds(pl.multiple_of(section * down_half + k * b_rows, b_rows), b_rows),
+            pl.ds(pl.multiple_of(section * down_half + index * b_rows, b_rows), b_rows),
             pl.ds(way * b_part, b_part),
         ]
 
-        @pl.when(section == 0)
+        @pl.when(section == keeper)
         def _():
             pltpu.make_async_copy(b_ref, at, b_out_send.at[slot]).start()
 
-        @pl.when(section == 1)
+        @pl.when(section != keeper)
         def _():
             pltpu.make_async_remote_copy(
                 src_ref=b_ref,
                 dst_ref=at,
                 send_sem=b_out_send.at[slot],
                 recv_sem=down_recv,
-                device_id={"section": 0},
+                device_id={"section": keeper},
                 device_id_type=MESH,
             ).start()
 
@@ -727,7 +660,7 @@
         b_ref = b_at(b_done, k, way)
         at = rest_out.at[
             section,
-            pl.ds(pl.multiple_of((k - down_chunks) * b_rows, b_rows), b_rows),
+            pl.ds(pl.multiple_of((k - mix_start) * b_rows, b_rows), b_rows),
             pl.ds(way * b_part, b_part),
         ]
         pltpu.make_async_copy(b_ref, at, b_keep_sem.at[slot]).start()
@@ -769,7 +702,9 @@
             return at[...].astype(F32) + a_at(a_other, k, way)[...].astype(F32)
 
     class Downs:
-        hand_out = staticmethod(down_hand_out)
+        @staticmethod
+        def hand_out(k, way):
+            down_hand_out(k, way, 0)
 
         @staticmethod
         def view(buffer, k, way):
@@ -786,6 +721,17 @@
             pltpu.make_async_copy(at, at, pair_recv.at[slot]).wait()
             return at[...].astype(F32) + b_at(b_other, k, way)[...].astype(F32)
 
+    class Seconds(Downs):
+        @staticmethod
+        def hand_out(k, way):
+            down_hand_out(k, way, 1)
+
+        @staticmethod
+        def term(k, way):
+            at = b_at(b_own, k, way)
+            pltpu.make_async_copy(at, at, own_sem.at[2 * a_chunks + 2 * k + way]).wait()
+            return at[...].astype(F32)
+
     class Mixed(Downs):
         hand_out = staticmethod(mix_hand_out)
 
@@ -845,11 +791,17 @@
             def _():
                 action(Downs, 3 * (at // 4) + lax.rem(at, 4), *where)
 
-        @pl.when(active & jnp.logical_not(early))
+        @pl.when(active & (step >= paired) & (step < second))
         def _():
-            at = jnp.clip(step - paired, 0, mix_chunks // 2 - 1)
+            at = jnp.clip(step - paired, 0, down_chunks // 2 - 1)
             for index in range(2):
-                action(Mixed, down_chunks + 2 * at + index, *where)
+                action(Seconds, down_chunks + 2 * at + index, *where)
+
+        @pl.when(active & (step >= second))
+        def _():
+            at = jnp.clip(step - second, 0, mix_chunks // 2 - 1)
+            for index in range(2):
+                action(Mixed, mix_start + 2 * at + index, *where)
 
     lanes = []
     for way in range(2):
@@ -869,10 +821,10 @@
         events = (
             (4, mixer_out, 0),
             (8, mixer_out, 1),
-            (9, mixer_on, 0),
-            (13, mixer_on, 1),
-            (paired - 1, mixer_in, 0),
-            (paired + 3, mixer_in, 1),
+            (10, mixer_on, 0),
+            (15, mixer_on, 1),
+            (second - 1, mixer_in, 0),
+            (second + 3, mixer_in, 1),
         )
         for moment, action, part in events:
 
@@ -906,38 +858,47 @@
         for copy in opening + onward:
             copy.wait_send()
 
-    def settle(k, carry):
+    def settle_item(item, k, out_send):
         for way, rank, ahead, behind in lanes:
             slot = 2 * k + way
-            a_ref, b_ref = a_at(a_own, k, way), b_at(b_own, k, way)
-            pltpu.make_async_copy(a_ref, a_ref, pair_send.at[slot]).wait()
+
+            @pl.when(rank < n_ctx - 1)
+            def _(slot=slot, way=way, ahead=ahead):
+                chain_copy(item.view(item.sums, k, way), item.up, slot, ahead).wait_send()
+
+            @pl.when(rank > 0)
+            def _(slot=slot, way=way, behind=behind):
+                chain_copy(item.view(item.done, k, way), item.back, slot, behind).wait_send()
+
+            ref = item.view(item.own, k, way)
+            pltpu.make_async_copy(ref, ref, out_send.at[slot]).wait()
+
+    def settle_gates(k, carry):
+        settle_item(Gates, k, a_out_send)
+        for way in range(2):
+            ref = a_at(a_own, k, way)
+            pltpu.make_async_copy(ref, ref, pair_send.at[2 * k + way]).wait()
+        return carry
+
+    lax.fori_loop(0, a_chunks, settle_gates, 0)
+
+    def settle_rest(k, carry):
+        settle_item(Mixed, k, b_out_send)
+        for way in range(2):
+            ref = b_at(b_own, k, way)
 
             @pl.when(k < down_chunks)
-            def _(b_ref=b_ref, slot=slot):
-                pltpu.make_async_copy(b_ref, b_ref, pair_send.at[2 * a_chunks + slot]).wait()
-
-            for item in (Gates, Mixed):
-
-                @pl.when(rank < n_ctx - 1)
-                def _(item=item, slot=slot, k=k, way=way, ahead=ahead):
-                    chain_copy(item.view(item.sums, k, way), item.up, slot, ahead).wait_send()
-
-                @pl.when(rank > 0)
-                def _(item=item, slot=slot, k=k, way=way, behind=behind):
-                    chain_copy(item.view(item.done, k, way), item.back, slot, behind).wait_send()
-
-            pltpu.make_async_copy(a_ref, a_ref, a_out_send.at[slot]).wait()
-            pltpu.make_async_copy(b_ref, b_ref, b_out_send.at[slot]).wait()
-
-            @pl.when(k >= down_chunks)
-            def _(b_ref=b_ref, slot=slot):
-                pltpu.make_async_copy(b_ref, b_ref, b_keep_sem.at[slot]).wait()
+            def _(ref=ref, way=way):
+                pltpu.make_async_copy(ref, ref, pair_send.at[2 * a_chunks + 2 * k + way]).wait()
+
+            @pl.when(k >= mix_start)
+            def _(ref=ref, way=way):
+                pltpu.make_async_copy(ref, ref, b_keep_sem.at[2 * k + way]).wait()
 
         return carry
 
-    lax.fori_loop(0, a_chunks, settle, 0)
+    lax.fori_loop(0, b_chunks, settle_rest, 0)
     pltpu.make_async_copy(second_gu_in, second_gu_in, second_send.at[0]).wait()
-    pltpu.make_async_copy(second_down_in, second_down_in, second_send.at[1]).wait()
 
     @pl.when(section == 0)
     def _():
@@ -972,12 +933,12 @@
     a_width, b_width = gate.shape[1], down.shape[1]
     c_rows = len(mixers) * half + small.shape[1]
     down_chunks = down.shape[0] // 2 // b_rows
-    b_chunks = down_chunks + c_rows // b_rows + 1
-    assert a_chunks == b_chunks and c_rows % b_rows == 0
-    assert down_chunks * 8 == a_chunks * 3 and (b_chunks - down_chunks) % 2 == 0
-    rest = b_chunks - down_chunks
+    b_chunks = 2 * down_chunks + c_rows // b_rows + 1
+    assert c_rows % b_rows == 0 and b_chunks % 2 == 0 and down_chunks % 2 == 0
+    assert down_chunks * 8 == a_chunks * 3
+    rest = b_chunks - 2 * down_chunks
     dma = pltpu.SemaphoreType.DMA
-    loads = 2 * (a_chunks + down_chunks)
+    loads = 2 * (a_chunks + 2 * down_chunks)
     pieces = n_fsdp * (len(mixers) + 1)
     return pl.pallas_call(
         functools.partial(tail_kernel, (n_ctx, n_fsdp)),
@@ -1836,6 +1797,190 @@
         ),
         cost_estimate=busy(70),
     )(x_low, gains, taps, conv_in, conv_out, gate, up, down)
+
+
+def ffn_grads_kernel(
+    blocks,
+    d_gate,
+    d_up,
+    act_in,
+    hidden_in,
+    d_all_in,
+    total,
+    shared_gu,
+    shared_down,
+    act,
+    hidden,
+    d_all,
+    load_sem,
+    gu_all,
+    gu_got,
+    gu_sum,
+    down_all,
+    down_got,
+    down_sum,
+    keep_sem,
+    beside_got,
+    across_got,
+    passed,
+    passed_got,
+    send_sem,
+    recv_sem,
+    pair_send,
+    pair_recv,
+):
+    section = lax.axis_index("section")
+    other = 1 - section
+    _, beside, across, _ = corners()
+    barrier = pltpu.get_barrier_semaphore()
+    for target in ({"fsdp": beside}, {"fsdp": across}, {"section": other}):
+        pl.semaphore_signal(barrier, inc=1, device_id=target, device_id_type=MESH)
+    pl.semaphore_wait(barrier, 3)
+    reduction = SideReduce(blocks, total, beside_got, across_got, passed, passed_got, send_sem, recv_sem)
+    reduction.start()
+    loads = [
+        pltpu.make_async_copy(src, dst, load_sem.at[index])
+        for index, (src, dst) in enumerate(((act_in, act), (hidden_in, hidden), (d_all_in, d_all)))
+    ]
+    for copy in loads:
+        copy.start()
+    tile = 256
+    half = gu_got.shape[2]
+    strips, owners, kinds, strip, _ = gu_sum.shape
+
+    def gate_swap(kind, owner):
+        start = owner * (2 * half) + other * half
+        return pltpu.make_async_remote_copy(
+            src_ref=gu_all.at[kind, pl.ds(pl.multiple_of(start, half), half)],
+            dst_ref=gu_got.at[kind, owner],
+            send_sem=pair_send.at[kind * owners + owner],
+            recv_sem=pair_recv.at[kind * owners + owner],
+            device_id={"section": other},
+            device_id_type=MESH,
+        )
+
+    loads[0].wait()
+    for kind, right in enumerate((d_gate, d_up)):
+
+        def column(owner, carry, kind=kind, right=right):
+            lanes = pl.ds(pl.multiple_of(owner * tile, tile), tile)
+            gu_all[kind, lanes] = dot_plain(act[:, lanes].T, right[...]).astype(BF16)
+            gate_swap(kind, owner).start()
+            return carry
+
+        lax.fori_loop(0, owners, column, 0)
+    reduction.relay()
+    for copy in loads[1:]:
+        copy.wait()
+    height = hidden.shape[1]
+
+    def down_tile(index, carry):
+        lanes = pl.ds(pl.multiple_of(index * tile, tile), tile)
+        down_all[lanes] = dot_plain(hidden[:, lanes].T, d_all[...]).astype(BF16)
+        return carry
+
+    lax.fori_loop(0, height // tile, down_tile, 0)
+    rest = height // tile * tile
+    if rest < height:
+        down_all[rest:] = dot_plain(hidden[:, rest:].T, d_all[...]).astype(BF16)
+    down_half = height // 2
+    down_swap = pltpu.make_async_remote_copy(
+        src_ref=down_all.at[pl.ds(pl.multiple_of(other * down_half, 16), down_half)],
+        dst_ref=down_got,
+        send_sem=pair_send.at[kinds * owners],
+        recv_sem=pair_recv.at[kinds * owners],
+        device_id={"section": other},
+        device_id_type=MESH,
+    )
+    down_swap.start()
+
+    def join(index, carry):
+        place = index // (owners * kinds)
+        left = lax.rem(index, owners * kinds)
+        owner, kind = left // kinds, lax.rem(left, kinds)
+
+        @pl.when(place == 0)
+        def _():
+            gate_swap(kind, owner).wait_recv()
+
+        mine = pl.ds(pl.multiple_of(owner * (2 * half) + section * half + place * strip, strip), strip)
+        theirs = pl.ds(pl.multiple_of(place * strip, strip), strip)
+        gu_sum[place, owner, kind] = (
+            gu_all[kind, mine].astype(F32) + gu_got[kind, owner, theirs].astype(F32)
+        ).astype(BF16)
+        return carry
+
+    lax.fori_loop(0, strips * owners * kinds, join, 0)
+    keeping = [pltpu.make_async_copy(gu_sum, shared_gu, keep_sem.at[0])]
+    keeping[0].start()
+    down_swap.wait_recv()
+    piece = 64
+
+    def join_down(index, carry):
+        theirs = pl.ds(pl.multiple_of(index * piece, piece), piece)
+        mine = pl.ds(pl.multiple_of(section * down_half + index * piece, piece), piece)
+        down_sum[theirs] = (down_all[mine].astype(F32) + down_got[theirs].astype(F32)).astype(BF16)
+        return carry
+
+    lax.fori_loop(0, down_half // piece, join_down, 0)
+    keeping.append(pltpu.make_async_copy(down_sum, shared_down, keep_sem.at[1]))
+    keeping[1].start()
+    reduction.finish()
+
+    def settle(index, carry):
+        gate_swap(index // owners, lax.rem(index, owners)).wait_send()
+        return carry
+
+    lax.fori_loop(0, kinds * owners, settle, 0)
+    down_swap.wait_send()
+    for copy in keeping:
+        copy.wait()
+
+
+def ffn_grads(blocks, d_gate, d_up, act, hidden, d_all, collective_id):
+    n_ctx, owners = lax.axis_size("ctx"), lax.axis_size("fsdp")
+    rows, width = blocks.shape[0] // owners, blocks.shape[1]
+    wide = d_gate.shape[1]
+    half = width // owners // 2
+    dma = pltpu.SemaphoreType.DMA
+    vmem = pl.BlockSpec(memory_space=pltpu.VMEM)
+    hbm = pl.BlockSpec(memory_space=pl.ANY)
+    pair = pltpu.VMEM((2, rows // 2, width), BF16)
+    summed = (n_ctx, owners, 2, half // n_ctx, wide)
+    assert width // owners == 256 and wide // 2 % 64 == 0
+    return pl.pallas_call(
+        ffn_grads_kernel,
+        out_shape=(
+            jax.ShapeDtypeStruct((rows, width), F32),
+            jax.ShapeDtypeStruct(summed, BF16),
+            jax.ShapeDtypeStruct((wide // 2, width), BF16),
+        ),
+        in_specs=[vmem] * 3 + [hbm] * 3,
+        out_specs=[vmem, hbm, hbm],
+        scratch_shapes=[pltpu.VMEM(k.shape, BF16) for k in (act, hidden, d_all)]
+        + [
+            dma((3,)),
+            pltpu.VMEM((2, width, wide), BF16),
+            pltpu.VMEM((2, owners, half, wide), BF16),
+            pltpu.VMEM(summed, BF16),
+            pltpu.VMEM((wide, width), BF16),
+            pltpu.VMEM((wide // 2, width), BF16),
+            pltpu.VMEM((wide // 2, width), BF16),
+            dma((2,)),
+            pair,
+            pair,
+            pair,
+            pair,
+            dma((6,)),
+            dma((6,)),
+            dma((2 * owners + 1,)),
+            dma((2 * owners + 1,)),
+        ],
+        compiler_params=pltpu.CompilerParams(
+            collective_id=collective_id, has_side_effects=True, vmem_limit_bytes=58 << 20
+        ),
+        cost_estimate=busy(25),
+    )(blocks, d_gate, d_up, act, hidden, d_all)
 
 
 def back_kernel(
@@ -2141,15 +2286,6 @@
     return terms, d_gate, d_up
 
 
-def ffn_weight_grads(d_all, kept, d_gate, d_up):
-    act, _, _, hidden = kept
-    return (
-        matmul_left(act, d_gate).astype(BF16),
-        matmul_left(act, d_up).astype(BF16),
-        matmul_left(hidden, d_all).astype(BF16),
-    )
-
-
 def ffn_norm_back(d_act, residual, gain):
     normed, inv_rms = norm_rows(residual)
     return norm_back(d_act * gain, normed, inv_rms), jnp.sum(d_act * normed, axis=0)
@@ -2185,9 +2321,10 @@
     mask = (positions < length).astype(F32)[:, None]
 
     def whole_rows(weight):
-        half = weight.shape[0] // micro
-        mine = lax.dynamic_slice_in_dim(weight, section * half, half, 0)
-        return lax.all_gather(mine, ("fsdp", "section"), axis=0, tiled=True)
+        share = weight.shape[0] // (micro * lax.axis_size("ctx"))
+        start = (section * lax.axis_size("ctx") + lax.axis_index("ctx")) * share
+        mine = lax.dynamic_slice_in_dim(weight, start, share, 0)
+        return lax.all_gather(mine, ("fsdp", "section", "ctx"), axis=0, tiled=True)
 
     part = ffn_gate.shape[1]
     attn_full = whole_rows(jnp.concatenate([attn_q, attn_k, attn_v, attn_out], axis=1))
@@ -2238,21 +2375,8 @@
 
     d_sum = d_sum_low.astype(F32)
     d_terms2, d_gate2, d_up2 = ffn_backward(d_sum_all, kept2, gate2, up2, down2)
-    grads2 = ffn_weight_grads(d_sum_all, kept2, d_gate2, d_up2)
-    half = part // 2
-    strip = half // lax.axis_size("ctx")
-
-    def column_half(which):
-        pieces = jnp.stack(grads2[:2]).reshape(2, fsdp, 2, half // strip, strip, -1)
-        pieces = lax.dynamic_index_in_dim(pieces, which, 2, keepdims=False)
-        return pieces.transpose(2, 1, 0, 3, 4).reshape(2 * fsdp * half, -1)
-
-    def down_half(which):
-        size = grads2[2].shape[0] // 2
-        return lax.dynamic_slice_in_dim(grads2[2], which * size, size, 0)
-
-    d_act3, got_gu, got_down = reduced_swapping(
-        d_terms2, column_half(1 - section), down_half(1 - section), 8
+    d_act3, shared_gu, shared_down = ffn_grads(
+        d_terms2, d_gate2, d_up2, act_all2, kept2[3], d_sum_all, 8
     )
     d_ffn, gain3 = ffn_norm_back(d_act3, res2, norm_gains[3])
     d_res2 = d_sum + d_ffn
@@ -2260,11 +2384,6 @@
     grad_proj = matmul_left(attended_low, d_attn)
     d_att = matmul_right(d_attn, proj_full).astype(BF16)
     delta = jnp.sum((d_att.astype(F32) * attended).reshape(rows, q_heads, head), axis=-1)
-    shared_terms = tuple(
-        (mine.astype(F32) + got.astype(F32)).astype(BF16)
-        for mine, got in ((column_half(section), got_gu), (down_half(section), got_down))
-    )
-    d_att, shared_terms = lax.optimization_barrier((d_att, shared_terms))
     d_query, d_kv, ffn2 = attend_back(
         length.reshape(1), query, kv_all, d_att, log_total, delta.T.reshape(q_heads, 1, rows), terms2, 4
     )
@@ -2274,8 +2393,8 @@
         return jnp.sum(mask * values * values, axis=0, keepdims=True)
 
     squares = [square(v) for v in (x, mixed, ffn1, h, attn_rows, res2, ffn2, result)]
-    second_gu, second_down = (
-        lax.psum_scatter(term, "ctx", scatter_dimension=0, tiled=True) for term in shared_terms
+    second_gu = lax.psum_scatter(
+        shared_gu.reshape(-1, shared_gu.shape[-1]), "ctx", scatter_dimension=0, tiled=True
     )
     d_qn = rounded(d_query)
     grad_qgain = jnp.sum(jnp.sum(d_qn * q_normed, axis=0).reshape(q_heads, head), axis=0)
@@ -2292,9 +2411,10 @@
     gain2 = jnp.sum(d_act2 * normed2, axis=0)
     d_h_low = (d_res2 + norm_back(d_act2 * norm_gains[2], normed2, inv2)).astype(BF16)
 
-    d_h_all, second_gu = gathered_swapped(d_h_low, second_gu.reshape(fsdp, 2 * strip, -1), 5)
+    d_h_all, second_gu = gathered_swapped(
+        d_h_low, second_gu.reshape(fsdp, -1, second_gu.shape[-1]), 5
+    )
     second_gu = lax.all_gather(second_gu, "ctx", axis=0)
-    second_down = lax.all_gather(second_down, "ctx", axis=0, tiled=True)
     d_terms1, d_gate1, d_up1 = ffn_backward(d_h_all, kept1, gate1, up1, down1)
     attn_mixers = [
         matmul_left(act2, d_qpre).astype(BF16),
@@ -2310,6 +2430,7 @@
         9,
     )
 
+    half = ffn_gate.shape[1] // 2
     y_low = result.astype(BF16)
     is_first = section == 0
     other_end = swapped(jnp.where(is_first, y_low, d_x), "section")
@@ -2327,8 +2448,8 @@
         grads[:3],
         attn_mixers + grads[3:],
         small,
-        second_gu.reshape(-1, fsdp, 2, strip, second_gu.shape[-1]),
-        second_down,
+        second_gu.reshape(-1, fsdp, 2, second_gu.shape[2] // 2, second_gu.shape[-1]),
+        shared_down,
     )
     rest_sum = rest_sum.astype(F32)
 

time: 733 us -> 715 us (0.975)
  matrix products: 99.4 us -> 85.8 us
    pallas_call x1, Pallas kernels: 164 us -> 182 us  [summed_gradients(): pl.pallas_call(functools.partial(tail_kernel, (n_ctx, n_fsdp)), out_shape...]
    pallas_call x1, Pallas kernels: 96.4 us -> 80.1 us  [attend_back(): pl.pallas_call(functools.partial(attend_back_kernel, n_ctx), out_shape=(w...]
    dot_general x6 -> x3, matrix products: 15.8 us -> 6.44 us  [matmul_left(): lax.dot_general(left_op, right_op, (((0,), (0,)), ((), ())), preferred_el...]
  transfers between devices with their start and end apart: 6 -> 4, of which waited for: 0 -> 0; matrix products, arithmetic and copies ran while one was open for 10% -> 10% of each run, Pallas kernels for 41% -> 35%
where the time goes in v10:
time: 715 us; the launch traced here: 706 us
  Pallas kernels  554 us (77%)
  matrix products  85.8 us (12%)
  other arithmetic  27 us (4%)
  local copies, waits for them, and re-layouts  22.3 us (3%)
  between operations  15.9 us (2%)
    pallas_call x1, Pallas kernels, summed_gradients(): pl.pallas_call(functools.partial(tail_kernel, (n_ctx, n_fsdp)), out_shape...  182 us
    pallas_call x1, Pallas kernels, front(): pl.pallas_call(functools.partial(front_kernel, n_ctx), out_shape=tuple((j...  108 us
    pallas_call x1, Pallas kernels, attend_back(): pl.pallas_call(functools.partial(attend_back_kernel, n_ctx), out_shape=(w...  80.1 us
    pallas_call x1, Pallas kernels, attend(): pl.pallas_call(functools.partial(attend_kernel, n_ctx), out_shape=(jax.Sh...  55.7 us
    pallas_call x1, Pallas kernels, conv_back(): pl.pallas_call(functools.partial(back_kernel, n_ctx), out_shape=(column,...  42.5 us
    dot_general x10, matrix products, matmul(): return jnp.dot(left_op, right_op, preferred_element_type=F32)  37.7 us
    dot_general x10, matrix products, matmul_right(): lax.dot_general(left_op, right_op, (((1,), (1,)), ((), ())), preferred_el...  33.5 us
    pallas_call x1, Pallas kernels, gathered_swapped(): pl.pallas_call(gather_swap_kernel, out_shape=(jax.ShapeDtypeStruct((4 * r...  26.1 us
  transfers between devices with their start and end apart: 4, of which 0 were waited for; matrix products, arithmetic and copies ran while one was open for 10% of the time, Pallas kernels for 35%

profile of v10, /device:TPU:0, one launch (start us, length us, event | category | flops | bytes accessed | tf_op | source)
XLA Modules:
  0.0 705.6 jit_solution(13797216051382306316)
XLA Ops:
  9.8 107.6 %shard_map.262 = (bf16[1024,3072]{1,0:T(8,128)(2,1)}, bf16[1024,1024]{1,0:T(8,128)(2,1)}, bf16[1024,1152]{1,0:T(8,128)(2,1)}, bf16[1024,1152]{1,0:T(8,128)(2,1)}...) custom-call(bf16[256,1024]{1,0:T(8,128)(2,1)} %dynamic-slice_bitcast, ...), custom_call_target="tpu_custom_call" | custom-call | flops 70 | bytes 65536 | tf_op jit(solution)/shard_map/pallas_call | solution.py:1761
  117.4 5.3 fusion.102
  122.8 4.5 multiply_convert_fusion.5
  127.3 3.1 convolution_convert_fusion.1.blocks
  130.5 19.7 %shard_map.263 = f32[256,1024]{1,0:T(8,128)S(1)} custom-call(bf16[1024,1024]{1,0:T(8,128)(2,1)S(1)} %convolution_convert_fusion.1.blocks), custom_call_target="tpu_custom_call" | custom-call | flops 25 | bytes 65536 | tf_op jit(solution)/shard_map/pallas_call | solution.py:268
  168.3 55.7 %shard_map.264 = (f32[256,1024]{1,0:T(8,128)}, f32[16,1,256]{2,1,0:T(1,128)}, bf16[1024,1024]{1,0:T(8,128)(2,1)}, bf16[1024,1024]{1,0:T(8,128)(2,1)}, bf16[1024,...) custom-call(s32[1]{0:T(128)} %dynamic_slice.26.length_ref, ...), custom_call_target="tpu_custom_call" | custom-call | flops 50 | bytes 65536 | tf_op jit(solution)/shard_map/pallas_call | solution.py:1317
  224.1 3.6 multiply_reduce_fusion.2
  227.9 18.6 %shard_map.265.act_in = bf16[1024,1024]{1,0:T(8,128)(2,1)S(1)} custom-call(bf16[256,1024]{1,0:T(8,128)(2,1)S(1)} %multiply_convert_fusion.6.block), custom_call_target="tpu_custom_call" | custom-call | flops 25 | bytes 65536 | tf_op jit(solution)/shard_map/pallas_call | solution.py:146
  249.6 2.9 fusion.103
  252.5 6.0 multiply_convert_fusion.2
  258.5 2.9 fusion.105
  261.5 4.2 add_convert_fusion.1.blocks
  265.7 22.3 %shard_map.266 = (f32[256,1024]{1,0:T(8,128)}, bf16[4,4,2,32,1152]{4,3,2,1,0:T(8,128)(2,1)}, bf16[576,1024]{1,0:T(8,128)(2,1)}) custom-call(bf16[1024,1024]{1,0:T(8,128)(2,1)} %add_convert_fusion.1.blocks, bf16[1024,1152]{1,0:T(8,128)(2,1)} %copy-done.25, bf16[1024,1152]{1,0:T(8,128)(2,1)} %copy-done.26, bf16[1024,1024]{1,0:T(8,128)(2,1)} %copy-done, ...), custom_call_target="tpu_custom_call" | custom-call | flops 25 | bytes 65536 | tf_op jit(solution)/shard_map/pallas_call | solution.py:1951
  290.4 4.1 convert_multiply_fusion.7
  298.9 6.6 convolution_convert_fusion.blocks
  305.5 80.1 %shard_map.267 = (f32[256,1024]{1,0:T(8,128)}, f32[256,1024]{1,0:T(8,128)}, f32[256,1024]{1,0:T(8,128)}) custom-call(s32[1]{0:T(128)} %dynamic_slice.26.length_ref, bf16[256,1024]{1,0:T(8,128)(2,1)} %get-tuple-element.108.query, bf16[1024,1024]{1,0:T(8,128)(2,1)} %get-tuple-element.64.kv_all, bf16[256,1024]{1,0:T(8,128)(2,1)} %get-tuple-element.145.d_out, ...), custom_call_target="tpu_custom_call" | custom-call | flops 50 | bytes 65536 | tf_op jit(solution)/shard_map/pallas_call | solution.py:1472
  404.2 26.1 %shard_map.268 = (bf16[1024,1024]{1,0:T(8,128)(2,1)S(1)}, bf16[4,64,1152]{2,1,0:T(8,128)(2,1)}) custom-call(bf16[256,1024]{1,0:T(8,128)(2,1)S(1)} %fusion.43.block.d_h, bf16[4,64,1152]{2,1,0:T(8,128)(2,1)S(1)} %bitcast.85), custom_call_target="tpu_custom_call" | custom-call | flops 25 | bytes 65536 | tf_op jit(solution)/shard_map/pallas_call | solution.py:188
  430.3 8.4 %multiply_convert_fusion = (bf16[1024,1152]{1,0:T(8,128)(2,1)S(1)}, bf16[1024,1152]{1,0:T(8,128)(2,1)S(1)}) fusion(f32[1024,1152]{1,0:T(8,128)} %copy-done.50, f32[1024,1152]{1,0:T(8,128)} %get-tuple-element.140, bf16[1024,1024]{1,0:T(8,128)(2,1)S(1)} %get-tuple-element.69.d_all_in, bf16[1152,1024]{1,0:T(8,128)(2,1)} %get-tuple-element.57), kind=kOutput, calls=%fused_computation | convolution fusion | flops 2431254528 | bytes 18612224 | tf_op jit(solution)/shard_map/dot_general | solution.py:40
  438.7 2.9 fusion.106
  442.1 4.1 add_convert_fusion.blocks
  446.2 42.5 %shard_map.269 = (bf16[1024,1152]{1,0:T(8,128)(2,1)}, bf16[1024,1152]{1,0:T(8,128)(2,1)}, bf16[1152,1024]{1,0:T(8,128)(2,1)}, bf16[1024,1024]{1,0:T(8,128)(2,1)}...) custom-call(bf16[1024,1024]{1,0:T(8,128)(2,1)} %add_convert_fusion.b, ...), custom_call_target="tpu_custom_call" | custom-call | flops 35 | bytes 65536 | tf_op jit(solution)/shard_map/pallas_call | solution.py:2228
  496.8 181.7 %shard_map.270 = (bf16[2,256,4608]{2,1,0:T(8,128)(2,1)}, bf16[1152,1024]{1,0:T(8,128)(2,1)}, bf16[2,960,1024]{2,1,0:T(8,128)(2,1)}) custom-call(bf16[1024,1152]{1,0:T(8,128)(2,1)} %get-tuple-element.78.gate_in, bf16[1024,1152]{1,0:T(8,128)(2,1)} %get-tuple-element.79.up_in, bf16[1152,1024]{1,0:T(8,128)(2,1)} %get-tuple-element.80.down_in, ...), custom_call_target="tpu_custom_call" | custom-call | flops 160 | bytes 65536 | tf_op jit(solution)/shard_map/pallas_call | solution.py:943
  679.5 4.4 fusion.98
  687.8 5.0 slice_convert_fusion
  (208 shorter events, 67.5 us)
Async XLA Ops:
  7.2 149.3 %all-gather.4.cloned.1.call-start = ((), (), s32[]{:S(2)}) async-start(), calls=%async_computation.1 | async-start | bytes 6488064 | tf_op jit(solution)/shard_map/all_gather | solution.py:2327
  8.9 394.0 %reduce-scatter.2.cloned.1.call-start = ((), (), s32[]{:S(2)}) async-start(), calls=%async_computation.2 | async-start | bytes 2949120 | tf_op jit(solution)/shard_map/reduce_scatter | solution.py:2396
  117.4 5.4 copy-start.27
  117.4 5.4 copy-start.42
  130.4 19.8 %copy-start.49 = (s32[8]{0:T(128)S(1)}, s32[8]{0:T(128)}, u32[]{:S(2)}) copy-start(s32[8]{0:T(128)} %param.17) | copy-start | bytes 100
  130.5 21.0 %copy-start.41 = (f32[2,64]{1,0:T(2,128)S(1)}, f32[2,64]{1,0:T(2,128)}, u32[]{:S(2)}) copy-start(f32[2,64]{1,0:T(2,128)} %param.26) | copy-start | bytes 1540
  130.5 22.5 %copy-start.11 = (f32[256,1024]{1,0:T(8,128)S(1)}, f32[256,1024]{1,0:T(8,128)}, u32[]{:S(2)}) copy-start(f32[256,1024]{1,0:T(8,128)} %get-tuple-element.53.mixed) | copy-start | bytes 3145732
  154.2 69.8 %copy-start.7 = (bf16[256,1024]{1,0:T(8,128)(2,1)}, bf16[256,1024]{1,0:T(8,128)(2,1)S(1)}, u32[]{:S(2)}) copy-start(bf16[256,1024]{1,0:T(8,128)(2,1)S(1)} %get-tuple-element.111) | copy-start | bytes 1572868
  227.9 18.6 %copy-start.48 = (bf16[1024,1152]{1,0:T(8,128)(2,1)S(1)}, bf16[1024,1152]{1,0:T(8,128)(2,1)}, u32[]{:S(2)}) copy-start(bf16[1024,1152]{1,0:T(8,128)(2,1)} %get-tuple-element.62) | copy-start | bytes 7077892
  246.5 6.0 copy-start
  290.3 112.3 %copy-start.5 = (f32[256,1024]{1,0:T(8,128)}, f32[256,1024]{1,0:T(8,128)S(1)}, u32[]{:S(2)}) copy-start(f32[256,1024]{1,0:T(8,128)S(1)} %subtract_add_fusion) | copy-start | bytes 3145732
  290.3 206.5 %all-gather.6.cloned.1.call-start = ((), (), s32[]{:S(2)}) async-start(), calls=%async_computation.3 | async-start | bytes 2949120 | tf_op jit(solution)/shard_map/all_gather | solution.py:2417
  305.4 87.5 %slice-start = ((s8[6291456]{0:T(1024)(128)(4,1)}), s8[2097152]{0:T(1024)(128)(4,1)S(1)}, s32[]{:S(2)}) async-start(s8[6291456]{0:T(1024)(128)(4,1)} %bitcast.92), calls=%async_computation.4 | async-start | bytes 4194304
  387.0 5.9 slice-start.1
  402.9 35.8 %copy-start.1 = (bf16[256,1024]{1,0:T(8,128)(2,1)}, bf16[256,1024]{1,0:T(8,128)(2,1)S(1)}, u32[]{:S(2)}) copy-start(bf16[256,1024]{1,0:T(8,128)(2,1)S(1)} %fusion.43.block.d_h) | copy-start | bytes 1572868
  430.3 8.4 %copy-start.2 = (bf16[1024,1024]{1,0:T(8,128)(2,1)}, bf16[1024,1024]{1,0:T(8,128)(2,1)S(1)}, u32[]{:S(2)}) copy-start(bf16[1024,1024]{1,0:T(8,128)(2,1)S(1)} %get-tuple-element.69.d_all_in) | copy-start | bytes 6291460
  430.3 8.4 %copy-start.44 = (bf16[1024,1152]{1,0:T(8,128)(2,1)S(1)}, bf16[1024,1152]{1,0:T(8,128)(2,1)}, u32[]{:S(2)}) copy-start(bf16[1024,1152]{1,0:T(8,128)(2,1)} %get-tuple-element.55) | copy-start | bytes 7077892
  446.2 42.5 %copy-start.16 = (bf16[256,1024]{1,0:T(8,128)(2,1)S(1)}, bf16[256,1024]{1,0:T(8,128)(2,1)}, u32[]{:S(2)}) copy-start(bf16[256,1024]{1,0:T(8,128)(2,1)} %get-tuple-element.103) | copy-start | bytes 1572868
  446.2 42.7 %copy-start.10 = (bf16[256,1024]{1,0:T(8,128)(2,1)S(1)}, bf16[256,1024]{1,0:T(8,128)(2,1)}, u32[]{:S(2)}) copy-start(bf16[256,1024]{1,0:T(8,128)(2,1)} %copy-done.7) | copy-start | bytes 1572868
  446.2 42.7 %copy-start.36 = (bf16[256,512]{1,0:T(8,128)(2,1)S(1)}, bf16[256,512]{1,0:T(8,128)(2,1)}, u32[]{:S(2)}) copy-start(bf16[256,512]{1,0:T(8,128)(2,1)} %copy-done.35) | copy-start | bytes 786436
  446.2 42.7 %copy-start.38 = (bf16[256,512]{1,0:T(8,128)(2,1)S(1)}, bf16[256,512]{1,0:T(8,128)(2,1)}, u32[]{:S(2)}) copy-start(bf16[256,512]{1,0:T(8,128)(2,1)} %get-tuple-element.128) | copy-start | bytes 786436
  488.8 7.0 collective-permute-start
  678.6 9.2 %slice-start.2 = ((s8[4718592]{0:T(1024)(128)(4,1)}), s8[4194304]{0:T(1024)(128)(4,1)S(1)}, s32[]{:S(2)}) async-start(s8[4718592]{0:T(1024)(128)(4,1)} %bitcast.94), calls=%async_computation.6 | async-start | bytes 8388608
  679.5 8.3 %slice-start.3 = ((s8[4718592]{0:T(1024)(128)(4,1)}), s8[524288]{0:T(1024)(128)(4,1)S(1)}, s32[]{:S(2)}) async-start(s8[4718592]{0:T(1024)(128)(4,1)} %bitcast.94), calls=%async_computation.7 | async-start | bytes 1048576
  (35 other events, 96.2 us)
Sparse Core Ops, SparseCore 0:
  11.5 93.7 all-gather.3
  290.4 76.4 reduce-scatter.1
  430.4 49.0 all-gather.5

commit v11 on v10

--- a/solution.py
+++ b/solution.py
@@ -1087,6 +1087,73 @@
                 self.handed(step, kind).wait_send()
 
 
+class SharedColumns(Columns):
+    def __init__(self, *args):
+        *args, plane_send, plane_recv = args
+        super().__init__(*args)
+        self.plane = plane_send, plane_recv
+        place = lax.axis_index("ctx")
+        self.odd = lax.rem(place, 2)
+        self.partner = place + 1 - 2 * self.odd
+
+    def passed_on(self, step, kind):
+        at = self.at_rows(self.targets[kind], lax.rem(self.me + self.count - step, self.count))
+        return pltpu.make_async_remote_copy(
+            src_ref=at,
+            dst_ref=at,
+            send_sem=self.plane[0].at[kind, step],
+            recv_sem=self.plane[1].at[kind, step],
+            device_id={"ctx": self.partner},
+            device_id_type=MESH,
+        )
+
+    def by_kind(self, action):
+        for kind in range(2):
+
+            @pl.when((self.section == self.holder) & (self.odd == kind))
+            def _(kind=kind):
+                for step in range(1, self.count):
+                    action(step, kind)
+
+    def start(self):
+        self.by_kind(lambda step, kind: self.crossing(step, kind).start())
+
+        @pl.when(self.section == self.holder)
+        def _():
+            for kind in range(3):
+                self.handed(0, kind).start()
+            for kind in range(3):
+                self.kept(kind).start()
+
+    def relay(self):
+        def moved(step, kind):
+            self.crossing(step, kind).wait_recv()
+            self.passed_on(step, kind).start()
+            self.handed(step, kind).start()
+
+        self.by_kind(moved)
+
+    def relay_passed(self):
+        def passed(step, kind):
+            self.passed_on(step, 1 - kind).wait_recv()
+            self.handed(step, 1 - kind).start()
+
+        self.by_kind(passed)
+
+    def finish(self):
+        def sent(step, kind):
+            self.crossing(step, kind).wait_send()
+            self.passed_on(step, kind).wait_send()
+
+        self.by_kind(sent)
+        every = [(0, kind) for kind in range(3)] + self.steps
+
+        @pl.when(self.section == self.holder)
+        def _():
+            for step, kind in every:
+                self.handed(step, kind).wait_send()
+
+
 class Chain:
     def __init__(self, count):
         self.count = count
@@ -1624,6 +1691,8 @@
     pair_send,
     pair_recv,
     own_sem,
+    plane_send,
+    plane_recv,
     act_send,
     act_recv,
     act_own,
@@ -1640,8 +1709,17 @@
         (conv_in, conv_out), (w_in, w_out), mix_send, mix_recv, mix_pair_send, mix_pair_recv, mix_own
     )
     mixers.start()
-    columns = Columns(
-        0, (gate_in, up_in, down_in), (w_gate, w_up, w_down), send_sem, recv_sem, pair_send, pair_recv, own_sem
+    columns = SharedColumns(
+        0,
+        (gate_in, up_in, down_in),
+        (w_gate, w_up, w_down),
+        send_sem,
+        recv_sem,
+        pair_send,
+        pair_recv,
+        own_sem,
+        plane_send,
+        plane_recv,
     )
     gather = SideGather(act2, act_all, act_send, act_recv, act_own)
     keeping = [
@@ -1728,8 +1806,9 @@
 
     lax.fori_loop(0, rows // strip, second_norm, 0)
     gather.start()
+    columns.relay()
     gather.relay()
-    columns.relay()
+    columns.relay_passed()
     columns.arrive()
     for copy in keeping[2:]:
         copy.start()
@@ -1787,6 +1866,8 @@
             dma((3, count)),
             dma((3, count)),
             dma((3,)),
+            dma((2, count)),
+            dma((2, count)),
             dma((4,)),
             dma((4,)),
             dma,
@@ -1799,20 +1880,29 @@
     )(x_low, gains, taps, conv_in, conv_out, gate, up, down)
 
 
-def ffn_grads_kernel(
-    blocks,
-    d_gate,
-    d_up,
-    act_in,
-    hidden_in,
+def turn_kernel(
+    act_block,
+    w_gate_in,
+    w_up_in,
+    w_down_in,
     d_all_in,
+    terms,
     total,
     shared_gu,
     shared_down,
+    w_gate,
+    w_up,
+    w_down,
+    d_all,
+    load_sem,
     act,
     hidden,
-    d_all,
-    load_sem,
+    d_gate,
+    d_up,
+    blocks,
+    act_send,
+    act_recv,
+    act_own,
     gu_all,
     gu_got,
     gu_sum,
@@ -1837,13 +1927,64 @@
         pl.semaphore_signal(barrier, inc=1, device_id=target, device_id_type=MESH)
     pl.semaphore_wait(barrier, 3)
     reduction = SideReduce(blocks, total, beside_got, across_got, passed, passed_got, send_sem, recv_sem)
-    reduction.start()
+    gather = SideGather(act_block, act, act_send, act_recv, act_own)
+    gather.start()
     loads = [
         pltpu.make_async_copy(src, dst, load_sem.at[index])
-        for index, (src, dst) in enumerate(((act_in, act), (hidden_in, hidden), (d_all_in, d_all)))
+        for index, (src, dst) in enumerate(
+            ((w_gate_in, w_gate), (w_up_in, w_up), (d_all_in, d_all), (w_down_in, w_down))
+        )
     ]
     for copy in loads:
         copy.start()
+    me, _, _, opposite = corners()
+    rows = act_block.shape[0]
+    wide, width = w_down.shape
+    lanes_wide, lanes_out = 384, 512
+
+    def turn(owner):
+        at = pl.ds(pl.multiple_of(owner * rows, rows), rows)
+
+        def hidden_part(index, carry):
+            lanes = pl.ds(pl.multiple_of(index * lanes_wide, 128), lanes_wide)
+            gate_pre = dot_plain(act[at], w_gate[:, lanes])
+            up_pre = dot_plain(act[at], w_up[:, lanes])
+            d_hidden = dot_right(d_all[at], w_down[lanes])
+            sigmoid = jax.nn.sigmoid(gate_pre)
+            silu = gate_pre * sigmoid
+            hidden[at, lanes] = (silu * up_pre).astype(BF16)
+            d_up[at, lanes] = (d_hidden * silu).astype(BF16)
+            d_gate[at, lanes] = (
+                d_hidden * up_pre * sigmoid * (1.0 + gate_pre * (1.0 - sigmoid))
+            ).astype(BF16)
+            return carry
+
+        lax.fori_loop(0, wide // lanes_wide, hidden_part, 0)
+
+        def out_part(index, carry):
+            lanes = pl.ds(pl.multiple_of(index * lanes_out, 128), lanes_out)
+            terms[at, lanes] = dot_plain(hidden[at], w_down[:, lanes]).astype(BF16)
+            blocks[at, lanes] = (
+                dot_right(d_gate[at], w_gate[lanes]) + dot_right(d_up[at], w_up[lanes])
+            ).astype(BF16)
+            return carry
+
+        lax.fori_loop(0, width // lanes_out, out_part, 0)
+
+    gather.own.wait()
+    for copy in loads:
+        copy.wait()
+    turn(me)
+    gather.relay()
+    turn(beside)
+    turn(across)
+    reduction.copies[1].start()
+    reduction.copies[3].start()
+    gather.third.wait_recv()
+    gather.fourth.wait_recv()
+    turn(opposite)
+    reduction.copies[0].start()
+    reduction.copies[2].start()
     tile = 256
     half = gu_got.shape[2]
     strips, owners, kinds, strip, _ = gu_sum.shape
@@ -1859,7 +2000,6 @@
             device_id_type=MESH,
         )
 
-    loads[0].wait()
     for kind, right in enumerate((d_gate, d_up)):
 
         def column(owner, carry, kind=kind, right=right):
@@ -1870,8 +2010,6 @@
 
         lax.fori_loop(0, owners, column, 0)
     reduction.relay()
-    for copy in loads[1:]:
-        copy.wait()
     height = hidden.shape[1]
 
     def down_tile(index, carry):
@@ -1933,33 +2071,46 @@
 
     lax.fori_loop(0, kinds * owners, settle, 0)
     down_swap.wait_send()
+    for copy in (gather.first, gather.second, gather.third, gather.fourth):
+        copy.wait_send()
     for copy in keeping:
         copy.wait()
 
 
-def ffn_grads(blocks, d_gate, d_up, act, hidden, d_all, collective_id):
+def ffn_turn(act_block, w_gate, w_up, w_down, d_all, collective_id):
     n_ctx, owners = lax.axis_size("ctx"), lax.axis_size("fsdp")
-    rows, width = blocks.shape[0] // owners, blocks.shape[1]
-    wide = d_gate.shape[1]
+    rows, width = act_block.shape
+    wide = w_gate.shape[1]
     half = width // owners // 2
     dma = pltpu.SemaphoreType.DMA
     vmem = pl.BlockSpec(memory_space=pltpu.VMEM)
     hbm = pl.BlockSpec(memory_space=pl.ANY)
     pair = pltpu.VMEM((2, rows // 2, width), BF16)
     summed = (n_ctx, owners, 2, half // n_ctx, wide)
-    assert width // owners == 256 and wide // 2 % 64 == 0
+    assert width // owners == 256 and wide // 2 % 64 == 0 and wide % 384 == 0
+    whole = (owners * rows, width)
+    columns = pltpu.VMEM((owners * rows, wide), BF16)
     return pl.pallas_call(
-        ffn_grads_kernel,
+        turn_kernel,
         out_shape=(
+            jax.ShapeDtypeStruct(whole, BF16),
             jax.ShapeDtypeStruct((rows, width), F32),
             jax.ShapeDtypeStruct(summed, BF16),
             jax.ShapeDtypeStruct((wide // 2, width), BF16),
         ),
-        in_specs=[vmem] * 3 + [hbm] * 3,
-        out_specs=[vmem, hbm, hbm],
-        scratch_shapes=[pltpu.VMEM(k.shape, BF16) for k in (act, hidden, d_all)]
+        in_specs=[vmem] + [hbm] * 4,
+        out_specs=[vmem, vmem, hbm, hbm],
+        scratch_shapes=[pltpu.VMEM(k.shape, BF16) for k in (w_gate, w_up, w_down, d_all)]
         + [
-            dma((3,)),
+            dma((4,)),
+            pltpu.VMEM(whole, BF16),
+            columns,
+            columns,
+            columns,
+            pltpu.VMEM(whole, BF16),
+            dma((4,)),
+            dma((4,)),
+            dma,
             pltpu.VMEM((2, width, wide), BF16),
             pltpu.VMEM((2, owners, half, wide), BF16),
             pltpu.VMEM(summed, BF16),
@@ -1979,8 +2130,8 @@
         compiler_params=pltpu.CompilerParams(
             collective_id=collective_id, has_side_effects=True, vmem_limit_bytes=58 << 20
         ),
-        cost_estimate=busy(25),
-    )(blocks, d_gate, d_up, act, hidden, d_all)
+        cost_estimate=busy(45),
+    )(act_block, w_gate, w_up, w_down, d_all)
 
 
 def back_kernel(
@@ -2370,14 +2521,11 @@
     attn_rows = matmul(attended_low, proj_full)
     res2 = h + attn_rows
     normed3, _ = norm_rows(res2)
-    act_all2 = gathered((normed3 * norm_gains[3]).astype(BF16), 0)
-    terms2, kept2 = ffn_forward(act_all2, gate2, up2, down2)
+    terms2, d_act3, shared_gu, shared_down = ffn_turn(
+        (normed3 * norm_gains[3]).astype(BF16), gate2, up2, down2, d_sum_all, 8
+    )
 
     d_sum = d_sum_low.astype(F32)
-    d_terms2, d_gate2, d_up2 = ffn_backward(d_sum_all, kept2, gate2, up2, down2)
-    d_act3, shared_gu, shared_down = ffn_grads(
-        d_terms2, d_gate2, d_up2, act_all2, kept2[3], d_sum_all, 8
-    )
     d_ffn, gain3 = ffn_norm_back(d_act3, res2, norm_gains[3])
     d_res2 = d_sum + d_ffn
     d_attn = d_res2.astype(BF16)

time: 715 us -> 691 us (0.966)
  matrix products: 85.8 us -> 60.3 us
    dot_general x10 -> x7, matrix products: 37.7 us -> 22.3 us  [matmul(): return jnp.dot(left_op, right_op, preferred_element_type=F32)]
    dot_general x10 -> x7, matrix products: 33.5 us -> 23.7 us  [matmul_right(): lax.dot_general(left_op, right_op, (((1,), (1,)), ((), ())), preferred_el...]
    pallas_call x2 -> x1, Pallas kernels: 40.9 us -> 48.2 us  [ffn_turn(): pl.pallas_call(turn_kernel, out_shape=(jax.ShapeDtypeStruct(whole, BF16),...]
    pallas_call x1, Pallas kernels: 108 us -> 100 us  [front(): pl.pallas_call(functools.partial(front_kernel, n_ctx), out_shape=tuple((j...]
  transfers between devices with their start and end apart: 4 -> 4, of which waited for: 0 -> 0; matrix products, arithmetic and copies ran while one was open for 10% -> 10% of each run, Pallas kernels for 35% -> 36%
where the time goes in v11:
time: 691 us; the launch traced here: 681 us
  Pallas kernels  554 us (80%)
  matrix products  60.3 us (9%)
  other arithmetic  29.1 us (4%)
  local copies, waits for them, and re-layouts  22.1 us (3%)
  between operations  15.5 us (2%)
    pallas_call x1, Pallas kernels, summed_gradients(): pl.pallas_call(functools.partial(tail_kernel, (n_ctx, n_fsdp)), out_shape...  181 us
    pallas_call x1, Pallas kernels, front(): pl.pallas_call(functools.partial(front_kernel, n_ctx), out_shape=tuple((j...  100 us
    pallas_call x1, Pallas kernels, attend_back(): pl.pallas_call(functools.partial(attend_back_kernel, n_ctx), out_shape=(w...  83.2 us
    pallas_call x1, Pallas kernels, attend(): pl.pallas_call(functools.partial(attend_kernel, n_ctx), out_shape=(jax.Sh...  54.4 us
    pallas_call x1, Pallas kernels, ffn_turn(): pl.pallas_call(turn_kernel, out_shape=(jax.ShapeDtypeStruct(whole, BF16),...  48.2 us
    pallas_call x1, Pallas kernels, conv_back(): pl.pallas_call(functools.partial(back_kernel, n_ctx), out_shape=(column,...  42.5 us
    pallas_call x1, Pallas kernels, gathered_swapped(): pl.pallas_call(gather_swap_kernel, out_shape=(jax.ShapeDtypeStruct((4 * r...  25 us
    dot_general x7, matrix products, matmul_right(): lax.dot_general(left_op, right_op, (((1,), (1,)), ((), ())), preferred_el...  23.7 us
  transfers between devices with their start and end apart: 4, of which 0 were waited for; matrix products, arithmetic and copies ran while one was open for 10% of the time, Pallas kernels for 36%

profile of v11, /device:TPU:0, one launch (start us, length us, event | category | flops | bytes accessed | tf_op | source)
XLA Modules:
  0.0 681.3 jit_solution(4963436100421816466)
XLA Ops:
  9.8 100.3 %shard_map.262 = (bf16[1024,3072]{1,0:T(8,128)(2,1)}, bf16[1024,1024]{1,0:T(8,128)(2,1)}, bf16[1024,1152]{1,0:T(8,128)(2,1)}, bf16[1024,1152]{1,0:T(8,128)(2,1)}...) custom-call(bf16[256,1024]{1,0:T(8,128)(2,1)} %dynamic-slice_bitcast, ...), custom_call_target="tpu_custom_call" | custom-call | flops 70 | bytes 65536 | tf_op jit(solution)/shard_map/pallas_call | solution.py:1840
  110.2 5.3 fusion.102
  115.5 4.5 multiply_convert_fusion.2
  120.1 3.1 convolution_convert_fusion.blocks
  123.2 19.6 %shard_map.263 = f32[256,1024]{1,0:T(8,128)S(1)} custom-call(bf16[1024,1024]{1,0:T(8,128)(2,1)S(1)} %convolution_convert_fusion.blocks), custom_call_target="tpu_custom_call" | custom-call | flops 25 | bytes 65536 | tf_op jit(solution)/shard_map/pallas_call | solution.py:268
  149.1 2.3 fusion.6
  160.7 54.4 %shard_map.264 = (f32[256,1024]{1,0:T(8,128)}, f32[16,1,256]{2,1,0:T(1,128)}, bf16[1024,1024]{1,0:T(8,128)(2,1)}, bf16[1024,1024]{1,0:T(8,128)(2,1)}, bf16[1024,...) custom-call(s32[1]{0:T(128)} %dynamic_slice.26.length_ref, ...), custom_call_target="tpu_custom_call" | custom-call | flops 50 | bytes 65536 | tf_op jit(solution)/shard_map/pallas_call | solution.py:1384
  215.1 3.6 multiply_reduce_fusion.2
  219.7 48.2 %shard_map.265 = (bf16[1024,1024]{1,0:T(8,128)(2,1)}, f32[256,1024]{1,0:T(8,128)}, bf16[4,4,2,32,1152]{4,3,2,1,0:T(8,128)(2,1)}, bf16[576,1024]{1,0:T(8,128)(2,1)}) custom-call(bf16[256,1024]{1,0:T(8,128)(2,1)} %multiply_convert_fusion.3.act_block, bf16[1024,1152]{1,0:T(8,128)(2,1)} %get-tuple-element.60.w_gate_in, ...), custom_call_target="tpu_custom_call" | custom-call | flops 45 | bytes 65536 | tf_op jit(solution)/shard_map/pallas_call | solution.py:2093
  271.5 3.9 convert_multiply_fusion.7
  275.4 2.5 copy.32
  279.8 83.2 %shard_map.266 = (f32[256,1024]{1,0:T(8,128)}, f32[256,1024]{1,0:T(8,128)}, f32[256,1024]{1,0:T(8,128)}) custom-call(s32[1]{0:T(128)} %dynamic_slice.26.length_ref, bf16[256,1024]{1,0:T(8,128)(2,1)} %get-tuple-element.110.query, bf16[1024,1024]{1,0:T(8,128)(2,1)} %get-tuple-element.65.kv_all, bf16[256,1024]{1,0:T(8,128)(2,1)} %get-tuple-element.144.d_out, ...), custom_call_target="tpu_custom_call" | custom-call | flops 50 | bytes 65536 | tf_op jit(solution)/shard_map/pallas_call | solution.py:1539
  373.1 2.8 fusion.38
  377.7 2.2 convolution_convert_fusion.3.query_in
  381.6 25.0 %shard_map.267 = (bf16[1024,1024]{1,0:T(8,128)(2,1)S(1)}, bf16[4,64,1152]{2,1,0:T(8,128)(2,1)}) custom-call(bf16[256,1024]{1,0:T(8,128)(2,1)S(1)} %fusion.43.block.d_h, bf16[4,64,1152]{2,1,0:T(8,128)(2,1)S(1)} %bitcast.73), custom_call_target="tpu_custom_call" | custom-call | flops 25 | bytes 65536 | tf_op jit(solution)/shard_map/pallas_call | solution.py:188
  406.7 8.8 %multiply_convert_fusion = (bf16[1024,1152]{1,0:T(8,128)(2,1)S(1)}, bf16[1024,1152]{1,0:T(8,128)(2,1)S(1)}) fusion(f32[1024,1152]{1,0:T(8,128)} %copy-done.43, f32[1024,1152]{1,0:T(8,128)} %get-tuple-element.139, bf16[1024,1024]{1,0:T(8,128)(2,1)S(1)} %get-tuple-element.71.d_all_in, bf16[1152,1024]{1,0:T(8,128)(2,1)} %get-tuple-element.58), kind=kOutput, calls=%fused_computation | convolution fusion | flops 2431254528 | bytes 18612224 | tf_op jit(solution)/shard_map/dot_general | solution.py:40
  415.5 2.9 fusion.103
  418.9 4.1 add_convert_fusion.blocks
  423.0 42.5 %shard_map.268 = (bf16[1024,1152]{1,0:T(8,128)(2,1)}, bf16[1024,1152]{1,0:T(8,128)(2,1)}, bf16[1152,1024]{1,0:T(8,128)(2,1)}, bf16[1024,1024]{1,0:T(8,128)(2,1)}...) custom-call(bf16[1024,1024]{1,0:T(8,128)(2,1)} %add_convert_fusion.b, ...), custom_call_target="tpu_custom_call" | custom-call | flops 35 | bytes 65536 | tf_op jit(solution)/shard_map/pallas_call | solution.py:2379
  470.0 2.5 concatenate.33
  473.7 180.8 %shard_map.269 = (bf16[2,256,4608]{2,1,0:T(8,128)(2,1)}, bf16[1152,1024]{1,0:T(8,128)(2,1)}, bf16[2,960,1024]{2,1,0:T(8,128)(2,1)}) custom-call(bf16[1024,1152]{1,0:T(8,128)(2,1)} %get-tuple-element.80.gate_in, bf16[1024,1152]{1,0:T(8,128)(2,1)} %get-tuple-element.81.up_in, bf16[1152,1024]{1,0:T(8,128)(2,1)} %get-tuple-element.82.down_in, ...), custom_call_target="tpu_custom_call" | custom-call | flops 160 | bytes 65536 | tf_op jit(solution)/shard_map/pallas_call | solution.py:943
  655.4 4.4 fusion.98
  663.7 5.0 slice_convert_fusion
  668.7 2.7 bitcast_convert_fusion
  (187 shorter events, 51.0 us)
Async XLA Ops:
  7.2 141.9 %all-gather.4.cloned.1.call-start = ((), (), s32[]{:S(2)}) async-start(), calls=%async_computation.1 | async-start | bytes 6488064 | tf_op jit(solution)/shard_map/all_gather | solution.py:2478
  8.9 371.4 %reduce-scatter.2.cloned.1.call-start = ((), (), s32[]{:S(2)}) async-start(), calls=%async_computation.2 | async-start | bytes 2949120 | tf_op jit(solution)/shard_map/reduce_scatter | solution.py:2544
  110.1 5.4 copy-start.25
  110.1 5.4 copy-start.38
  123.2 19.7 %copy-start.42 = (s32[8]{0:T(128)S(1)}, s32[8]{0:T(128)}, u32[]{:S(2)}) copy-start(s32[8]{0:T(128)} %param.17) | copy-start | bytes 100
  123.2 20.9 %copy-start.37 = (f32[2,64]{1,0:T(2,128)S(1)}, f32[2,64]{1,0:T(2,128)}, u32[]{:S(2)}) copy-start(f32[2,64]{1,0:T(2,128)} %param.26) | copy-start | bytes 1540
  123.2 22.4 %copy-start.11 = (f32[256,1024]{1,0:T(8,128)S(1)}, f32[256,1024]{1,0:T(8,128)}, u32[]{:S(2)}) copy-start(f32[256,1024]{1,0:T(8,128)} %get-tuple-element.54.mixed) | copy-start | bytes 3145732
  146.9 11.2 %copy-start.6 = (bf16[256,1024]{1,0:T(8,128)(2,1)}, bf16[256,1024]{1,0:T(8,128)(2,1)S(1)}, u32[]{:S(2)}) copy-start(bf16[256,1024]{1,0:T(8,128)(2,1)S(1)} %get-tuple-element.113) | copy-start | bytes 1572868
  160.7 54.4 %copy-start.7 = (bf16[256,1024]{1,0:T(8,128)(2,1)S(1)}, bf16[256,1024]{1,0:T(8,128)(2,1)}, u32[]{:S(2)}) copy-start(bf16[256,1024]{1,0:T(8,128)(2,1)} %copy-done.6) | copy-start | bytes 1572868
  269.6 204.1 %all-gather.6.cloned.1.call-start = ((), (), s32[]{:S(2)}) async-start(), calls=%async_computation.3 | async-start | bytes 2949120 | tf_op jit(solution)/shard_map/all_gather | solution.py:2565
  279.8 90.5 %slice-start = ((s8[6291456]{0:T(1024)(128)(4,1)}), s8[2097152]{0:T(1024)(128)(4,1)S(1)}, s32[]{:S(2)}) async-start(s8[6291456]{0:T(1024)(128)(4,1)} %bitcast.80), calls=%async_computation.4 | async-start | bytes 4194304
  364.4 5.9 slice-start.1
  380.3 35.1 %copy-start = (bf16[256,1024]{1,0:T(8,128)(2,1)}, bf16[256,1024]{1,0:T(8,128)(2,1)S(1)}, u32[]{:S(2)}) copy-start(bf16[256,1024]{1,0:T(8,128)(2,1)S(1)} %fusion.43.block.d_h) | copy-start | bytes 1572868
  406.6 8.9 %copy-start.1 = (bf16[1024,1024]{1,0:T(8,128)(2,1)}, bf16[1024,1024]{1,0:T(8,128)(2,1)S(1)}, u32[]{:S(2)}) copy-start(bf16[1024,1024]{1,0:T(8,128)(2,1)S(1)} %get-tuple-element.71.d_all_in) | copy-start | bytes 6291460
  406.6 8.9 %copy-start.40 = (bf16[1024,1152]{1,0:T(8,128)(2,1)S(1)}, bf16[1024,1152]{1,0:T(8,128)(2,1)}, u32[]{:S(2)}) copy-start(bf16[1024,1152]{1,0:T(8,128)(2,1)} %get-tuple-element.56) | copy-start | bytes 7077892
  423.0 42.5 %copy-start.17 = (bf16[256,1024]{1,0:T(8,128)(2,1)S(1)}, bf16[256,1024]{1,0:T(8,128)(2,1)}, u32[]{:S(2)}) copy-start(bf16[256,1024]{1,0:T(8,128)(2,1)} %get-tuple-element.105) | copy-start | bytes 1572868
  423.0 42.7 %copy-start.10 = (bf16[256,1024]{1,0:T(8,128)(2,1)S(1)}, bf16[256,1024]{1,0:T(8,128)(2,1)}, u32[]{:S(2)}) copy-start(bf16[256,1024]{1,0:T(8,128)(2,1)} %copy-done.6) | copy-start | bytes 1572868
  423.0 42.7 %copy-start.32 = (bf16[256,512]{1,0:T(8,128)(2,1)S(1)}, bf16[256,512]{1,0:T(8,128)(2,1)}, u32[]{:S(2)}) copy-start(bf16[256,512]{1,0:T(8,128)(2,1)} %copy-done.31) | copy-start | bytes 786436
  423.0 42.7 %copy-start.34 = (bf16[256,512]{1,0:T(8,128)(2,1)S(1)}, bf16[256,512]{1,0:T(8,128)(2,1)}, u32[]{:S(2)}) copy-start(bf16[256,512]{1,0:T(8,128)(2,1)} %get-tuple-element.127) | copy-start | bytes 786436
  465.6 7.0 %collective-permute-start = (bf16[256,1024]{1,0:T(8,128)(2,1)S(1)}, bf16[256,1024]{1,0:T(8,128)(2,1)S(1)}, u32[]{:S(2)}, u32[]{:S(2)}) collective-permute-start(bf16[256,1024]{1,0:T(8,128)(2,1)S(1)} %broadcast_select_fusion), channel_id=1, source_target_pairs={{0,16},{16,0},{1,17},{17,1},{2,18},{18,2},{3,19},{19,3},{4,20},{20... | collective-permute-start | bytes 1572872 | tf_op jit(solution)/shard_map/ppermute | solution.py:24
  467.9 4.7 copy-start.27
  654.5 9.2 %slice-start.2 = ((s8[4718592]{0:T(1024)(128)(4,1)}), s8[4194304]{0:T(1024)(128)(4,1)S(1)}, s32[]{:S(2)}) async-start(s8[4718592]{0:T(1024)(128)(4,1)} %bitcast.82), calls=%async_computation.6 | async-start | bytes 8388608
  655.4 8.3 %slice-start.3 = ((s8[4718592]{0:T(1024)(128)(4,1)}), s8[524288]{0:T(1024)(128)(4,1)S(1)}, s32[]{:S(2)}) async-start(s8[4718592]{0:T(1024)(128)(4,1)} %bitcast.82), calls=%async_computation.7 | async-start | bytes 1048576
  663.7 5.0 copy-start.24
  (28 other events, 74.5 us)
Sparse Core Ops, SparseCore 0:
  11.5 90.3 all-gather.3
  269.7 76.1 reduce-scatter.1
  406.8 48.3 all-gather.5

commit v12 on v11

--- a/solution.py
+++ b/solution.py
@@ -129,76 +129,6 @@
         self.second.wait_send()
         self.third.wait()
         self.fourth.wait()
-
-
-def gather_kernel(block, whole, send_sem, recv_sem, own_sem):
-    greet_sides()
-    gather = SideGather(block, whole, send_sem, recv_sem, own_sem)
-    gather.start()
-    gather.relay()
-    gather.finish()
-
-
-def gathered(array, collective_id):
-    rows, width = array.shape
-    assert lax.axis_size("fsdp") == 4
-    dma = pltpu.SemaphoreType.DMA
-    return pl.pallas_call(
-        gather_kernel,
-        out_shape=jax.ShapeDtypeStruct((4 * rows, width), array.dtype),
-        in_specs=[pl.BlockSpec(memory_space=pltpu.VMEM)],
-        out_specs=pl.BlockSpec(memory_space=pltpu.VMEM),
-        scratch_shapes=[dma((4,)), dma((4,)), dma],
-        compiler_params=pltpu.CompilerParams(
-            collective_id=collective_id, has_side_effects=True, vmem_limit_bytes=8 << 20
-        ),
-        cost_estimate=busy(25),
-    )(array)
-
-
-def gather_swap_kernel(block, pieces, whole, swapped_out, send_sem, recv_sem, own_sem, cross_send, cross_recv, keep_sem):
-    me, beside, across, opposite = corners()
-    barrier = pltpu.get_barrier_semaphore()
-    for target in (beside, across, opposite):
-        pl.semaphore_signal(barrier, inc=1, device_id={"fsdp": target}, device_id_type=MESH)
-    pl.semaphore_wait(barrier, 3)
-    gather = SideGather(block, whole, send_sem, recv_sem, own_sem)
-    gather.start()
-    crossing = []
-    for step in range(1, 4):
-        target = lax.rem(me + step, 4)
-        crossing.append(
-            to_side(pieces.at[target], swapped_out.at[me], cross_send.at[step], cross_recv.at[step], target)
-        )
-        crossing[-1].start()
-    keep = pltpu.make_async_copy(pieces.at[me], swapped_out.at[me], keep_sem)
-    keep.start()
-    gather.relay()
-    gather.finish()
-    keep.wait()
-    for copy in crossing:
-        copy.wait()
-
-
-def gathered_swapped(array, pieces, collective_id):
-    rows, width = array.shape
-    dma = pltpu.SemaphoreType.DMA
-    vmem = pl.BlockSpec(memory_space=pltpu.VMEM)
-    hbm = pl.BlockSpec(memory_space=pl.ANY)
-    return pl.pallas_call(
-        gather_swap_kernel,
-        out_shape=(
-            jax.ShapeDtypeStruct((4 * rows, width), array.dtype),
-            jax.ShapeDtypeStruct(pieces.shape, pieces.dtype),
-        ),
-        in_specs=[vmem, hbm],
-        out_specs=[vmem, hbm],
-        scratch_shapes=[dma((4,)), dma((4,)), dma, dma((4,)), dma((4,)), dma],
-        compiler_params=pltpu.CompilerParams(
-            collective_id=collective_id, has_side_effects=True, vmem_limit_bytes=8 << 20
-        ),
-        cost_estimate=busy(25),
-    )(array, pieces)
 
 
 class SideReduce:
@@ -330,7 +260,6 @@
     down_recv,
     rest_recv,
     second_send,
-    second_recv,
 ):
     n_ctx, n_fsdp = counts
     section = lax.axis_index("section")
@@ -387,34 +316,27 @@
     def half_rows(owner, which):
         return pl.ds(pl.multiple_of(owner * (2 * half) + which * half, half), half)
 
-    a_part, b_part = a_rows // 2, b_width // 2
-
-    def a_at(buffer, k, way):
-        return buffer.at[k, pl.ds(way * a_part, a_part)]
-
-    def b_at(buffer, k, way):
-        return buffer.at[k, :, pl.ds(way * b_part, b_part)]
-
-    def opening(k, way):
+    def a_at(buffer, k):
+        return buffer.at[k]
+
+    b_at = a_at
+
+    def opening(k):
         copies = []
         kind, rest = divmod(k, per_kind)
         owner, sub = divmod(rest, subs)
         source = (gate_in, up_in)[kind]
         spots = []
         for which in (section, other):
-            start = owner * (2 * half) + which * half + sub * a_rows + way * a_part
-            spots.append(source.at[pl.ds(pl.multiple_of(start, a_part), a_part)])
-        spot = 2 * k + way
-        copies.append((spots, a_at(a_own, k, way), a_at(a_other, k, way), spot))
+            start = owner * (2 * half) + which * half + sub * a_rows
+            spots.append(source.at[pl.ds(pl.multiple_of(start, a_rows), a_rows)])
+        copies.append((spots, a_own.at[k], a_other.at[k], k))
         if k < down_chunks:
             spots = [
-                down_in.at[
-                    pl.ds(pl.multiple_of(which * down_half + k * b_rows, b_rows), b_rows),
-                    pl.ds(way * b_part, b_part),
-                ]
+                down_in.at[pl.ds(pl.multiple_of(which * down_half + k * b_rows, b_rows), b_rows)]
                 for which in (section, other)
             ]
-            copies.append((spots, b_at(b_own, k, way), b_at(b_other, k, way), 2 * a_chunks + spot))
+            copies.append((spots, b_own.at[k], b_other.at[k], a_chunks + k))
         for (mine, theirs), own_dst, other_dst, spot in copies:
             pltpu.make_async_copy(mine, own_dst, own_sem.at[spot]).start()
             pltpu.make_async_remote_copy(
@@ -427,15 +349,13 @@
             ).start()
 
     for k in range(a_chunks):
-        for way in range(2):
-            opening(k, way)
+        opening(k)
     for k in range(down_chunks):
-        for way in range(2):
-            pltpu.make_async_copy(
-                second_down_in.at[pl.ds(k * b_rows, b_rows), pl.ds(way * b_part, b_part)],
-                b_at(b_own, down_chunks + k, way),
-                own_sem.at[2 * (a_chunks + down_chunks + k) + way],
-            ).start()
+        pltpu.make_async_copy(
+            second_down_in.at[pl.ds(k * b_rows, b_rows)],
+            b_own.at[down_chunks + k],
+            own_sem.at[a_chunks + down_chunks + k],
+        ).start()
     c_local, c_pair = ([], []), ([], [])
     for kind, source in enumerate(mixers):
         part = 0 if kind < 3 else 1
@@ -566,55 +486,51 @@
 
     strip = half // n_ctx
 
-    def second_copies(remote):
-        for index in range(n_ctx * n_fsdp * 2):
-            source, kind = index // 2, index % 2
-            turn, owner = source // n_fsdp, source % n_fsdp
-            src = second_gu_in.at[turn, owner, kind]
-            dst = gu_out.at[
-                kind,
-                pl.ds(pl.multiple_of(section * half + turn * strip, strip), strip),
-                pl.ds(owner * a_width, a_width),
-            ]
-            if remote:
-                pltpu.make_async_remote_copy(
-                    src_ref=src,
-                    dst_ref=dst,
-                    send_sem=second_send.at[0],
-                    recv_sem=second_recv,
-                    device_id={"section": 1},
-                    device_id_type=MESH,
-                ).start()
-            else:
-                pltpu.make_async_copy(src, dst, second_send.at[0]).start()
-
     def second_start():
-        @pl.when(section == 1)
-        def _():
-            second_copies(False)
-
-        @pl.when(section == 0)
-        def _():
-            second_copies(True)
-
-    def a_target(k, way):
+        for owner in range(n_fsdp):
+            is_mine = (section == 1) & (group == owner)
+            for index in range(2 * n_ctx):
+                turn, kind = index // 2, index % 2
+                src = second_gu_in.at[turn, owner, kind]
+                dst = gu_out.at[
+                    kind,
+                    pl.ds(pl.multiple_of(section * half + turn * strip, strip), strip),
+                    pl.ds(pl.multiple_of(group * a_width, 128), a_width),
+                ]
+
+                @pl.when(is_mine)
+                def _(src=src, dst=dst):
+                    pltpu.make_async_copy(src, dst, second_send.at[0]).start()
+
+                @pl.when(jnp.logical_not(is_mine))
+                def _(src=src, dst=dst, kind=kind, owner=owner):
+                    pltpu.make_async_remote_copy(
+                        src_ref=src,
+                        dst_ref=dst,
+                        send_sem=second_send.at[0],
+                        recv_sem=gu_recv.at[kind, section * n_fsdp + group],
+                        device_id={"section": 1, "fsdp": owner},
+                        device_id_type=MESH,
+                    ).start()
+
+    def a_target(k):
         kind = k // per_kind
         rest = lax.rem(k, per_kind)
         owner = rest // subs
         sub = lax.rem(rest, subs)
-        start = section * half + sub * a_rows + way * a_part
+        start = section * half + sub * a_rows
         spot = gu_out.at[
             kind,
-            pl.ds(pl.multiple_of(start, a_part), a_part),
+            pl.ds(pl.multiple_of(start, a_rows), a_rows),
             pl.ds(pl.multiple_of(group * a_width, 128), a_width),
         ]
         return kind, owner, spot
 
-    def a_hand_out(k, way):
-        kind, owner, spot = a_target(k, way)
+    def a_hand_out(k):
+        kind, owner, spot = a_target(k)
         is_mine = (section == 0) & (group == owner)
-        slot = 2 * k + way
-        a_ref = a_at(a_done, k, way)
+        slot = k
+        a_ref = a_at(a_done, k)
 
         @pl.when(is_mine)
         def _():
@@ -631,13 +547,12 @@
                 device_id_type=MESH,
             ).start()
 
-    def down_hand_out(k, way, keeper):
-        slot = 2 * k + way
-        b_ref = b_at(b_done, k, way)
+    def down_hand_out(k, keeper):
+        slot = k
+        b_ref = b_at(b_done, k)
         index = k - keeper * down_chunks
         at = down_out.at[
             pl.ds(pl.multiple_of(section * down_half + index * b_rows, b_rows), b_rows),
-            pl.ds(way * b_part, b_part),
         ]
 
         @pl.when(section == keeper)
@@ -655,13 +570,12 @@
                 device_id_type=MESH,
             ).start()
 
-    def mix_hand_out(k, way):
-        slot = 2 * k + way
-        b_ref = b_at(b_done, k, way)
+    def mix_hand_out(k):
+        slot = k
+        b_ref = b_at(b_done, k)
         at = rest_out.at[
             section,
             pl.ds(pl.multiple_of((k - mix_start) * b_rows, b_rows), b_rows),
-            pl.ds(way * b_part, b_part),
         ]
         pltpu.make_async_copy(b_ref, at, b_keep_sem.at[slot]).start()
         pltpu.make_async_remote_copy(
@@ -687,62 +601,62 @@
         hand_out = staticmethod(a_hand_out)
 
         @staticmethod
-        def view(buffer, k, way):
-            return a_at(buffer, k, way)
+        def view(buffer, k):
+            return a_at(buffer, k)
 
         own, sums, done = a_own, a_sum, a_done
         up, back = (a_up_send, a_up_recv), (a_back_send, a_back_recv)
 
         @staticmethod
-        def term(k, way):
-            slot = 2 * k + way
-            at = a_at(a_own, k, way)
+        def term(k):
+            slot = k
+            at = a_at(a_own, k)
             pltpu.make_async_copy(at, at, own_sem.at[slot]).wait()
             pltpu.make_async_copy(at, at, pair_recv.at[slot]).wait()
-            return at[...].astype(F32) + a_at(a_other, k, way)[...].astype(F32)
+            return at[...].astype(F32) + a_at(a_other, k)[...].astype(F32)
 
     class Downs:
         @staticmethod
-        def hand_out(k, way):
-            down_hand_out(k, way, 0)
+        def hand_out(k):
+            down_hand_out(k, 0)
 
         @staticmethod
-        def view(buffer, k, way):
-            return b_at(buffer, k, way)
+        def view(buffer, k):
+            return b_at(buffer, k)
 
         own, sums, done = b_own, b_sum, b_done
         up, back = (b_up_send, b_up_recv), (b_back_send, b_back_recv)
 
         @staticmethod
-        def term(k, way):
-            slot = 2 * a_chunks + 2 * k + way
-            at = b_at(b_own, k, way)
+        def term(k):
+            slot = a_chunks + k
+            at = b_at(b_own, k)
             pltpu.make_async_copy(at, at, own_sem.at[slot]).wait()
             pltpu.make_async_copy(at, at, pair_recv.at[slot]).wait()
-            return at[...].astype(F32) + b_at(b_other, k, way)[...].astype(F32)
+            return at[...].astype(F32) + b_at(b_other, k)[...].astype(F32)
 
     class Seconds(Downs):
         @staticmethod
-        def hand_out(k, way):
-            down_hand_out(k, way, 1)
+        def hand_out(k):
+            down_hand_out(k, 1)
 
         @staticmethod
-        def term(k, way):
-            at = b_at(b_own, k, way)
-            pltpu.make_async_copy(at, at, own_sem.at[2 * a_chunks + 2 * k + way]).wait()
+        def term(k):
+            at = b_at(b_own, k)
+            pltpu.make_async_copy(at, at, own_sem.at[a_chunks + k]).wait()
             return at[...].astype(F32)
 
     class Mixed(Downs):
         hand_out = staticmethod(mix_hand_out)
 
         @staticmethod
-        def term(k, way):
-            return b_at(b_own, k, way)[...].astype(F32)
-
-    def upward(item, k, way, rank, ahead, behind):
-        slot = 2 * k + way
-        term = item.term(k, way)
-        sums = item.view(item.sums, k, way)
+        def term(k):
+            return b_at(b_own, k)[...].astype(F32)
+
+    def upward(item, k, rank, ahead, behind):
+        slot = k
+        term = item.term(k)
+        sums = item.view(item.sums, k)
 
         @pl.when(rank == 0)
         def _():
@@ -762,46 +676,41 @@
 
         @pl.when(rank == n_ctx - 1)
         def _():
-            done = item.view(item.done, k, way)
+            done = item.view(item.done, k)
             done[...] = (term + sums[...].astype(F32)).astype(BF16)
             chain_copy(done, item.back, slot, behind).start()
-            item.hand_out(k, way)
-
-    def backward(item, k, way, rank, ahead, behind):
-        slot = 2 * k + way
-        done = item.view(item.done, k, way)
+            item.hand_out(k)
+
+    def backward(item, k, rank, ahead, behind):
+        slot = k
+        done = item.view(item.done, k)
         chain_copy(done, item.back, slot, ahead).wait_recv()
 
         @pl.when(rank > 0)
         def _():
             chain_copy(done, item.back, slot, behind).start()
 
-        item.hand_out(k, way)
-
-    def on_step(action, step, active, *where):
-        early = active & (step < paired)
-
-        @pl.when(early)
+        item.hand_out(k)
+
+    def on_step(action, step, active, way, *where):
+        @pl.when(active & (step < paired))
         def _():
             at = jnp.clip(step, 0, paired - 1)
-            for index in range(2):
-                action(Gates, 2 * at + index, *where)
-
-            @pl.when(lax.rem(at, 4) < 3)
+            action(Gates, 2 * at + way, *where)
+
+            @pl.when(lax.rem(3 * at, 8) < 3)
             def _():
-                action(Downs, 3 * (at // 4) + lax.rem(at, 4), *where)
+                action(Downs, 2 * (3 * at // 8) + way, *where)
 
         @pl.when(active & (step >= paired) & (step < second))
         def _():
             at = jnp.clip(step - paired, 0, down_chunks // 2 - 1)
-            for index in range(2):
-                action(Seconds, down_chunks + 2 * at + index, *where)
+            action(Seconds, down_chunks + 2 * at + way, *where)
 
         @pl.when(active & (step >= second))
         def _():
             at = jnp.clip(step - second, 0, mix_chunks // 2 - 1)
-            for index in range(2):
-                action(Mixed, mix_start + 2 * at + index, *where)
+            action(Mixed, mix_start + 2 * at + way, *where)
 
     lanes = []
     for way in range(2):
@@ -858,65 +767,58 @@
         for copy in opening + onward:
             copy.wait_send()
 
-    def settle_item(item, k, out_send):
+    def settle_item(item, k, rank, ahead, behind, out_send):
+        @pl.when(rank < n_ctx - 1)
+        def _():
+            chain_copy(item.view(item.sums, k), item.up, k, ahead).wait_send()
+
+        @pl.when(rank > 0)
+        def _():
+            chain_copy(item.view(item.done, k), item.back, k, behind).wait_send()
+
+        ref = item.view(item.own, k)
+        pltpu.make_async_copy(ref, ref, out_send.at[k]).wait()
+
+    def settle_gates(index, carry):
         for way, rank, ahead, behind in lanes:
-            slot = 2 * k + way
-
-            @pl.when(rank < n_ctx - 1)
-            def _(slot=slot, way=way, ahead=ahead):
-                chain_copy(item.view(item.sums, k, way), item.up, slot, ahead).wait_send()
-
-            @pl.when(rank > 0)
-            def _(slot=slot, way=way, behind=behind):
-                chain_copy(item.view(item.done, k, way), item.back, slot, behind).wait_send()
-
-            ref = item.view(item.own, k, way)
-            pltpu.make_async_copy(ref, ref, out_send.at[slot]).wait()
-
-    def settle_gates(k, carry):
-        settle_item(Gates, k, a_out_send)
-        for way in range(2):
-            ref = a_at(a_own, k, way)
-            pltpu.make_async_copy(ref, ref, pair_send.at[2 * k + way]).wait()
+            k = 2 * index + way
+            settle_item(Gates, k, rank, ahead, behind, a_out_send)
+            ref = a_own.at[k]
+            pltpu.make_async_copy(ref, ref, pair_send.at[k]).wait()
         return carry
 
-    lax.fori_loop(0, a_chunks, settle_gates, 0)
-
-    def settle_rest(k, carry):
-        settle_item(Mixed, k, b_out_send)
-        for way in range(2):
-            ref = b_at(b_own, k, way)
+    lax.fori_loop(0, a_chunks // 2, settle_gates, 0)
+
+    def settle_rest(index, carry):
+        for way, rank, ahead, behind in lanes:
+            k = 2 * index + way
+            settle_item(Mixed, k, rank, ahead, behind, b_out_send)
+            ref = b_own.at[k]
 
             @pl.when(k < down_chunks)
-            def _(ref=ref, way=way):
-                pltpu.make_async_copy(ref, ref, pair_send.at[2 * a_chunks + 2 * k + way]).wait()
+            def _(ref=ref, k=k):
+                pltpu.make_async_copy(ref, ref, pair_send.at[a_chunks + k]).wait()
 
             @pl.when(k >= mix_start)
-            def _(ref=ref, way=way):
-                pltpu.make_async_copy(ref, ref, b_keep_sem.at[2 * k + way]).wait()
+            def _(ref=ref, k=k):
+                pltpu.make_async_copy(ref, ref, b_keep_sem.at[k]).wait()
 
         return carry
 
-    lax.fori_loop(0, b_chunks, settle_rest, 0)
+    lax.fori_loop(0, b_chunks // 2, settle_rest, 0)
     pltpu.make_async_copy(second_gu_in, second_gu_in, second_send.at[0]).wait()
 
-    @pl.when(section == 0)
-    def _():
-        for kind in range(2):
-            for source in range(2 * n_fsdp):
-
-                @pl.when(group != source)
-                def _(kind=kind, source=source):
-                    region = gu_out.at[
-                        kind,
-                        pl.ds((source // n_fsdp) * half, half),
-                        pl.ds((source % n_fsdp) * a_width, a_width),
-                    ]
-                    pltpu.make_async_copy(region, region, gu_recv.at[kind, source]).wait()
-
-    @pl.when(section == 1)
-    def _():
-        pltpu.make_async_copy(second_gu_in, second_gu_in, second_recv).wait()
+    for kind in range(2):
+        for source in range(2 * n_fsdp):
+
+            @pl.when(section * n_fsdp + group != source)
+            def _(kind=kind, source=source):
+                region = gu_out.at[
+                    kind,
+                    pl.ds((source // n_fsdp) * half, half),
+                    pl.ds((source % n_fsdp) * a_width, a_width),
+                ]
+                pltpu.make_async_copy(region, region, gu_recv.at[kind, source]).wait()
 
     region = down_out.at[pl.ds(pl.multiple_of(other * down_half, b_rows), down_half)]
     pltpu.make_async_copy(region, region, down_recv).wait()
@@ -938,7 +840,7 @@
     assert down_chunks * 8 == a_chunks * 3
     rest = b_chunks - 2 * down_chunks
     dma = pltpu.SemaphoreType.DMA
-    loads = 2 * (a_chunks + 2 * down_chunks)
+    loads = a_chunks + 2 * down_chunks
     pieces = n_fsdp * (len(mixers) + 1)
     return pl.pallas_call(
         functools.partial(tail_kernel, (n_ctx, n_fsdp)),
@@ -969,22 +871,21 @@
             dma((pieces,)),
             dma((2, 6)),
             dma((2, 6)),
-            dma((2 * a_chunks,)),
-            dma((2 * a_chunks,)),
-            dma((2 * a_chunks,)),
-            dma((2 * a_chunks,)),
-            dma((2 * a_chunks,)),
-            dma((2 * b_chunks,)),
-            dma((2 * b_chunks,)),
-            dma((2 * b_chunks,)),
-            dma((2 * b_chunks,)),
-            dma((2 * b_chunks,)),
-            dma((2 * b_chunks,)),
+            dma((a_chunks,)),
+            dma((a_chunks,)),
+            dma((a_chunks,)),
+            dma((a_chunks,)),
+            dma((a_chunks,)),
+            dma((b_chunks,)),
+            dma((b_chunks,)),
+            dma((b_chunks,)),
+            dma((b_chunks,)),
+            dma((b_chunks,)),
+            dma((b_chunks,)),
             dma((2, 2 * n_fsdp)),
             dma,
             dma,
             dma((2,)),
-            dma,
         ],
         compiler_params=pltpu.CompilerParams(
             collective_id=6, has_side_effects=True, vmem_limit_bytes=56 << 20
@@ -1940,7 +1841,7 @@
     me, _, _, opposite = corners()
     rows = act_block.shape[0]
     wide, width = w_down.shape
-    lanes_wide, lanes_out = 384, 512
+    lanes_wide, lanes_out = 384, 1024
 
     def turn(owner):
         at = pl.ds(pl.multiple_of(owner * rows, rows), rows)
@@ -2136,9 +2037,6 @@
 
 def back_kernel(
     n_ctx,
-    blocks,
-    d_gate,
-    d_up,
     x_ref,
     mixed,
     d_h,
@@ -2146,9 +2044,18 @@
     taps,
     z_low,
     rim,
+    act_qkv,
+    d_query,
+    d_key_value,
+    attended,
+    d_attended,
+    gate_pre_in,
+    up_pre_in,
+    w_down_in,
+    w_gate_in,
+    w_up_in,
     act_in,
     hidden_in,
-    d_all_in,
     w_in_in,
     w_out_in,
     projected_in,
@@ -2156,20 +2063,34 @@
     gate_grad,
     up_grad,
     down_grad,
+    q_grad,
+    kv_grad,
+    proj_grad,
     b_grad,
     c_grad,
     x_grad,
     o_grad,
     d_x,
     small,
+    w_down,
+    w_gate,
+    w_up,
     act,
     hidden,
-    d_all,
     w_in,
     w_out,
     projected,
     convolved,
     load_sem,
+    pre,
+    pre_sem,
+    d_all,
+    d_gate,
+    d_up,
+    blocks,
+    d_send,
+    d_recv,
+    d_own,
     stage_wide,
     stage,
     stage_sem,
@@ -2190,17 +2111,28 @@
     edge_sem,
 ):
     chain = Chain(n_ctx)
-    _, beside, across, _ = corners()
+    me, beside, across, opposite = corners()
     greet_mixed(chain, [{"fsdp": beside}, {"fsdp": across}])
+    gather = SideGather(d_h, d_all, d_send, d_recv, d_own)
+    gather.start()
     reduction = SideReduce(blocks, d_act, beside_got, across_got, passed, passed_got, send_sem, recv_sem)
-    reduction.start()
+
+    def fetch(owner, slot):
+        at = pl.ds(pl.multiple_of(owner * x_ref.shape[0], x_ref.shape[0]), x_ref.shape[0])
+        return [
+            pltpu.make_async_copy(source.at[at], pre.at[slot, kind], pre_sem.at[slot, kind])
+            for kind, source in enumerate((gate_pre_in, up_pre_in))
+        ]
+
     loads = [
         pltpu.make_async_copy(src, dst, load_sem.at[index])
         for index, (src, dst) in enumerate(
             (
+                (w_down_in, w_down),
+                (w_gate_in, w_gate),
+                (w_up_in, w_up),
                 (act_in, act),
                 (hidden_in, hidden),
-                (d_all_in, d_all),
                 (convolved_in, convolved),
                 (projected_in, projected),
                 (w_out_in, w_out),
@@ -2208,10 +2140,10 @@
             )
         )
     ]
-    for copy in loads:
+    for copy in fetch(me, 0) + loads[:3] + fetch(beside, 1) + loads[3:]:
         copy.start()
     rows, width = x_ref.shape
-    wide = d_gate.shape[1]
+    wide = w_gate.shape[1]
     tile = 256
     small[...] = jnp.zeros(small.shape, F32)
 
@@ -2237,12 +2169,63 @@
         for index in range(min(2, count)):
             leaving(pl.ds(0, tile), index).wait()
 
-    loads[0].wait()
+    lanes_wide, lanes_out = 384, 512
+
+    def turn(owner, slot, after):
+        at = pl.ds(pl.multiple_of(owner * rows, rows), rows)
+        for copy in fetch(owner, slot):
+            copy.wait()
+
+        def hidden_part(index, carry):
+            lanes = pl.ds(pl.multiple_of(index * lanes_wide, 128), lanes_wide)
+            gate_pre, up_pre = pre[slot, 0, :, lanes], pre[slot, 1, :, lanes]
+            d_hidden = dot_right(d_all[at], w_down[lanes])
+            sigmoid = jax.nn.sigmoid(gate_pre)
+            d_up[at, lanes] = (d_hidden * gate_pre * sigmoid).astype(BF16)
+            d_gate[at, lanes] = (
+                d_hidden * up_pre * sigmoid * (1.0 + gate_pre * (1.0 - sigmoid))
+            ).astype(BF16)
+            return carry
+
+        lax.fori_loop(0, wide // lanes_wide, hidden_part, 0)
+        if after is not None:
+            for copy in fetch(after, slot):
+                copy.start()
+
+        def out_part(index, carry):
+            lanes = pl.ds(pl.multiple_of(index * lanes_out, 128), lanes_out)
+            blocks[at, lanes] = (
+                dot_right(d_gate[at], w_gate[lanes]) + dot_right(d_up[at], w_up[lanes])
+            ).astype(BF16)
+            return carry
+
+        lax.fori_loop(0, width // lanes_out, out_part, 0)
+
+    gather.own.wait()
+    for copy in loads[:3]:
+        copy.wait()
+    turn(me, 0, across)
+    for left, right, target in (
+        (act_qkv, d_query, q_grad),
+        (act_qkv, d_key_value, kv_grad),
+        (attended, d_attended, proj_grad),
+    ):
+        weight_grad(left, right, slice(None), target, stage, 2)
+    gather.relay()
+    turn(beside, 1, opposite)
+    turn(across, 0, None)
+    reduction.copies[1].start()
+    reduction.copies[3].start()
+    gather.third.wait_recv()
+    gather.fourth.wait_recv()
+    turn(opposite, 1, None)
+    reduction.copies[0].start()
+    reduction.copies[2].start()
+    loads[3].wait()
     weight_grad(act, d_gate, slice(None), gate_grad, stage_wide, 0)
     weight_grad(act, d_up, slice(None), up_grad, stage_wide, 0)
     reduction.relay()
-    loads[1].wait()
-    loads[2].wait()
+    loads[4].wait()
     odd = hidden.shape[1] % tile
 
     weight_grad(hidden, d_all, slice(None), down_grad, stage, 2)
@@ -2273,7 +2256,7 @@
         return carry
 
     lax.fori_loop(0, rows // strip, second_norm, 0)
-    for index in range(3, 6):
+    for index in range(5, 8):
         loads[index].wait()
 
     def to_z(index, carry):
@@ -2340,7 +2323,7 @@
         return carry
 
     lax.fori_loop(0, width // part, products_back, 0)
-    loads[6].wait()
+    loads[8].wait()
 
     def to_act(index, carry):
         at = pl.ds(pl.multiple_of(index * tile, tile), tile)
@@ -2358,18 +2341,22 @@
         return carry
 
     lax.fori_loop(0, rows // strip, first_norm, 0)
+    for copy in (gather.first, gather.second, gather.third, gather.fourth):
+        copy.wait_send()
 
     @pl.when(chain.has_last)
     def _():
         to_last.wait_send()
 
 
-def conv_back(blocks, d_gate, d_up, local, kept, collective_id):
+def conv_back(local, before, kept, collective_id):
     n_ctx = lax.axis_size("ctx")
     x_low = local[0]
-    act, hidden = kept[0], kept[1]
     rows, width = x_low.shape
-    wide = d_gate.shape[1]
+    wide = before[0].shape[1]
+    assert wide % 384 == 0 and width % 512 == 0
+    columns = pltpu.VMEM((4 * rows, wide), BF16)
+    whole = pltpu.VMEM((4 * rows, width), BF16)
     dma = pltpu.SemaphoreType.DMA
     vmem = pl.BlockSpec(memory_space=pltpu.VMEM)
     hbm = pl.BlockSpec(memory_space=pl.ANY)
@@ -2386,14 +2373,26 @@
             square,
             square,
             square,
+            square,
+            square,
+            square,
             jax.ShapeDtypeStruct((rows, width), BF16),
             jax.ShapeDtypeStruct((8, width), F32),
         ),
-        in_specs=[vmem] * (3 + len(local)) + [hbm] * len(kept),
-        out_specs=[hbm] * 7 + [vmem] * 2,
+        in_specs=[vmem] * len(local) + [hbm] * (len(before) + len(kept)),
+        out_specs=[hbm] * 10 + [vmem] * 2,
         scratch_shapes=[pltpu.VMEM(k.shape, k.dtype) for k in kept]
         + [
-            dma((7,)),
+            dma((9,)),
+            pltpu.VMEM((2, 2, rows, wide), F32),
+            dma((2, 2)),
+            whole,
+            columns,
+            columns,
+            whole,
+            dma((4,)),
+            dma((4,)),
+            dma,
             pltpu.VMEM((2, 256, wide), BF16),
             pltpu.VMEM((2, 256, width), BF16),
             dma((4,)),
@@ -2416,8 +2415,8 @@
         compiler_params=pltpu.CompilerParams(
             collective_id=collective_id, has_side_effects=True, vmem_limit_bytes=58 << 20
         ),
-        cost_estimate=busy(35),
-    )(blocks, d_gate, d_up, *local, *kept)
+        cost_estimate=busy(55),
+    )(*local, *before, *kept)
 
 
 def ffn_forward(act, w_gate, w_up, w_down):
@@ -2425,16 +2424,6 @@
     up_pre = matmul(act, w_up)
     hidden = (jax.nn.silu(gate_pre) * up_pre).astype(BF16)
     return matmul(hidden, w_down).astype(BF16), (act, gate_pre, up_pre, hidden)
-
-
-def ffn_backward(d_all, kept, w_gate, w_up, w_down):
-    act, gate_pre, up_pre, hidden = kept
-    d_hidden = matmul_right(d_all, w_down)
-    sigmoid = jax.nn.sigmoid(gate_pre)
-    d_up = (d_hidden * gate_pre * sigmoid).astype(BF16)
-    d_gate = (d_hidden * up_pre * sigmoid * (1.0 + gate_pre * (1.0 - sigmoid))).astype(BF16)
-    terms = (matmul_right(d_gate, w_gate) + matmul_right(d_up, w_up)).astype(BF16)
-    return terms, d_gate, d_up
 
 
 def ffn_norm_back(d_act, residual, gain):
@@ -2529,7 +2518,6 @@
     d_ffn, gain3 = ffn_norm_back(d_act3, res2, norm_gains[3])
     d_res2 = d_sum + d_ffn
     d_attn = d_res2.astype(BF16)
-    grad_proj = matmul_left(attended_low, d_attn)
     d_att = matmul_right(d_attn, proj_full).astype(BF16)
     delta = jnp.sum((d_att.astype(F32) * attended).reshape(rows, q_heads, head), axis=-1)
     d_query, d_kv, ffn2 = attend_back(
@@ -2559,22 +2547,24 @@
     gain2 = jnp.sum(d_act2 * normed2, axis=0)
     d_h_low = (d_res2 + norm_back(d_act2 * norm_gains[2], normed2, inv2)).astype(BF16)
 
-    d_h_all, second_gu = gathered_swapped(
-        d_h_low, second_gu.reshape(fsdp, -1, second_gu.shape[-1]), 5
-    )
     second_gu = lax.all_gather(second_gu, "ctx", axis=0)
-    d_terms1, d_gate1, d_up1 = ffn_backward(d_h_all, kept1, gate1, up1, down1)
-    attn_mixers = [
-        matmul_left(act2, d_qpre).astype(BF16),
-        matmul_left(act2, jnp.concatenate([d_kpre, d_vpre], axis=1)).astype(BF16),
-        grad_proj.astype(BF16),
-    ]
     *grads, d_x, conv_small = conv_back(
-        d_terms1,
-        d_gate1,
-        d_up1,
-        (x_low, mixed, d_h_low, norm_gains, conv_kernel, z_low, rim),
-        (act_all1, kept1[3], d_h_all, in_full, out_full, projected, convolved),
+        (
+            x_low,
+            mixed,
+            d_h_low,
+            norm_gains,
+            conv_kernel,
+            z_low,
+            rim,
+            act2,
+            d_qpre,
+            jnp.concatenate([d_kpre, d_vpre], axis=1),
+            attended_low,
+            d_attn,
+        ),
+        kept1[1:3],
+        (down1, gate1, up1, act_all1, kept1[3], in_full, out_full, projected, convolved),
         9,
     )
 
@@ -2594,9 +2584,9 @@
     small = small.reshape(2, 16, width)
     gu_sum, down_sum, rest_sum = summed_gradients(
         grads[:3],
-        attn_mixers + grads[3:],
+        grads[3:],
         small,
-        second_gu.reshape(-1, fsdp, 2, second_gu.shape[2] // 2, second_gu.shape[-1]),
+        second_gu.reshape((-1,) + shared_gu.shape[1:]),
         shared_down,
     )
     rest_sum = rest_sum.astype(F32)

time: 691 us -> 667 us (0.965)
  matrix products: 60.3 us -> 41.4 us
    pallas_call x1 -> x0, Pallas kernels: 25 us -> none  [gathered_swapped(): pl.pallas_call(gather_swap_kernel, out_shape=(jax.ShapeDtypeStruct((4 * r...]
    pallas_call x1, Pallas kernels: 42.5 us -> 65.2 us  [conv_back(): pl.pallas_call(functools.partial(back_kernel, n_ctx), out_shape=(column,...]
    dot_general x7 -> x4, matrix products: 23.7 us -> 10.2 us  [matmul_right(): lax.dot_general(left_op, right_op, (((1,), (1,)), ((), ())), preferred_el...]
  transfers between devices with their start and end apart: 4 -> 4, of which waited for: 0 -> 0; matrix products, arithmetic and copies ran while one was open for 10% -> 8% of each run, Pallas kernels for 36% -> 41%
where the time goes in v12:
time: 667 us; the launch traced here: 658 us
  Pallas kernels  548 us (82%)
  matrix products  41.4 us (6%)
  other arithmetic  32.2 us (5%)
  local copies, waits for them, and re-layouts  20.2 us (3%)
  between operations  15.7 us (2%)
    pallas_call x1, Pallas kernels, summed_gradients(): pl.pallas_call(functools.partial(tail_kernel, (n_ctx, n_fsdp)), out_shape...  178 us
    pallas_call x1, Pallas kernels, front(): pl.pallas_call(functools.partial(front_kernel, n_ctx), out_shape=tuple((j...  100 us
    pallas_call x1, Pallas kernels, attend_back(): pl.pallas_call(functools.partial(attend_back_kernel, n_ctx), out_shape=(w...  83 us
    pallas_call x1, Pallas kernels, conv_back(): pl.pallas_call(functools.partial(back_kernel, n_ctx), out_shape=(column,...  65.2 us
    pallas_call x1, Pallas kernels, attend(): pl.pallas_call(functools.partial(attend_kernel, n_ctx), out_shape=(jax.Sh...  54.3 us
    pallas_call x1, Pallas kernels, ffn_turn(): pl.pallas_call(turn_kernel, out_shape=(jax.ShapeDtypeStruct(whole, BF16),...  47.9 us
    dot_general x7, matrix products, matmul(): return jnp.dot(left_op, right_op, preferred_element_type=F32)  22.2 us
    pallas_call x1, Pallas kernels, reduced(): pl.pallas_call(reduce_kernel, out_shape=jax.ShapeDtypeStruct((rows, width...  19.6 us
  transfers between devices with their start and end apart: 4, of which 0 were waited for; matrix products, arithmetic and copies ran while one was open for 8% of the time, Pallas kernels for 41%

profile of v12, /device:TPU:0, one launch (start us, length us, event | category | flops | bytes accessed | tf_op | source)
XLA Modules:
  0.0 658.1 jit_solution(18337886504717219085)
XLA Ops:
  9.8 100.2 %shard_map.262 = (bf16[1024,3072]{1,0:T(8,128)(2,1)}, bf16[1024,1024]{1,0:T(8,128)(2,1)}, bf16[1024,1152]{1,0:T(8,128)(2,1)}, bf16[1024,1152]{1,0:T(8,128)(2,1)}...) custom-call(bf16[256,1024]{1,0:T(8,128)(2,1)} %dynamic-slice_bitcast, ...), custom_call_target="tpu_custom_call" | custom-call | flops 70 | bytes 65536 | tf_op jit(solution)/shard_map/pallas_call | solution.py:1741
  110.1 5.3 fusion.90.gate_pre_in
  115.5 4.5 multiply_convert_fusion
  120.0 3.1 convolution_convert_fusion.blocks
  123.1 19.6 %shard_map.263 = f32[256,1024]{1,0:T(8,128)S(1)} custom-call(bf16[1024,1024]{1,0:T(8,128)(2,1)S(1)} %convolution_convert_fusion.blocks), custom_call_target="tpu_custom_call" | custom-call | flops 25 | bytes 65536 | tf_op jit(solution)/shard_map/pallas_call | solution.py:198
  144.3 2.1 fusion.46
  147.4 2.5 fusion.6
  150.7 2.1 multiply_convert_fusion.2
  159.0 54.3 %shard_map.264 = (f32[256,1024]{1,0:T(8,128)}, f32[16,1,256]{2,1,0:T(1,128)}, bf16[1024,1024]{1,0:T(8,128)(2,1)}, bf16[1024,1024]{1,0:T(8,128)(2,1)}, bf16[1024,...) custom-call(s32[1]{0:T(128)} %dynamic_slice.27.length_ref, ...), custom_call_target="tpu_custom_call" | custom-call | flops 50 | bytes 65536 | tf_op jit(solution)/shard_map/pallas_call | solution.py:1285
  214.6 3.5 multiply_reduce_fusion.2
  219.1 47.9 %shard_map.265 = (bf16[1024,1024]{1,0:T(8,128)(2,1)}, f32[256,1024]{1,0:T(8,128)}, bf16[4,4,2,32,1152]{4,3,2,1,0:T(8,128)(2,1)}, bf16[576,1024]{1,0:T(8,128)(2,1)}) custom-call(bf16[256,1024]{1,0:T(8,128)(2,1)} %multiply_convert_fusion.1.act_block, bf16[1024,1152]{1,0:T(8,128)(2,1)} %get-tuple-element.61.w_gate_in, ...), custom_call_target="tpu_custom_call" | custom-call | flops 45 | bytes 65536 | tf_op jit(solution)/shard_map/pallas_call | solution.py:1994
  269.3 3.7 convert_multiply_fusion.7
  273.0 2.5 copy.31
  277.5 83.0 %shard_map.266 = (f32[256,1024]{1,0:T(8,128)}, f32[256,1024]{1,0:T(8,128)}, f32[256,1024]{1,0:T(8,128)}) custom-call(s32[1]{0:T(128)} %dynamic_slice.27.length_ref, bf16[256,1024]{1,0:T(8,128)(2,1)} %get-tuple-element.112.query, bf16[1024,1024]{1,0:T(8,128)(2,1)} %get-tuple-element.66.kv_all, bf16[256,1024]{1,0:T(8,128)(2,1)} %get-tuple-element.142.d_out, ...), custom_call_target="tpu_custom_call" | custom-call | flops 50 | bytes 65536 | tf_op jit(solution)/shard_map/pallas_call | solution.py:1440
  369.9 2.5 fusion.4
  374.4 2.2 fusion.45
  377.0 2.1 fusion.38
  379.1 65.2 %shard_map.267 = (bf16[1024,1152]{1,0:T(8,128)(2,1)}, bf16[1024,1152]{1,0:T(8,128)(2,1)}, bf16[1152,1024]{1,0:T(8,128)(2,1)}, bf16[1024,1024]{1,0:T(8,128)(2,1)}...) custom-call(bf16[256,1024]{1,0:T(8,128)(2,1)} %dynamic-slice_bitcast, ...), custom_call_target="tpu_custom_call" | custom-call | flops 55 | bytes 65536 | tf_op jit(solution)/shard_map/pallas_call | solution.py:2366
  447.9 2.5 concatenate.33
  450.5 2.4 maximum_select_fusion
  452.9 178.2 %shard_map.268 = (bf16[2,256,4608]{2,1,0:T(8,128)(2,1)}, bf16[1152,1024]{1,0:T(8,128)(2,1)}, bf16[2,960,1024]{2,1,0:T(8,128)(2,1)}) custom-call(bf16[1024,1152]{1,0:T(8,128)(2,1)} %get-tuple-element.79.gate_in, bf16[1024,1152]{1,0:T(8,128)(2,1)} %get-tuple-element.80.up_in, bf16[1152,1024]{1,0:T(8,128)(2,1)} %get-tuple-element.81.down_in, ...), custom_call_target="tpu_custom_call" | custom-call | flops 160 | bytes 65536 | tf_op jit(solution)/shard_map/pallas_call | solution.py:845
  632.0 4.4 fusion.86
  640.3 5.0 slice_convert_fusion
  645.3 2.7 bitcast_convert_fusion
  (165 shorter events, 40.8 us)
Async XLA Ops:
  7.2 140.2 %all-gather.4.cloned.1.call-start = ((), (), s32[]{:S(2)}) async-start(), calls=%async_computation.1 | async-start | bytes 6488064 | tf_op jit(solution)/shard_map/all_gather | solution.py:2467
  8.9 354.8 %reduce-scatter.2.cloned.1.call-start = ((), (), s32[]{:S(2)}) async-start(), calls=%async_computation.2 | async-start | bytes 2949120 | tf_op jit(solution)/shard_map/reduce_scatter | solution.py:2532
  110.1 5.4 copy-start.21
  110.1 5.4 copy-start.29
  115.4 4.6 copy-start.15
  115.5 4.5 copy-start.22
  123.1 19.7 %copy-start.36 = (f32[2,64]{1,0:T(2,128)S(1)}, f32[2,64]{1,0:T(2,128)}, u32[]{:S(2)}) copy-start(f32[2,64]{1,0:T(2,128)} %param.26) | copy-start | bytes 1540
  123.1 19.9 %copy-start.37 = (s32[8]{0:T(128)S(1)}, s32[8]{0:T(128)}, u32[]{:S(2)}) copy-start(s32[8]{0:T(128)} %param.17) | copy-start | bytes 100
  123.1 21.1 %copy-start = (f32[256,1024]{1,0:T(8,128)S(1)}, f32[256,1024]{1,0:T(8,128)}, u32[]{:S(2)}) copy-start(f32[256,1024]{1,0:T(8,128)} %get-tuple-element.55.mixed) | copy-start | bytes 3145732
  142.8 3.6 copy-start.35
  147.4 9.1 %copy-start.27 = (bf16[256,1024]{1,0:T(8,128)(2,1)}, bf16[256,1024]{1,0:T(8,128)(2,1)S(1)}, u32[]{:S(2)}) copy-start(bf16[256,1024]{1,0:T(8,128)(2,1)S(1)} %fusion.39.act_qkv) | copy-start | bytes 1572868
  159.0 55.6 %copy-start.11 = (bf16[256,1024]{1,0:T(8,128)(2,1)S(1)}, bf16[256,1024]{1,0:T(8,128)(2,1)}, u32[]{:S(2)}) copy-start(bf16[256,1024]{1,0:T(8,128)(2,1)} %copy-done.10) | copy-start | bytes 1572868
  214.6 3.5 copy-start.14
  267.0 185.9 %all-gather.6.cloned.1.call-start = ((), (), s32[]{:S(2)}) async-start(), calls=%async_computation.3 | async-start | bytes 2949120 | tf_op jit(solution)/shard_map/all_gather | solution.py:2550
  269.3 3.7 copy-start.13
  372.5 4.1 copy-start.33
  379.1 65.2 %copy-start.16 = (bf16[256,1024]{1,0:T(8,128)(2,1)}, bf16[256,1024]{1,0:T(8,128)(2,1)S(1)}, u32[]{:S(2)}) copy-start(bf16[256,1024]{1,0:T(8,128)(2,1)S(1)} %get-tuple-element.107) | copy-start | bytes 1572868
  379.1 68.2 %copy-start.7 = (bf16[256,1024]{1,0:T(8,128)(2,1)S(1)}, bf16[256,1024]{1,0:T(8,128)(2,1)}, u32[]{:S(2)}) copy-start(bf16[256,1024]{1,0:T(8,128)(2,1)} %copy-done.6) | copy-start | bytes 1572868
  444.3 6.2 copy-start.32
  445.2 5.3 copy-start.17
  445.2 5.3 collective-permute-start
  631.1 9.2 %slice-start = ((s8[4718592]{0:T(1024)(128)(4,1)}), s8[4194304]{0:T(1024)(128)(4,1)S(1)}, s32[]{:S(2)}) async-start(s8[4718592]{0:T(1024)(128)(4,1)} %bitcast.76), calls=%async_computation.4 | async-start | bytes 8388608
  632.0 8.3 %slice-start.1 = ((s8[4718592]{0:T(1024)(128)(4,1)}), s8[524288]{0:T(1024)(128)(4,1)S(1)}, s32[]{:S(2)}) async-start(s8[4718592]{0:T(1024)(128)(4,1)} %bitcast.76), calls=%async_computation.5 | async-start | bytes 1048576
  640.3 5.0 copy-start.24
  (20 other events, 44.9 us)
Sparse Core Ops, SparseCore 0:
  11.5 90.3 all-gather.3
  267.1 75.8 reduce-scatter.1
  364.0 47.7 all-gather.5

commit v13 on v12

--- a/solution.py
+++ b/solution.py
@@ -180,32 +180,6 @@
             total[at] = total[at] + passed_got[turn].astype(F32)
         for copy in self.copies + self.onward:
             copy.wait_send()
-
-
-def reduce_kernel(blocks, total, beside_got, across_got, passed, passed_got, send_sem, recv_sem):
-    greet_sides()
-    reduction = SideReduce(blocks, total, beside_got, across_got, passed, passed_got, send_sem, recv_sem)
-    reduction.start()
-    reduction.relay()
-    reduction.finish()
-
-
-def reduced(partial, collective_id):
-    rows, width = partial.shape[0] // 4, partial.shape[1]
-    assert lax.axis_size("fsdp") == 4
-    dma = pltpu.SemaphoreType.DMA
-    pair = pltpu.VMEM((2, rows // 2, width), BF16)
-    return pl.pallas_call(
-        reduce_kernel,
-        out_shape=jax.ShapeDtypeStruct((rows, width), F32),
-        in_specs=[pl.BlockSpec(memory_space=pltpu.VMEM)],
-        out_specs=pl.BlockSpec(memory_space=pltpu.VMEM),
-        scratch_shapes=[pair, pair, pair, pair, dma((6,)), dma((6,))],
-        compiler_params=pltpu.CompilerParams(
-            collective_id=collective_id, has_side_effects=True, vmem_limit_bytes=16 << 20
-        ),
-        cost_estimate=busy(25),
-    )(partial.astype(BF16))
 
 
 def tail_kernel(
@@ -2419,11 +2393,137 @@
     )(*local, *before, *kept)
 
 
-def ffn_forward(act, w_gate, w_up, w_down):
-    gate_pre = matmul(act, w_gate)
-    up_pre = matmul(act, w_up)
-    hidden = (jax.nn.silu(gate_pre) * up_pre).astype(BF16)
-    return matmul(hidden, w_down).astype(BF16), (act, gate_pre, up_pre, hidden)
+def forward_kernel(
+    act,
+    w_gate_in,
+    w_up_in,
+    w_down_in,
+    total,
+    gate_out,
+    up_out,
+    hidden_out,
+    w_gate,
+    w_up,
+    w_down,
+    load_sem,
+    pre,
+    pre_sem,
+    hidden,
+    keep_sem,
+    blocks,
+    beside_got,
+    across_got,
+    passed,
+    passed_got,
+    send_sem,
+    recv_sem,
+):
+    me, beside, across, opposite = corners()
+    loads = [
+        pltpu.make_async_copy(src, dst, load_sem.at[index])
+        for index, (src, dst) in enumerate(((w_gate_in, w_gate), (w_up_in, w_up), (w_down_in, w_down)))
+    ]
+    for copy in loads:
+        copy.start()
+    greet_sides()
+    reduction = SideReduce(blocks, total, beside_got, across_got, passed, passed_got, send_sem, recv_sem)
+    rows = total.shape[0]
+    wide, width = w_down.shape
+    lanes_wide, lanes_out = 384, 1024
+
+    def at_rows(owner):
+        return pl.ds(pl.multiple_of(owner * rows, rows), rows)
+
+    def leaving(owner, slot):
+        return [
+            pltpu.make_async_copy(pre.at[slot, kind], out.at[at_rows(owner)], pre_sem.at[slot, kind])
+            for kind, out in enumerate((gate_out, up_out))
+        ]
+
+    def turn(owner, slot, before):
+        at = at_rows(owner)
+        if before is not None:
+            for copy in leaving(before, slot):
+                copy.wait()
+
+        def hidden_part(index, carry):
+            lanes = pl.ds(pl.multiple_of(index * lanes_wide, 128), lanes_wide)
+            gate_pre = dot_plain(act[at], w_gate[:, lanes])
+            up_pre = dot_plain(act[at], w_up[:, lanes])
+            pre[slot, 0, :, lanes] = gate_pre
+            pre[slot, 1, :, lanes] = up_pre
+            hidden[at, lanes] = (gate_pre * jax.nn.sigmoid(gate_pre) * up_pre).astype(BF16)
+            return carry
+
+        lax.fori_loop(0, wide // lanes_wide, hidden_part, 0)
+        for copy in leaving(owner, slot):
+            copy.start()
+
+        def out_part(index, carry):
+            lanes = pl.ds(pl.multiple_of(index * lanes_out, 128), lanes_out)
+            blocks[at, lanes] = dot_plain(hidden[at], w_down[:, lanes]).astype(BF16)
+            return carry
+
+        lax.fori_loop(0, width // lanes_out, out_part, 0)
+
+    for copy in loads:
+        copy.wait()
+    turn(opposite, 0, None)
+    reduction.copies[0].start()
+    reduction.copies[2].start()
+    turn(beside, 1, None)
+    reduction.copies[1].start()
+    turn(across, 0, opposite)
+    reduction.copies[3].start()
+    reduction.relay()
+    turn(me, 1, beside)
+    keep = pltpu.make_async_copy(hidden, hidden_out, keep_sem)
+    keep.start()
+    reduction.finish()
+    for copy in leaving(across, 0) + leaving(me, 1) + [keep]:
+        copy.wait()
+
+
+def ffn_forward(act, w_gate, w_up, w_down, collective_id):
+    count = lax.axis_size("fsdp")
+    rows, width = act.shape[0] // count, act.shape[1]
+    wide = w_gate.shape[1]
+    assert count == 4 and wide % 384 == 0 and width % 1024 == 0
+    dma = pltpu.SemaphoreType.DMA
+    vmem = pl.BlockSpec(memory_space=pltpu.VMEM)
+    hbm = pl.BlockSpec(memory_space=pl.ANY)
+    pair = pltpu.VMEM((2, rows // 2, width), BF16)
+    column = jax.ShapeDtypeStruct((count * rows, wide), F32)
+    return pl.pallas_call(
+        forward_kernel,
+        out_shape=(
+            jax.ShapeDtypeStruct((rows, width), F32),
+            column,
+            column,
+            jax.ShapeDtypeStruct((count * rows, wide), BF16),
+        ),
+        in_specs=[vmem] + [hbm] * 3,
+        out_specs=[vmem] + [hbm] * 3,
+        scratch_shapes=[pltpu.VMEM(w.shape, BF16) for w in (w_gate, w_up, w_down)]
+        + [
+            dma((3,)),
+            pltpu.VMEM((2, 2, rows, wide), F32),
+            dma((2, 2)),
+            pltpu.VMEM((count * rows, wide), BF16),
+            dma,
+            pltpu.VMEM((count * rows, width), BF16),
+            pair,
+            pair,
+            pair,
+            pair,
+            dma((6,)),
+            dma((6,)),
+        ],
+        compiler_params=pltpu.CompilerParams(
+            collective_id=collective_id, has_side_effects=True, vmem_limit_bytes=58 << 20
+        ),
+        cost_estimate=busy(25),
+    )(act, w_gate, w_up, w_down)
 
 
 def ffn_norm_back(d_act, residual, gain):
@@ -2481,8 +2581,7 @@
     )
     x = x_low.astype(F32)
     res1 = x + mixed
-    terms1, kept1 = ffn_forward(act_all1, gate1, up1, down1)
-    ffn1 = reduced(terms1, 1)
+    ffn1, gate_pre1, up_pre1, hidden1 = ffn_forward(act_all1, gate1, up1, down1, 1)
     h_low = (res1 + ffn1).astype(BF16)
 
     h = h_low.astype(F32)
@@ -2529,9 +2628,8 @@
         return jnp.sum(mask * values * values, axis=0, keepdims=True)
 
     squares = [square(v) for v in (x, mixed, ffn1, h, attn_rows, res2, ffn2, result)]
-    second_gu = lax.psum_scatter(
-        shared_gu.reshape(-1, shared_gu.shape[-1]), "ctx", scatter_dimension=0, tiled=True
-    )
+    d_query, shared_gu = lax.optimization_barrier((d_query, shared_gu))
+    second_gu = lax.psum(shared_gu.reshape(-1, shared_gu.shape[-1]), "ctx")
     d_qn = rounded(d_query)
     grad_qgain = jnp.sum(jnp.sum(d_qn * q_normed, axis=0).reshape(q_heads, head), axis=0)
     d_qpre = norm_heads_back(d_qn * q_gain, q_normed, q_inv, head).astype(BF16)
@@ -2547,7 +2645,6 @@
     gain2 = jnp.sum(d_act2 * normed2, axis=0)
     d_h_low = (d_res2 + norm_back(d_act2 * norm_gains[2], normed2, inv2)).astype(BF16)
 
-    second_gu = lax.all_gather(second_gu, "ctx", axis=0)
     *grads, d_x, conv_small = conv_back(
         (
             x_low,
@@ -2563,8 +2660,8 @@
             attended_low,
             d_attn,
         ),
-        kept1[1:3],
-        (down1, gate1, up1, act_all1, kept1[3], in_full, out_full, projected, convolved),
+        (gate_pre1, up_pre1),
+        (down1, gate1, up1, act_all1, hidden1, in_full, out_full, projected, convolved),
         9,
     )
 

time: 667 us -> 652 us (0.978)
  matrix products: 41.4 us -> 29.6 us
    pallas_call x1, Pallas kernels: 83 us -> 65.4 us  [attend_back(): pl.pallas_call(functools.partial(attend_back_kernel, n_ctx), out_shape=(w...]
    dot_general x7 -> x4, matrix products: 22.2 us -> 9.25 us  [matmul(): return jnp.dot(left_op, right_op, preferred_element_type=F32)]
    pallas_call x1, Pallas kernels: 19.6 us -> 27.8 us  [ffn_forward(): pl.pallas_call(forward_kernel, out_shape=(jax.ShapeDtypeStruct((rows, wid...]
  transfers between devices with their start and end apart: 4 -> 3, of which waited for: 0 -> 1; matrix products, arithmetic and copies ran while one was open for 8% -> 4% of each run, Pallas kernels for 41% -> 31%
where the time goes in v13:
time: 652 us; the launch traced here: 643 us
  Pallas kernels  542 us (83%)
  other arithmetic  32.9 us (5%)
  matrix products  29.6 us (5%)
  local copies, waits for them, and re-layouts  20.2 us (3%)
  between operations  15.9 us (2%)
    pallas_call x1, Pallas kernels, summed_gradients(): pl.pallas_call(functools.partial(tail_kernel, (n_ctx, n_fsdp)), out_shape...  179 us
    pallas_call x1, Pallas kernels, front(): pl.pallas_call(functools.partial(front_kernel, n_ctx), out_shape=tuple((j...  100 us
    pallas_call x1, Pallas kernels, conv_back(): pl.pallas_call(functools.partial(back_kernel, n_ctx), out_shape=(column,...  68.3 us
    pallas_call x1, Pallas kernels, attend_back(): pl.pallas_call(functools.partial(attend_back_kernel, n_ctx), out_shape=(w...  65.4 us
    pallas_call x1, Pallas kernels, attend(): pl.pallas_call(functools.partial(attend_kernel, n_ctx), out_shape=(jax.Sh...  53.9 us
    pallas_call x1, Pallas kernels, ffn_turn(): pl.pallas_call(turn_kernel, out_shape=(jax.ShapeDtypeStruct(whole, BF16),...  47.7 us
    pallas_call x1, Pallas kernels, ffn_forward(): pl.pallas_call(forward_kernel, out_shape=(jax.ShapeDtypeStruct((rows, wid...  27.8 us
  transfers between devices with their start and end apart: 3, of which 1 were waited for; matrix products, arithmetic and copies ran while one was open for 4% of the time, Pallas kernels for 31%

profile of v13, /device:TPU:0, one launch (start us, length us, event | category | flops | bytes accessed | tf_op | source)
XLA Modules:
  0.0 643.2 jit_solution(6636975399051080304)
XLA Ops:
  9.8 100.2 %shard_map.262 = (bf16[1024,3072]{1,0:T(8,128)(2,1)}, bf16[1024,1024]{1,0:T(8,128)(2,1)}, bf16[1024,1152]{1,0:T(8,128)(2,1)}, bf16[1024,1152]{1,0:T(8,128)(2,1)}...) custom-call(bf16[256,1024]{1,0:T(8,128)(2,1)} %dynamic-slice_bitcast, ...), custom_call_target="tpu_custom_call" | custom-call | flops 70 | bytes 65536 | tf_op jit(solution)/shard_map/pallas_call | solution.py:1715
  110.1 27.8 %shard_map.263 = (f32[256,1024]{1,0:T(8,128)}, f32[1024,1152]{1,0:T(8,128)}, f32[1024,1152]{1,0:T(8,128)}, bf16[1024,1152]{1,0:T(8,128)(2,1)}) custom-call(bf16[1024,1024]{1,0:T(8,128)(2,1)} %get-tuple-element.62.act.act_in, bf16[1024,1152]{1,0:T(8,128)(2,1)} %get-tuple-element.63.w_gate_in, bf16[1024,1152]{1,0:T(8,128)(2,1)} %get-tuple-element.64.w_up_in, ...), custom_call_target="tpu_custom_call" | custom-call | flops 25 | bytes 65536 | tf_op jit(solution)/shard_map/pallas_call | solution.py:2497
  139.4 2.3 fusion.46
  142.7 2.5 fusion.6
  146.0 2.1 multiply_convert_fusion.1
  154.2 53.9 %shard_map.264 = (f32[256,1024]{1,0:T(8,128)}, f32[16,1,256]{2,1,0:T(1,128)}, bf16[1024,1024]{1,0:T(8,128)(2,1)}, bf16[1024,1024]{1,0:T(8,128)(2,1)}, bf16[1024,...) custom-call(s32[1]{0:T(128)} %dynamic_slice.27.length_ref, ...), custom_call_target="tpu_custom_call" | custom-call | flops 50 | bytes 65536 | tf_op jit(solution)/shard_map/pallas_call | solution.py:1259
  209.4 3.5 multiply_reduce_fusion.2
  213.9 47.7 %shard_map.265 = (bf16[1024,1024]{1,0:T(8,128)(2,1)}, f32[256,1024]{1,0:T(8,128)}, bf16[4,4,2,32,1152]{4,3,2,1,0:T(8,128)(2,1)}, bf16[576,1024]{1,0:T(8,128)(2,1)}) custom-call(bf16[256,1024]{1,0:T(8,128)(2,1)} %multiply_convert_fusion.act_block, bf16[1024,1152]{1,0:T(8,128)(2,1)} %get-tuple-element.68.w_gate_in, ...), custom_call_target="tpu_custom_call" | custom-call | flops 45 | bytes 65536 | tf_op jit(solution)/shard_map/pallas_call | solution.py:1968
  263.9 3.7 convert_multiply_fusion.7
  267.5 2.5 copy.31
  272.0 65.4 %shard_map.266 = (f32[256,1024]{1,0:T(8,128)}, f32[256,1024]{1,0:T(8,128)}, f32[256,1024]{1,0:T(8,128)}) custom-call(s32[1]{0:T(128)} %dynamic_slice.27.length_ref, bf16[256,1024]{1,0:T(8,128)(2,1)} %get-tuple-element.124.query, bf16[1024,1024]{1,0:T(8,128)(2,1)} %get-tuple-element.73.kv_all, bf16[256,1024]{1,0:T(8,128)(2,1)} %get-tuple-element.152.d_out, ...), custom_call_target="tpu_custom_call" | custom-call | flops 50 | bytes 65536 | tf_op jit(solution)/shard_map/pallas_call | solution.py:1414
  337.4 2.1 convert_element_type.125
  344.3 2.4 fusion.16.d_query
  348.7 2.3 fusion.4
  353.0 2.2 fusion.45
  355.6 2.1 fusion.38
  357.7 68.3 %shard_map.267 = (bf16[1024,1152]{1,0:T(8,128)(2,1)}, bf16[1024,1152]{1,0:T(8,128)(2,1)}, bf16[1152,1024]{1,0:T(8,128)(2,1)}, bf16[1024,1024]{1,0:T(8,128)(2,1)}...) custom-call(bf16[256,1024]{1,0:T(8,128)(2,1)} %dynamic-slice_bitcast, ...), custom_call_target="tpu_custom_call" | custom-call | flops 55 | bytes 65536 | tf_op jit(solution)/shard_map/pallas_call | solution.py:2340
  429.6 2.5 concatenate.33
  432.2 2.4 maximum_select_fusion
  434.5 2.5 all-reduce.4.cloned.1.call-done.second_gu_in
  437.1 178.8 %shard_map.268 = (bf16[2,256,4608]{2,1,0:T(8,128)(2,1)}, bf16[1152,1024]{1,0:T(8,128)(2,1)}, bf16[2,960,1024]{2,1,0:T(8,128)(2,1)}) custom-call(bf16[1024,1152]{1,0:T(8,128)(2,1)} %get-tuple-element.91.gate_in, bf16[1024,1152]{1,0:T(8,128)(2,1)} %get-tuple-element.92.up_in, bf16[1152,1024]{1,0:T(8,128)(2,1)} %get-tuple-element.93.down_in, ...), custom_call_target="tpu_custom_call" | custom-call | flops 160 | bytes 65536 | tf_op jit(solution)/shard_map/pallas_call | solution.py:819
  616.7 4.4 fusion.86
  625.0 5.0 slice_convert_fusion
  630.0 2.7 bitcast_convert_fusion
  (149 shorter events, 38.1 us)
Async XLA Ops:
  7.2 135.5 %all-gather.2.cloned.1.call-start = ((), (), s32[]{:S(2)}) async-start(), calls=%async_computation | async-start | bytes 6488064 | tf_op jit(solution)/shard_map/all_gather | solution.py:2567
  8.9 428.1 %all-reduce.4.cloned.1.call-start = ((), (), s32[]{:S(2)}) async-start(), calls=%async_computation.1 | async-start | bytes 4718592 | tf_op jit(solution)/shard_map/psum | solution.py:2632
  110.0 27.9 %copy-start.31 = (f32[2,64]{1,0:T(2,128)S(1)}, f32[2,64]{1,0:T(2,128)}, u32[]{:S(2)}) copy-start(f32[2,64]{1,0:T(2,128)} %param.26) | copy-start | bytes 1540
  110.0 28.1 %copy-start.32 = (s32[8]{0:T(128)S(1)}, s32[8]{0:T(128)}, u32[]{:S(2)}) copy-start(s32[8]{0:T(128)} %param.17) | copy-start | bytes 100
  110.0 29.3 %copy-start = (f32[256,1024]{1,0:T(8,128)S(1)}, f32[256,1024]{1,0:T(8,128)}, u32[]{:S(2)}) copy-start(f32[256,1024]{1,0:T(8,128)} %get-tuple-element.61.mixed) | copy-start | bytes 3145732
  110.0 29.3 %copy-start.29 = (bf16[2,256,1024]{2,1,0:T(8,128)(2,1)S(1)}, bf16[2,256,1024]{2,1,0:T(8,128)(2,1)}, u32[]{:S(2)}) copy-start(bf16[2,256,1024]{2,1,0:T(8,128)(2,1)} %param.16) | copy-start | bytes 3145732
  137.9 3.8 copy-start.30
  142.6 9.1 %copy-start.21 = (bf16[256,1024]{1,0:T(8,128)(2,1)}, bf16[256,1024]{1,0:T(8,128)(2,1)S(1)}, u32[]{:S(2)}) copy-start(bf16[256,1024]{1,0:T(8,128)(2,1)S(1)} %fusion.39.act_qkv) | copy-start | bytes 1572868
  154.2 55.2 %copy-start.9 = (bf16[256,1024]{1,0:T(8,128)(2,1)S(1)}, bf16[256,1024]{1,0:T(8,128)(2,1)}, u32[]{:S(2)}) copy-start(bf16[256,1024]{1,0:T(8,128)(2,1)} %copy-done.8) | copy-start | bytes 1572868
  209.4 3.5 copy-start.12
  263.9 3.7 copy-start.11
  342.4 4.4 copy-start.3
  344.3 3.5 copy-start.28
  346.7 4.3 copy-start.22
  351.0 4.1 copy-start.27
  357.7 68.3 %copy-start.13 = (bf16[256,1024]{1,0:T(8,128)(2,1)}, bf16[256,1024]{1,0:T(8,128)(2,1)S(1)}, u32[]{:S(2)}) copy-start(bf16[256,1024]{1,0:T(8,128)(2,1)S(1)} %get-tuple-element.119) | copy-start | bytes 1572868
  357.7 71.3 %copy-start.5 = (bf16[256,1024]{1,0:T(8,128)(2,1)S(1)}, bf16[256,1024]{1,0:T(8,128)(2,1)}, u32[]{:S(2)}) copy-start(bf16[256,1024]{1,0:T(8,128)(2,1)} %convert_element_type.125) | copy-start | bytes 1572868
  426.0 3.2 copy-start.4
  426.0 6.2 copy-start.26
  426.9 5.3 copy-start.14
  426.9 5.3 collective-permute-start
  615.9 9.2 %slice-start = ((s8[4718592]{0:T(1024)(128)(4,1)}), s8[4194304]{0:T(1024)(128)(4,1)S(1)}, s32[]{:S(2)}) async-start(s8[4718592]{0:T(1024)(128)(4,1)} %bitcast.68), calls=%async_computation.2 | async-start | bytes 8388608
  616.7 8.3 %slice-start.1 = ((s8[4718592]{0:T(1024)(128)(4,1)}), s8[524288]{0:T(1024)(128)(4,1)S(1)}, s32[]{:S(2)}) async-start(s8[4718592]{0:T(1024)(128)(4,1)} %bitcast.68), calls=%async_computation.3 | async-start | bytes 1048576
  625.0 5.0 copy-start.18
  (14 other events, 27.8 us)
Sparse Core Ops, SparseCore 0:
  11.5 90.3 all-gather.1
  342.5 94.5 all-reduce.3
